TPU v7x, 32 devices: a whole 2x2x4 slice. The times are simulated.
32 devices in a mesh: wide: 4 (over x, core), narrow: 8 (over z, y).
Axes of the slice: x: 2, y: 2, z: 4, core: 2. Of those that a mesh axis runs over, the one named last changes fastest.
Arguments:
- stream: bfloat16 [8256, 1152], P('wide', 'narrow'), may hold values from -6 to 6
- skip_in: bfloat16 [8256, 1152], P('wide', 'narrow'), may hold values from -6 to 6
- cotangent: bfloat16 [8256, 1152], P('wide', 'narrow'), may hold values from -6 to 6
- skip_weight: bfloat16 [2, 1152, 1152], P(None, 'narrow'), may hold values from -0.125 to 0.125
- qkv_weight: bfloat16 [1152, 3, 1152], P(None, None, 'narrow'), may hold values from -0.1875 to 0.1875
- out_weight: bfloat16 [1152, 1152], P('narrow'), may hold values from -1.5 to 1.5
- up_weight: bfloat16 [1152, 4608], P(None, 'narrow'), may hold values from -0.1875 to 0.1875
- down_weight: bfloat16 [4608, 1152], P('narrow'), may hold values from -0.09375 to 0.09375
- norm_gain: float32 [2, 1152], replicated, may hold values from 0.5 to 1.5
- norm_bias: float32 [2, 1152], replicated, may hold values from -3 to 3
- row_skip: float32 [2, 1152], P(None, 'narrow'), may hold values from 7.5 to 12000
- col_skip: float32 [1152], replicated, may hold values from 30 to 3000
- row_qkv: float32 [1152], replicated, may hold values from 30 to 3000
- col_qkv: float32 [3, 1152], P(None, 'narrow'), may hold values from 7.5 to 12000
- row_out: float32 [1152], P('narrow'), may hold values from 7.5 to 12000
- col_out: float32 [1152], replicated, may hold values from 30 to 3000
- row_up: float32 [1152], replicated, may hold values from 30 to 3000
- col_up: float32 [4608], P('narrow'), may hold values from 7.5 to 12000
- row_down: float32 [4608], P('narrow'), may hold values from 7.5 to 12000
- col_down: float32 [1152], replicated, may hold values from 30 to 3000
- second_gain: float32 [2, 1152], replicated, may hold values from 100 to 10000
- second_bias: float32 [2, 1152], replicated, may hold values from 100 to 10000
Outputs:
- block_out: bfloat16 [8256, 1152], P('wide', 'narrow')
- grad_stream: float32 [8256, 1152], P('wide', 'narrow')
- grad_skip_in: float32 [8256, 1152], P('wide', 'narrow')
- grad_skip_weight: float32 [2, 1152, 1152], P(None, 'narrow', 'wide')
- grad_qkv_weight: float32 [1152, 3, 1152], P('wide', None, 'narrow')
- grad_out_weight: float32 [1152, 1152], P('narrow', 'wide')
- grad_up_weight: float32 [1152, 4608], P('wide', 'narrow')
- grad_down_weight: float32 [4608, 1152], P('narrow', 'wide')
- grad_norm_gain: float32 [2, 1152], replicated
- grad_norm_bias: float32 [2, 1152], replicated
- new_row_skip: float32 [2, 1152], P(None, 'narrow')
- new_col_skip: float32 [1152], replicated
- new_row_qkv: float32 [1152], replicated
- new_col_qkv: float32 [3, 1152], P(None, 'narrow')
- new_row_out: float32 [1152], P('narrow')
- new_col_out: float32 [1152], replicated
- new_row_up: float32 [1152], replicated
- new_col_up: float32 [4608], P('narrow')
- new_row_down: float32 [4608], P('narrow')
- new_col_down: float32 [1152], replicated
- new_second_gain: float32 [2, 1152], replicated
- new_second_bias_one: float32 [1152], replicated
- new_second_bias_two: float32 [1152], replicated
- new_skip_weight: float32 [2, 1152, 1152], P(None, 'narrow')
- new_qkv_weight: float32 [1152, 3, 1152], P(None, None, 'narrow')
- out_weight_step: float32 [1152, 1152], P('narrow')
- new_up_weight: float32 [1152, 4608], P(None, 'narrow')
- new_down_weight: float32 [4608, 1152], P('narrow')
- norm_gain_step: float32 [2, 1152], replicated
- norm_bias_step: float32 [2, 1152], replicated
- clip_ratio: float32 [5], replicated
All inputs are finite; a program needn't handle non-finite values.
Results may differ from a plain program's by a relative error of at most 0.023.
Values may be sent and summed in bfloat16 or wider, within the bound.
No kernel may reach another device: no remote copies, remote signals or barrier semaphores. Data moves between devices by JAX's collectives and lax.ppermute only.
A program may use at most 192 MiB of HBM per device.

v0:
```python
import math

import jax
import jax.numpy as jnp
from jax import lax
from jax.sharding import PartitionSpec as P

D = 1152
FF = 4608
SEQ = 258
HEAD = 72


NORM_EPS = 1e-05
EPS_SQUARE = 1e-30
DECAY = 0.5
STEP_RATE = 0.05
CLIP_LEVEL = 0.25


def layer_norm(values, gain, shift):
    average = jnp.mean(values, axis=-1, keepdims=True)
    centered = values - average
    variance = jnp.mean(centered * centered, axis=-1, keepdims=True)
    return centered * lax.rsqrt(variance + NORM_EPS) * gain + shift


def norm_back(values, grad, gain, own_rows):
    average = jnp.mean(values, axis=-1, keepdims=True)
    centered = values - average
    variance = jnp.mean(centered * centered, axis=-1, keepdims=True)
    inverse = lax.rsqrt(variance + NORM_EPS)
    unit = centered * inverse
    scaled = grad * gain
    inner = (
        scaled
        - jnp.mean(scaled, axis=-1, keepdims=True)
        - unit * jnp.mean(scaled * unit, axis=-1, keepdims=True)
    )
    weighted = grad * own_rows
    return (inner * inverse, jnp.sum(weighted * unit, axis=0), jnp.sum(weighted, axis=0))


def gelu_exact(inputs):
    return jax.nn.gelu(inputs, approximate=False)


def matmul(left, right, form):
    return jnp.einsum(form, left, right, preferred_element_type=jnp.float32)


def plain_update(grad, second_old):
    second_new = DECAY * second_old + (1.0 - DECAY) * (grad * grad + EPS_SQUARE)
    update = grad * lax.rsqrt(second_new)
    spread = jnp.sqrt(jnp.mean(update * update))
    update = update / jnp.maximum(1.0, spread / CLIP_LEVEL)
    return (second_new, -(STEP_RATE * update))


def wide_slice(array, dim_index, count, wide_index):
    piece_size = array.shape[dim_index] // count
    return lax.dynamic_slice_in_dim(array, wide_index * piece_size, piece_size, dim_index)


def local(
    stream,
    skip_in,
    cotangent,
    skip_weight,
    qkv_weight,
    out_weight,
    up_weight,
    down_weight,
    norm_gain,
    norm_bias,
    row_skip,
    col_skip,
    row_qkv,
    col_qkv,
    row_out,
    col_out,
    row_up,
    col_up,
    row_down,
    col_down,
    second_gain,
    second_bias,
):
    rows_local, feat_local = stream.shape
    images = rows_local // SEQ
    heads_local = feat_local // HEAD
    scale_factor = 1.0 / math.sqrt(HEAD)
    split_shape = (images, SEQ, heads_local, HEAD)
    narrow_count = lax.axis_size("narrow")
    narrow_index = lax.axis_index("narrow")
    share_rows = -(-rows_local // narrow_count)
    row_start = narrow_index * share_rows
    row_ids = lax.broadcasted_iota(jnp.int32, (rows_local, 1), 0)
    own_mask = ((row_ids >= row_start) & (row_ids < row_start + share_rows)).astype(jnp.float32)

    def full_sum(values):
        return lax.psum(values, "narrow")

    partial_in = matmul(stream, skip_weight[0], "rc,cd->rd") + matmul(
        skip_in, skip_weight[1], "rc,cd->rd"
    )
    hidden_in = full_sum(partial_in)
    normed = layer_norm(hidden_in, norm_gain[0], norm_bias[0]).astype(jnp.bfloat16)
    projected = matmul(normed, qkv_weight, "rd,dtc->rtc").astype(jnp.bfloat16)
    queries = projected[:, 0].reshape(split_shape)
    key_vectors = projected[:, 1].reshape(split_shape)
    value_vectors = projected[:, 2].reshape(split_shape)
    scores = matmul(queries, key_vectors, "bqhe,bkhe->bhqk") * scale_factor
    row_max = jnp.max(scores, axis=-1, keepdims=True)
    exponent = jnp.exp(scores - row_max)
    row_total = jnp.sum(exponent, axis=-1, keepdims=True)
    log_total = row_max + jnp.log(row_total)
    probs_low = (exponent / row_total).astype(jnp.bfloat16)
    attended = (
        matmul(probs_low, value_vectors, "bhqk,bkhe->bqhe")
        .reshape(rows_local, feat_local)
        .astype(jnp.bfloat16)
    )
    attn_part = matmul(attended, out_weight, "rc,cd->rd")
    middle = hidden_in + full_sum(attn_part)
    mixed_in = layer_norm(middle, norm_gain[1], norm_bias[1]).astype(jnp.bfloat16)
    middle_own = lax.dynamic_slice_in_dim(middle, narrow_index * feat_local, feat_local, 1)
    up_input = matmul(mixed_in, up_weight, "rd,df->rf")
    activation = gelu_exact(up_input).astype(jnp.bfloat16)
    down_part = matmul(activation, down_weight, "rf,fd->rd")
    block_out = (
        middle_own + lax.psum_scatter(down_part, "narrow", scatter_dimension=1, tiled=True)
    ).astype(jnp.bfloat16)
    grad_full = lax.all_gather(cotangent, "narrow", axis=1, tiled=True)
    grad_down = matmul(activation, grad_full, "rf,rd->fd")
    grad_act = matmul(grad_full, down_weight, "rd,fd->rf")
    gelu_value, gelu_back = jax.vjp(gelu_exact, up_input)
    grad_up_in = gelu_back(grad_act)[0].astype(jnp.bfloat16)
    grad_up = matmul(mixed_in, grad_up_in, "rd,rf->df")
    mixed_part = matmul(grad_up_in, up_weight, "rf,df->rd")
    grad_mixed = full_sum(mixed_part)
    back_middle, back_gain_two, back_bias_two = norm_back(
        middle, grad_mixed, norm_gain[1], own_mask
    )
    grad_middle = grad_full.astype(jnp.float32) + back_middle
    middle_low = grad_middle.astype(jnp.bfloat16)
    grad_out = matmul(attended, middle_low, "rc,rd->cd")
    grad_attended = (
        matmul(middle_low, out_weight, "rd,cd->rc").astype(jnp.bfloat16).reshape(split_shape)
    )
    scores_again = matmul(queries, key_vectors, "bqhe,bkhe->bhqk") * scale_factor
    probs = jnp.exp(scores_again - log_total)
    probs_again = probs.astype(jnp.bfloat16)
    grad_values = matmul(probs_again, grad_attended, "bhqk,bqhe->bkhe")
    grad_probs = matmul(grad_attended, value_vectors, "bqhe,bkhe->bhqk")
    inner_sum = jnp.sum(probs * grad_probs, axis=-1, keepdims=True)
    grad_scores = (probs * (grad_probs - inner_sum) * scale_factor).astype(jnp.bfloat16)
    grad_queries = matmul(grad_scores, key_vectors, "bhqk,bkhe->bqhe")
    grad_keys = matmul(grad_scores, queries, "bhqk,bqhe->bkhe")
    grad_projected = jnp.stack(
        [
            grad_queries.reshape(rows_local, feat_local),
            grad_keys.reshape(rows_local, feat_local),
            grad_values.reshape(rows_local, feat_local),
        ],
        axis=1,
    ).astype(jnp.bfloat16)
    grad_qkv = matmul(normed, grad_projected, "rd,rtc->dtc")
    normed_part = matmul(grad_projected, qkv_weight, "rtc,dtc->rd")
    grad_normed = full_sum(normed_part)
    back_hidden, back_gain_one, back_bias_one = norm_back(
        hidden_in, grad_normed, norm_gain[0], own_mask
    )
    hidden_low = (grad_middle + back_hidden).astype(jnp.bfloat16)
    grad_skip = jnp.stack(
        [matmul(stream, hidden_low, "rc,rd->cd"), matmul(skip_in, hidden_low, "rc,rd->cd")]
    )
    grad_stream = matmul(hidden_low, skip_weight[0], "rd,cd->rc")
    grad_skip_in = matmul(hidden_low, skip_weight[1], "rd,cd->rc")
    gain_grads = jnp.stack([back_gain_one, back_gain_two])
    bias_grads = jnp.stack([back_bias_one, back_bias_two])
    wide_count = lax.axis_size("wide")
    wide_index = lax.axis_index("wide")
    wide_dims = (2, 0, 1, 0, 1)
    wide_axes = ((0, 1), (1, 2), (0,), (1,), (0,))
    narrow_axes = ((2,), (0,), (1,), (0,), (1,))
    wide_counts = (2 * D, 3 * D, D, FF, FF)
    row_along_wide = (False, True, False, True, False)
    entry_counts = (2 * D * D, 3 * D * D, D * D, D * FF, FF * D)
    old_slots = (0, 0, 1, 0, 2)
    weights = (skip_weight, qkv_weight, out_weight, up_weight, down_weight)
    old_wide = (col_skip, row_qkv, col_out, row_up, col_down)
    old_narrow = (row_skip, col_qkv, row_out, col_up, row_down)
    summed = lax.psum(
        (grad_skip, grad_qkv, grad_out, grad_up, grad_down, gain_grads, bias_grads), "wide"
    )
    pieces = summed[:5]
    gain_section = summed[5]
    bias_section = summed[6]
    squares = [piece * piece + EPS_SQUARE for piece in pieces]
    wide_parts = [jnp.sum(squares[number], axis=wide_axes[number]) for number in range(5)]
    narrow_parts = [jnp.sum(squares[number], axis=narrow_axes[number]) for number in range(5)]
    old_sums = jnp.stack([jnp.sum(row_skip), jnp.sum(row_out), jnp.sum(row_down)])
    stat_total = lax.psum(
        (
            wide_parts[0],
            wide_parts[1],
            wide_parts[2],
            wide_parts[3],
            wide_parts[4],
            old_sums,
            gain_section,
            bias_section,
        ),
        "narrow",
    )
    old_row_means = (stat_total[5][0] / (2 * D), stat_total[5][1] / D, stat_total[5][2] / FF)
    wide_stats = stat_total[:5]
    gain_total = stat_total[6]
    bias_total = stat_total[7]
    new_wide = []
    new_narrow = []
    updates = []
    for number in range(5):
        wide_mean = wide_stats[number] / wide_counts[number]
        wide_new = DECAY * old_wide[number] + (1.0 - DECAY) * wide_mean
        narrow_new = DECAY * old_narrow[number] + (1.0 - DECAY) * narrow_parts[number] / D
        if row_along_wide[number]:
            row_mean = jnp.mean(wide_new)
        else:
            row_mean = DECAY * old_row_means[old_slots[number]] + (1.0 - DECAY) * jnp.mean(
                wide_mean
            )
        dim_index = wide_dims[number]
        piece_size = pieces[number].shape[dim_index]
        broadcast_shape = [1] * pieces[number].ndim
        broadcast_shape[dim_index] = piece_size
        second = (
            jnp.expand_dims(narrow_new, dim_index) * wide_new.reshape(broadcast_shape) / row_mean
        )
        updates.append(pieces[number] * lax.rsqrt(second))
        new_wide.append(wide_new)
        new_narrow.append(narrow_new)
    update_squares = jnp.stack([jnp.sum(update * update) for update in updates])
    square_totals = lax.psum(update_squares, "narrow")
    counts_array = jnp.array(entry_counts, jnp.float32)
    clip_ratio = jnp.sqrt(square_totals / counts_array) / CLIP_LEVEL
    new_pieces = []
    for number in range(5):
        spread = jnp.sqrt(square_totals[number] / entry_counts[number])
        step_piece = -(STEP_RATE * (updates[number] / jnp.maximum(1.0, spread / CLIP_LEVEL)))
        if number == 2:
            new_pieces.append(step_piece)
        else:
            weight_piece = weights[number]
            new_pieces.append(weight_piece.astype(jnp.float32) + step_piece)
    grad_outs = [
        wide_slice(pieces[number], wide_dims[number], wide_count, wide_index) for number in range(5)
    ]
    new_second_gain, gain_step = plain_update(gain_total, second_gain)
    new_second_bias, bias_step = plain_update(bias_total, second_bias)
    return (
        block_out,
        grad_stream,
        grad_skip_in,
        grad_outs[0],
        grad_outs[1],
        grad_outs[2],
        grad_outs[3],
        grad_outs[4],
        gain_total,
        bias_total,
        new_narrow[0],
        new_wide[0],
        new_wide[1],
        new_narrow[1],
        new_narrow[2],
        new_wide[2],
        new_wide[3],
        new_narrow[3],
        new_narrow[4],
        new_wide[4],
        new_second_gain,
        new_second_bias[0],
        new_second_bias[1],
        new_pieces[0],
        new_pieces[1],
        new_pieces[2],
        new_pieces[3],
        new_pieces[4],
        gain_step,
        bias_step,
        clip_ratio,
    )


def solution(mesh):
    in_specs = (
        P("wide", "narrow"),
        P("wide", "narrow"),
        P("wide", "narrow"),
        P(None, "narrow", None),
        P(None, None, "narrow"),
        P("narrow", None),
        P(None, "narrow"),
        P("narrow", None),
        P(),
        P(),
        P(None, "narrow"),
        P(),
        P(),
        P(None, "narrow"),
        P("narrow"),
        P(),
        P(),
        P("narrow"),
        P("narrow"),
        P(),
        P(),
        P(),
    )
    out_specs = (
        P("wide", "narrow"),
        P("wide", "narrow"),
        P("wide", "narrow"),
        P(None, "narrow", "wide"),
        P("wide", None, "narrow"),
        P("narrow", "wide"),
        P("wide", "narrow"),
        P("narrow", "wide"),
        P(),
        P(),
        P(None, "narrow"),
        P(),
        P(),
        P(None, "narrow"),
        P("narrow"),
        P(),
        P(),
        P("narrow"),
        P("narrow"),
        P(),
        P(),
        P(),
        P(),
        P(None, "narrow", None),
        P(None, None, "narrow"),
        P("narrow", None),
        P(None, "narrow"),
        P("narrow", None),
        P(),
        P(),
        P(),
    )
    return jax.shard_map(local, mesh=mesh, in_specs=in_specs, out_specs=out_specs, check_vma=False)
```

profile of v0, /device:TPU:0, one launch (start us, length us, event | category | flops | bytes accessed | tf_op | source)
XLA Modules:
  0.0 1932.7 jit_solution(12931089210974659093)
XLA Ops:
  8.3 2.6 fusion.79
  10.9 5.3 convolution_add_fusion
  16.9 302.8 %all-reduce.10.cloned.1.call-done = f32[2064,1152]{1,0:T(8,128)} async-done(((f32[2064,1152]{1,0:T(8,128)}), f32[2064,1152]{1,0:T(8,128)}) %all-reduce.10.cloned.1.call-update) | async-done | bytes 9510928 | tf_op jit(solution)/shard_map/psum | solution.py:102
  319.7 4.2 reduce_sum.367
  323.9 5.0 multiply_reduce_fusion.5
  330.3 1.8 add_convert_fusion.2
  332.2 2.8 fusion.103
  338.2 3.0 reshape_squeeze.10
  346.4 6.5 fusion.104
  353.7 299.1 %all-reduce.12.cloned.1.call-done = f32[2064,1152]{1,0:T(8,128)} async-done(((f32[2064,1152]{1,0:T(8,128)}), f32[2064,1152]{1,0:T(8,128)}) %all-reduce.12.cloned.1.call-update) | async-done | bytes 9510928 | tf_op jit(solution)/shard_map/psum | solution.py:102
  652.8 11.2 fusion.99
  664.0 5.0 multiply_reduce_fusion.4
  670.5 2.0 add_convert_fusion.1
  672.5 2.3 copy-done.17
  674.8 5.3 fusion.105
  680.1 57.5 %all-gather.2.cloned.1.call-done = bf16[2064,1152]{0,1:T(8,128)(2,1)} async-done(((bf16[2064,144]{0,1:T(8,128)(2,1)}), bf16[2064,1152]{0,1:T(8,128)(2,1)}) %all-gather.2.cloned.1.call-update) | async-done | bytes 4755472 | tf_op jit(solution)/shard_map/all_gather | solution.py:134
  737.6 18.6 add_convert_fusion.3
  757.6 7.0 fusion.106
  764.7 8.6 copy.98
  773.3 290.3 %all-reduce.14.cloned.1.call-done = f32[2064,1152]{1,0:T(8,128)} async-done(((f32[2064,1152]{1,0:T(8,128)}), f32[2064,1152]{1,0:T(8,128)}) %all-reduce.14.cloned.1.call-update) | async-done | bytes 9510928 | tf_op jit(solution)/shard_map/psum | solution.py:102
  1063.6 10.4 multiply_reduce_fusion
  1074.1 9.6 multiply_add_fusion
  1083.7 3.7 copy-done.3
  1090.1 4.1 fusion.63
  1094.2 4.3 fusion.56
  1098.5 12.9 fusion.53
  1111.4 12.3 fusion.50
  1129.0 7.8 convolution_bitcast_fusion
  1136.8 4.5 multiply_convert_fusion.1
  1141.3 6.6 convolution_bitcast_fusion.1
  1148.3 8.4 fusion.109
  1156.6 7.7 fusion.107
  1164.4 1.9 fusion.31
  1166.3 4.0 fusion.108
  1170.4 266.3 %all-reduce.16.cloned.1.call-done = f32[2064,1152]{1,0:T(8,128)} async-done(((f32[2064,1152]{1,0:T(8,128)}), f32[2064,1152]{1,0:T(8,128)}) %all-reduce.16.cloned.1.call-update) | async-done | bytes 9510928 | tf_op jit(solution)/shard_map/psum | solution.py:102
  1436.6 10.6 multiply_reduce_fusion.1
  1447.3 10.6 add_convert_fusion
  1461.7 150.0 %reduce-scatter.4.cloned.1.call-done = f32[144,2064]{1,0:T(8,128)} async-done(((f32[1152,2064]{1,0:T(8,128)}), f32[144,2064]{1,0:T(8,128)}) %reduce-scatter.4.cloned.1.call-update) | async-done | bytes 1188880
  1611.8 2.2 copy.119
  1614.0 3.6 add_convert_fusion.4
  1617.6 2.3 copy.110
  1619.9 12.4 all-reduce.2
  1632.3 5.3 fusion.74
  1637.6 2.7 fusion.77
  1640.3 144.3 %all-reduce.18.cloned.1.call-done = (f32[2,144,1152]{2,1,0:T(8,128)}, f32[1152,3,144]{0,2,1:T(8,128)}, f32[144,1152]{1,0:T(8,128)}, f32[1152,576]{0,1:T(8,128)}, f32[576,1152]{1,0:T(8,128)}) async-done(((f32[2,144,1152]{2,1,0:T(8,128)}, f32[1152,3,144]{0,2,1:T(8,128)}, f32[144,1152]{1,0:T(8,128)}, f32[1152,576]{0,1:T(8,128)}, f32[576,1152]{1,0:T(8,128)}), (f32[2,144,1152]{2,1,0:T(8,128)}, ...) | async-done | bytes 9289744 | tf_op jit(solution)/shard_map/psum | solution.py:194
  1786.0 1.8 fusion.60
  1787.9 1.8 constant_dynamic-slice_fusion.2
  1789.6 2.0 constant_dynamic-slice_fusion.4
  1791.7 2.1 fusion.38
  1793.8 2.3 constant_dynamic-slice_fusion.3
  1801.4 2.0 pad_maximum_fusion.3
  1803.4 37.8 %all-reduce.1 = (f32[1152]{0:T(1024)S(1)}, f32[1152]{0:T(1024)S(1)}, f32[1152]{0:T(1024)S(1)}, f32[1152]{0:T(1024)S(1)}, f32[1152]{0:T(1024)S(1)}, /*index=5*/f32[3]{0:T(128)S(1)}) all-reduce(f32[1152]{0:T(1024)S(1)} %get-tuple-element.138, f32[1152]{0:T(1024)S(1)} %get-tuple-element.137, ...), channel_id=1, replica_groups=mesh['wide'=4,'narrow'=8] {'narrow'}, use_global_device_ids=true, to_apply=%region_31.0 | all-reduce | flops 5763 | bytes 46104 | tf_op jit(solution)/shard_map/psum | solution.py:204
  1849.0 2.4 multiply_reduce_fusion.15
  1851.4 2.8 multiply_reduce_fusion.14
  1854.3 3.3 multiply_reduce_fusion.13
  1860.2 3.3 stack.80
  1863.5 33.0 %all-reduce = (f32[2,1152]{1,0:T(2,128)S(1)}, f32[2,1152]{1,0:T(2,128)S(1)}, f32[5]{0:T(128)S(1)}) all-reduce(f32[2,1152]{1,0:T(2,128)S(1)} %get-tuple-element.157, f32[2,1152]{1,0:T(2,128)S(1)} %get-tuple-element.158, f32[5]{0:T(128)S(1)} %stack.80), channel_id=1, replica_groups=mesh['wide'=4,'narrow'=8] {'narrow'}, use_global_device_ids=true, to_apply=%region_24.0 | all-reduce | flops 4613 | bytes 36904 | tf_op jit(solution)/shard_map/psum | solution.py:204
  1905.0 2.1 multiply_negate_fusion.1
  1907.2 3.0 negate_add_fusion.3
  1910.2 1.9 negate_add_fusion.2
  1912.1 2.3 copy.111
  1914.4 4.4 negate_add_fusion.1
  1918.9 2.3 copy.112
  1921.2 3.6 negate_add_fusion
  (222 shorter events, 43.6 us)
Async XLA Ops:
  7.2 3.6 copy-start.12
  7.2 312.4 %all-reduce.10.cloned.1.call-start = ((), (), s32[]{:S(2)}) async-start(), calls=%async_computation.1 | async-start | bytes 19021824 | tf_op jit(solution)/shard_map/psum | solution.py:102
  16.2 636.7 %all-reduce.12.cloned.1.call-start = ((), (), s32[]{:S(2)}) async-start(), calls=%async_computation.2 | async-start | bytes 19021824 | tf_op jit(solution)/shard_map/psum | solution.py:102
  16.9 312.0 %copy-start.34 = (f32[1152]{0:T(1024)}, f32[1152]{0:T(1024)S(1)}, u32[]{:S(2)}) copy-start(f32[1152]{0:T(1024)S(1)} %get-tuple-element.145) | copy-start | bytes 13828
  323.9 6.4 copy-start.1
  323.9 8.2 copy-start.28
  338.2 5.6 copy-start.18
  346.4 6.5 copy-start.10
  353.0 384.6 %all-gather.2.cloned.1.call-start = ((), (), s32[]{:S(2)}) async-start(), calls=%async_computation.3 | async-start | bytes 5640192 | tf_op jit(solution)/shard_map/all_gather | solution.py:134
  353.7 709.9 %all-reduce.14.cloned.1.call-start = ((), (), s32[]{:S(2)}) async-start(), calls=%async_computation.4 | async-start | bytes 19021824 | tf_op jit(solution)/shard_map/psum | solution.py:102
  664.0 6.4 copy-start.2
  670.5 4.3 copy-start.22
  737.6 20.1 %copy-start.23 = (bf16[1152,576]{0,1:T(8,128)(2,1)S(1)}, bf16[1152,576]{0,1:T(8,128)(2,1)}, u32[]{:S(2)}) copy-start(bf16[1152,576]{0,1:T(8,128)(2,1)} %param.29) | copy-start | bytes 3981316
  764.6 672.0 %all-reduce.16.cloned.1.call-start = ((), (), s32[]{:S(2)}) async-start(), calls=%async_computation.5 | async-start | bytes 19021824 | tf_op jit(solution)/shard_map/psum | solution.py:102
  1074.1 13.3 copy-start.25
  1083.7 3.7 copy-start.3
  1094.2 4.3 copy-start.19
  1098.5 12.9 copy-start.21
  1136.8 475.0 %reduce-scatter.4.cloned.1.call-start = ((), (), s32[]{:S(2)}) async-start(), calls=%async_computation.6 | async-start | bytes 11280384
  1136.8 4.5 copy-start.24
  1148.0 636.6 %all-reduce.18.cloned.1.call-start = ((), (), s32[]{:S(2)}) async-start(), calls=%async_computation.7 | async-start | bytes 18579456 | tf_op jit(solution)/shard_map/psum | solution.py:194
  1148.2 16.1 slice-start
  1148.2 16.1 slice-start.1
  1148.2 18.1 slice-start.5
  1156.6 7.7 slice-start.2
  1156.6 7.7 copy-start.11
  1156.6 9.7 slice-start.6
  1166.3 270.3 %copy-start.29 = (f32[2064]{0:T(1024)S(1)}, f32[2064]{0:T(1024)}, u32[]{:S(2)}) copy-start(f32[2064]{0:T(1024)} %copy-done.28) | copy-start | bytes 24772
  1166.3 270.3 %copy-start.33 = (f32[2064]{0:T(1024)S(1)}, f32[2064]{0:T(1024)}, u32[]{:S(2)}) copy-start(f32[2064]{0:T(1024)} %copy-done.32) | copy-start | bytes 24772
  1166.3 270.3 %copy-start.35 = (f32[1152]{0:T(1024)S(1)}, f32[1152]{0:T(1024)}, u32[]{:S(2)}) copy-start(f32[1152]{0:T(1024)} %copy-done.34) | copy-start | bytes 13828
  1611.8 20.5 %copy-start.13 = (bf16[2,144,1152]{2,1,0:T(8,128)(2,1)S(1)}, bf16[2,144,1152]{2,1,0:T(8,128)(2,1)}, u32[]{:S(2)}) copy-start(bf16[2,144,1152]{2,1,0:T(8,128)(2,1)} %param.26) | copy-start | bytes 1990660
  1617.6 20.0 %slice-start.3 = ((s8[4755456]{0:T(1024)(128)(4,1)}), s8[561152]{0:T(1024)(128)(4,1)S(1)}, s32[]{:S(2)}) async-start(s8[4755456]{0:T(1024)(128)(4,1)} %bitcast.110), calls=%async_computation.11 | async-start | bytes 1122304
  1632.3 5.3 slice-start.4
  1784.6 11.5 copy-start.7
  1786.0 11.8 copy-start.6
  1793.7 5.8 copy-start.62
  1793.7 6.4 copy-start.61
  1793.7 7.0 copy-start.58
  1793.7 48.1 %copy-start.53 = (f32[1152]{0:T(1024)S(1)}, f32[1152]{0:T(1024)}, u32[]{:S(2)}) copy-start(f32[1152]{0:T(1024)} %param.39) | copy-start | bytes 13828
  1793.8 48.1 %copy-start.54 = (f32[1152]{0:T(1024)S(1)}, f32[1152]{0:T(1024)}, u32[]{:S(2)}) copy-start(f32[1152]{0:T(1024)} %param.35) | copy-start | bytes 13828
  1793.8 50.0 %copy-start.55 = (f32[1152]{0:T(1024)S(1)}, f32[1152]{0:T(1024)}, u32[]{:S(2)}) copy-start(f32[1152]{0:T(1024)} %param.34) | copy-start | bytes 13828
  1793.8 51.2 %copy-start.56 = (f32[1152]{0:T(1024)S(1)}, f32[1152]{0:T(1024)}, u32[]{:S(2)}) copy-start(f32[1152]{0:T(1024)} %param.42) | copy-start | bytes 13828
  1793.8 51.2 %copy-start.57 = (f32[1152]{0:T(1024)S(1)}, f32[1152]{0:T(1024)}, u32[]{:S(2)}) copy-start(f32[1152]{0:T(1024)} %param.38) | copy-start | bytes 13828
  1793.8 53.2 %copy-start.59 = (f32[3,144]{1,0:T(4,128)S(1)}, f32[3,144]{1,0:T(4,128)}, u32[]{:S(2)}) copy-start(f32[3,144]{1,0:T(4,128)} %param.36) | copy-start | bytes 5188
  1793.8 53.2 %copy-start.60 = (f32[576]{0:T(1024)S(1)}, f32[576]{0:T(1024)}, u32[]{:S(2)}) copy-start(f32[576]{0:T(1024)} %param.40) | copy-start | bytes 6916
  1799.5 97.0 %copy-start.45 = (f32[2,1152]{1,0:T(2,128)S(1)}, f32[2,1152]{1,0:T(2,128)}, u32[]{:S(2)}) copy-start(f32[2,1152]{1,0:T(2,128)} %param.44) | copy-start | bytes 27652
  1799.5 98.9 %copy-start.63 = (f32[5]{0:T(128)S(1)}, f32[5]{0:T(128)}, u32[]{:S(2)}) copy-start(f32[5]{0:T(128)} %constant.220) | copy-start | bytes 64
  1799.5 102.9 %copy-start.51 = (f32[2,1152]{1,0:T(2,128)S(1)}, f32[2,1152]{1,0:T(2,128)}, u32[]{:S(2)}) copy-start(f32[2,1152]{1,0:T(2,128)} %param.43) | copy-start | bytes 27652
  1800.2 107.0 %copy-start.52 = (f32[144]{0:T(256)}, f32[144]{0:T(256)S(1)}, u32[]{:S(2)}) copy-start(f32[144]{0:T(256)S(1)} %get-tuple-element.189) | copy-start | bytes 1732
  1800.8 106.4 %copy-start.48 = (f32[2,144]{1,0:T(2,128)}, f32[2,144]{1,0:T(2,128)S(1)}, u32[]{:S(2)}) copy-start(f32[2,144]{1,0:T(2,128)S(1)} %get-tuple-element.187) | copy-start | bytes 3460
  1801.4 119.8 %copy-start.41 = (f32[576]{0:T(1024)}, f32[576]{0:T(1024)S(1)}, u32[]{:S(2)}) copy-start(f32[576]{0:T(1024)S(1)} %get-tuple-element.185) | copy-start | bytes 6916
  1842.4 67.8 %copy-start.37 = (f32[1152]{0:T(1024)}, f32[1152]{0:T(1024)S(1)}, u32[]{:S(2)}) copy-start(f32[1152]{0:T(1024)S(1)} %get-tuple-element.202) | copy-start | bytes 13828
  1842.4 72.0 %copy-start.36 = (f32[1152]{0:T(1024)}, f32[1152]{0:T(1024)S(1)}, u32[]{:S(2)}) copy-start(f32[1152]{0:T(1024)S(1)} %get-tuple-element.167) | copy-start | bytes 13828
  1844.4 62.8 %copy-start.38 = (f32[1152]{0:T(1024)}, f32[1152]{0:T(1024)S(1)}, u32[]{:S(2)}) copy-start(f32[1152]{0:T(1024)S(1)} %get-tuple-element.183) | copy-start | bytes 13828
  1845.6 61.5 %copy-start.40 = (f32[1152]{0:T(1024)}, f32[1152]{0:T(1024)S(1)}, u32[]{:S(2)}) copy-start(f32[1152]{0:T(1024)S(1)} %get-tuple-element.204) | copy-start | bytes 13828
  1845.6 75.6 %copy-start.39 = (f32[1152]{0:T(1024)}, f32[1152]{0:T(1024)S(1)}, u32[]{:S(2)}) copy-start(f32[1152]{0:T(1024)S(1)} %get-tuple-element.179) | copy-start | bytes 13828
  1847.0 63.2 %copy-start.47 = (f32[3,144]{1,0:T(4,128)}, f32[3,144]{1,0:T(4,128)S(1)}, u32[]{:S(2)}) copy-start(f32[3,144]{1,0:T(4,128)S(1)} %multiply_add_fusion.13) | copy-start | bytes 5188
  1847.0 67.4 %copy-start.42 = (f32[576]{0:T(1024)}, f32[576]{0:T(1024)S(1)}, u32[]{:S(2)}) copy-start(f32[576]{0:T(1024)S(1)} %multiply_add_fusion.12) | copy-start | bytes 6916
  1849.0 8.5 copy-start.9
  1896.5 17.9 copy-start.46
  1896.5 28.3 %copy-start.43 = (f32[2,1152]{1,0:T(2,128)}, f32[2,1152]{1,0:T(2,128)S(1)}, u32[]{:S(2)}) copy-start(f32[2,1152]{1,0:T(2,128)S(1)} %get-tuple-element.148) | copy-start | bytes 27652
  1903.0 21.8 %copy-start.44 = (f32[2,1152]{1,0:T(2,128)}, f32[2,1152]{1,0:T(2,128)S(1)}, u32[]{:S(2)}) copy-start(f32[2,1152]{1,0:T(2,128)S(1)} %get-tuple-element.165) | copy-start | bytes 27652
  1903.8 6.4 copy-start.8
  1903.8 6.4 copy-start.27
  (15 other events, 30.8 us)
Sparse Core Ops, SparseCore 0:
  16.3 303.3 all-reduce.9
  353.1 299.7 all-reduce.11
  655.0 82.5 all-gather.1
  764.7 298.8 all-reduce.13
  1136.9 299.6 all-reduce.15
  1440.1 171.5 reduce-scatter.3
  1615.9 168.6 all-reduce.17
where the time goes:
time: 1940 us; the launch traced here: 1930 us
  waiting for transfers between devices  1510 us (78%)
  matrix products  133 us (7%)
  other arithmetic  122 us (6%)
  blocking collectives  83.2 us (4%)
  local copies, waits for them, and re-layouts  57.2 us (3%)
  between operations  25.6 us (1%)
    psum x4, waiting for transfers between devices, full_sum(): return lax.psum(values, 'narrow')  1160 us
    unnamed x8, waiting for transfers between devices  151 us
    psum x1, waiting for transfers between devices, local(): lax.psum((grad_skip, grad_qkv, grad_out, grad_up, grad_down, gain_grads,...  144 us
    dot_general x21, matrix products, matmul(): return jnp.einsum(form, left, right, preferred_element_type=jnp.float32)  119 us
    psum x2, blocking collectives, local(): lax.psum((wide_parts[0], wide_parts[1], wide_parts[2], wide_parts[3], wid...  70.9 us
    all_gather x1, waiting for transfers between devices, local(): grad_full = lax.all_gather(cotangent, 'narrow', axis=1, tiled=True)  57.5 us
  transfers between devices with their start and end apart: 7, of which 7 were waited for; matrix products, arithmetic and copies ran while one was open for 5% of the time, Pallas kernels for 0%

commit v1 on v0

--- a/solution.py
+++ b/solution.py
@@ -294,7 +294,451 @@
     )
 
 
+def unit_parts(values):
+    average = jnp.mean(values, axis=-1, keepdims=True)
+    centered = values - average
+    variance = jnp.mean(centered * centered, axis=-1, keepdims=True)
+    inverse = lax.rsqrt(variance + NORM_EPS)
+    return centered * inverse, inverse
+
+
+def norm_back_own(unit, inverse, grad, gain):
+    scaled = grad * gain
+    inner = (
+        scaled
+        - jnp.mean(scaled, axis=-1, keepdims=True)
+        - unit * jnp.mean(scaled * unit, axis=-1, keepdims=True)
+    )
+    rows = tuple(range(grad.ndim - 1))
+    return inner * inverse, jnp.sum(grad * unit, axis=rows), jnp.sum(grad, axis=rows)
+
+
+def pick(array, index, axis):
+    return lax.dynamic_index_in_dim(array, index, axis, keepdims=False)
+
+
+def chips(
+    stream,
+    skip_in,
+    cotangent,
+    skip_weight,
+    qkv_weight,
+    out_weight,
+    up_weight,
+    down_weight,
+    norm_gain,
+    norm_bias,
+    row_skip,
+    col_skip,
+    row_qkv,
+    col_qkv,
+    row_out,
+    col_out,
+    row_up,
+    col_up,
+    row_down,
+    col_down,
+    second_gain,
+    second_bias,
+):
+    bf16 = jnp.bfloat16
+    f32 = jnp.float32
+    axes = ("wide", "narrow")
+    wide_count = lax.axis_size("wide")
+    narrow_count = lax.axis_size("narrow")
+    ZS, YS = narrow_count // 2, 2
+    wide_index = lax.axis_index("wide")
+    narrow_index = lax.axis_index("narrow")
+    xi = wide_index // 2
+    ci = wide_index % 2
+    zi = narrow_index // 2
+    yi = narrow_index % 2
+    rows_local, feat = stream.shape
+    half_head = feat // 2
+    hidden = up_weight.shape[1]
+    quarter = hidden // 4
+    scale_factor = 1.0 / math.sqrt(HEAD)
+
+    def perm(move):
+        pairs = []
+        for wide in range(wide_count):
+            for narrow in range(narrow_count):
+                x, c, z, y = move(wide // 2, wide % 2, narrow // 2, narrow % 2)
+                target = (x * 2 + c) * narrow_count + z * 2 + y
+                pairs.append((wide * narrow_count + narrow, target))
+        return pairs
+
+    def send(value, move):
+        return lax.ppermute(value, axes, perm(move))
+
+    def core(value):
+        return send(value, lambda x, c, z, y: (x, 1 - c, z, y))
+
+    def over_x(value):
+        return send(value, lambda x, c, z, y: (1 - x, c, z, y))
+
+    def over_y(value):
+        return send(value, lambda x, c, z, y: (x, c, z, 1 - y))
+
+    def over_z(value, step):
+        return send(value, lambda x, c, z, y: (x, c, (z + step) % ZS, y))
+
+    def xor_z(value, bit):
+        return send(value, lambda x, c, z, y: (x, c, z ^ bit, y))
+
+    def to_images(array):
+        grid = array.reshape((ZS, YS) + array.shape[1:])
+        mine = pick(grid, yi, 1)
+        other = over_y(pick(grid, 1 - yi, 1))
+        both = jnp.stack([mine, other])
+        blocks = [pick(both, zi, 1)]
+        for step in range(1, ZS):
+            blocks.append(over_z(pick(both, (zi + step) % ZS, 1), step))
+        return blocks
+
+    def canonical(blocks):
+        stacked = jnp.stack(blocks)
+        out = []
+        for number in range(narrow_count):
+            step = (zi - number // 2) % ZS
+            j = yi ^ (number % 2)
+            out.append(pick(pick(stacked, step, 0), j, 0))
+        return jnp.stack(out)
+
+    def ring(block):
+        blocks = [block]
+        for _ in range(ZS - 1):
+            blocks.append(over_z(blocks[-1], 1))
+        return jnp.stack(blocks)
+
+    def gather_plane(block):
+        first = ring(block)
+        return [first, over_y(first)]
+
+    def gather_all(own, other):
+        plane = gather_plane(own)
+        near = jnp.concatenate([other[None], over_x(plane[0][1:])])
+        return [plane, [near, over_x(plane[1])]]
+
+    def reduce_ring(total):
+        carry = total[ZS - 1]
+        for step in range(ZS - 2, -1, -1):
+            carry = over_z(carry.astype(bf16), -1).astype(f32) + total[step].astype(f32)
+        return carry
+
+    def add_low(left, right):
+        return (left.astype(f32) + right.astype(f32)).astype(bf16)
+
+    def reduce_plane(pieces):
+        total = add_low(pieces[0], over_y(pieces[1]))
+        return reduce_ring(total)
+
+    def reduce_all(pieces):
+        return reduce_plane([add_low(pieces[0][j], over_x(pieces[1][j])) for j in range(2)])
+
+    def reduce_then_x(pieces):
+        total = reduce_plane(pieces)
+        halves = total.reshape((2, total.shape[0] // 2) + total.shape[1:])
+        kept = pick(halves, xi, 0)
+        given = over_x(pick(halves, 1 - xi, 0).astype(bf16))
+        return kept + given.astype(f32)
+
+    def spread(piece):
+        low = piece.astype(bf16)
+        pair = jnp.stack([low, over_x(low)])
+        four = jnp.stack([pair, core(pair)])
+        parts = []
+        for c in range(2):
+            for x in range(2):
+                parts.append(pick(pick(four, c ^ ci, 0), x ^ xi, 0))
+        return jnp.stack(parts)
+
+    is_first = ci == 0
+    mine = jnp.where(is_first, stream, skip_in)
+    given = core(jnp.where(is_first, skip_in, stream))
+    tokens = jnp.stack([mine, given]).reshape(2, narrow_count, SEQ, feat).transpose(1, 0, 2, 3)
+    token_blocks = to_images(tokens)
+    token_pairs = [
+        jnp.concatenate([block[j] for block in token_blocks], axis=-1) for j in range(2)
+    ]
+
+    skip_half = pick(skip_weight, ci, 0)
+    skip_full = gather_plane(skip_half)
+    qkv_rows = qkv_weight.transpose(1, 2, 0).reshape(3, 2, half_head, D)
+    attn_half = jnp.concatenate(
+        [pick(qkv_rows, ci, 1), pick(out_weight.reshape(2, half_head, D), ci, 0)[None]]
+    )
+    attn_full = gather_plane(attn_half)
+    up_rows = pick(up_weight.T.reshape(2, 2, quarter, D), ci, 0)
+    up_full = gather_all(pick(up_rows, xi, 0), pick(up_rows, 1 - xi, 0))
+    down_rows = pick(down_weight.reshape(2, 2, quarter, D), ci, 0)
+    down_full = gather_all(pick(down_rows, xi, 0), pick(down_rows, 1 - xi, 0))
+
+    cot_blocks = to_images(cotangent.reshape(narrow_count, SEQ, feat))
+    cot_own = canonical(cot_blocks).transpose(1, 0, 2).reshape(SEQ, D)
+
+    def both_images(own):
+        return jnp.concatenate([own[None], core(own)[None]]).reshape(2 * SEQ, -1)
+
+    def core_sum(partial):
+        parts = partial.reshape(2, SEQ, D)
+        return parts[0] + core(parts[1])
+
+    flat = [pair.reshape(2 * SEQ, -1) for pair in token_pairs]
+    skip_mats = [piece.reshape(-1, D) for piece in skip_full]
+    hidden_in = core_sum(
+        matmul(flat[0], skip_mats[0], "rc,cd->rd") + matmul(flat[1], skip_mats[1], "rc,cd->rd")
+    )
+    unit_one, inverse_one = unit_parts(hidden_in)
+    normed = both_images((unit_one * norm_gain[0] + norm_bias[0]).astype(bf16))
+
+    heads = ZS
+    attended = []
+    kept = []
+    attn_part = 0.0
+    for j in range(2):
+        weights = attn_full[j]
+        rows = [weights[:, t].reshape(heads * half_head, D) for t in range(4)]
+        q, k, v = [
+            matmul(normed, rows[t], "rd,cd->rc").astype(bf16).reshape(2, SEQ, heads, half_head)
+            for t in range(3)
+        ]
+        scores = matmul(q, k, "bqhe,bkhe->bhqk") * scale_factor
+        row_max = jnp.max(scores, axis=-1, keepdims=True)
+        exponent = jnp.exp(scores - row_max)
+        row_total = jnp.sum(exponent, axis=-1, keepdims=True)
+        probs = exponent / row_total
+        probs_low = probs.astype(bf16)
+        out = (
+            matmul(probs_low, v, "bhqk,bkhe->bqhe")
+            .reshape(2 * SEQ, heads * half_head)
+            .astype(bf16)
+        )
+        attended.append(out)
+        attn_part = attn_part + matmul(out, rows[3], "rc,cd->rd")
+        kept.append((q, k, v, probs, probs_low, rows))
+    middle = hidden_in + core_sum(attn_part)
+    unit_two, inverse_two = unit_parts(middle)
+    mixed = both_images((unit_two * norm_gain[1] + norm_bias[1]).astype(bf16))
+    cot = both_images(cot_own)
+
+    down_part = 0.0
+    mixed_part = 0.0
+    grad_down = [[None, None], [None, None]]
+    grad_up = [[None, None], [None, None]]
+    for i in range(2):
+        for j in range(2):
+            up_mat = up_full[i][j].reshape(-1, D)
+            down_mat = down_full[i][j].reshape(-1, D)
+            shape = (ZS, quarter, D)
+            up_input = matmul(mixed, up_mat, "rd,fd->rf")
+            gelu_value, gelu_back = jax.vjp(gelu_exact, up_input)
+            activation = gelu_value.astype(bf16)
+            down_part = down_part + matmul(activation, down_mat, "rf,fd->rd")
+            grad_down[i][j] = matmul(activation, cot, "rf,rd->fd").astype(bf16).reshape(shape)
+            grad_act = matmul(cot, down_mat, "rd,fd->rf")
+            grad_up_in = gelu_back(grad_act)[0].astype(bf16)
+            grad_up[i][j] = matmul(grad_up_in, mixed, "rf,rd->fd").astype(bf16).reshape(shape)
+            mixed_part = mixed_part + matmul(grad_up_in, up_mat, "rf,fd->rd")
+    down_own = reduce_all(grad_down)
+    up_own = reduce_all(grad_up)
+    block_own = (middle + core_sum(down_part)).astype(bf16)
+
+    back_middle, gain_two, bias_two = norm_back_own(
+        unit_two, inverse_two, core_sum(mixed_part), norm_gain[1]
+    )
+    grad_middle = cot_own.astype(f32) + back_middle
+    middle_low = both_images(grad_middle.astype(bf16))
+    normed_part = 0.0
+    grad_attn = []
+    for j in range(2):
+        q, k, v, probs, probs_low, rows = kept[j]
+        grad_out = matmul(attended[j], middle_low, "rc,rd->cd").astype(bf16)
+        grad_attended = (
+            matmul(middle_low, rows[3], "rd,cd->rc").astype(bf16).reshape(2, SEQ, heads, half_head)
+        )
+        grad_v = matmul(probs_low, grad_attended, "bhqk,bqhe->bkhe")
+        grad_probs = matmul(grad_attended, v, "bqhe,bkhe->bhqk")
+        inner_sum = jnp.sum(probs * grad_probs, axis=-1, keepdims=True)
+        grad_scores = (probs * (grad_probs - inner_sum) * scale_factor).astype(bf16)
+        grad_q = matmul(grad_scores, k, "bhqk,bkhe->bqhe")
+        grad_k = matmul(grad_scores, q, "bhqk,bqhe->bkhe")
+        mats = []
+        for t, grad in enumerate((grad_q, grad_k, grad_v)):
+            low = grad.astype(bf16).reshape(2 * SEQ, heads * half_head)
+            mats.append(matmul(low, normed, "rc,rd->cd").astype(bf16))
+            normed_part = normed_part + matmul(low, rows[t], "rc,cd->rd")
+        mats.append(grad_out)
+        grad_attn.append(
+            jnp.stack([mat.reshape(heads, half_head, D) for mat in mats], axis=1).reshape(
+                heads, 4 * half_head, D
+            )
+        )
+    attn_own = reduce_then_x(grad_attn)
+    back_hidden, gain_one, bias_one = norm_back_own(
+        unit_one, inverse_one, core_sum(normed_part), norm_gain[0]
+    )
+    hidden_own = (grad_middle + back_hidden).astype(bf16)
+    hidden_low = both_images(hidden_own)
+    grad_skip = [
+        matmul(part, hidden_low, "rc,rd->cd").astype(bf16).reshape(ZS, feat, D) for part in flat
+    ]
+    skip_own = reduce_then_x(grad_skip)
+
+    def to_features(grid):
+        blocks = to_images(grid.reshape((narrow_count,) + grid.shape[2:]))
+        return canonical(blocks)
+
+    block_out = to_features(
+        block_own.reshape(SEQ, ZS, YS, feat).transpose(1, 2, 0, 3)
+    ).reshape(rows_local, feat)
+    token_grads = [
+        matmul(hidden_low, mat, "rd,cd->rc").astype(bf16).reshape(2, SEQ, ZS, feat)
+        for mat in skip_mats
+    ]
+    kept_grads = jnp.stack([grad.transpose(2, 0, 1, 3) for grad in token_grads])
+    returned = jnp.stack([kept_grads[0], over_y(kept_grads[1])])
+    backs = [returned[:, 0]]
+    for step in range(1, ZS):
+        backs.append(over_z(returned[:, step], -step))
+    stacked = jnp.stack(backs)
+    ordered = []
+    for number in range(narrow_count):
+        step = (number // 2 - zi) % ZS
+        ordered.append(pick(pick(stacked, step, 0), yi ^ (number % 2), 0))
+    ordered = jnp.stack(ordered)
+    grad_mine = ordered[:, 0].reshape(rows_local, feat)
+    grad_given = core(ordered[:, 1].reshape(rows_local, feat))
+    grad_stream = jnp.where(is_first, grad_mine, grad_given).astype(f32)
+    grad_skip_in = jnp.where(is_first, grad_given, grad_mine).astype(f32)
+
+    down_all = spread(down_own).reshape(hidden, D)
+    up_all = spread(up_own).reshape(hidden, D)
+    attn_all = spread(attn_own).reshape(2, 4, half_head, D)
+    skip_all = spread(skip_own).reshape(2, feat, D)
+    qkv_all = attn_all[:, :3].transpose(1, 0, 2, 3).reshape(3, feat, D)
+    out_all = attn_all[:, 3].reshape(feat, D)
+
+    def all_narrow(value):
+        value = value + over_y(value)
+        bit = 1
+        while bit < ZS:
+            value = value + xor_z(value, bit)
+            bit *= 2
+        return value
+
+    norm_sums = jnp.stack([gain_one, gain_two, bias_one, bias_two])
+    norm_sums = norm_sums + core(norm_sums)
+    norm_sums = norm_sums + over_x(norm_sums)
+
+    grads = [
+        skip_all.reshape(-1, D).astype(f32),
+        qkv_all.reshape(-1, D).astype(f32),
+        out_all.astype(f32),
+        up_all.astype(f32),
+        down_all.astype(f32),
+    ]
+    old_wide = (col_skip, row_qkv, col_out, row_up, col_down)
+    old_narrow = (row_skip.reshape(-1), col_qkv.reshape(-1), row_out, col_up, row_down)
+    row_along_wide = (False, True, False, True, False)
+    wide_counts = (2 * D, 3 * D, D, FF, FF)
+    entry_counts = (2 * D * D, 3 * D * D, D * D, D * FF, FF * D)
+    new_narrow = []
+    sums = []
+    for number in range(5):
+        grad = grads[number]
+        squares = grad * grad + EPS_SQUARE
+        narrow_new = DECAY * old_narrow[number] + (1.0 - DECAY) * (jnp.sum(squares, axis=1) / D)
+        new_narrow.append(narrow_new)
+        old_sum = jnp.zeros((D,), f32).at[0].set(jnp.sum(old_narrow[number]))
+        sums.append(
+            jnp.stack(
+                [
+                    jnp.sum(squares, axis=0),
+                    jnp.sum(grad * grad * (1.0 / narrow_new)[:, None], axis=0),
+                    old_sum,
+                ]
+            )
+        )
+    early = all_narrow(jnp.concatenate([sums[number] for number in range(1, 5)]))
+    late = all_narrow(jnp.concatenate([sums[0], norm_sums]))
+    totals = [late[:3]] + [early[3 * number : 3 * number + 3] for number in range(4)]
+    gain_total = late[3:5]
+    bias_total = late[5:7]
+
+    new_wide = []
+    steps = []
+    ratios = []
+    for number in range(5):
+        wide_mean = totals[number][0] / wide_counts[number]
+        wide_new = DECAY * old_wide[number] + (1.0 - DECAY) * wide_mean
+        if row_along_wide[number]:
+            row_mean = jnp.mean(wide_new)
+        else:
+            row_mean = DECAY * (totals[number][2][0] / wide_counts[number]) + (
+                1.0 - DECAY
+            ) * jnp.mean(wide_mean)
+        square_total = jnp.sum(totals[number][1] / wide_new) * row_mean
+        ratio = jnp.sqrt(square_total / entry_counts[number]) / CLIP_LEVEL
+        ratios.append(ratio)
+        factor = -(STEP_RATE * jnp.sqrt(row_mean) / jnp.maximum(1.0, ratio))
+        step = (
+            grads[number]
+            * lax.rsqrt(new_narrow[number])[:, None]
+            * (lax.rsqrt(wide_new) * factor)[None, :]
+        )
+        new_wide.append(wide_new)
+        steps.append(step)
+    clip_ratio = jnp.stack(ratios)
+
+    def columns(array):
+        size = D // wide_count
+        return lax.dynamic_slice_in_dim(array, wide_index * size, size, array.ndim - 1)
+
+    new_skip = skip_weight.astype(f32) + steps[0].reshape(2, feat, D)
+    new_qkv = qkv_weight.astype(f32) + steps[1].reshape(3, feat, D).transpose(2, 0, 1)
+    new_up = up_weight.astype(f32) + steps[3].T
+    new_down = down_weight.astype(f32) + steps[4]
+    new_second_gain, gain_step = plain_update(gain_total, second_gain)
+    new_second_bias, bias_step = plain_update(bias_total, second_bias)
+    return (
+        block_out,
+        grad_stream,
+        grad_skip_in,
+        columns(grads[0]).reshape(2, feat, -1),
+        columns(grads[1]).reshape(3, feat, -1).transpose(2, 0, 1),
+        columns(grads[2]),
+        columns(grads[3]).T,
+        columns(grads[4]),
+        gain_total,
+        bias_total,
+        new_narrow[0].reshape(2, feat),
+        new_wide[0],
+        new_wide[1],
+        new_narrow[1].reshape(3, feat),
+        new_narrow[2],
+        new_wide[2],
+        new_wide[3],
+        new_narrow[3],
+        new_narrow[4],
+        new_wide[4],
+        new_second_gain,
+        new_second_bias[0],
+        new_second_bias[1],
+        new_skip,
+        new_qkv,
+        steps[2],
+        new_up,
+        new_down,
+        gain_step,
+        bias_step,
+        clip_ratio,
+    )
+
+
 def solution(mesh):
+    wide, narrow = mesh.shape["wide"], mesh.shape["narrow"]
+    body = chips if (wide == 4 and narrow == 8) else local
     in_specs = (
         P("wide", "narrow"),
         P("wide", "narrow"),
@@ -352,4 +796,4 @@
         P(),
         P(),
     )
-    return jax.shard_map(local, mesh=mesh, in_specs=in_specs, out_specs=out_specs, check_vma=False)
+    return jax.shard_map(body, mesh=mesh, in_specs=in_specs, out_specs=out_specs, check_vma=False)

time: 1940 us -> 972 us (0.50)
  waiting for transfers between devices: 1510 us -> 339 us
  starting transfers between devices: 0.46 us -> 182 us
  blocking collectives: 83.2 us -> 0 us
  local copies, waits for them, and re-layouts: 57.2 us -> 125 us
  matrix products: 133 us -> 176 us
    psum x5 -> x0, waiting for transfers between devices: 1300 us -> none  [the longest x4 1160 us: full_sum(): return lax.psum(values, 'narrow')]
    ppermute x0 -> x86, waiting for transfers between devices: none -> 339 us  [send(): return lax.ppermute(value, axes, perm(move))]
    ppermute x0 -> x86, starting transfers between devices: none -> 182 us  [send(): return lax.ppermute(value, axes, perm(move))]
    unnamed x8 -> x0, waiting for transfers between devices: 151 us -> none
    psum x3 -> x0, blocking collectives: 83.2 us -> none  [the longest x2 70.9 us: local(): lax.psum((wide_parts[0], wide_parts[1], wide_parts[2], wide_parts[3], wid...]
    all_gather x1 -> x0, waiting for transfers between devices: 57.5 us -> none  [local(): grad_full = lax.all_gather(cotangent, 'narrow', axis=1, tiled=True)]
    dot_general x21 -> x66, matrix products: 119 us -> 176 us  [matmul(): return jnp.einsum(form, left, right, preferred_element_type=jnp.float32)]
    reduce_sum x18 -> x19, other arithmetic: 65.7 us -> 11.8 us  [the longest x2 3.19 us: unit_parts(): average = jnp.mean(values, axis=-1, keepdims=True)]
  transfers between devices with their start and end apart: 7 -> 86, of which waited for: 7 -> 39; matrix products, arithmetic and copies ran while one was open for 5% -> 36% of each run, Pallas kernels for 0% -> 0%
where the time goes in v1:
time: 972 us; the launch traced here: 961 us
  waiting for transfers between devices  339 us (35%)
  starting transfers between devices  182 us (19%)
  matrix products  176 us (18%)
  local copies, waits for them, and re-layouts  125 us (13%)
  other arithmetic  125 us (13%)
  between operations  14.6 us (2%)
    ppermute x86, waiting for transfers between devices, send(): return lax.ppermute(value, axes, perm(move))  339 us
    ppermute x86, starting transfers between devices, send(): return lax.ppermute(value, axes, perm(move))  182 us
    dot_general x66, matrix products, matmul(): return jnp.einsum(form, left, right, preferred_element_type=jnp.float32)  176 us
    unnamed x391, local copies, waits for them, and re-layouts  25.1 us
  transfers between devices with their start and end apart: 86, of which 39 were waited for; matrix products, arithmetic and copies ran while one was open for 36% of the time, Pallas kernels for 0%

profile of v1, /device:TPU:0, one launch (start us, length us, event | category | flops | bytes accessed | tf_op | source)
XLA Modules:
  0.0 960.7 jit_solution(8232605591030346617)
XLA Ops:
  0.7 3.5 reshape_reshape.2
  6.9 3.0 collective-permute-start.34
  20.7 5.1 collective-permute-done.5
  30.7 3.0 collective-permute-start.36
  37.4 9.8 %collective-permute-done.6 = bf16[144,1152]{1,0:T(8,128)(2,1)S(1)} collective-permute-done((bf16[144,1152]{1,0:T(8,128)(2,1)}, bf16[144,1152]{1,0:T(8,128)(2,1)S(1)}, u32[]{:S(2)}, u32[]{:S(2)}) %collective-permute-start.6) | collective-permute-done | bytes 331808 | tf_op jit(solution)/shard_map/ppermute | solution.py:372
  48.6 3.3 collective-permute-done.35
  51.9 7.9 collective-permute-start.17
  61.4 3.6 collective-permute-start.20
  72.5 15.4 %collective-permute-done.1 = bf16[4,2,258,144]{2,3,1,0:T(8,128)(2,1)} collective-permute-done((bf16[4,2,258,144]{2,3,1,0:T(8,128)(2,1)}, bf16[4,2,258,144]{2,3,1,0:T(8,128)(2,1)}, u32[]{:S(2)}, u32[]{:S(2)}) %collective-permute-start.1) | collective-permute-done | bytes 594464 | tf_op jit(solution)/shard_map/ppermute | solution.py:372
  95.1 22.9 %collective-permute-start.2 = (bf16[2,2,258,144]{2,3,1,0:T(8,128)(2,1)}, bf16[2,2,258,144]{2,3,1,0:T(8,128)(2,1)}, u32[]{:S(2)}, u32[]{:S(2)}) collective-permute-start(bf16[2,2,258,144]{2,3,1,0:T(8,128)(2,1)} %bitcast.5), channel_id=1, source_target_pairs={{0,2},{1,3},{2,4},{3,5},{4,6},{5,7},{6,0},{7,1},{8,10},{9,11},{10,... | collective-permute-start | bytes 891656 | tf_op jit(solution)/shard_map/ppermute | solution.py:372
  123.7 5.3 collective-permute-done.2
  131.2 17.0 %collective-permute-start.18 = (bf16[144,1152]{1,0:T(8,128)(2,1)}, bf16[144,1152]{1,0:T(8,128)(2,1)S(1)}, u32[]{:S(2)}, u32[]{:S(2)}) collective-permute-start(bf16[144,1152]{1,0:T(8,128)(2,1)} %collective-permute-done.17), channel_id=1, source_target_pairs={{0,2},{1,3},{2,4},{3,5},{4,6},{5,7},{6,0},{7,1},{8,10},{9,11},{10,... | collective-permute-start | bytes 995336 | tf_op jit(solution)/shard_map/ppermute | solution.py:372
  148.1 3.0 collective-permute-start.21
  151.1 6.3 collective-permute-start.12
  163.8 2.9 fusion.121
  170.5 9.4 collective-permute-done.12
  179.9 24.8 %collective-permute-start.13 = (bf16[4,72,1152]{2,1,0:T(8,128)(2,1)}, bf16[4,72,1152]{2,1,0:T(8,128)(2,1)S(1)}, u32[]{:S(2)}, u32[]{:S(2)}) collective-permute-start(bf16[4,72,1152]{2,1,0:T(8,128)(2,1)} %collective-permute-done.12), channel_id=1, source_target_pairs={{0,2},{1,3},{2,4},{3,5},{4,6},{5,7},{6,0},{7,1},{8,10},{9,11},{10,... | collective-permute-start | bytes 1990664 | tf_op jit(solution)/shard_map/ppermute | solution.py:372
  207.3 20.1 %collective-permute-done.19 = bf16[144,1152]{1,0:T(8,128)(2,1)S(1)} collective-permute-done((bf16[144,1152]{1,0:T(8,128)(2,1)S(1)}, bf16[144,1152]{1,0:T(8,128)(2,1)S(1)}, u32[]{:S(2)}, u32[]{:S(2)}) %collective-permute-start.19) | collective-permute-done | bytes 331808 | tf_op jit(solution)/shard_map/ppermute | solution.py:372
  231.1 3.3 pad_maximum_fusion
  237.3 3.0 fusion.281
  244.5 3.1 convolution_convert_fusion.27
  249.1 2.9 convolution_convert_fusion.29
  262.1 26.7 %collective-permute-done.14 = bf16[4,4,72,1152]{3,2,1,0:T(8,128)(2,1)} collective-permute-done((bf16[4,4,72,1152]{3,2,1,0:T(8,128)(2,1)}, bf16[4,4,72,1152]{3,2,1,0:T(8,128)(2,1)}, u32[]{:S(2)}, u32[]{:S(2)}) %collective-permute-start.14) | collective-permute-done | bytes 2654240 | tf_op jit(solution)/shard_map/ppermute | solution.py:372
  295.4 2.9 convolution_convert_fusion.24
  331.3 15.8 %collective-permute-done.26 = bf16[3,144,1152]{2,1,0:T(8,128)(2,1)} collective-permute-done((bf16[3,144,1152]{2,1,0:T(8,128)(2,1)}, bf16[3,144,1152]{2,1,0:T(8,128)(2,1)}, u32[]{:S(2)}, u32[]{:S(2)}) %collective-permute-start.26) | collective-permute-done | bytes 995360 | tf_op jit(solution)/shard_map/ppermute | solution.py:372
  349.5 27.0 %collective-permute-done.24 = bf16[4,144,1152]{2,1,0:T(8,128)(2,1)} collective-permute-done((bf16[4,144,1152]{2,1,0:T(8,128)(2,1)}, bf16[4,144,1152]{2,1,0:T(8,128)(2,1)}, u32[]{:S(2)}, u32[]{:S(2)}) %collective-permute-start.24) | collective-permute-done | bytes 1327136 | tf_op jit(solution)/shard_map/ppermute | solution.py:372
  381.3 3.0 fusion.291
  384.3 5.2 add_convert_fusion.4
  397.2 9.8 %collective-permute-done.28 = bf16[4,144,1152]{2,1,0:T(8,128)(2,1)} collective-permute-done((bf16[4,144,1152]{2,1,0:T(8,128)(2,1)}, bf16[4,144,1152]{2,1,0:T(8,128)(2,1)}, u32[]{:S(2)}, u32[]{:S(2)}) %collective-permute-start.28) | collective-permute-done | bytes 1327136 | tf_op jit(solution)/shard_map/ppermute | solution.py:372
  407.0 5.2 add_convert_fusion.2
  412.4 2.9 convolution_convert_fusion
  416.6 3.9 add_convert_fusion.3
  425.6 5.2 add_convert_fusion.5
  468.8 20.2 %collective-permute-done.71 = bf16[4,144,1152]{2,1,0:T(8,128)(2,1)} collective-permute-done((bf16[4,144,1152]{2,1,0:T(8,128)(2,1)}, bf16[4,144,1152]{2,1,0:T(8,128)(2,1)}, u32[]{:S(2)}, u32[]{:S(2)}) %collective-permute-start.71) | collective-permute-done | bytes 1327136 | tf_op jit(solution)/shard_map/ppermute | solution.py:372
  494.5 51.4 %collective-permute-done.63 = bf16[4,144,1152]{2,1,0:T(8,128)(2,1)} collective-permute-done((bf16[4,144,1152]{2,1,0:T(8,128)(2,1)}, bf16[4,144,1152]{2,1,0:T(8,128)(2,1)}, u32[]{:S(2)}, u32[]{:S(2)}) %collective-permute-start.63) | collective-permute-done | bytes 1327136 | tf_op jit(solution)/shard_map/ppermute | solution.py:372
  559.9 3.5 fusion.96
  567.5 7.0 fusion.98
  574.5 6.3 fusion.101
  586.1 6.8 fusion.107
  592.9 6.7 fusion.104
  599.5 3.6 fusion.97
  623.7 3.0 convolution_convert_fusion.14
  652.7 3.2 collective-permute-done.73
  655.9 4.3 collective-permute-start.74
  663.1 4.3 collective-permute-start.66
  670.2 4.3 collective-permute-start.75
  678.0 4.3 collective-permute-start.67
  689.3 3.8 convolution_convert_fusion.16
  695.3 3.2 reshape.729
  700.0 3.8 convolution_convert_fusion.17
  719.1 19.8 %collective-permute-done.43 = bf16[4,2,258,144]{2,1,3,0:T(2,128)(2,1)} collective-permute-done((bf16[4,2,258,144]{2,1,3,0:T(2,128)(2,1)}, bf16[4,2,258,144]{2,1,3,0:T(2,128)(2,1)}, u32[]{:S(2)}, u32[]{:S(2)}) %collective-permute-start.43) | collective-permute-done | bytes 594464 | tf_op jit(solution)/shard_map/ppermute | solution.py:372
  738.9 4.1 fusion.161
  750.8 5.3 collective-permute-done.44
  756.1 27.9 %collective-permute-done.45 = bf16[2,2,258,144]{2,1,3,0:T(2,128)(2,1)S(1)} collective-permute-done((bf16[2,2,258,144]{2,1,3,0:T(2,128)(2,1)S(1)}, bf16[2,2,258,144]{2,1,3,0:T(2,128)(2,1)S(1)}, u32[]{:S(2)}, u32[]{:S(2)}) %collective-permute-start.45) | collective-permute-done | bytes 297248 | tf_op jit(solution)/shard_map/ppermute | solution.py:372
  784.3 3.4 pad_maximum_fusion.3
  814.6 9.2 collective-permute-done.49
  836.7 3.3 collective-permute-start.51
  841.3 6.9 collective-permute-done.51
  849.9 10.3 %collective-permute-done.57 = bf16[288,1152]{1,0:T(8,128)(2,1)S(1)} collective-permute-done((bf16[288,1152]{1,0:T(8,128)(2,1)S(1)}, bf16[288,1152]{1,0:T(8,128)(2,1)S(1)}, u32[]{:S(2)}, u32[]{:S(2)}) %collective-permute-start.57) | collective-permute-done | bytes 663584 | tf_op jit(solution)/shard_map/ppermute | solution.py:372
  860.4 4.5 collective-permute-start.58
  870.5 6.7 collective-permute-done.58
  881.4 10.7 %collective-permute-start.80 = (f32[7,1152]{1,0:T(8,128)S(1)}, f32[7,1152]{1,0:T(8,128)S(1)}, u32[]{:S(2)}, u32[]{:S(2)}) collective-permute-start(f32[7,1152]{1,0:T(8,128)S(1)} %fusion.234), channel_id=1, source_target_pairs={{0,1},{1,0},{2,3},{3,2},{4,5},{5,4},{6,7},{7,6},{8,9},{9,8},{10,11... | collective-permute-start | bytes 96776 | tf_op jit(solution)/shard_map/ppermute | solution.py:372
  913.3 3.2 collective-permute-done.60
  951.2 3.5 multiply_add_fusion
  (844 shorter events, 400.9 us)
Async XLA Ops:
  6.9 20.4 %collective-permute-start.34 = (bf16[4,258,144]{1,2,0:T(8,128)(2,1)}, bf16[4,258,144]{1,2,0:T(8,128)(2,1)}, u32[]{:S(2)}, u32[]{:S(2)}) collective-permute-start(bf16[4,258,144]{1,2,0:T(8,128)(2,1)} %bitcast.610), channel_id=1, source_target_pairs={{0,1},{1,0},{2,3},{3,2},{4,5},{5,4},{6,7},{7,6},{8,9},{9,8},{10,11... | collective-permute-start | bytes 891656 | tf_op jit(solution)/shard_map/ppermute | solution.py:372
  12.4 21.4 %collective-permute-start = (bf16[2064,144]{0,1:T(8,128)(2,1)}, bf16[2064,144]{0,1:T(8,128)(2,1)}, u32[]{:S(2)}, u32[]{:S(2)}) collective-permute-start(bf16[2064,144]{0,1:T(8,128)(2,1)} %get-tuple-element.375), channel_id=1, source_target_pairs={{0,8},{1,9},{2,10},{3,11},{4,12},{5,13},{6,14},{7,15},{8,0},{9,1},... | collective-permute-start | bytes 1783304 | tf_op jit(solution)/shard_map/ppermute | solution.py:372
  13.1 12.7 %collective-permute-start.5 = (bf16[144,1152]{1,0:T(8,128)(2,1)}, bf16[144,1152]{1,0:T(8,128)(2,1)}, u32[]{:S(2)}, u32[]{:S(2)}) collective-permute-start(bf16[144,1152]{1,0:T(8,128)(2,1)} %fusion.404), channel_id=1, source_target_pairs={{0,2},{1,3},{2,4},{3,5},{4,6},{5,7},{6,0},{7,1},{8,10},{9,11},{10,... | collective-permute-start | bytes 995336 | tf_op jit(solution)/shard_map/ppermute | solution.py:372
  15.9 132.2 %collective-permute-start.11 = (bf16[4,72,1152]{2,1,0:T(8,128)(2,1)}, bf16[4,72,1152]{2,1,0:T(8,128)(2,1)}, u32[]{:S(2)}, u32[]{:S(2)}) collective-permute-start(bf16[4,72,1152]{2,1,0:T(8,128)(2,1)} %get-tuple-element.400), channel_id=1, source_target_pairs={{0,2},{1,3},{2,4},{3,5},{4,6},{5,7},{6,0},{7,1},{8,10},{9,11},{10,... | collective-permute-start | bytes 1990664 | tf_op jit(solution)/shard_map/ppermute | solution.py:372
  25.8 21.4 %collective-permute-start.6 = (bf16[144,1152]{1,0:T(8,128)(2,1)}, bf16[144,1152]{1,0:T(8,128)(2,1)S(1)}, u32[]{:S(2)}, u32[]{:S(2)}) collective-permute-start(bf16[144,1152]{1,0:T(8,128)(2,1)} %collective-permute-done.5), channel_id=1, source_target_pairs={{0,2},{1,3},{2,4},{3,5},{4,6},{5,7},{6,0},{7,1},{8,10},{9,11},{10,... | collective-permute-start | bytes 995336 | tf_op jit(solution)/shard_map/ppermute | solution.py:372
  29.3 22.6 %collective-permute-start.35 = (bf16[2,258,144]{1,2,0:T(8,128)(2,1)}, bf16[2,258,144]{1,2,0:T(8,128)(2,1)S(1)}, u32[]{:S(2)}, u32[]{:S(2)}) collective-permute-start(bf16[2,258,144]{1,2,0:T(8,128)(2,1)} %get-tuple-element.384), channel_id=1, source_target_pairs={{0,2},{1,3},{2,4},{3,5},{4,6},{5,7},{6,0},{7,1},{8,10},{9,11},{10,... | collective-permute-start | bytes 445832 | tf_op jit(solution)/shard_map/ppermute | solution.py:372
  30.7 30.7 %collective-permute-start.36 = (bf16[2,258,144]{1,2,0:T(8,128)(2,1)}, bf16[2,258,144]{1,2,0:T(8,128)(2,1)S(1)}, u32[]{:S(2)}, u32[]{:S(2)}) collective-permute-start(bf16[2,258,144]{1,2,0:T(8,128)(2,1)} %get-tuple-element.385), channel_id=1, source_target_pairs={{0,4},{1,5},{2,6},{3,7},{4,0},{5,1},{6,2},{7,3},{8,12},{9,13},{10,... | collective-permute-start | bytes 445832 | tf_op jit(solution)/shard_map/ppermute | solution.py:372
  33.7 31.3 %collective-permute-start.37 = (bf16[2,258,144]{1,2,0:T(8,128)(2,1)}, bf16[2,258,144]{1,2,0:T(8,128)(2,1)S(1)}, u32[]{:S(2)}, u32[]{:S(2)}) collective-permute-start(bf16[2,258,144]{1,2,0:T(8,128)(2,1)} %get-tuple-element.386), channel_id=1, source_target_pairs={{0,6},{1,7},{2,0},{3,1},{4,2},{5,3},{6,4},{7,5},{8,14},{9,15},{10,... | collective-permute-start | bytes 445832 | tf_op jit(solution)/shard_map/ppermute | solution.py:372
  47.2 21.3 %collective-permute-start.7 = (bf16[144,1152]{1,0:T(8,128)(2,1)S(1)}, bf16[144,1152]{1,0:T(8,128)(2,1)S(1)}, u32[]{:S(2)}, u32[]{:S(2)}) collective-permute-start(bf16[144,1152]{1,0:T(8,128)(2,1)S(1)} %collective-permute-done.6), channel_id=1, source_target_pairs={{0,2},{1,3},{2,4},{3,5},{4,6},{5,7},{6,0},{7,1},{8,10},{9,11},{10,... | collective-permute-start | bytes 995336 | tf_op jit(solution)/shard_map/ppermute | solution.py:372
  51.9 68.7 %collective-permute-start.17 = (bf16[144,1152]{1,0:T(8,128)(2,1)}, bf16[144,1152]{1,0:T(8,128)(2,1)}, u32[]{:S(2)}, u32[]{:S(2)}) collective-permute-start(bf16[144,1152]{1,0:T(8,128)(2,1)} %get-tuple-element.367), channel_id=1, source_target_pairs={{0,2},{1,3},{2,4},{3,5},{4,6},{5,7},{6,0},{7,1},{8,10},{9,11},{10,... | collective-permute-start | bytes 995336 | tf_op jit(solution)/shard_map/ppermute | solution.py:372
  61.4 69.7 %collective-permute-start.20 = (bf16[144,1152]{1,0:T(8,128)(2,1)}, bf16[144,1152]{1,0:T(8,128)(2,1)}, u32[]{:S(2)}, u32[]{:S(2)}) collective-permute-start(bf16[144,1152]{1,0:T(8,128)(2,1)} %get-tuple-element.370), channel_id=1, source_target_pairs={{0,2},{1,3},{2,4},{3,5},{4,6},{5,7},{6,0},{7,1},{8,10},{9,11},{10,... | collective-permute-start | bytes 995336 | tf_op jit(solution)/shard_map/ppermute | solution.py:372
  65.0 22.9 %collective-permute-start.1 = (bf16[4,2,258,144]{2,3,1,0:T(8,128)(2,1)}, bf16[4,2,258,144]{2,3,1,0:T(8,128)(2,1)}, u32[]{:S(2)}, u32[]{:S(2)}) collective-permute-start(bf16[4,2,258,144]{2,3,1,0:T(8,128)(2,1)} %get-tuple-element.352), channel_id=1, source_target_pairs={{0,1},{1,0},{2,3},{3,2},{4,5},{5,4},{6,7},{7,6},{8,9},{9,8},{10,11... | collective-permute-start | bytes 1783304 | tf_op jit(solution)/shard_map/ppermute | solution.py:372
  69.7 94.0 %collective-permute-start.8 = (bf16[4,144,1152]{2,1,0:T(8,128)(2,1)S(1)}, bf16[4,144,1152]{2,1,0:T(8,128)(2,1)}, u32[]{:S(2)}, u32[]{:S(2)}) collective-permute-start(bf16[4,144,1152]{2,1,0:T(8,128)(2,1)S(1)} %pad_maximum_fusion.4), channel_id=1, source_target_pairs={{0,1},{1,0},{2,3},{3,2},{4,5},{5,4},{6,7},{7,6},{8,9},{9,8},{10,11... | collective-permute-start | bytes 3981320 | tf_op jit(solution)/shard_map/ppermute | solution.py:372
  95.1 33.9 %collective-permute-start.2 = (bf16[2,2,258,144]{2,3,1,0:T(8,128)(2,1)}, bf16[2,2,258,144]{2,3,1,0:T(8,128)(2,1)}, u32[]{:S(2)}, u32[]{:S(2)}) collective-permute-start(bf16[2,2,258,144]{2,3,1,0:T(8,128)(2,1)} %bitcast.5), channel_id=1, source_target_pairs={{0,2},{1,3},{2,4},{3,5},{4,6},{5,7},{6,0},{7,1},{8,10},{9,11},{10,... | collective-permute-start | bytes 891656 | tf_op jit(solution)/shard_map/ppermute | solution.py:372
  120.6 30.5 %collective-permute-start.3 = (bf16[2,2,258,144]{2,3,1,0:T(8,128)(2,1)}, bf16[2,2,258,144]{2,3,1,0:T(8,128)(2,1)}, u32[]{:S(2)}, u32[]{:S(2)}) collective-permute-start(bf16[2,2,258,144]{2,3,1,0:T(8,128)(2,1)} %bitcast.707), channel_id=1, source_target_pairs={{0,4},{1,5},{2,6},{3,7},{4,0},{5,1},{6,2},{7,3},{8,12},{9,13},{10,... | collective-permute-start | bytes 891656 | tf_op jit(solution)/shard_map/ppermute | solution.py:372
  129.0 30.6 %collective-permute-start.4 = (bf16[2,2,258,144]{2,3,1,0:T(8,128)(2,1)}, bf16[2,2,258,144]{2,3,1,0:T(8,128)(2,1)}, u32[]{:S(2)}, u32[]{:S(2)}) collective-permute-start(bf16[2,2,258,144]{2,3,1,0:T(8,128)(2,1)} %bitcast.7), channel_id=1, source_target_pairs={{0,6},{1,7},{2,0},{3,1},{4,2},{5,3},{6,4},{7,5},{8,14},{9,15},{10,... | collective-permute-start | bytes 891656 | tf_op jit(solution)/shard_map/ppermute | solution.py:372
  131.2 73.6 %collective-permute-start.18 = (bf16[144,1152]{1,0:T(8,128)(2,1)}, bf16[144,1152]{1,0:T(8,128)(2,1)S(1)}, u32[]{:S(2)}, u32[]{:S(2)}) collective-permute-start(bf16[144,1152]{1,0:T(8,128)(2,1)} %collective-permute-done.17), channel_id=1, source_target_pairs={{0,2},{1,3},{2,4},{3,5},{4,6},{5,7},{6,0},{7,1},{8,10},{9,11},{10,... | collective-permute-start | bytes 995336 | tf_op jit(solution)/shard_map/ppermute | solution.py:372
  148.1 59.2 %collective-permute-start.21 = (bf16[144,1152]{1,0:T(8,128)(2,1)}, bf16[144,1152]{1,0:T(8,128)(2,1)}, u32[]{:S(2)}, u32[]{:S(2)}) collective-permute-start(bf16[144,1152]{1,0:T(8,128)(2,1)} %collective-permute-done.20), channel_id=1, source_target_pairs={{0,2},{1,3},{2,4},{3,5},{4,6},{5,7},{6,0},{7,1},{8,10},{9,11},{10,... | collective-permute-start | bytes 995336 | tf_op jit(solution)/shard_map/ppermute | solution.py:372
  151.1 28.8 %collective-permute-start.12 = (bf16[4,72,1152]{2,1,0:T(8,128)(2,1)}, bf16[4,72,1152]{2,1,0:T(8,128)(2,1)}, u32[]{:S(2)}, u32[]{:S(2)}) collective-permute-start(bf16[4,72,1152]{2,1,0:T(8,128)(2,1)} %collective-permute-done.11), channel_id=1, source_target_pairs={{0,2},{1,3},{2,4},{3,5},{4,6},{5,7},{6,0},{7,1},{8,10},{9,11},{10,... | collective-permute-start | bytes 1990664 | tf_op jit(solution)/shard_map/ppermute | solution.py:372
  168.2 66.7 %collective-permute-start.9 = (f32[258,1152]{1,0:T(8,128)S(1)}, f32[258,1152]{1,0:T(8,128)}, u32[]{:S(2)}, u32[]{:S(2)}) collective-permute-start(f32[258,1152]{1,0:T(8,128)S(1)} %slice.383), channel_id=1, source_target_pairs={{0,8},{1,9},{2,10},{3,11},{4,12},{5,13},{6,14},{7,15},{8,0},{9,1},... | collective-permute-start | bytes 3566600 | tf_op jit(solution)/shard_map/ppermute | solution.py:372
  179.9 51.2 %collective-permute-start.13 = (bf16[4,72,1152]{2,1,0:T(8,128)(2,1)}, bf16[4,72,1152]{2,1,0:T(8,128)(2,1)S(1)}, u32[]{:S(2)}, u32[]{:S(2)}) collective-permute-start(bf16[4,72,1152]{2,1,0:T(8,128)(2,1)} %collective-permute-done.12), channel_id=1, source_target_pairs={{0,2},{1,3},{2,4},{3,5},{4,6},{5,7},{6,0},{7,1},{8,10},{9,11},{10,... | collective-permute-start | bytes 1990664 | tf_op jit(solution)/shard_map/ppermute | solution.py:372
  204.8 22.6 %collective-permute-start.19 = (bf16[144,1152]{1,0:T(8,128)(2,1)S(1)}, bf16[144,1152]{1,0:T(8,128)(2,1)S(1)}, u32[]{:S(2)}, u32[]{:S(2)}) collective-permute-start(bf16[144,1152]{1,0:T(8,128)(2,1)S(1)} %collective-permute-done.18), channel_id=1, source_target_pairs={{0,2},{1,3},{2,4},{3,5},{4,6},{5,7},{6,0},{7,1},{8,10},{9,11},{10,... | collective-permute-start | bytes 995336 | tf_op jit(solution)/shard_map/ppermute | solution.py:372
  206.1 117.3 %collective-permute-start.38 = (bf16[258,1152]{1,0:T(8,128)(2,1)}, bf16[258,1152]{1,0:T(8,128)(2,1)}, u32[]{:S(2)}, u32[]{:S(2)}) collective-permute-start(bf16[258,1152]{1,0:T(8,128)(2,1)} %copy.434), channel_id=1, source_target_pairs={{0,8},{1,9},{2,10},{3,11},{4,12},{5,13},{6,14},{7,15},{8,0},{9,1},... | collective-permute-start | bytes 1783304 | tf_op jit(solution)/shard_map/ppermute | solution.py:372
  207.3 109.9 %collective-permute-start.22 = (bf16[144,1152]{1,0:T(8,128)(2,1)}, bf16[144,1152]{1,0:T(8,128)(2,1)}, u32[]{:S(2)}, u32[]{:S(2)}) collective-permute-start(bf16[144,1152]{1,0:T(8,128)(2,1)} %collective-permute-done.21), channel_id=1, source_target_pairs={{0,2},{1,3},{2,4},{3,5},{4,6},{5,7},{6,0},{7,1},{8,10},{9,11},{10,... | collective-permute-start | bytes 995336 | tf_op jit(solution)/shard_map/ppermute | solution.py:372
  229.6 96.8 %collective-permute-start.25 = (bf16[3,144,1152]{2,1,0:T(8,128)(2,1)}, bf16[3,144,1152]{2,1,0:T(8,128)(2,1)}, u32[]{:S(2)}, u32[]{:S(2)}) collective-permute-start(bf16[3,144,1152]{2,1,0:T(8,128)(2,1)} %pad_maximum_fusion.17), channel_id=1, source_target_pairs={{0,16},{1,17},{2,18},{3,19},{4,20},{5,21},{6,22},{7,23},{8,24},{9,... | collective-permute-start | bytes 2985992 | tf_op jit(solution)/shard_map/ppermute | solution.py:372
  234.5 54.3 %collective-permute-start.14 = (bf16[4,4,72,1152]{3,2,1,0:T(8,128)(2,1)}, bf16[4,4,72,1152]{3,2,1,0:T(8,128)(2,1)}, u32[]{:S(2)}, u32[]{:S(2)}) collective-permute-start(bf16[4,4,72,1152]{3,2,1,0:T(8,128)(2,1)} %pad_maximum_fusion), channel_id=1, source_target_pairs={{0,1},{1,0},{2,3},{3,2},{4,5},{5,4},{6,7},{7,6},{8,9},{9,8},{10,11... | collective-permute-start | bytes 7962632 | tf_op jit(solution)/shard_map/ppermute | solution.py:372
  313.9 15.1 %collective-permute-start.15 = (f32[258,1152]{1,0:T(8,128)}, f32[258,1152]{1,0:T(8,128)}, u32[]{:S(2)}, u32[]{:S(2)}) collective-permute-start(f32[258,1152]{1,0:T(8,128)} %slice.393), channel_id=1, source_target_pairs={{0,8},{1,9},{2,10},{3,11},{4,12},{5,13},{6,14},{7,15},{8,0},{9,1},... | collective-permute-start | bytes 3566600 | tf_op jit(solution)/shard_map/ppermute | solution.py:372
  316.7 32.3 %collective-permute-start.23 = (bf16[4,144,1152]{2,1,0:T(8,128)(2,1)}, bf16[4,144,1152]{2,1,0:T(8,128)(2,1)}, u32[]{:S(2)}, u32[]{:S(2)}) collective-permute-start(bf16[4,144,1152]{2,1,0:T(8,128)(2,1)} %pad_maximum_fusion.5), channel_id=1, source_target_pairs={{0,1},{1,0},{2,3},{3,2},{4,5},{5,4},{6,7},{7,6},{8,9},{9,8},{10,11... | collective-permute-start | bytes 3981320 | tf_op jit(solution)/shard_map/ppermute | solution.py:372
  319.6 56.9 %collective-permute-start.24 = (bf16[4,144,1152]{2,1,0:T(8,128)(2,1)}, bf16[4,144,1152]{2,1,0:T(8,128)(2,1)}, u32[]{:S(2)}, u32[]{:S(2)}) collective-permute-start(bf16[4,144,1152]{2,1,0:T(8,128)(2,1)} %pad_maximum_fusion.6), channel_id=1, source_target_pairs={{0,1},{1,0},{2,3},{3,2},{4,5},{5,4},{6,7},{7,6},{8,9},{9,8},{10,11... | collective-permute-start | bytes 3981320 | tf_op jit(solution)/shard_map/ppermute | solution.py:372
  323.4 23.7 %collective-permute-start.26 = (bf16[3,144,1152]{2,1,0:T(8,128)(2,1)}, bf16[3,144,1152]{2,1,0:T(8,128)(2,1)}, u32[]{:S(2)}, u32[]{:S(2)}) collective-permute-start(bf16[3,144,1152]{2,1,0:T(8,128)(2,1)} %pad_maximum_fusion.18), channel_id=1, source_target_pairs={{0,16},{1,17},{2,18},{3,19},{4,20},{5,21},{6,22},{7,23},{8,24},{9,... | collective-permute-start | bytes 2985992 | tf_op jit(solution)/shard_map/ppermute | solution.py:372
  331.2 46.1 %collective-permute-start.16 = (bf16[258,1152]{1,0:T(8,128)(2,1)S(1)}, bf16[258,1152]{1,0:T(8,128)(2,1)S(1)}, u32[]{:S(2)}, u32[]{:S(2)}) collective-permute-start(bf16[258,1152]{1,0:T(8,128)(2,1)S(1)} %add_convert_fusion.7), channel_id=1, source_target_pairs={{0,8},{1,9},{2,10},{3,11},{4,12},{5,13},{6,14},{7,15},{8,0},{9,1},... | collective-permute-start | bytes 1783304 | tf_op jit(solution)/shard_map/ppermute | solution.py:372
  349.0 43.1 %collective-permute-start.27 = (bf16[4,144,1152]{2,1,0:T(8,128)(2,1)}, bf16[4,144,1152]{2,1,0:T(8,128)(2,1)}, u32[]{:S(2)}, u32[]{:S(2)}) collective-permute-start(bf16[4,144,1152]{2,1,0:T(8,128)(2,1)} %collective-permute-done.23), channel_id=1, source_target_pairs={{0,16},{1,17},{2,18},{3,19},{4,20},{5,21},{6,22},{7,23},{8,24},{9,... | collective-permute-start | bytes 3981320 | tf_op jit(solution)/shard_map/ppermute | solution.py:372
  376.5 30.5 %collective-permute-start.28 = (bf16[4,144,1152]{2,1,0:T(8,128)(2,1)}, bf16[4,144,1152]{2,1,0:T(8,128)(2,1)}, u32[]{:S(2)}, u32[]{:S(2)}) collective-permute-start(bf16[4,144,1152]{2,1,0:T(8,128)(2,1)} %collective-permute-done.24), channel_id=1, source_target_pairs={{0,16},{1,17},{2,18},{3,19},{4,20},{5,21},{6,22},{7,23},{8,24},{9,... | collective-permute-start | bytes 3981320 | tf_op jit(solution)/shard_map/ppermute | solution.py:372
  439.9 24.9 %collective-permute-start.29 = (f32[258,1152]{1,0:T(8,128)S(1)}, f32[258,1152]{1,0:T(8,128)S(1)}, u32[]{:S(2)}, u32[]{:S(2)}) collective-permute-start(f32[258,1152]{1,0:T(8,128)S(1)} %slice.395), channel_id=1, source_target_pairs={{0,8},{1,9},{2,10},{3,11},{4,12},{5,13},{6,14},{7,15},{8,0},{9,1},... | collective-permute-start | bytes 3566600 | tf_op jit(solution)/shard_map/ppermute | solution.py:372
  448.9 13.1 %collective-permute-start.39 = (f32[258,1152]{1,0:T(8,128)S(1)}, f32[258,1152]{1,0:T(8,128)S(1)}, u32[]{:S(2)}, u32[]{:S(2)}) collective-permute-start(f32[258,1152]{1,0:T(8,128)S(1)} %slice.397), channel_id=1, source_target_pairs={{0,8},{1,9},{2,10},{3,11},{4,12},{5,13},{6,14},{7,15},{8,0},{9,1},... | collective-permute-start | bytes 3566600 | tf_op jit(solution)/shard_map/ppermute | solution.py:372
  456.7 32.3 %collective-permute-start.71 = (bf16[4,144,1152]{2,1,0:T(8,128)(2,1)}, bf16[4,144,1152]{2,1,0:T(8,128)(2,1)}, u32[]{:S(2)}, u32[]{:S(2)}) collective-permute-start(bf16[4,144,1152]{2,1,0:T(8,128)(2,1)} %bitcast.222), channel_id=1, source_target_pairs={{0,16},{1,17},{2,18},{3,19},{4,20},{5,21},{6,22},{7,23},{8,24},{9,... | collective-permute-start | bytes 3981320 | tf_op jit(solution)/shard_map/ppermute | solution.py:372
  457.2 183.9 %collective-permute-start.70 = (bf16[4,144,1152]{2,1,0:T(8,128)(2,1)}, bf16[4,144,1152]{2,1,0:T(8,128)(2,1)}, u32[]{:S(2)}, u32[]{:S(2)}) collective-permute-start(bf16[4,144,1152]{2,1,0:T(8,128)(2,1)} %bitcast.220), channel_id=1, source_target_pairs={{0,16},{1,17},{2,18},{3,19},{4,20},{5,21},{6,22},{7,23},{8,24},{9,... | collective-permute-start | bytes 3981320 | tf_op jit(solution)/shard_map/ppermute | solution.py:372
  458.7 87.2 %collective-permute-start.63 = (bf16[4,144,1152]{2,1,0:T(8,128)(2,1)}, bf16[4,144,1152]{2,1,0:T(8,128)(2,1)}, u32[]{:S(2)}, u32[]{:S(2)}) collective-permute-start(bf16[4,144,1152]{2,1,0:T(8,128)(2,1)} %bitcast.204), channel_id=1, source_target_pairs={{0,16},{1,17},{2,18},{3,19},{4,20},{5,21},{6,22},{7,23},{8,24},{9,... | collective-permute-start | bytes 3981320 | tf_op jit(solution)/shard_map/ppermute | solution.py:372
  462.0 185.6 %collective-permute-start.62 = (bf16[4,144,1152]{2,1,0:T(8,128)(2,1)}, bf16[4,144,1152]{2,1,0:T(8,128)(2,1)}, u32[]{:S(2)}, u32[]{:S(2)}) collective-permute-start(bf16[4,144,1152]{2,1,0:T(8,128)(2,1)} %bitcast.202), channel_id=1, source_target_pairs={{0,16},{1,17},{2,18},{3,19},{4,20},{5,21},{6,22},{7,23},{8,24},{9,... | collective-permute-start | bytes 3981320 | tf_op jit(solution)/shard_map/ppermute | solution.py:372
  468.2 23.5 %collective-permute-start.30 = (bf16[4,258,144]{1,2,0:T(8,128)(2,1)S(1)}, bf16[4,258,144]{1,2,0:T(8,128)(2,1)S(1)}, u32[]{:S(2)}, u32[]{:S(2)}) collective-permute-start(bf16[4,258,144]{1,2,0:T(8,128)(2,1)S(1)} %get-tuple-element.381), channel_id=1, source_target_pairs={{0,1},{1,0},{2,3},{3,2},{4,5},{5,4},{6,7},{7,6},{8,9},{9,8},{10,11... | collective-permute-start | bytes 891656 | tf_op jit(solution)/shard_map/ppermute | solution.py:372
  491.9 58.2 %collective-permute-start.31 = (bf16[2,258,144]{1,2,0:T(8,128)(2,1)S(1)}, bf16[2,258,144]{1,2,0:T(8,128)(2,1)S(1)}, u32[]{:S(2)}, u32[]{:S(2)}) collective-permute-start(bf16[2,258,144]{1,2,0:T(8,128)(2,1)S(1)} %get-tuple-element.378), channel_id=1, source_target_pairs={{0,2},{1,3},{2,4},{3,5},{4,6},{5,7},{6,0},{7,1},{8,10},{9,11},{10,... | collective-permute-start | bytes 445832 | tf_op jit(solution)/shard_map/ppermute | solution.py:372
  494.4 55.7 %collective-permute-start.32 = (bf16[2,258,144]{1,2,0:T(8,128)(2,1)S(1)}, bf16[2,258,144]{1,2,0:T(8,128)(2,1)S(1)}, u32[]{:S(2)}, u32[]{:S(2)}) collective-permute-start(bf16[2,258,144]{1,2,0:T(8,128)(2,1)S(1)} %get-tuple-element.379), channel_id=1, source_target_pairs={{0,4},{1,5},{2,6},{3,7},{4,0},{5,1},{6,2},{7,3},{8,12},{9,13},{10,... | collective-permute-start | bytes 445832 | tf_op jit(solution)/shard_map/ppermute | solution.py:372
  550.0 91.2 %collective-permute-start.72 = (bf16[4,144,1152]{2,1,0:T(8,128)(2,1)}, bf16[4,144,1152]{2,1,0:T(8,128)(2,1)}, u32[]{:S(2)}, u32[]{:S(2)}) collective-permute-start(bf16[4,144,1152]{2,1,0:T(8,128)(2,1)} %fusion.17), channel_id=1, source_target_pairs={{0,1},{1,0},{2,3},{3,2},{4,5},{5,4},{6,7},{7,6},{8,9},{9,8},{10,11... | collective-permute-start | bytes 3981320 | tf_op jit(solution)/shard_map/ppermute | solution.py:372
  552.2 95.4 %collective-permute-start.64 = (bf16[4,144,1152]{2,1,0:T(8,128)(2,1)}, bf16[4,144,1152]{2,1,0:T(8,128)(2,1)}, u32[]{:S(2)}, u32[]{:S(2)}) collective-permute-start(bf16[4,144,1152]{2,1,0:T(8,128)(2,1)} %fusion.19), channel_id=1, source_target_pairs={{0,1},{1,0},{2,3},{3,2},{4,5},{5,4},{6,7},{7,6},{8,9},{9,8},{10,11... | collective-permute-start | bytes 3981320 | tf_op jit(solution)/shard_map/ppermute | solution.py:372
  632.4 113.2 %collective-permute-start.55 = (bf16[4,288,1152]{2,1,0:T(8,128)(2,1)}, bf16[4,288,1152]{2,1,0:T(8,128)(2,1)}, u32[]{:S(2)}, u32[]{:S(2)}) collective-permute-start(bf16[4,288,1152]{2,1,0:T(8,128)(2,1)} %bitcast.179), channel_id=1, source_target_pairs={{0,1},{1,0},{2,3},{3,2},{4,5},{5,4},{6,7},{7,6},{8,9},{9,8},{10,11... | collective-permute-start | bytes 7962632 | tf_op jit(solution)/shard_map/ppermute | solution.py:372
  650.0 12.9 %collective-permute-start.65 = (bf16[144,1152]{1,0:T(8,128)(2,1)S(1)}, bf16[144,1152]{1,0:T(8,128)(2,1)S(1)}, u32[]{:S(2)}, u32[]{:S(2)}) collective-permute-start(bf16[144,1152]{1,0:T(8,128)(2,1)S(1)} %slice_bitcast_fusion.11), channel_id=1, source_target_pairs={{0,6},{1,7},{2,0},{3,1},{4,2},{5,3},{6,4},{7,5},{8,14},{9,15},{10,... | collective-permute-start | bytes 995336 | tf_op jit(solution)/shard_map/ppermute | solution.py:372
  652.0 30.3 %collective-permute-start.42 = (bf16[258,1152]{1,0:T(8,128)(2,1)S(1)}, bf16[258,1152]{1,0:T(8,128)(2,1)S(1)}, u32[]{:S(2)}, u32[]{:S(2)}) collective-permute-start(bf16[258,1152]{1,0:T(8,128)(2,1)S(1)} %add_convert_fusion.6), channel_id=1, source_target_pairs={{0,8},{1,9},{2,10},{3,11},{4,12},{5,13},{6,14},{7,15},{8,0},{9,1},... | collective-permute-start | bytes 1783304 | tf_op jit(solution)/shard_map/ppermute | solution.py:372
  655.9 14.1 %collective-permute-start.74 = (bf16[144,1152]{1,0:T(8,128)(2,1)S(1)}, bf16[144,1152]{1,0:T(8,128)(2,1)S(1)}, u32[]{:S(2)}, u32[]{:S(2)}) collective-permute-start(bf16[144,1152]{1,0:T(8,128)(2,1)S(1)} %fusion.145), channel_id=1, source_target_pairs={{0,6},{1,7},{2,0},{3,1},{4,2},{5,3},{6,4},{7,5},{8,14},{9,15},{10,... | collective-permute-start | bytes 995336 | tf_op jit(solution)/shard_map/ppermute | solution.py:372
  663.1 14.1 %collective-permute-start.66 = (bf16[144,1152]{1,0:T(8,128)(2,1)S(1)}, bf16[144,1152]{1,0:T(8,128)(2,1)S(1)}, u32[]{:S(2)}, u32[]{:S(2)}) collective-permute-start(bf16[144,1152]{1,0:T(8,128)(2,1)S(1)} %fusion.148), channel_id=1, source_target_pairs={{0,6},{1,7},{2,0},{3,1},{4,2},{5,3},{6,4},{7,5},{8,14},{9,15},{10,... | collective-permute-start | bytes 995336 | tf_op jit(solution)/shard_map/ppermute | solution.py:372
  670.2 33.7 %collective-permute-start.75 = (bf16[144,1152]{1,0:T(8,128)(2,1)S(1)}, bf16[144,1152]{1,0:T(8,128)(2,1)}, u32[]{:S(2)}, u32[]{:S(2)}) collective-permute-start(bf16[144,1152]{1,0:T(8,128)(2,1)S(1)} %fusion.144), channel_id=1, source_target_pairs={{0,6},{1,7},{2,0},{3,1},{4,2},{5,3},{6,4},{7,5},{8,14},{9,15},{10,... | collective-permute-start | bytes 995336 | tf_op jit(solution)/shard_map/ppermute | solution.py:372
  678.0 27.7 %collective-permute-start.67 = (bf16[144,1152]{1,0:T(8,128)(2,1)}, bf16[144,1152]{1,0:T(8,128)(2,1)}, u32[]{:S(2)}, u32[]{:S(2)}) collective-permute-start(bf16[144,1152]{1,0:T(8,128)(2,1)} %fusion.147), channel_id=1, source_target_pairs={{0,6},{1,7},{2,0},{3,1},{4,2},{5,3},{6,4},{7,5},{8,14},{9,15},{10,... | collective-permute-start | bytes 995336 | tf_op jit(solution)/shard_map/ppermute | solution.py:372
  686.3 124.2 %collective-permute-start.48 = (bf16[4,144,1152]{2,1,0:T(8,128)(2,1)}, bf16[4,144,1152]{2,1,0:T(8,128)(2,1)}, u32[]{:S(2)}, u32[]{:S(2)}) collective-permute-start(bf16[4,144,1152]{2,1,0:T(8,128)(2,1)} %bitcast.144), channel_id=1, source_target_pairs={{0,1},{1,0},{2,3},{3,2},{4,5},{5,4},{6,7},{7,6},{8,9},{9,8},{10,11... | collective-permute-start | bytes 3981320 | tf_op jit(solution)/shard_map/ppermute | solution.py:372
  698.5 40.4 %collective-permute-start.43 = (bf16[4,2,258,144]{2,1,3,0:T(2,128)(2,1)}, bf16[4,2,258,144]{2,1,3,0:T(2,128)(2,1)}, u32[]{:S(2)}, u32[]{:S(2)}) collective-permute-start(bf16[4,2,258,144]{2,1,3,0:T(2,128)(2,1)} %bitcast.684), channel_id=1, source_target_pairs={{0,1},{1,0},{2,3},{3,2},{4,5},{5,4},{6,7},{7,6},{8,9},{9,8},{10,11... | collective-permute-start | bytes 1783304 | tf_op jit(solution)/shard_map/ppermute | solution.py:372
  716.6 82.2 %collective-permute-start.77 = (bf16[2,144,1152]{2,1,0:T(8,128)(2,1)}, bf16[2,144,1152]{2,1,0:T(8,128)(2,1)}, u32[]{:S(2)}, u32[]{:S(2)}) collective-permute-start(bf16[2,144,1152]{2,1,0:T(8,128)(2,1)} %get-tuple-element.389), channel_id=1, source_target_pairs={{0,8},{1,9},{2,10},{3,11},{4,12},{5,13},{6,14},{7,15},{8,0},{9,1},... | collective-permute-start | bytes 1990664 | tf_op jit(solution)/shard_map/ppermute | solution.py:372
  743.0 13.1 %collective-permute-start.44 = (bf16[2,2,258,144]{2,1,3,0:T(2,128)(2,1)S(1)}, bf16[2,2,258,144]{2,1,3,0:T(2,128)(2,1)S(1)}, u32[]{:S(2)}, u32[]{:S(2)}) collective-permute-start(bf16[2,2,258,144]{2,1,3,0:T(2,128)(2,1)S(1)} %get-tuple-element.349), channel_id=1, source_target_pairs={{0,6},{1,7},{2,0},{3,1},{4,2},{5,3},{6,4},{7,5},{8,14},{9,15},{10,... | collective-permute-start | bytes 891656 | tf_op jit(solution)/shard_map/ppermute | solution.py:372
  745.5 38.6 %collective-permute-start.45 = (bf16[2,2,258,144]{2,1,3,0:T(2,128)(2,1)S(1)}, bf16[2,2,258,144]{2,1,3,0:T(2,128)(2,1)S(1)}, u32[]{:S(2)}, u32[]{:S(2)}) collective-permute-start(bf16[2,2,258,144]{2,1,3,0:T(2,128)(2,1)S(1)} %get-tuple-element.351), channel_id=1, source_target_pairs={{0,4},{1,5},{2,6},{3,7},{4,0},{5,1},{6,2},{7,3},{8,12},{9,13},{10,... | collective-permute-start | bytes 891656 | tf_op jit(solution)/shard_map/ppermute | solution.py:372
  745.6 38.7 %collective-permute-start.46 = (bf16[2,2,258,144]{2,1,3,0:T(2,128)(2,1)S(1)}, bf16[2,2,258,144]{2,1,3,0:T(2,128)(2,1)S(1)}, u32[]{:S(2)}, u32[]{:S(2)}) collective-permute-start(bf16[2,2,258,144]{2,1,3,0:T(2,128)(2,1)S(1)} %get-tuple-element.350), channel_id=1, source_target_pairs={{0,2},{1,3},{2,4},{3,5},{4,6},{5,7},{6,0},{7,1},{8,10},{9,11},{10,... | collective-permute-start | bytes 891656 | tf_op jit(solution)/shard_map/ppermute | solution.py:372
  756.1 47.0 %collective-permute-start.69 = (bf16[2,144,1152]{2,1,0:T(8,128)(2,1)}, bf16[2,144,1152]{2,1,0:T(8,128)(2,1)}, u32[]{:S(2)}, u32[]{:S(2)}) collective-permute-start(bf16[2,144,1152]{2,1,0:T(8,128)(2,1)} %get-tuple-element.391), channel_id=1, source_target_pairs={{0,8},{1,9},{2,10},{3,11},{4,12},{5,13},{6,14},{7,15},{8,0},{9,1},... | collective-permute-start | bytes 1990664 | tf_op jit(solution)/shard_map/ppermute | solution.py:372
  784.1 55.9 %collective-permute-start.56 = (bf16[288,1152]{1,0:T(8,128)(2,1)}, bf16[288,1152]{1,0:T(8,128)(2,1)}, u32[]{:S(2)}, u32[]{:S(2)}) collective-permute-start(bf16[288,1152]{1,0:T(8,128)(2,1)} %slice_bitcast_fusion.3), channel_id=1, source_target_pairs={{0,6},{1,7},{2,0},{3,1},{4,2},{5,3},{6,4},{7,5},{8,14},{9,15},{10,... | collective-permute-start | bytes 1990664 | tf_op jit(solution)/shard_map/ppermute | solution.py:372
  794.0 71.6 %collective-permute-start.47 = (bf16[2064,144]{0,1:T(8,128)(2,1)}, bf16[2064,144]{0,1:T(8,128)(2,1)}, u32[]{:S(2)}, u32[]{:S(2)}) collective-permute-start(bf16[2064,144]{0,1:T(8,128)(2,1)} %reshape_squeeze.40), channel_id=1, source_target_pairs={{0,8},{1,9},{2,10},{3,11},{4,12},{5,13},{6,14},{7,15},{8,0},{9,1},... | collective-permute-start | bytes 1783304 | tf_op jit(solution)/shard_map/ppermute | solution.py:372
  841.2 19.0 %collective-permute-start.57 = (bf16[288,1152]{1,0:T(8,128)(2,1)S(1)}, bf16[288,1152]{1,0:T(8,128)(2,1)S(1)}, u32[]{:S(2)}, u32[]{:S(2)}) collective-permute-start(bf16[288,1152]{1,0:T(8,128)(2,1)S(1)} %fusion.76), channel_id=1, source_target_pairs={{0,6},{1,7},{2,0},{3,1},{4,2},{5,3},{6,4},{7,5},{8,14},{9,15},{10,... | collective-permute-start | bytes 1990664 | tf_op jit(solution)/shard_map/ppermute | solution.py:372
  849.3 15.6 %collective-permute-start.52 = (bf16[72,1152]{1,0:T(8,128)(2,1)S(1)}, bf16[72,1152]{1,0:T(8,128)(2,1)S(1)}, u32[]{:S(2)}, u32[]{:S(2)}) collective-permute-start(bf16[72,1152]{1,0:T(8,128)(2,1)S(1)} %fusion.225), channel_id=1, source_target_pairs={{0,16},{1,17},{2,18},{3,19},{4,20},{5,21},{6,22},{7,23},{8,24},{9,... | collective-permute-start | bytes 497672 | tf_op jit(solution)/shard_map/ppermute | solution.py:372
  860.4 16.8 %collective-permute-start.58 = (bf16[288,1152]{1,0:T(8,128)(2,1)S(1)}, bf16[288,1152]{1,0:T(8,128)(2,1)S(1)}, u32[]{:S(2)}, u32[]{:S(2)}) collective-permute-start(bf16[288,1152]{1,0:T(8,128)(2,1)S(1)} %fusion.75), channel_id=1, source_target_pairs={{0,6},{1,7},{2,0},{3,1},{4,2},{5,3},{6,4},{7,5},{8,14},{9,15},{10,... | collective-permute-start | bytes 1990664 | tf_op jit(solution)/shard_map/ppermute | solution.py:372
  892.8 14.7 %collective-permute-start.59 = (bf16[144,1152]{1,0:T(8,128)(2,1)}, bf16[144,1152]{1,0:T(8,128)(2,1)}, u32[]{:S(2)}, u32[]{:S(2)}) collective-permute-start(bf16[144,1152]{1,0:T(8,128)(2,1)} %fusion.183), channel_id=1, source_target_pairs={{0,16},{1,17},{2,18},{3,19},{4,20},{5,21},{6,22},{7,23},{8,24},{9,... | collective-permute-start | bytes 995336 | tf_op jit(solution)/shard_map/ppermute | solution.py:372
  (203 other events, 1710.6 us)

commit v2 on v1

--- a/solution.py
+++ b/solution.py
@@ -3,6 +3,8 @@
 import jax
 import jax.numpy as jnp
 from jax import lax
+from jax.experimental import pallas as pl
+from jax.experimental.pallas import tpu as pltpu
 from jax.sharding import PartitionSpec as P
 
 D = 1152
@@ -317,6 +319,227 @@
     return lax.dynamic_index_in_dim(array, index, axis, keepdims=False)
 
 
+PAD = 272
+
+
+def dot_nt(left, right):
+    return lax.dot_general(left, right, (((1,), (1,)), ((), ())), preferred_element_type=jnp.float32)
+
+
+def dot_nn(left, right):
+    return lax.dot_general(left, right, (((1,), (0,)), ((), ())), preferred_element_type=jnp.float32)
+
+
+def dot_tn(left, right):
+    return lax.dot_general(left, right, (((0,), (0,)), ((), ())), preferred_element_type=jnp.float32)
+
+
+def accumulate(step, refs, value):
+    size = refs[0].shape[0]
+
+    @pl.when(step == 0)
+    def _():
+        for number, ref in enumerate(refs):
+            ref[...] = value[number * size : (number + 1) * size]
+
+    @pl.when(step > 0)
+    def _():
+        for number, ref in enumerate(refs):
+            ref[...] += value[number * size : (number + 1) * size]
+
+
+def ffn_kernel(mixed_ref, cot_ref, weight_ref, down_a, down_b, mixed_a, mixed_b, grad_ref):
+    step = pl.program_id(0)
+    blocks, _, rows, _ = weight_ref.shape
+    mixed = mixed_ref[...]
+    cot = cot_ref[...]
+    up = jnp.concatenate([weight_ref[n, 0] for n in range(blocks)], axis=0)
+    down = jnp.concatenate([weight_ref[n, 1] for n in range(blocks)], axis=0)
+    up_input = dot_nt(mixed, up)
+    gate = 0.5 * (1.0 + lax.erf(up_input * (1.0 / math.sqrt(2.0))))
+    activation = (up_input * gate).astype(jnp.bfloat16)
+    slope = gate + up_input * (jnp.exp(-0.5 * up_input * up_input) * (1.0 / math.sqrt(2.0 * math.pi)))
+    grad_up_in = (dot_nt(cot, down) * slope).astype(jnp.bfloat16)
+    grad_up = dot_tn(grad_up_in, mixed).astype(jnp.bfloat16)
+    grad_down = dot_tn(activation, cot).astype(jnp.bfloat16)
+    for n in range(blocks):
+        grad_ref[n, 0] = grad_up[n * rows : (n + 1) * rows]
+        grad_ref[n, 1] = grad_down[n * rows : (n + 1) * rows]
+    accumulate(step, (mixed_a, mixed_b), dot_nn(grad_up_in, up))
+    accumulate(step, (down_a, down_b), dot_nn(activation, down))
+
+
+def ffn(mixed, cot, weights):
+    count, _, rows, _ = weights.shape
+    tokens = mixed.shape[0]
+    blocks = 4
+    whole = pl.BlockSpec((tokens, D), lambda t: (0, 0))
+    half = pl.BlockSpec((tokens // 2, D), lambda t: (0, 0))
+    block = pl.BlockSpec((blocks, 2, rows, D), lambda t: (t, 0, 0, 0))
+    part = jax.ShapeDtypeStruct((tokens // 2, D), jnp.float32)
+    return pl.pallas_call(
+        ffn_kernel,
+        out_shape=[part] * 4 + [jax.ShapeDtypeStruct(weights.shape, jnp.bfloat16)],
+        grid=(count // blocks,),
+        in_specs=[whole, whole, block],
+        out_specs=[half] * 4 + [block],
+        compiler_params=pltpu.CompilerParams(
+            dimension_semantics=("arbitrary",), vmem_limit_bytes=60 * 1024 * 1024
+        ),
+        cost_estimate=pl.CostEstimate(
+            flops=12 * tokens * D * count * rows, transcendentals=0, bytes_accessed=32 * 1024 * 1024
+        ),
+        name="ffn",
+    )(mixed, cot, weights)
+
+
+def soft(q, k):
+    scores = dot_nt(q, k) * (1.0 / math.sqrt(HEAD))
+    column = lax.broadcasted_iota(jnp.int32, scores.shape, 1)
+    scores = jnp.where(column < SEQ, scores, -1e30)
+    exponent = jnp.exp(scores - jnp.max(scores, axis=-1, keepdims=True))
+    return exponent / jnp.sum(exponent, axis=-1, keepdims=True)
+
+
+def attn_forward_kernel(meta_ref, normed_ref, qk_ref, vo_ref, part_a, part_b, qkv_ref, attended_ref):
+    step = pl.program_id(0)
+    normed = normed_ref[...]
+    qk = dot_nt(normed, qk_ref[0, 0])
+    v_all = dot_nt(normed, vo_ref[0, 0, :HEAD])
+    out_weight = vo_ref[0, 0, HEAD:]
+    qkv_ref[0, :, : 2 * HEAD] = qk.astype(jnp.bfloat16)
+    qkv_ref[0, :, 2 * HEAD :] = v_all.astype(jnp.bfloat16)
+    for image in range(2):
+        rows = slice(image * PAD, (image + 1) * PAD)
+        q = qk[rows, :HEAD].astype(jnp.bfloat16)
+        k = qk[rows, HEAD:].astype(jnp.bfloat16)
+        v = v_all[rows].astype(jnp.bfloat16)
+        probs = soft(q, k).astype(jnp.bfloat16)
+        attended_ref[0, rows] = dot_nn(probs, v).astype(jnp.bfloat16)
+    add = dot_nn(attended_ref[0], out_weight)
+
+    accumulate(step, (part_a, part_b), add)
+
+
+def attn_specs(rows, tokens):
+    whole = pl.BlockSpec((tokens, D), lambda s, m: (0, 0))
+    half = pl.BlockSpec((tokens // 2, D), lambda s, m: (0, 0))
+    qk = pl.BlockSpec((1, 1, rows, D), lambda s, m: (m[0], s, 0, 0))
+    vo = pl.BlockSpec((1, 1, rows, D), lambda s, m: (1 - m[0], s, 0, 0))
+    qkv = pl.BlockSpec((1, tokens, 3 * HEAD), lambda s, m: (s, 0, 0))
+    att = pl.BlockSpec((1, tokens, HEAD), lambda s, m: (s, 0, 0))
+    return whole, half, qk, vo, qkv, att
+
+
+def attn_forward(meta, normed, weights):
+    heads, rows = weights.shape[1:3]
+    tokens = normed.shape[0]
+    whole, half, qk, vo, qkv, att = attn_specs(rows, tokens)
+    return pl.pallas_call(
+        attn_forward_kernel,
+        out_shape=[
+            jax.ShapeDtypeStruct((tokens // 2, D), jnp.float32),
+            jax.ShapeDtypeStruct((tokens // 2, D), jnp.float32),
+            jax.ShapeDtypeStruct((heads, tokens, 3 * HEAD), jnp.bfloat16),
+            jax.ShapeDtypeStruct((heads, tokens, HEAD), jnp.bfloat16),
+        ],
+        grid_spec=pltpu.PrefetchScalarGridSpec(
+            num_scalar_prefetch=1,
+            grid=(heads,),
+            in_specs=[whole, qk, vo],
+            out_specs=[half, half, qkv, att],
+        ),
+        compiler_params=pltpu.CompilerParams(
+            dimension_semantics=("arbitrary",), vmem_limit_bytes=40 * 1024 * 1024
+        ),
+        cost_estimate=pl.CostEstimate(
+            flops=2 * tokens * D * heads * 2 * rows,
+            transcendentals=0,
+            bytes_accessed=16 * 1024 * 1024,
+        ),
+        name="attn_forward",
+    )(meta, normed, weights, weights)
+
+
+def attn_backward_kernel(
+    meta_ref,
+    normed_ref,
+    low_ref,
+    qk_ref,
+    vo_ref,
+    qkv_ref,
+    attended_ref,
+    part_a,
+    part_b,
+    grad_ref,
+    grads_s,
+    mat_s,
+):
+    step = pl.program_id(0)
+    normed = normed_ref[...]
+    low = low_ref[...]
+    out_weight = vo_ref[0, 0, HEAD:]
+    grad_attended = dot_nt(low, out_weight)
+    for image in range(2):
+        rows = slice(image * PAD, (image + 1) * PAD)
+        q = qkv_ref[0, rows, :HEAD]
+        k = qkv_ref[0, rows, HEAD : 2 * HEAD]
+        v = qkv_ref[0, rows, 2 * HEAD :]
+        grad = grad_attended[rows].astype(jnp.bfloat16)
+        probs = soft(q, k)
+        grad_v = dot_tn(probs.astype(jnp.bfloat16), grad)
+        grad_probs = dot_nt(grad, v)
+        inner = jnp.sum(probs * grad_probs, axis=-1, keepdims=True)
+        grad_scores = (probs * (grad_probs - inner) * (1.0 / math.sqrt(HEAD))).astype(jnp.bfloat16)
+        grads_s[rows, :HEAD] = dot_nn(grad_scores, k)
+        grads_s[rows, HEAD : 2 * HEAD] = dot_tn(grad_scores, q)
+        grads_s[rows, 2 * HEAD :] = grad_v
+    projected = grads_s[...].astype(jnp.bfloat16)
+    mat_s[: 3 * HEAD] = dot_tn(projected, normed)
+    mat_s[3 * HEAD :] = dot_tn(attended_ref[0], low)
+    which = meta_ref[0]
+    grad_ref[which, 0] = mat_s[: 2 * HEAD].astype(jnp.bfloat16)
+    grad_ref[1 - which, 0] = mat_s[2 * HEAD :].astype(jnp.bfloat16)
+    add = dot_nn(projected[:, : 2 * HEAD], qk_ref[0, 0]) + dot_nn(
+        projected[:, 2 * HEAD :], vo_ref[0, 0, :HEAD]
+    )
+
+    accumulate(step, (part_a, part_b), add)
+
+
+def attn_backward(meta, normed, low, weights, qkv_kept, attended):
+    heads, rows = weights.shape[1:3]
+    tokens = normed.shape[0]
+    whole, half, qk, vo, qkv, att = attn_specs(rows, tokens)
+    return pl.pallas_call(
+        attn_backward_kernel,
+        out_shape=[
+            jax.ShapeDtypeStruct((tokens // 2, D), jnp.float32),
+            jax.ShapeDtypeStruct((tokens // 2, D), jnp.float32),
+            jax.ShapeDtypeStruct((2, heads, rows, D), jnp.bfloat16),
+        ],
+        grid_spec=pltpu.PrefetchScalarGridSpec(
+            num_scalar_prefetch=1,
+            grid=(heads,),
+            in_specs=[whole, whole, qk, vo, qkv, att],
+            out_specs=[half, half, pl.BlockSpec((2, 1, rows, D), lambda s, m: (0, s, 0, 0))],
+            scratch_shapes=[
+                pltpu.VMEM((tokens, 3 * HEAD), jnp.float32),
+                pltpu.VMEM((2 * rows, D), jnp.float32),
+            ],
+        ),
+        compiler_params=pltpu.CompilerParams(
+            dimension_semantics=("arbitrary",), vmem_limit_bytes=48 * 1024 * 1024
+        ),
+        cost_estimate=pl.CostEstimate(
+            flops=4 * tokens * D * heads * 2 * rows,
+            transcendentals=0,
+            bytes_accessed=24 * 1024 * 1024,
+        ),
+        name="attn_backward",
+    )(meta, normed, low, weights, weights, qkv_kept, attended)
+
+
 def chips(
     stream,
     skip_in,
@@ -386,236 +609,243 @@
     def xor_z(value, bit):
         return send(value, lambda x, c, z, y: (x, c, z ^ bit, y))
 
-    def to_images(array):
-        grid = array.reshape((ZS, YS) + array.shape[1:])
-        mine = pick(grid, yi, 1)
-        other = over_y(pick(grid, 1 - yi, 1))
-        both = jnp.stack([mine, other])
-        blocks = [pick(both, zi, 1)]
-        for step in range(1, ZS):
-            blocks.append(over_z(pick(both, (zi + step) % ZS, 1), step))
-        return blocks
-
-    def canonical(blocks):
+    def tie(*values):
+        return lax.optimization_barrier(values)
+
+    def tie(*values):
+        return lax.optimization_barrier(values)
+
+    def add_low(left, right):
+        return (left.astype(f32) + right.astype(f32)).astype(bf16)
+
+    def padded(own):
+        return jnp.pad(own, ((0, PAD - SEQ), (0, 0)))
+
+    def shifted(line, sign=1):
+        return [pick(line, (zi + sign * step) % ZS, 0) for step in range(ZS)]
+
+    def canonical(blocks, sign=1):
         stacked = jnp.stack(blocks)
         out = []
         for number in range(narrow_count):
-            step = (zi - number // 2) % ZS
-            j = yi ^ (number % 2)
-            out.append(pick(pick(stacked, step, 0), j, 0))
+            step = (sign * (zi - number // 2)) % ZS
+            out.append(pick(pick(stacked, step, 0), yi ^ (number % 2), 0))
         return jnp.stack(out)
 
-    def ring(block):
-        blocks = [block]
-        for _ in range(ZS - 1):
-            blocks.append(over_z(blocks[-1], 1))
-        return jnp.stack(blocks)
-
-    def gather_plane(block):
-        first = ring(block)
-        return [first, over_y(first)]
-
-    def gather_all(own, other):
-        plane = gather_plane(own)
-        near = jnp.concatenate([other[None], over_x(plane[0][1:])])
-        return [plane, [near, over_x(plane[1])]]
-
-    def reduce_ring(total):
-        carry = total[ZS - 1]
-        for step in range(ZS - 2, -1, -1):
-            carry = over_z(carry.astype(bf16), -1).astype(f32) + total[step].astype(f32)
-        return carry
-
-    def add_low(left, right):
-        return (left.astype(f32) + right.astype(f32)).astype(bf16)
-
-    def reduce_plane(pieces):
-        total = add_low(pieces[0], over_y(pieces[1]))
-        return reduce_ring(total)
-
-    def reduce_all(pieces):
-        return reduce_plane([add_low(pieces[0][j], over_x(pieces[1][j])) for j in range(2)])
-
-    def reduce_then_x(pieces):
-        total = reduce_plane(pieces)
-        halves = total.reshape((2, total.shape[0] // 2) + total.shape[1:])
-        kept = pick(halves, xi, 0)
-        given = over_x(pick(halves, 1 - xi, 0).astype(bf16))
-        return kept + given.astype(f32)
-
-    def spread(piece):
-        low = piece.astype(bf16)
-        pair = jnp.stack([low, over_x(low)])
-        four = jnp.stack([pair, core(pair)])
-        parts = []
-        for c in range(2):
-            for x in range(2):
-                parts.append(pick(pick(four, c ^ ci, 0), x ^ xi, 0))
-        return jnp.stack(parts)
-
+    def split_y(array):
+        grid = array.reshape((ZS, YS) + array.shape[1:])
+        return pick(grid, yi, 1), pick(grid, 1 - yi, 1)
+
+    def z_pieces(near, far):
+        both = jnp.stack([near, far])
+        return [pick(both, (zi + step) % ZS, 1) for step in range(ZS)]
+
+    def z_line(pieces):
+        return [pieces[0]] + [over_z(pieces[step], step) for step in range(1, ZS)]
+
+    half = ZS // 2
+    meta = xi.astype(jnp.int32)[None]
     is_first = ci == 0
+
     mine = jnp.where(is_first, stream, skip_in)
     given = core(jnp.where(is_first, skip_in, stream))
+    skip_block = pick(pick(skip_weight, ci, 0).reshape(2, feat // 2, D), xi, 0)
+    skip_line = jnp.stack(z_line([skip_block] * ZS))
     tokens = jnp.stack([mine, given]).reshape(2, narrow_count, SEQ, feat).transpose(1, 0, 2, 3)
-    token_blocks = to_images(tokens)
-    token_pairs = [
-        jnp.concatenate([block[j] for block in token_blocks], axis=-1) for j in range(2)
-    ]
-
-    skip_half = pick(skip_weight, ci, 0)
-    skip_full = gather_plane(skip_half)
-    qkv_rows = qkv_weight.transpose(1, 2, 0).reshape(3, 2, half_head, D)
-    attn_half = jnp.concatenate(
-        [pick(qkv_rows, ci, 1), pick(out_weight.reshape(2, half_head, D), ci, 0)[None]]
-    )
-    attn_full = gather_plane(attn_half)
-    up_rows = pick(up_weight.T.reshape(2, 2, quarter, D), ci, 0)
-    up_full = gather_all(pick(up_rows, xi, 0), pick(up_rows, 1 - xi, 0))
-    down_rows = pick(down_weight.reshape(2, 2, quarter, D), ci, 0)
-    down_full = gather_all(pick(down_rows, xi, 0), pick(down_rows, 1 - xi, 0))
-
-    cot_blocks = to_images(cotangent.reshape(narrow_count, SEQ, feat))
-    cot_own = canonical(cot_blocks).transpose(1, 0, 2).reshape(SEQ, D)
+    token_near, token_give = split_y(tokens)
+    token_far = over_y(token_give)
+
+    skip_line, token_far, cotangent, qkv_weight, out_weight = tie(
+        skip_line, token_far, cotangent, qkv_weight, out_weight
+    )
+    token_blocks = z_line(z_pieces(token_near, token_far))
+    skip_beside = over_y(skip_line)
+    skip_across = over_x(skip_line)
+    attn_rows = jnp.concatenate(
+        [
+            pick(qkv_weight.transpose(1, 2, 0).reshape(3, 2, half_head, D), ci, 1),
+            pick(out_weight.reshape(2, half_head, D), ci, 0)[None],
+        ]
+    ).reshape(2, 2 * half_head, D)
+    attn_block = pick(attn_rows, xi, 0)
+    cot_near, cot_give = split_y(cotangent.reshape(narrow_count, SEQ, feat))
+
+    *token_blocks, skip_beside, skip_across, attn_block, cot_give = tie(
+        *token_blocks, skip_beside, skip_across, attn_block, cot_give
+    )
+    attn_line = jnp.stack(z_line([attn_block] * ZS))
+    skip_corner = jnp.concatenate([over_x(skip_beside[:half]), over_y(skip_across[half:])])
+    cot_far = over_y(cot_give)
+    flat = jnp.concatenate([block[j] for j in range(2) for block in token_blocks], axis=-1)
+    flat = jnp.pad(flat, ((0, 0), (0, PAD - SEQ), (0, 0))).reshape(2 * PAD, D)
+    skip_near = jnp.concatenate([skip_line, skip_beside])
+    skip_away = jnp.concatenate([skip_across, skip_corner])
+    skip_mat = jnp.where(
+        xi == 0,
+        jnp.stack([skip_near, skip_away], axis=1),
+        jnp.stack([skip_away, skip_near], axis=1),
+    ).reshape(D, D)
+    ffn_block = jnp.stack(
+        [
+            lax.dynamic_slice_in_dim(up_weight, (ci * 2 + xi) * quarter, quarter, 1).T,
+            lax.dynamic_slice_in_dim(down_weight, (ci * 2 + xi) * quarter, quarter, 0),
+        ]
+    )
+
+    attn_line, cot_far, skip_mat, ffn_block = tie(attn_line, cot_far, skip_mat, ffn_block)
+    attn_beside = over_y(attn_line)
+    attn_across = over_x(attn_line)
+    cot_blocks = z_line(z_pieces(cot_near, cot_far))
+    ffn_full = lax.all_gather(ffn_block[None], "narrow", tiled=True)
 
     def both_images(own):
-        return jnp.concatenate([own[None], core(own)[None]]).reshape(2 * SEQ, -1)
-
-    def core_sum(partial):
-        parts = partial.reshape(2, SEQ, D)
-        return parts[0] + core(parts[1])
-
-    flat = [pair.reshape(2 * SEQ, -1) for pair in token_pairs]
-    skip_mats = [piece.reshape(-1, D) for piece in skip_full]
-    hidden_in = core_sum(
-        matmul(flat[0], skip_mats[0], "rc,cd->rd") + matmul(flat[1], skip_mats[1], "rc,cd->rd")
-    )
+        own = padded(own)
+        return jnp.concatenate([own, core(own)])
+
+    def core_sum(kept, given):
+        return (kept + core(given))[:SEQ]
+
+    skip_part = matmul(flat, skip_mat, "rc,cd->rd")
+    hidden_in = core_sum(skip_part[:PAD], skip_part[PAD:])
     unit_one, inverse_one = unit_parts(hidden_in)
     normed = both_images((unit_one * norm_gain[0] + norm_bias[0]).astype(bf16))
 
-    heads = ZS
-    attended = []
-    kept = []
-    attn_part = 0.0
-    for j in range(2):
-        weights = attn_full[j]
-        rows = [weights[:, t].reshape(heads * half_head, D) for t in range(4)]
-        q, k, v = [
-            matmul(normed, rows[t], "rd,cd->rc").astype(bf16).reshape(2, SEQ, heads, half_head)
-            for t in range(3)
+    normed, attn_beside, attn_across, *cot_blocks = tie(
+        normed, attn_beside, attn_across, *cot_blocks
+    )
+    attn_corner = jnp.concatenate([over_x(attn_beside[:half]), over_y(attn_across[half:])])
+    cot_own = canonical(cot_blocks).transpose(1, 0, 2).reshape(SEQ, D)
+    cot_pair = padded(cot_own)
+    cot_pair = jnp.concatenate([cot_pair, over_x(cot_pair)])
+    attn_full = jnp.stack(
+        [
+            jnp.concatenate([attn_line, attn_beside]),
+            jnp.concatenate([attn_across, attn_corner]),
         ]
-        scores = matmul(q, k, "bqhe,bkhe->bhqk") * scale_factor
-        row_max = jnp.max(scores, axis=-1, keepdims=True)
-        exponent = jnp.exp(scores - row_max)
-        row_total = jnp.sum(exponent, axis=-1, keepdims=True)
-        probs = exponent / row_total
-        probs_low = probs.astype(bf16)
-        out = (
-            matmul(probs_low, v, "bhqk,bkhe->bqhe")
-            .reshape(2 * SEQ, heads * half_head)
-            .astype(bf16)
-        )
-        attended.append(out)
-        attn_part = attn_part + matmul(out, rows[3], "rc,cd->rd")
-        kept.append((q, k, v, probs, probs_low, rows))
-    middle = hidden_in + core_sum(attn_part)
+    )
+    attn_a, attn_b, qkv_kept, attended = attn_forward(meta, normed, attn_full)
+    attn_b, cot_pair = tie(attn_b, cot_pair)
+    middle = hidden_in + core_sum(attn_a, attn_b)
     unit_two, inverse_two = unit_parts(middle)
-    mixed = both_images((unit_two * norm_gain[1] + norm_bias[1]).astype(bf16))
-    cot = both_images(cot_own)
-
-    down_part = 0.0
-    mixed_part = 0.0
-    grad_down = [[None, None], [None, None]]
-    grad_up = [[None, None], [None, None]]
-    for i in range(2):
-        for j in range(2):
-            up_mat = up_full[i][j].reshape(-1, D)
-            down_mat = down_full[i][j].reshape(-1, D)
-            shape = (ZS, quarter, D)
-            up_input = matmul(mixed, up_mat, "rd,fd->rf")
-            gelu_value, gelu_back = jax.vjp(gelu_exact, up_input)
-            activation = gelu_value.astype(bf16)
-            down_part = down_part + matmul(activation, down_mat, "rf,fd->rd")
-            grad_down[i][j] = matmul(activation, cot, "rf,rd->fd").astype(bf16).reshape(shape)
-            grad_act = matmul(cot, down_mat, "rd,fd->rf")
-            grad_up_in = gelu_back(grad_act)[0].astype(bf16)
-            grad_up[i][j] = matmul(grad_up_in, mixed, "rf,rd->fd").astype(bf16).reshape(shape)
-            mixed_part = mixed_part + matmul(grad_up_in, up_mat, "rf,fd->rd")
-    down_own = reduce_all(grad_down)
-    up_own = reduce_all(grad_up)
-    block_own = (middle + core_sum(down_part)).astype(bf16)
-
+    mixed_own = padded((unit_two * norm_gain[1] + norm_bias[1]).astype(bf16))
+    mixed_pair = jnp.concatenate([mixed_own, over_x(mixed_own)])
+    mixed = jnp.concatenate([mixed_pair, core(mixed_pair)])
+    cot = jnp.concatenate([cot_pair, core(cot_pair)])
+
+    down_a, down_b, mixed_a, mixed_b, ffn_grad = ffn(mixed, cot, ffn_full)
+    mixed_sum = mixed_a + core(mixed_b)
+    mixed_far = over_x(mixed_sum[PAD:].astype(bf16))
+    ffn_near, ffn_give = split_y(ffn_grad)
+    ffn_far = over_y(ffn_give)
+
+    mixed_far, down_b = tie(mixed_far, down_b)
+    down_sum = down_a + core(down_b)
+    down_far = over_x(down_sum[PAD:].astype(bf16))
     back_middle, gain_two, bias_two = norm_back_own(
-        unit_two, inverse_two, core_sum(mixed_part), norm_gain[1]
+        unit_two,
+        inverse_two,
+        (mixed_sum[:PAD] + mixed_far.astype(f32))[:SEQ],
+        norm_gain[1],
     )
     grad_middle = cot_own.astype(f32) + back_middle
     middle_low = both_images(grad_middle.astype(bf16))
-    normed_part = 0.0
-    grad_attn = []
-    for j in range(2):
-        q, k, v, probs, probs_low, rows = kept[j]
-        grad_out = matmul(attended[j], middle_low, "rc,rd->cd").astype(bf16)
-        grad_attended = (
-            matmul(middle_low, rows[3], "rd,cd->rc").astype(bf16).reshape(2, SEQ, heads, half_head)
+    normed_a, normed_b, attn_grad = attn_backward(
+        meta, normed, middle_low, attn_full, qkv_kept, attended
+    )
+
+    normed_b, ffn_far, down_far = tie(normed_b, ffn_far, down_far)
+    own, other = attn_grad[0], attn_grad[1]
+    attn_from_x = over_x(other[ZS : ZS + half])
+    attn_from_y = over_y(other[ZS + half :])
+    ffn_total = add_low(ffn_near, ffn_far)
+    ffn_pieces = z_line(shifted(ffn_total))
+    block_own = (middle + (down_sum[:PAD] + down_far.astype(f32))[:SEQ]).astype(bf16)
+    block_near, block_give = split_y(
+        block_own.reshape(SEQ, narrow_count, feat).transpose(1, 0, 2)
+    )
+    block_far = over_y(block_give)
+    back_hidden, gain_one, bias_one = norm_back_own(
+        unit_one, inverse_one, core_sum(normed_a, normed_b), norm_gain[0]
+    )
+    hidden_low = both_images((grad_middle + back_hidden).astype(bf16))
+
+    hidden_low, attn_from_x, attn_from_y, block_far = tie(
+        hidden_low, attn_from_x, attn_from_y, block_far
+    )
+    attn_beside = over_y(
+        jnp.concatenate([add_low(own[ZS : ZS + half], attn_from_x), own[ZS + half :]])
+    )
+    attn_across = over_x(
+        jnp.concatenate([other[:half], add_low(other[half:ZS], attn_from_y)])
+    )
+    grad_skip = matmul(flat, hidden_low, "rc,rd->cd").astype(bf16)
+    grad_skip = grad_skip.reshape(narrow_count, 2, feat // 2, D)
+    skip_own, skip_other = pick(grad_skip, xi, 1), pick(grad_skip, 1 - xi, 1)
+    token_grad = matmul(hidden_low, skip_mat, "rd,cd->rc").astype(bf16)
+    kept_grads = token_grad.reshape(2, PAD, 2, ZS, feat)[:, :SEQ].transpose(2, 3, 0, 1, 4)
+
+    attn_beside, attn_across, skip_own, skip_other, kept_grads, *ffn_pieces = tie(
+        attn_beside, attn_across, skip_own, skip_other, kept_grads, *ffn_pieces
+    )
+    skip_from_x = over_x(skip_other[ZS : ZS + half])
+    skip_from_y = over_y(skip_other[ZS + half :])
+    attn_total = (
+        own[:ZS].astype(f32) + attn_beside.astype(f32) + attn_across.astype(f32)
+    ).astype(bf16)
+    attn_pieces = [attn_total[0]] + [over_z(attn_total[step], -step) for step in range(1, ZS)]
+    grads_far = over_y(kept_grads[1])
+    ffn_own = sum(piece.astype(f32) for piece in ffn_pieces).astype(bf16)
+    ffn_x = over_x(ffn_own)
+
+    skip_from_x, skip_from_y, grads_far, ffn_x = tie(skip_from_x, skip_from_y, grads_far, ffn_x)
+    skip_beside = over_y(
+        jnp.concatenate(
+            [add_low(skip_own[ZS : ZS + half], skip_from_x), skip_own[ZS + half :]]
         )
-        grad_v = matmul(probs_low, grad_attended, "bhqk,bqhe->bkhe")
-        grad_probs = matmul(grad_attended, v, "bqhe,bkhe->bhqk")
-        inner_sum = jnp.sum(probs * grad_probs, axis=-1, keepdims=True)
-        grad_scores = (probs * (grad_probs - inner_sum) * scale_factor).astype(bf16)
-        grad_q = matmul(grad_scores, k, "bhqk,bkhe->bqhe")
-        grad_k = matmul(grad_scores, q, "bhqk,bqhe->bkhe")
-        mats = []
-        for t, grad in enumerate((grad_q, grad_k, grad_v)):
-            low = grad.astype(bf16).reshape(2 * SEQ, heads * half_head)
-            mats.append(matmul(low, normed, "rc,rd->cd").astype(bf16))
-            normed_part = normed_part + matmul(low, rows[t], "rc,cd->rd")
-        mats.append(grad_out)
-        grad_attn.append(
-            jnp.stack([mat.reshape(heads, half_head, D) for mat in mats], axis=1).reshape(
-                heads, 4 * half_head, D
-            )
-        )
-    attn_own = reduce_then_x(grad_attn)
-    back_hidden, gain_one, bias_one = norm_back_own(
-        unit_one, inverse_one, core_sum(normed_part), norm_gain[0]
-    )
-    hidden_own = (grad_middle + back_hidden).astype(bf16)
-    hidden_low = both_images(hidden_own)
-    grad_skip = [
-        matmul(part, hidden_low, "rc,rd->cd").astype(bf16).reshape(ZS, feat, D) for part in flat
-    ]
-    skip_own = reduce_then_x(grad_skip)
-
-    def to_features(grid):
-        blocks = to_images(grid.reshape((narrow_count,) + grid.shape[2:]))
-        return canonical(blocks)
-
-    block_out = to_features(
-        block_own.reshape(SEQ, ZS, YS, feat).transpose(1, 2, 0, 3)
-    ).reshape(rows_local, feat)
-    token_grads = [
-        matmul(hidden_low, mat, "rd,cd->rc").astype(bf16).reshape(2, SEQ, ZS, feat)
-        for mat in skip_mats
-    ]
-    kept_grads = jnp.stack([grad.transpose(2, 0, 1, 3) for grad in token_grads])
-    returned = jnp.stack([kept_grads[0], over_y(kept_grads[1])])
-    backs = [returned[:, 0]]
-    for step in range(1, ZS):
-        backs.append(over_z(returned[:, step], -step))
-    stacked = jnp.stack(backs)
-    ordered = []
-    for number in range(narrow_count):
-        step = (number // 2 - zi) % ZS
-        ordered.append(pick(pick(stacked, step, 0), yi ^ (number % 2), 0))
-    ordered = jnp.stack(ordered)
+    )
+    skip_across = over_x(
+        jnp.concatenate([skip_other[:half], add_low(skip_other[half:ZS], skip_from_y)])
+    )
+    returned = jnp.stack([kept_grads[0], grads_far])
+    backs = [returned[:, 0]] + [over_z(returned[:, step], -step) for step in range(1, ZS)]
+    ffn_pair = jnp.stack([ffn_own, ffn_x])
+    ffn_core = core(ffn_pair)
+
+    skip_beside, skip_across, ffn_core, *attn_pieces = tie(
+        skip_beside, skip_across, ffn_core, *attn_pieces
+    )
+    skip_total = (
+        skip_own[:ZS].astype(f32) + skip_beside.astype(f32) + skip_across.astype(f32)
+    ).astype(bf16)
+    skip_pieces = [skip_total[0]] + [over_z(skip_total[step], -step) for step in range(1, ZS)]
+    attn_own = sum(piece.astype(f32) for piece in attn_pieces).astype(bf16)
+    attn_x = over_x(attn_own)
+    block_blocks = z_line(z_pieces(block_near, block_far))
+
+    *backs, attn_x = tie(*backs, attn_x)
+    attn_pair = jnp.stack([attn_own, attn_x])
+    attn_core = core(attn_pair)
+    ordered = canonical(backs, -1)
     grad_mine = ordered[:, 0].reshape(rows_local, feat)
     grad_given = core(ordered[:, 1].reshape(rows_local, feat))
     grad_stream = jnp.where(is_first, grad_mine, grad_given).astype(f32)
     grad_skip_in = jnp.where(is_first, grad_given, grad_mine).astype(f32)
-
-    down_all = spread(down_own).reshape(hidden, D)
-    up_all = spread(up_own).reshape(hidden, D)
-    attn_all = spread(attn_own).reshape(2, 4, half_head, D)
-    skip_all = spread(skip_own).reshape(2, feat, D)
+    block_out = canonical(block_blocks).reshape(rows_local, feat)
+    skip_last = sum(piece.astype(f32) for piece in skip_pieces).astype(bf16)
+    skip_pair = jnp.stack([skip_last, over_x(skip_last)])
+    skip_core = core(skip_pair)
+
+    def in_order(pair, other_core):
+        four = jnp.stack([pair, other_core])
+        return jnp.stack(
+            [pick(pick(four, c ^ ci, 0), x ^ xi, 0) for c in range(2) for x in range(2)]
+        )
+
+    ffn_all = in_order(ffn_pair, ffn_core)
+    up_all = ffn_all[:, 0].reshape(hidden, D)
+    down_all = ffn_all[:, 1].reshape(hidden, D)
+    attn_all = in_order(attn_pair, attn_core).reshape(2, 4, half_head, D)
+    skip_all = in_order(skip_pair, skip_core).reshape(2, feat, D)
     qkv_all = attn_all[:, :3].transpose(1, 0, 2, 3).reshape(3, feat, D)
     out_all = attn_all[:, 3].reshape(feat, D)
 

time: 972 us -> 725 us (0.75)
  matrix products: 176 us -> 6.34 us
  Pallas kernels: 0 us -> 91.9 us
  waiting for transfers between devices: 339 us -> 266 us
  local copies, waits for them, and re-layouts: 125 us -> 73.4 us
  starting transfers between devices: 182 us -> 154 us
  other arithmetic: 125 us -> 97.7 us
  between operations: 14.6 us -> 26.6 us
    dot_general x66 -> x3, matrix products: 176 us -> 6.34 us  [matmul(): return jnp.einsum(form, left, right, preferred_element_type=jnp.float32)]
    pallas_call x0 -> x3, Pallas kernels: none -> 91.9 us  [the longest x1 36.2 us: attn_backward(): pl.pallas_call(attn_backward_kernel, out_shape=[jax.ShapeDtypeStruct((tok...]
    ppermute x86 -> x78, waiting for transfers between devices: 339 us -> 266 us  [send(): return lax.ppermute(value, axes, perm(move))]
    ppermute x86 -> x78, starting transfers between devices: 182 us -> 154 us  [send(): return lax.ppermute(value, axes, perm(move))]
    reshape x22 -> x3, local copies, waits for them, and re-layouts: 25.5 us -> 4.59 us  [the longest x1 1.7 us: chips(): token_grad.reshape(2, PAD, 2, ZS, feat)[:, :SEQ].transpose(2, 3, 0, 1, 4)]
    another operation x17 -> x14, other arithmetic: 33.3 us -> 15.4 us  [the longest x3 4.22 us: chips(): jnp.stack([jnp.concatenate([attn_line, attn_beside]), jnp.concatenate([at...]
    unnamed x391 -> x203, local copies, waits for them, and re-layouts: 25.1 us -> 15.6 us
  transfers between devices with their start and end apart: 86 -> 79, of which waited for: 39 -> 36; matrix products, arithmetic and copies ran while one was open for 36% -> 19% of each run, Pallas kernels for 0% -> 8%
where the time goes in v2:
time: 725 us; the launch traced here: 717 us
  waiting for transfers between devices  266 us (37%)
  starting transfers between devices  154 us (21%)
  other arithmetic  97.7 us (13%)
  Pallas kernels  91.9 us (13%)
  local copies, waits for them, and re-layouts  73.4 us (10%)
  between operations  26.6 us (4%)
    ppermute x78, waiting for transfers between devices, send(): return lax.ppermute(value, axes, perm(move))  266 us
    ppermute x78, starting transfers between devices, send(): return lax.ppermute(value, axes, perm(move))  154 us
    pallas_call x1, Pallas kernels, attn_backward(): pl.pallas_call(attn_backward_kernel, out_shape=[jax.ShapeDtypeStruct((tok...  36.2 us
    pallas_call x1, Pallas kernels, ffn(): pl.pallas_call(ffn_kernel, out_shape=[part] * 4 + [jax.ShapeDtypeStruct(w...  36.1 us
    pallas_call x1, Pallas kernels, attn_forward(): pl.pallas_call(attn_forward_kernel, out_shape=[jax.ShapeDtypeStruct((toke...  19.5 us
    unnamed x203, local copies, waits for them, and re-layouts  15.6 us
  transfers between devices with their start and end apart: 79, of which 36 were waited for; matrix products, arithmetic and copies ran while one was open for 19% of the time, Pallas kernels for 8%

profile of v2, /device:TPU:0, one launch (start us, length us, event | category | flops | bytes accessed | tf_op | source)
XLA Modules:
  0.0 716.8 jit_solution(7904002311850141178)
XLA Ops:
  10.0 2.6 collective-permute-start.1
  12.6 2.6 collective-permute-start.2
  21.2 2.2 stack.334
  28.6 17.8 %collective-permute-done.4 = bf16[4,2,258,144]{2,3,1,0:T(8,128)(2,1)} collective-permute-done((bf16[4,2,258,144]{2,3,1,0:T(8,128)(2,1)}, bf16[4,2,258,144]{2,3,1,0:T(8,128)(2,1)}, u32[]{:S(2)}, u32[]{:S(2)}) %collective-permute-start.4) | collective-permute-done | bytes 594464 | tf_op jit(solution)/shard_map/ppermute | solution.py:595
  49.6 2.7 fusion.29
  54.4 2.8 collective-permute-start.7
  59.9 8.6 %collective-permute-done.5 = bf16[2,2,258,144]{2,3,1,0:T(8,128)(2,1)S(1)} collective-permute-done((bf16[2,2,258,144]{2,3,1,0:T(8,128)(2,1)}, bf16[2,2,258,144]{2,3,1,0:T(8,128)(2,1)S(1)}, u32[]{:S(2)}, u32[]{:S(2)}) %collective-permute-start.5) | collective-permute-done | bytes 297248 | tf_op jit(solution)/shard_map/ppermute | solution.py:595
  68.5 16.2 %collective-permute-done.6 = bf16[2,2,258,144]{2,3,1,0:T(8,128)(2,1)S(1)} collective-permute-done((bf16[2,2,258,144]{2,3,1,0:T(8,128)(2,1)}, bf16[2,2,258,144]{2,3,1,0:T(8,128)(2,1)S(1)}, u32[]{:S(2)}, u32[]{:S(2)}) %collective-permute-start.6) | collective-permute-done | bytes 297248 | tf_op jit(solution)/shard_map/ppermute | solution.py:595
  84.8 16.5 %collective-permute-start.10 = (bf16[144,1152]{1,0:T(8,128)(2,1)S(1)}, bf16[144,1152]{1,0:T(8,128)(2,1)}, u32[]{:S(2)}, u32[]{:S(2)}) collective-permute-start(bf16[144,1152]{1,0:T(8,128)(2,1)S(1)} %dynamic-slice_bitcast_fusion.15), channel_id=1, source_target_pairs={{0,2},{1,3},{2,4},{3,5},{4,6},{5,7},{6,0},{7,1},{8,10},{9,11},{10,... | collective-permute-start | bytes 995336 | tf_op jit(solution)/shard_map/ppermute | solution.py:595
  101.2 2.6 collective-permute-start.12
  122.2 2.7 pad_maximum_fusion.6
  124.9 3.2 collective-permute-done.13
  136.4 3.4 collective-permute-start.20
  139.8 3.5 collective-permute-start.21
  144.7 4.5 collective-permute-done.20
  149.1 19.2 %collective-permute-done.21 = bf16[2,258,144]{1,2,0:T(8,128)(2,1)S(1)} collective-permute-done((bf16[2,258,144]{1,2,0:T(8,128)(2,1)S(1)}, bf16[2,258,144]{1,2,0:T(8,128)(2,1)S(1)}, u32[]{:S(2)}, u32[]{:S(2)}) %collective-permute-start.21) | collective-permute-done | bytes 148640 | tf_op jit(solution)/shard_map/ppermute | solution.py:595
  180.4 9.1 %collective-permute-done.25 = bf16[272,1152]{1,0:T(8,128)(2,1)S(1)} collective-permute-done((bf16[272,1152]{1,0:T(8,128)(2,1)S(1)}, bf16[272,1152]{1,0:T(8,128)(2,1)S(1)}, u32[]{:S(2)}, u32[]{:S(2)}) %collective-permute-start.25) | collective-permute-done | bytes 626720 | tf_op jit(solution)/shard_map/ppermute | solution.py:595
  189.7 12.3 %collective-permute-done.23 = bf16[2,144,1152]{2,1,0:T(8,128)(2,1)S(1)} collective-permute-done((bf16[2,144,1152]{2,1,0:T(8,128)(2,1)S(1)}, bf16[2,144,1152]{2,1,0:T(8,128)(2,1)S(1)}, u32[]{:S(2)}, u32[]{:S(2)}) %collective-permute-start.23) | collective-permute-done | bytes 663584 | tf_op jit(solution)/shard_map/ppermute | solution.py:595
  204.2 19.5 %attn_forward.1 = (f32[272,1152]{1,0:T(8,128)S(1)}, f32[272,1152]{1,0:T(8,128)S(1)}, bf16[8,544,216]{2,1,0:T(8,128)(2,1)S(1)}, bf16[8,544,72]{2,1,0:T(8,128)(2,1)S(1)}) custom-call(s32[1]{0:T(128)} %bitcast.41.meta_ref, bf16[544,1152]{1,0:T(8,128)(2,1)S(1)} %pad_maximum_fusion.11.normed_ref, bf16[2,8,144,1152]{3,2,1,0:T(8,128)(2,1)S(1)} %pad_maximum_fusion.qk_ref.vo_ref, ...), custom_call_target="tpu_custom_call" | custom-call | flops 2887778304 | bytes 16777216 | tf_op jit(solution)/shard_map/attn_forward/pallas_call | solution.py:438
  223.9 2.9 collective-permute-done.26
  229.8 14.6 %collective-permute-done.27 = bf16[272,1152]{1,0:T(8,128)(2,1)S(1)} collective-permute-done((bf16[272,1152]{1,0:T(8,128)(2,1)S(1)}, bf16[272,1152]{1,0:T(8,128)(2,1)S(1)}, u32[]{:S(2)}, u32[]{:S(2)}) %collective-permute-start.27) | collective-permute-done | bytes 626720 | tf_op jit(solution)/shard_map/ppermute | solution.py:595
  249.2 36.1 %ffn.1 = (f32[544,1152]{1,0:T(8,128)}, f32[544,1152]{1,0:T(8,128)}, f32[544,1152]{1,0:T(8,128)}, f32[544,1152]{1,0:T(8,128)}, bf16[8,2,144,1152]{3,2,1,0:T(8,128)(2,1)}) custom-call(bf16[1088,1152]{1,0:T(8,128)(2,1)} %pad_maximum_fusion.2.mixed_ref, bf16[1088,1152]{1,0:T(8,128)(2,1)} %pad_maximum_fusion.3.cot_ref, bf16[8,2,144,1152]{3,2,1,0:T(8,128)(2,1)} %bitcast.406), custom_call_target="tpu_custom_call" | custom-call | flops 17326669824 | bytes 33554432 | tf_op jit(solution)/shard_map/ffn/pallas_call | solution.py:380
  285.5 4.8 collective-permute-done.30
  290.4 2.1 add.758
  294.1 14.7 %collective-permute-done.31 = bf16[272,1152]{1,0:T(8,128)(2,1)S(1)} collective-permute-done((bf16[272,1152]{1,0:T(8,128)(2,1)S(1)}, bf16[272,1152]{1,0:T(8,128)(2,1)S(1)}, u32[]{:S(2)}, u32[]{:S(2)}) %collective-permute-start.31) | collective-permute-done | bytes 626720 | tf_op jit(solution)/shard_map/ppermute | solution.py:595
  316.8 2.2 add.759
  320.6 36.2 %attn_backward.1 = (f32[272,1152]{1,0:T(8,128)S(1)}, f32[272,1152]{1,0:T(8,128)}, bf16[2,8,144,1152]{3,2,1,0:T(8,128)(2,1)}) custom-call(s32[1]{0:T(128)} %bitcast.41.meta_ref, bf16[544,1152]{1,0:T(8,128)(2,1)S(1)} %pad_maximum_fusion.11.normed_ref, bf16[544,1152]{1,0:T(8,128)(2,1)S(1)} %pad_maximum_fusion.14.low_ref, bf16[2,8,144,1152]{3,2,1,0:T(8,128)(2,1)} %copy-done.2, ...), custom_call_target="tpu_custom_call" | custom-call | flops 5775556608 | bytes 25165824 | tf_op jit(solution)/shard_map/attn_backward/pallas_call | solution.py:514
  356.8 3.2 slice_bitcast_fusion.2
  362.0 9.2 %collective-permute-done.34 = bf16[4,2,144,1152]{3,2,1,0:T(8,128)(2,1)} collective-permute-done((bf16[4,2,144,1152]{3,2,1,0:T(8,128)(2,1)}, bf16[4,2,144,1152]{3,2,1,0:T(8,128)(2,1)}, u32[]{:S(2)}, u32[]{:S(2)}) %collective-permute-start.34) | collective-permute-done | bytes 2654240 | tf_op jit(solution)/shard_map/ppermute | solution.py:595
  374.1 3.2 fusion
  379.3 2.1 multiply_reduce_fusion.4
  387.0 10.6 %collective-permute-done.40 = bf16[4,258,144]{1,2,0:T(8,128)(2,1)} collective-permute-done((bf16[4,258,144]{1,2,0:T(8,128)(2,1)S(1)}, bf16[4,258,144]{1,2,0:T(8,128)(2,1)}, u32[]{:S(2)}, u32[]{:S(2)}) %collective-permute-start.40) | collective-permute-done | bytes 297248 | tf_op jit(solution)/shard_map/ppermute | solution.py:595
  409.7 19.6 %collective-permute-start.41 = (bf16[2,258,144]{1,2,0:T(8,128)(2,1)S(1)}, bf16[2,258,144]{1,2,0:T(8,128)(2,1)S(1)}, u32[]{:S(2)}, u32[]{:S(2)}) collective-permute-start(bf16[2,258,144]{1,2,0:T(8,128)(2,1)S(1)} %get-tuple-element.492), channel_id=1, source_target_pairs={{0,2},{1,3},{2,4},{3,5},{4,6},{5,7},{6,0},{7,1},{8,10},{9,11},{10,... | collective-permute-start | bytes 445832 | tf_op jit(solution)/shard_map/ppermute | solution.py:595
  429.3 2.4 collective-permute-start.43
  431.7 2.4 convolution_convert_fusion
  435.3 7.4 %collective-permute-start.46 = (bf16[2,144,1152]{2,1,0:T(8,128)(2,1)S(1)}, bf16[2,144,1152]{2,1,0:T(8,128)(2,1)S(1)}, u32[]{:S(2)}, u32[]{:S(2)}) collective-permute-start(bf16[2,144,1152]{2,1,0:T(8,128)(2,1)S(1)} %copy-done.49), channel_id=1, source_target_pairs={{0,2},{1,3},{2,4},{3,5},{4,6},{5,7},{6,0},{7,1},{8,10},{9,11},{10,... | collective-permute-start | bytes 1990664 | tf_op jit(solution)/shard_map/ppermute | solution.py:595
  442.9 2.3 collective-permute-start.47
  445.2 7.5 %collective-permute-start.48 = (bf16[2,144,1152]{2,1,0:T(8,128)(2,1)S(1)}, bf16[2,144,1152]{2,1,0:T(8,128)(2,1)S(1)}, u32[]{:S(2)}, u32[]{:S(2)}) collective-permute-start(bf16[2,144,1152]{2,1,0:T(8,128)(2,1)S(1)} %copy-done.47), channel_id=1, source_target_pairs={{0,6},{1,7},{2,0},{3,1},{4,2},{5,3},{6,4},{7,5},{8,14},{9,15},{10,... | collective-permute-start | bytes 1990664 | tf_op jit(solution)/shard_map/ppermute | solution.py:595
  453.1 5.8 collective-permute-done.46
  458.9 29.3 %collective-permute-done.47 = bf16[2,144,1152]{2,1,0:T(8,128)(2,1)S(1)} collective-permute-done((bf16[2,144,1152]{2,1,0:T(8,128)(2,1)S(1)}, bf16[2,144,1152]{2,1,0:T(8,128)(2,1)S(1)}, u32[]{:S(2)}, u32[]{:S(2)}) %collective-permute-start.47) | collective-permute-done | bytes 663584 | tf_op jit(solution)/shard_map/ppermute | solution.py:595
  488.3 14.1 %collective-permute-done.48 = bf16[2,144,1152]{2,1,0:T(8,128)(2,1)S(1)} collective-permute-done((bf16[2,144,1152]{2,1,0:T(8,128)(2,1)S(1)}, bf16[2,144,1152]{2,1,0:T(8,128)(2,1)S(1)}, u32[]{:S(2)}, u32[]{:S(2)}) %collective-permute-start.48) | collective-permute-done | bytes 663584 | tf_op jit(solution)/shard_map/ppermute | solution.py:595
  511.2 5.0 collective-permute-start.59
  516.2 10.6 %collective-permute-done.49 = bf16[2,72,1152]{2,1,0:T(8,128)(2,1)S(1)} collective-permute-done((bf16[2,72,1152]{2,1,0:T(8,128)(2,1)S(1)}, bf16[2,72,1152]{2,1,0:T(8,128)(2,1)S(1)}, u32[]{:S(2)}, u32[]{:S(2)}) %collective-permute-start.49) | collective-permute-done | bytes 331808 | tf_op jit(solution)/shard_map/ppermute | solution.py:595
  526.7 6.9 collective-permute-done.50
  540.6 3.5 collective-permute-start.61
  544.1 4.9 fusion.36
  549.0 16.6 %collective-permute-done.60 = bf16[144,1152]{1,0:T(8,128)(2,1)S(1)} collective-permute-done((bf16[144,1152]{1,0:T(8,128)(2,1)}, bf16[144,1152]{1,0:T(8,128)(2,1)S(1)}, u32[]{:S(2)}, u32[]{:S(2)}) %collective-permute-start.60) | collective-permute-done | bytes 331808 | tf_op jit(solution)/shard_map/ppermute | solution.py:595
  565.9 2.4 fusion.20
  569.5 2.7 slice_convert_fusion.2
  578.2 4.1 collective-permute-start.64
  586.3 2.2 dynamic-slice_bitcast_fusion.3
  590.9 25.3 %collective-permute-start.55 = (bf16[2,2,258,144]{2,1,3,0:T(2,128)(2,1)}, bf16[2,2,258,144]{2,1,3,0:T(2,128)(2,1)S(1)}, u32[]{:S(2)}, u32[]{:S(2)}) collective-permute-start(bf16[2,2,258,144]{2,1,3,0:T(2,128)(2,1)} %get-tuple-element.462), channel_id=1, source_target_pairs={{0,2},{1,3},{2,4},{3,5},{4,6},{5,7},{6,0},{7,1},{8,10},{9,11},{10,... | collective-permute-start | bytes 891656 | tf_op jit(solution)/shard_map/ppermute | solution.py:595
  616.1 2.1 collective-permute-done.65
  621.4 2.7 collective-permute-done.55
  624.2 4.7 collective-permute-done.62
  630.8 4.6 pad_maximum_fusion.5
  647.8 3.8 collective-permute-done.73
  652.6 3.9 collective-permute-done.74
  663.7 2.5 fusion.13
  666.2 2.7 select_convert_fusion
  677.9 2.6 collective-permute-done.75
  681.7 3.3 collective-permute-done.76
  685.9 5.2 collective-permute-done.77
  700.5 3.4 multiply_add_fusion
  (528 shorter events, 179.8 us)
Async XLA Ops:
  7.2 242.0 %all-gather.3.cloned.1.call-start = ((), (), s32[]{:S(2)}) async-start(), calls=%async_computation | async-start | bytes 5971968 | tf_op jit(solution)/shard_map/all_gather | solution.py:699
  8.8 12.4 %collective-permute-start = (bf16[2064,144]{0,1:T(8,128)(2,1)S(1)}, bf16[2064,144]{0,1:T(8,128)(2,1)}, u32[]{:S(2)}, u32[]{:S(2)}) collective-permute-start(bf16[2064,144]{0,1:T(8,128)(2,1)S(1)} %get-tuple-element.490), channel_id=1, source_target_pairs={{0,8},{1,9},{2,10},{3,11},{4,12},{5,13},{6,14},{7,15},{8,0},{9,1},... | collective-permute-start | bytes 1783304 | tf_op jit(solution)/shard_map/ppermute | solution.py:595
  10.0 17.4 %collective-permute-start.1 = (bf16[72,1152]{1,0:T(8,128)(2,1)}, bf16[72,1152]{1,0:T(8,128)(2,1)}, u32[]{:S(2)}, u32[]{:S(2)}) collective-permute-start(bf16[72,1152]{1,0:T(8,128)(2,1)} %fusion.113), channel_id=1, source_target_pairs={{0,2},{1,3},{2,4},{3,5},{4,6},{5,7},{6,0},{7,1},{8,10},{9,11},{10,... | collective-permute-start | bytes 497672 | tf_op jit(solution)/shard_map/ppermute | solution.py:595
  12.6 14.8 %collective-permute-start.2 = (bf16[72,1152]{1,0:T(8,128)(2,1)}, bf16[72,1152]{1,0:T(8,128)(2,1)}, u32[]{:S(2)}, u32[]{:S(2)}) collective-permute-start(bf16[72,1152]{1,0:T(8,128)(2,1)} %fusion.113), channel_id=1, source_target_pairs={{0,4},{1,5},{2,6},{3,7},{4,0},{5,1},{6,2},{7,3},{8,12},{9,13},{10,... | collective-permute-start | bytes 497672 | tf_op jit(solution)/shard_map/ppermute | solution.py:595
  15.2 12.2 %collective-permute-start.3 = (bf16[72,1152]{1,0:T(8,128)(2,1)}, bf16[72,1152]{1,0:T(8,128)(2,1)}, u32[]{:S(2)}, u32[]{:S(2)}) collective-permute-start(bf16[72,1152]{1,0:T(8,128)(2,1)} %fusion.113), channel_id=1, source_target_pairs={{0,6},{1,7},{2,0},{3,1},{4,2},{5,3},{6,4},{7,5},{8,14},{9,15},{10,... | collective-permute-start | bytes 497672 | tf_op jit(solution)/shard_map/ppermute | solution.py:595
  25.0 21.5 %collective-permute-start.4 = (bf16[4,2,258,144]{2,3,1,0:T(8,128)(2,1)}, bf16[4,2,258,144]{2,3,1,0:T(8,128)(2,1)}, u32[]{:S(2)}, u32[]{:S(2)}) collective-permute-start(bf16[4,2,258,144]{2,3,1,0:T(8,128)(2,1)} %get-tuple-element.472), channel_id=1, source_target_pairs={{0,1},{1,0},{2,3},{3,2},{4,5},{5,4},{6,7},{7,6},{8,9},{9,8},{10,11... | collective-permute-start | bytes 1783304 | tf_op jit(solution)/shard_map/ppermute | solution.py:595
  46.5 38.3 %collective-permute-start.8 = (bf16[4,72,1152]{2,1,0:T(8,128)(2,1)S(1)}, bf16[4,72,1152]{2,1,0:T(8,128)(2,1)}, u32[]{:S(2)}, u32[]{:S(2)}) collective-permute-start(bf16[4,72,1152]{2,1,0:T(8,128)(2,1)S(1)} %pad_maximum_fusion.18), channel_id=1, source_target_pairs={{0,1},{1,0},{2,3},{3,2},{4,5},{5,4},{6,7},{7,6},{8,9},{9,8},{10,11... | collective-permute-start | bytes 1990664 | tf_op jit(solution)/shard_map/ppermute | solution.py:595
  48.0 36.8 %collective-permute-start.9 = (bf16[4,72,1152]{2,1,0:T(8,128)(2,1)S(1)}, bf16[4,72,1152]{2,1,0:T(8,128)(2,1)}, u32[]{:S(2)}, u32[]{:S(2)}) collective-permute-start(bf16[4,72,1152]{2,1,0:T(8,128)(2,1)S(1)} %pad_maximum_fusion.18), channel_id=1, source_target_pairs={{0,16},{1,17},{2,18},{3,19},{4,20},{5,21},{6,22},{7,23},{8,24},{9,... | collective-permute-start | bytes 1990664 | tf_op jit(solution)/shard_map/ppermute | solution.py:595
  53.3 15.2 %collective-permute-start.5 = (bf16[2,2,258,144]{2,3,1,0:T(8,128)(2,1)}, bf16[2,2,258,144]{2,3,1,0:T(8,128)(2,1)S(1)}, u32[]{:S(2)}, u32[]{:S(2)}) collective-permute-start(bf16[2,2,258,144]{2,3,1,0:T(8,128)(2,1)} %get-tuple-element.470), channel_id=1, source_target_pairs={{0,2},{1,3},{2,4},{3,5},{4,6},{5,7},{6,0},{7,1},{8,10},{9,11},{10,... | collective-permute-start | bytes 891656 | tf_op jit(solution)/shard_map/ppermute | solution.py:595
  54.0 30.7 %collective-permute-start.6 = (bf16[2,2,258,144]{2,3,1,0:T(8,128)(2,1)}, bf16[2,2,258,144]{2,3,1,0:T(8,128)(2,1)S(1)}, u32[]{:S(2)}, u32[]{:S(2)}) collective-permute-start(bf16[2,2,258,144]{2,3,1,0:T(8,128)(2,1)} %get-tuple-element.471), channel_id=1, source_target_pairs={{0,4},{1,5},{2,6},{3,7},{4,0},{5,1},{6,2},{7,3},{8,12},{9,13},{10,... | collective-permute-start | bytes 891656 | tf_op jit(solution)/shard_map/ppermute | solution.py:595
  54.4 30.4 %collective-permute-start.7 = (bf16[2,2,258,144]{2,3,1,0:T(8,128)(2,1)}, bf16[2,2,258,144]{2,3,1,0:T(8,128)(2,1)S(1)}, u32[]{:S(2)}, u32[]{:S(2)}) collective-permute-start(bf16[2,2,258,144]{2,3,1,0:T(8,128)(2,1)} %get-tuple-element.468), channel_id=1, source_target_pairs={{0,6},{1,7},{2,0},{3,1},{4,2},{5,3},{6,4},{7,5},{8,14},{9,15},{10,... | collective-permute-start | bytes 891656 | tf_op jit(solution)/shard_map/ppermute | solution.py:595
  84.8 36.8 %collective-permute-start.10 = (bf16[144,1152]{1,0:T(8,128)(2,1)S(1)}, bf16[144,1152]{1,0:T(8,128)(2,1)}, u32[]{:S(2)}, u32[]{:S(2)}) collective-permute-start(bf16[144,1152]{1,0:T(8,128)(2,1)S(1)} %dynamic-slice_bitcast_fusion.15), channel_id=1, source_target_pairs={{0,2},{1,3},{2,4},{3,5},{4,6},{5,7},{6,0},{7,1},{8,10},{9,11},{10,... | collective-permute-start | bytes 995336 | tf_op jit(solution)/shard_map/ppermute | solution.py:595
  101.2 20.3 %collective-permute-start.11 = (bf16[144,1152]{1,0:T(8,128)(2,1)S(1)}, bf16[144,1152]{1,0:T(8,128)(2,1)}, u32[]{:S(2)}, u32[]{:S(2)}) collective-permute-start(bf16[144,1152]{1,0:T(8,128)(2,1)S(1)} %dynamic-slice_bitcast_fusion.15), channel_id=1, source_target_pairs={{0,4},{1,5},{2,6},{3,7},{4,0},{5,1},{6,2},{7,3},{8,12},{9,13},{10,... | collective-permute-start | bytes 995336 | tf_op jit(solution)/shard_map/ppermute | solution.py:595
  101.2 20.9 %collective-permute-start.12 = (bf16[144,1152]{1,0:T(8,128)(2,1)S(1)}, bf16[144,1152]{1,0:T(8,128)(2,1)}, u32[]{:S(2)}, u32[]{:S(2)}) collective-permute-start(bf16[144,1152]{1,0:T(8,128)(2,1)S(1)} %dynamic-slice_bitcast_fusion.15), channel_id=1, source_target_pairs={{0,6},{1,7},{2,0},{3,1},{4,2},{5,3},{6,4},{7,5},{8,14},{9,15},{10,... | collective-permute-start | bytes 995336 | tf_op jit(solution)/shard_map/ppermute | solution.py:595
  105.5 12.1 %collective-permute-start.14 = (bf16[2,72,1152]{2,1,0:T(8,128)(2,1)}, bf16[2,72,1152]{2,1,0:T(8,128)(2,1)}, u32[]{:S(2)}, u32[]{:S(2)}) collective-permute-start(bf16[2,72,1152]{2,1,0:T(8,128)(2,1)} %slice.345), channel_id=1, source_target_pairs={{0,16},{1,17},{2,18},{3,19},{4,20},{5,21},{6,22},{7,23},{8,24},{9,... | collective-permute-start | bytes 995336 | tf_op jit(solution)/shard_map/ppermute | solution.py:595
  107.8 11.4 %collective-permute-start.15 = (bf16[2,72,1152]{2,1,0:T(8,128)(2,1)}, bf16[2,72,1152]{2,1,0:T(8,128)(2,1)}, u32[]{:S(2)}, u32[]{:S(2)}) collective-permute-start(bf16[2,72,1152]{2,1,0:T(8,128)(2,1)} %slice.346), channel_id=1, source_target_pairs={{0,1},{1,0},{2,3},{3,2},{4,5},{5,4},{6,7},{7,6},{8,9},{9,8},{10,11... | collective-permute-start | bytes 995336 | tf_op jit(solution)/shard_map/ppermute | solution.py:595
  117.6 10.5 %collective-permute-start.13 = (bf16[4,258,144]{1,2,0:T(8,128)(2,1)S(1)}, bf16[4,258,144]{1,2,0:T(8,128)(2,1)S(1)}, u32[]{:S(2)}, u32[]{:S(2)}) collective-permute-start(bf16[4,258,144]{1,2,0:T(8,128)(2,1)S(1)} %bitcast.396), channel_id=1, source_target_pairs={{0,1},{1,0},{2,3},{3,2},{4,5},{5,4},{6,7},{7,6},{8,9},{9,8},{10,11... | collective-permute-start | bytes 891656 | tf_op jit(solution)/shard_map/ppermute | solution.py:595
  130.9 38.6 %collective-permute-start.18 = (bf16[4,144,1152]{2,1,0:T(8,128)(2,1)}, bf16[4,144,1152]{2,1,0:T(8,128)(2,1)}, u32[]{:S(2)}, u32[]{:S(2)}) collective-permute-start(bf16[4,144,1152]{2,1,0:T(8,128)(2,1)} %pad_maximum_fusion.6), channel_id=1, source_target_pairs={{0,1},{1,0},{2,3},{3,2},{4,5},{5,4},{6,7},{7,6},{8,9},{9,8},{10,11... | collective-permute-start | bytes 3981320 | tf_op jit(solution)/shard_map/ppermute | solution.py:595
  132.4 37.0 %collective-permute-start.19 = (bf16[4,144,1152]{2,1,0:T(8,128)(2,1)}, bf16[4,144,1152]{2,1,0:T(8,128)(2,1)}, u32[]{:S(2)}, u32[]{:S(2)}) collective-permute-start(bf16[4,144,1152]{2,1,0:T(8,128)(2,1)} %pad_maximum_fusion.6), channel_id=1, source_target_pairs={{0,16},{1,17},{2,18},{3,19},{4,20},{5,21},{6,22},{7,23},{8,24},{9,... | collective-permute-start | bytes 3981320 | tf_op jit(solution)/shard_map/ppermute | solution.py:595
  134.9 8.4 %collective-permute-start.17 = (bf16[272,1152]{1,0:T(8,128)(2,1)S(1)}, bf16[272,1152]{1,0:T(8,128)(2,1)}, u32[]{:S(2)}, u32[]{:S(2)}) collective-permute-start(bf16[272,1152]{1,0:T(8,128)(2,1)S(1)} %pad.36), channel_id=1, source_target_pairs={{0,8},{1,9},{2,10},{3,11},{4,12},{5,13},{6,14},{7,15},{8,0},{9,1},... | collective-permute-start | bytes 1880072 | tf_op jit(solution)/shard_map/ppermute | solution.py:595
  136.4 12.7 %collective-permute-start.20 = (bf16[2,258,144]{1,2,0:T(8,128)(2,1)S(1)}, bf16[2,258,144]{1,2,0:T(8,128)(2,1)S(1)}, u32[]{:S(2)}, u32[]{:S(2)}) collective-permute-start(bf16[2,258,144]{1,2,0:T(8,128)(2,1)S(1)} %get-tuple-element.499), channel_id=1, source_target_pairs={{0,2},{1,3},{2,4},{3,5},{4,6},{5,7},{6,0},{7,1},{8,10},{9,11},{10,... | collective-permute-start | bytes 445832 | tf_op jit(solution)/shard_map/ppermute | solution.py:595
  139.8 28.5 %collective-permute-start.21 = (bf16[2,258,144]{1,2,0:T(8,128)(2,1)S(1)}, bf16[2,258,144]{1,2,0:T(8,128)(2,1)S(1)}, u32[]{:S(2)}, u32[]{:S(2)}) collective-permute-start(bf16[2,258,144]{1,2,0:T(8,128)(2,1)S(1)} %get-tuple-element.500), channel_id=1, source_target_pairs={{0,4},{1,5},{2,6},{3,7},{4,0},{5,1},{6,2},{7,3},{8,12},{9,13},{10,... | collective-permute-start | bytes 445832 | tf_op jit(solution)/shard_map/ppermute | solution.py:595
  143.3 25.1 %collective-permute-start.22 = (bf16[2,258,144]{1,2,0:T(8,128)(2,1)S(1)}, bf16[2,258,144]{1,2,0:T(8,128)(2,1)S(1)}, u32[]{:S(2)}, u32[]{:S(2)}) collective-permute-start(bf16[2,258,144]{1,2,0:T(8,128)(2,1)S(1)} %get-tuple-element.497), channel_id=1, source_target_pairs={{0,6},{1,7},{2,0},{3,1},{4,2},{5,3},{6,4},{7,5},{8,14},{9,15},{10,... | collective-permute-start | bytes 445832 | tf_op jit(solution)/shard_map/ppermute | solution.py:595
  172.4 17.1 %collective-permute-start.25 = (bf16[272,1152]{1,0:T(8,128)(2,1)S(1)}, bf16[272,1152]{1,0:T(8,128)(2,1)S(1)}, u32[]{:S(2)}, u32[]{:S(2)}) collective-permute-start(bf16[272,1152]{1,0:T(8,128)(2,1)S(1)} %pad.37), channel_id=1, source_target_pairs={{0,16},{1,17},{2,18},{3,19},{4,20},{5,21},{6,22},{7,23},{8,24},{9,... | collective-permute-start | bytes 1880072 | tf_op jit(solution)/shard_map/ppermute | solution.py:595
  175.1 26.8 %collective-permute-start.23 = (bf16[2,144,1152]{2,1,0:T(8,128)(2,1)S(1)}, bf16[2,144,1152]{2,1,0:T(8,128)(2,1)S(1)}, u32[]{:S(2)}, u32[]{:S(2)}) collective-permute-start(bf16[2,144,1152]{2,1,0:T(8,128)(2,1)S(1)} %slice.352), channel_id=1, source_target_pairs={{0,16},{1,17},{2,18},{3,19},{4,20},{5,21},{6,22},{7,23},{8,24},{9,... | collective-permute-start | bytes 1990664 | tf_op jit(solution)/shard_map/ppermute | solution.py:595
  176.9 25.1 %collective-permute-start.24 = (bf16[2,144,1152]{2,1,0:T(8,128)(2,1)S(1)}, bf16[2,144,1152]{2,1,0:T(8,128)(2,1)S(1)}, u32[]{:S(2)}, u32[]{:S(2)}) collective-permute-start(bf16[2,144,1152]{2,1,0:T(8,128)(2,1)S(1)} %slice.353), channel_id=1, source_target_pairs={{0,1},{1,0},{2,3},{3,2},{4,5},{5,4},{6,7},{7,6},{8,9},{9,8},{10,11... | collective-permute-start | bytes 1990664 | tf_op jit(solution)/shard_map/ppermute | solution.py:595
  228.2 16.2 %collective-permute-start.27 = (bf16[272,1152]{1,0:T(8,128)(2,1)S(1)}, bf16[272,1152]{1,0:T(8,128)(2,1)S(1)}, u32[]{:S(2)}, u32[]{:S(2)}) collective-permute-start(bf16[272,1152]{1,0:T(8,128)(2,1)S(1)} %pad.38), channel_id=1, source_target_pairs={{0,16},{1,17},{2,18},{3,19},{4,20},{5,21},{6,22},{7,23},{8,24},{9,... | collective-permute-start | bytes 1880072 | tf_op jit(solution)/shard_map/ppermute | solution.py:595
  229.8 14.8 %collective-permute-start.29 = (bf16[544,1152]{1,0:T(8,128)(2,1)S(1)}, bf16[544,1152]{1,0:T(8,128)(2,1)S(1)}, u32[]{:S(2)}, u32[]{:S(2)}) collective-permute-start(bf16[544,1152]{1,0:T(8,128)(2,1)S(1)} %pad_maximum_fusion.12), channel_id=1, source_target_pairs={{0,8},{1,9},{2,10},{3,11},{4,12},{5,13},{6,14},{7,15},{8,0},{9,1},... | collective-permute-start | bytes 3760136 | tf_op jit(solution)/shard_map/ppermute | solution.py:595
  292.6 16.2 %collective-permute-start.31 = (bf16[272,1152]{1,0:T(8,128)(2,1)S(1)}, bf16[272,1152]{1,0:T(8,128)(2,1)S(1)}, u32[]{:S(2)}, u32[]{:S(2)}) collective-permute-start(bf16[272,1152]{1,0:T(8,128)(2,1)S(1)} %slice.612), channel_id=1, source_target_pairs={{0,16},{1,17},{2,18},{3,19},{4,20},{5,21},{6,22},{7,23},{8,24},{9,... | collective-permute-start | bytes 1880072 | tf_op jit(solution)/shard_map/ppermute | solution.py:595
  308.8 8.0 %collective-permute-start.32 = (f32[544,1152]{1,0:T(8,128)}, f32[544,1152]{1,0:T(8,128)}, u32[]{:S(2)}, u32[]{:S(2)}) collective-permute-start(f32[544,1152]{1,0:T(8,128)} %get-tuple-element.195), channel_id=1, source_target_pairs={{0,8},{1,9},{2,10},{3,11},{4,12},{5,13},{6,14},{7,15},{8,0},{9,1},... | collective-permute-start | bytes 7520264 | tf_op jit(solution)/shard_map/ppermute | solution.py:595
  310.5 60.7 %collective-permute-start.34 = (bf16[4,2,144,1152]{3,2,1,0:T(8,128)(2,1)}, bf16[4,2,144,1152]{3,2,1,0:T(8,128)(2,1)}, u32[]{:S(2)}, u32[]{:S(2)}) collective-permute-start(bf16[4,2,144,1152]{3,2,1,0:T(8,128)(2,1)} %dynamic-slice_bitcast_fusion), channel_id=1, source_target_pairs={{0,1},{1,0},{2,3},{3,2},{4,5},{5,4},{6,7},{7,6},{8,9},{9,8},{10,11... | collective-permute-start | bytes 7962632 | tf_op jit(solution)/shard_map/ppermute | solution.py:595
  319.0 52.2 %collective-permute-start.35 = (bf16[272,1152]{1,0:T(8,128)(2,1)S(1)}, bf16[272,1152]{1,0:T(8,128)(2,1)S(1)}, u32[]{:S(2)}, u32[]{:S(2)}) collective-permute-start(bf16[272,1152]{1,0:T(8,128)(2,1)S(1)} %slice.611), channel_id=1, source_target_pairs={{0,16},{1,17},{2,18},{3,19},{4,20},{5,21},{6,22},{7,23},{8,24},{9,... | collective-permute-start | bytes 1880072 | tf_op jit(solution)/shard_map/ppermute | solution.py:595
  360.0 27.0 %collective-permute-start.38 = (bf16[2,144,1152]{2,1,0:T(8,128)(2,1)}, bf16[2,144,1152]{2,1,0:T(8,128)(2,1)}, u32[]{:S(2)}, u32[]{:S(2)}) collective-permute-start(bf16[2,144,1152]{2,1,0:T(8,128)(2,1)} %get-tuple-element.435), channel_id=1, source_target_pairs={{0,16},{1,17},{2,18},{3,19},{4,20},{5,21},{6,22},{7,23},{8,24},{9,... | collective-permute-start | bytes 1990664 | tf_op jit(solution)/shard_map/ppermute | solution.py:595
  360.5 26.4 %collective-permute-start.39 = (bf16[2,144,1152]{2,1,0:T(8,128)(2,1)}, bf16[2,144,1152]{2,1,0:T(8,128)(2,1)}, u32[]{:S(2)}, u32[]{:S(2)}) collective-permute-start(bf16[2,144,1152]{2,1,0:T(8,128)(2,1)} %get-tuple-element.434), channel_id=1, source_target_pairs={{0,1},{1,0},{2,3},{3,2},{4,5},{5,4},{6,7},{7,6},{8,9},{9,8},{10,11... | collective-permute-start | bytes 1990664 | tf_op jit(solution)/shard_map/ppermute | solution.py:595
  371.2 7.7 %collective-permute-start.36 = (f32[272,1152]{1,0:T(8,128)}, f32[272,1152]{1,0:T(8,128)}, u32[]{:S(2)}, u32[]{:S(2)}) collective-permute-start(f32[272,1152]{1,0:T(8,128)} %get-tuple-element.203), channel_id=1, source_target_pairs={{0,8},{1,9},{2,10},{3,11},{4,12},{5,13},{6,14},{7,15},{8,0},{9,1},... | collective-permute-start | bytes 3760136 | tf_op jit(solution)/shard_map/ppermute | solution.py:595
  385.3 12.2 %collective-permute-start.40 = (bf16[4,258,144]{1,2,0:T(8,128)(2,1)S(1)}, bf16[4,258,144]{1,2,0:T(8,128)(2,1)}, u32[]{:S(2)}, u32[]{:S(2)}) collective-permute-start(bf16[4,258,144]{1,2,0:T(8,128)(2,1)S(1)} %get-tuple-element.495), channel_id=1, source_target_pairs={{0,1},{1,0},{2,3},{3,2},{4,5},{5,4},{6,7},{7,6},{8,9},{9,8},{10,11... | collective-permute-start | bytes 891656 | tf_op jit(solution)/shard_map/ppermute | solution.py:595
  405.9 96.5 %collective-permute-start.45 = (bf16[4,144,1152]{2,1,0:T(8,128)(2,1)S(1)}, bf16[4,144,1152]{2,1,0:T(8,128)(2,1)S(1)}, u32[]{:S(2)}, u32[]{:S(2)}) collective-permute-start(bf16[4,144,1152]{2,1,0:T(8,128)(2,1)S(1)} %pad_maximum_fusion.8), channel_id=1, source_target_pairs={{0,16},{1,17},{2,18},{3,19},{4,20},{5,21},{6,22},{7,23},{8,24},{9,... | collective-permute-start | bytes 3981320 | tf_op jit(solution)/shard_map/ppermute | solution.py:595
  407.0 95.4 %collective-permute-start.44 = (bf16[4,144,1152]{2,1,0:T(8,128)(2,1)S(1)}, bf16[4,144,1152]{2,1,0:T(8,128)(2,1)S(1)}, u32[]{:S(2)}, u32[]{:S(2)}) collective-permute-start(bf16[4,144,1152]{2,1,0:T(8,128)(2,1)S(1)} %pad_maximum_fusion.7), channel_id=1, source_target_pairs={{0,1},{1,0},{2,3},{3,2},{4,5},{5,4},{6,7},{7,6},{8,9},{9,8},{10,11... | collective-permute-start | bytes 3981320 | tf_op jit(solution)/shard_map/ppermute | solution.py:595
  409.7 25.4 %collective-permute-start.41 = (bf16[2,258,144]{1,2,0:T(8,128)(2,1)S(1)}, bf16[2,258,144]{1,2,0:T(8,128)(2,1)S(1)}, u32[]{:S(2)}, u32[]{:S(2)}) collective-permute-start(bf16[2,258,144]{1,2,0:T(8,128)(2,1)S(1)} %get-tuple-element.492), channel_id=1, source_target_pairs={{0,2},{1,3},{2,4},{3,5},{4,6},{5,7},{6,0},{7,1},{8,10},{9,11},{10,... | collective-permute-start | bytes 445832 | tf_op jit(solution)/shard_map/ppermute | solution.py:595
  429.3 13.6 %collective-permute-start.42 = (bf16[2,258,144]{1,2,0:T(8,128)(2,1)S(1)}, bf16[2,258,144]{1,2,0:T(8,128)(2,1)S(1)}, u32[]{:S(2)}, u32[]{:S(2)}) collective-permute-start(bf16[2,258,144]{1,2,0:T(8,128)(2,1)S(1)} %get-tuple-element.493), channel_id=1, source_target_pairs={{0,4},{1,5},{2,6},{3,7},{4,0},{5,1},{6,2},{7,3},{8,12},{9,13},{10,... | collective-permute-start | bytes 445832 | tf_op jit(solution)/shard_map/ppermute | solution.py:595
  429.3 15.9 %collective-permute-start.43 = (bf16[2,258,144]{1,2,0:T(8,128)(2,1)S(1)}, bf16[2,258,144]{1,2,0:T(8,128)(2,1)S(1)}, u32[]{:S(2)}, u32[]{:S(2)}) collective-permute-start(bf16[2,258,144]{1,2,0:T(8,128)(2,1)S(1)} %get-tuple-element.494), channel_id=1, source_target_pairs={{0,6},{1,7},{2,0},{3,1},{4,2},{5,3},{6,4},{7,5},{8,14},{9,15},{10,... | collective-permute-start | bytes 445832 | tf_op jit(solution)/shard_map/ppermute | solution.py:595
  435.3 23.7 %collective-permute-start.46 = (bf16[2,144,1152]{2,1,0:T(8,128)(2,1)S(1)}, bf16[2,144,1152]{2,1,0:T(8,128)(2,1)S(1)}, u32[]{:S(2)}, u32[]{:S(2)}) collective-permute-start(bf16[2,144,1152]{2,1,0:T(8,128)(2,1)S(1)} %copy-done.49), channel_id=1, source_target_pairs={{0,2},{1,3},{2,4},{3,5},{4,6},{5,7},{6,0},{7,1},{8,10},{9,11},{10,... | collective-permute-start | bytes 1990664 | tf_op jit(solution)/shard_map/ppermute | solution.py:595
  442.9 45.4 %collective-permute-start.47 = (bf16[2,144,1152]{2,1,0:T(8,128)(2,1)S(1)}, bf16[2,144,1152]{2,1,0:T(8,128)(2,1)S(1)}, u32[]{:S(2)}, u32[]{:S(2)}) collective-permute-start(bf16[2,144,1152]{2,1,0:T(8,128)(2,1)S(1)} %copy-done.48), channel_id=1, source_target_pairs={{0,4},{1,5},{2,6},{3,7},{4,0},{5,1},{6,2},{7,3},{8,12},{9,13},{10,... | collective-permute-start | bytes 1990664 | tf_op jit(solution)/shard_map/ppermute | solution.py:595
  445.2 57.2 %collective-permute-start.48 = (bf16[2,144,1152]{2,1,0:T(8,128)(2,1)S(1)}, bf16[2,144,1152]{2,1,0:T(8,128)(2,1)S(1)}, u32[]{:S(2)}, u32[]{:S(2)}) collective-permute-start(bf16[2,144,1152]{2,1,0:T(8,128)(2,1)S(1)} %copy-done.47), channel_id=1, source_target_pairs={{0,6},{1,7},{2,0},{3,1},{4,2},{5,3},{6,4},{7,5},{8,14},{9,15},{10,... | collective-permute-start | bytes 1990664 | tf_op jit(solution)/shard_map/ppermute | solution.py:595
  502.7 30.9 %collective-permute-start.52 = (bf16[2,144,1152]{2,1,0:T(8,128)(2,1)S(1)}, bf16[2,144,1152]{2,1,0:T(8,128)(2,1)S(1)}, u32[]{:S(2)}, u32[]{:S(2)}) collective-permute-start(bf16[2,144,1152]{2,1,0:T(8,128)(2,1)S(1)} %add_convert_fusion.1), channel_id=1, source_target_pairs={{0,16},{1,17},{2,18},{3,19},{4,20},{5,21},{6,22},{7,23},{8,24},{9,... | collective-permute-start | bytes 1990664 | tf_op jit(solution)/shard_map/ppermute | solution.py:595
  505.1 28.5 %collective-permute-start.51 = (bf16[4,2,258,144]{2,1,3,0:T(2,128)(2,1)S(1)}, bf16[4,2,258,144]{2,1,3,0:T(2,128)(2,1)S(1)}, u32[]{:S(2)}, u32[]{:S(2)}) collective-permute-start(bf16[4,2,258,144]{2,1,3,0:T(2,128)(2,1)S(1)} %get-tuple-element.467), channel_id=1, source_target_pairs={{0,1},{1,0},{2,3},{3,2},{4,5},{5,4},{6,7},{7,6},{8,9},{9,8},{10,11... | collective-permute-start | bytes 1783304 | tf_op jit(solution)/shard_map/ppermute | solution.py:595
  506.2 20.5 %collective-permute-start.49 = (bf16[2,72,1152]{2,1,0:T(8,128)(2,1)S(1)}, bf16[2,72,1152]{2,1,0:T(8,128)(2,1)S(1)}, u32[]{:S(2)}, u32[]{:S(2)}) collective-permute-start(bf16[2,72,1152]{2,1,0:T(8,128)(2,1)S(1)} %get-tuple-element.486), channel_id=1, source_target_pairs={{0,16},{1,17},{2,18},{3,19},{4,20},{5,21},{6,22},{7,23},{8,24},{9,... | collective-permute-start | bytes 995336 | tf_op jit(solution)/shard_map/ppermute | solution.py:595
  507.2 26.4 %collective-permute-start.50 = (bf16[2,72,1152]{2,1,0:T(8,128)(2,1)S(1)}, bf16[2,72,1152]{2,1,0:T(8,128)(2,1)S(1)}, u32[]{:S(2)}, u32[]{:S(2)}) collective-permute-start(bf16[2,72,1152]{2,1,0:T(8,128)(2,1)S(1)} %get-tuple-element.485), channel_id=1, source_target_pairs={{0,1},{1,0},{2,3},{3,2},{4,5},{5,4},{6,7},{7,6},{8,9},{9,8},{10,11... | collective-permute-start | bytes 995336 | tf_op jit(solution)/shard_map/ppermute | solution.py:595
  511.2 29.4 %collective-permute-start.59 = (bf16[144,1152]{1,0:T(8,128)(2,1)}, bf16[144,1152]{1,0:T(8,128)(2,1)S(1)}, u32[]{:S(2)}, u32[]{:S(2)}) collective-permute-start(bf16[144,1152]{1,0:T(8,128)(2,1)} %get-tuple-element.482), channel_id=1, source_target_pairs={{0,6},{1,7},{2,0},{3,1},{4,2},{5,3},{6,4},{7,5},{8,14},{9,15},{10,... | collective-permute-start | bytes 995336 | tf_op jit(solution)/shard_map/ppermute | solution.py:595
  535.0 30.9 %collective-permute-start.58 = (bf16[2,2,144,1152]{3,2,1,0:T(8,128)(2,1)}, bf16[2,2,144,1152]{3,2,1,0:T(8,128)(2,1)}, u32[]{:S(2)}, u32[]{:S(2)}) collective-permute-start(bf16[2,2,144,1152]{3,2,1,0:T(8,128)(2,1)} %get-tuple-element.475), channel_id=1, source_target_pairs={{0,8},{1,9},{2,10},{3,11},{4,12},{5,13},{6,14},{7,15},{8,0},{9,1},... | collective-permute-start | bytes 3981320 | tf_op jit(solution)/shard_map/ppermute | solution.py:595
  536.0 29.9 %collective-permute-start.57 = (bf16[4,72,1152]{2,1,0:T(8,128)(2,1)}, bf16[4,72,1152]{2,1,0:T(8,128)(2,1)}, u32[]{:S(2)}, u32[]{:S(2)}) collective-permute-start(bf16[4,72,1152]{2,1,0:T(8,128)(2,1)} %pad_maximum_fusion.22), channel_id=1, source_target_pairs={{0,16},{1,17},{2,18},{3,19},{4,20},{5,21},{6,22},{7,23},{8,24},{9,... | collective-permute-start | bytes 1990664 | tf_op jit(solution)/shard_map/ppermute | solution.py:595
  537.9 28.0 %collective-permute-start.56 = (bf16[4,72,1152]{2,1,0:T(8,128)(2,1)}, bf16[4,72,1152]{2,1,0:T(8,128)(2,1)}, u32[]{:S(2)}, u32[]{:S(2)}) collective-permute-start(bf16[4,72,1152]{2,1,0:T(8,128)(2,1)} %pad_maximum_fusion.21), channel_id=1, source_target_pairs={{0,1},{1,0},{2,3},{3,2},{4,5},{5,4},{6,7},{7,6},{8,9},{9,8},{10,11... | collective-permute-start | bytes 1990664 | tf_op jit(solution)/shard_map/ppermute | solution.py:595
  540.6 25.0 %collective-permute-start.60 = (bf16[144,1152]{1,0:T(8,128)(2,1)}, bf16[144,1152]{1,0:T(8,128)(2,1)S(1)}, u32[]{:S(2)}, u32[]{:S(2)}) collective-permute-start(bf16[144,1152]{1,0:T(8,128)(2,1)} %get-tuple-element.481), channel_id=1, source_target_pairs={{0,4},{1,5},{2,6},{3,7},{4,0},{5,1},{6,2},{7,3},{8,12},{9,13},{10,... | collective-permute-start | bytes 995336 | tf_op jit(solution)/shard_map/ppermute | solution.py:595
  540.6 25.0 %collective-permute-start.61 = (bf16[144,1152]{1,0:T(8,128)(2,1)}, bf16[144,1152]{1,0:T(8,128)(2,1)S(1)}, u32[]{:S(2)}, u32[]{:S(2)}) collective-permute-start(bf16[144,1152]{1,0:T(8,128)(2,1)} %get-tuple-element.480), channel_id=1, source_target_pairs={{0,2},{1,3},{2,4},{3,5},{4,6},{5,7},{6,0},{7,1},{8,10},{9,11},{10,... | collective-permute-start | bytes 995336 | tf_op jit(solution)/shard_map/ppermute | solution.py:595
  565.6 55.8 %collective-permute-start.53 = (bf16[2,2,258,144]{2,1,3,0:T(2,128)(2,1)}, bf16[2,2,258,144]{2,1,3,0:T(2,128)(2,1)}, u32[]{:S(2)}, u32[]{:S(2)}) collective-permute-start(bf16[2,2,258,144]{2,1,3,0:T(2,128)(2,1)} %get-tuple-element.464), channel_id=1, source_target_pairs={{0,6},{1,7},{2,0},{3,1},{4,2},{5,3},{6,4},{7,5},{8,14},{9,15},{10,... | collective-permute-start | bytes 891656 | tf_op jit(solution)/shard_map/ppermute | solution.py:595
  565.6 55.8 %collective-permute-start.54 = (bf16[2,2,258,144]{2,1,3,0:T(2,128)(2,1)}, bf16[2,2,258,144]{2,1,3,0:T(2,128)(2,1)}, u32[]{:S(2)}, u32[]{:S(2)}) collective-permute-start(bf16[2,2,258,144]{2,1,3,0:T(2,128)(2,1)} %get-tuple-element.465), channel_id=1, source_target_pairs={{0,4},{1,5},{2,6},{3,7},{4,0},{5,1},{6,2},{7,3},{8,12},{9,13},{10,... | collective-permute-start | bytes 891656 | tf_op jit(solution)/shard_map/ppermute | solution.py:595
  578.2 12.6 %collective-permute-start.64 = (bf16[72,1152]{1,0:T(8,128)(2,1)}, bf16[72,1152]{1,0:T(8,128)(2,1)S(1)}, u32[]{:S(2)}, u32[]{:S(2)}) collective-permute-start(bf16[72,1152]{1,0:T(8,128)(2,1)} %get-tuple-element.509), channel_id=1, source_target_pairs={{0,6},{1,7},{2,0},{3,1},{4,2},{5,3},{6,4},{7,5},{8,14},{9,15},{10,... | collective-permute-start | bytes 497672 | tf_op jit(solution)/shard_map/ppermute | solution.py:595
  582.3 35.9 %collective-permute-start.65 = (bf16[72,1152]{1,0:T(8,128)(2,1)}, bf16[72,1152]{1,0:T(8,128)(2,1)}, u32[]{:S(2)}, u32[]{:S(2)}) collective-permute-start(bf16[72,1152]{1,0:T(8,128)(2,1)} %get-tuple-element.511), channel_id=1, source_target_pairs={{0,4},{1,5},{2,6},{3,7},{4,0},{5,1},{6,2},{7,3},{8,12},{9,13},{10,... | collective-permute-start | bytes 497672 | tf_op jit(solution)/shard_map/ppermute | solution.py:595
  582.3 36.8 %collective-permute-start.66 = (bf16[72,1152]{1,0:T(8,128)(2,1)}, bf16[72,1152]{1,0:T(8,128)(2,1)}, u32[]{:S(2)}, u32[]{:S(2)}) collective-permute-start(bf16[72,1152]{1,0:T(8,128)(2,1)} %get-tuple-element.510), channel_id=1, source_target_pairs={{0,2},{1,3},{2,4},{3,5},{4,6},{5,7},{6,0},{7,1},{8,10},{9,11},{10,... | collective-permute-start | bytes 497672 | tf_op jit(solution)/shard_map/ppermute | solution.py:595
  590.9 33.3 %collective-permute-start.55 = (bf16[2,2,258,144]{2,1,3,0:T(2,128)(2,1)}, bf16[2,2,258,144]{2,1,3,0:T(2,128)(2,1)S(1)}, u32[]{:S(2)}, u32[]{:S(2)}) collective-permute-start(bf16[2,2,258,144]{2,1,3,0:T(2,128)(2,1)} %get-tuple-element.462), channel_id=1, source_target_pairs={{0,2},{1,3},{2,4},{3,5},{4,6},{5,7},{6,0},{7,1},{8,10},{9,11},{10,... | collective-permute-start | bytes 891656 | tf_op jit(solution)/shard_map/ppermute | solution.py:595
  618.2 10.6 %collective-permute-start.62 = (bf16[144,1152]{1,0:T(8,128)(2,1)S(1)}, bf16[144,1152]{1,0:T(8,128)(2,1)S(1)}, u32[]{:S(2)}, u32[]{:S(2)}) collective-permute-start(bf16[144,1152]{1,0:T(8,128)(2,1)S(1)} %copy-done.39), channel_id=1, source_target_pairs={{0,16},{1,17},{2,18},{3,19},{4,20},{5,21},{6,22},{7,23},{8,24},{9,... | collective-permute-start | bytes 995336 | tf_op jit(solution)/shard_map/ppermute | solution.py:595
  620.3 10.4 %collective-permute-start.67 = (bf16[72,1152]{1,0:T(8,128)(2,1)S(1)}, bf16[72,1152]{1,0:T(8,128)(2,1)S(1)}, u32[]{:S(2)}, u32[]{:S(2)}) collective-permute-start(bf16[72,1152]{1,0:T(8,128)(2,1)S(1)} %fusion.50), channel_id=1, source_target_pairs={{0,16},{1,17},{2,18},{3,19},{4,20},{5,21},{6,22},{7,23},{8,24},{9,... | collective-permute-start | bytes 497672 | tf_op jit(solution)/shard_map/ppermute | solution.py:595
  629.8 39.1 %collective-permute-start.69 = (bf16[2,144,1152]{2,1,0:T(8,128)(2,1)}, bf16[2,144,1152]{2,1,0:T(8,128)(2,1)}, u32[]{:S(2)}, u32[]{:S(2)}) collective-permute-start(bf16[2,144,1152]{2,1,0:T(8,128)(2,1)} %get-tuple-element.503), channel_id=1, source_target_pairs={{0,8},{1,9},{2,10},{3,11},{4,12},{5,13},{6,14},{7,15},{8,0},{9,1},... | collective-permute-start | bytes 1990664 | tf_op jit(solution)/shard_map/ppermute | solution.py:595
  645.0 21.1 %collective-permute-start.63 = (bf16[2064,144]{0,1:T(8,128)(2,1)}, bf16[2064,144]{0,1:T(8,128)(2,1)}, u32[]{:S(2)}, u32[]{:S(2)}) collective-permute-start(bf16[2064,144]{0,1:T(8,128)(2,1)} %reshape_squeeze.10), channel_id=1, source_target_pairs={{0,8},{1,9},{2,10},{3,11},{4,12},{5,13},{6,14},{7,15},{8,0},{9,1},... | collective-permute-start | bytes 1783304 | tf_op jit(solution)/shard_map/ppermute | solution.py:595
  (101 other events, 1006.8 us)
Sparse Core Ops, SparseCore 0:
  135.1 113.8 all-gather.2

commit v3 on v2

--- a/solution.py
+++ b/solution.py
@@ -348,13 +348,14 @@
             ref[...] += value[number * size : (number + 1) * size]
 
 
-def ffn_kernel(mixed_ref, cot_ref, weight_ref, down_a, down_b, mixed_a, mixed_b, grad_ref):
+def ffn_kernel(order_ref, mixed_ref, cot_ref, *refs):
+    blocks = 4
+    weights, (down_a, down_b, mixed_a, mixed_b), grads = refs[:blocks], refs[blocks : blocks + 4], refs[blocks + 4 :]
     step = pl.program_id(0)
-    blocks, _, rows, _ = weight_ref.shape
     mixed = mixed_ref[...]
     cot = cot_ref[...]
-    up = jnp.concatenate([weight_ref[n, 0] for n in range(blocks)], axis=0)
-    down = jnp.concatenate([weight_ref[n, 1] for n in range(blocks)], axis=0)
+    up = jnp.concatenate([ref[0, 0] for ref in weights], axis=0)
+    down = jnp.concatenate([ref[0, 1] for ref in weights], axis=0)
     up_input = dot_nt(mixed, up)
     gate = 0.5 * (1.0 + lax.erf(up_input * (1.0 / math.sqrt(2.0))))
     activation = (up_input * gate).astype(jnp.bfloat16)
@@ -362,27 +363,39 @@
     grad_up_in = (dot_nt(cot, down) * slope).astype(jnp.bfloat16)
     grad_up = dot_tn(grad_up_in, mixed).astype(jnp.bfloat16)
     grad_down = dot_tn(activation, cot).astype(jnp.bfloat16)
-    for n in range(blocks):
-        grad_ref[n, 0] = grad_up[n * rows : (n + 1) * rows]
-        grad_ref[n, 1] = grad_down[n * rows : (n + 1) * rows]
+    for j in range(2):
+
+        @pl.when(step == j)
+        def _():
+            grads[j][...] = grad_up.reshape(grads[j].shape)
+            grads[2 + j][...] = grad_down.reshape(grads[j].shape)
+
     accumulate(step, (mixed_a, mixed_b), dot_nn(grad_up_in, up))
     accumulate(step, (down_a, down_b), dot_nn(activation, down))
 
 
-def ffn(mixed, cot, weights):
+def ffn(order, mixed, cot, weights):
     count, _, rows, _ = weights.shape
     tokens = mixed.shape[0]
     blocks = 4
-    whole = pl.BlockSpec((tokens, D), lambda t: (0, 0))
-    half = pl.BlockSpec((tokens // 2, D), lambda t: (0, 0))
-    block = pl.BlockSpec((blocks, 2, rows, D), lambda t: (t, 0, 0, 0))
+    whole = pl.BlockSpec((tokens, D), lambda t, m: (0, 0))
+    half = pl.BlockSpec((tokens // 2, D), lambda t, m: (0, 0))
+
+    def weight_spec(slot):
+        return pl.BlockSpec((1, 2, rows, D), lambda t, m: (m[blocks * t + slot], 0, 0, 0))
+
+    grad_block = pl.BlockSpec((blocks, rows, D), lambda t, m: (0, 0, 0))
     part = jax.ShapeDtypeStruct((tokens // 2, D), jnp.float32)
+    grad = jax.ShapeDtypeStruct((blocks, rows, D), jnp.bfloat16)
     return pl.pallas_call(
         ffn_kernel,
-        out_shape=[part] * 4 + [jax.ShapeDtypeStruct(weights.shape, jnp.bfloat16)],
-        grid=(count // blocks,),
-        in_specs=[whole, whole, block],
-        out_specs=[half] * 4 + [block],
+        out_shape=[part] * 4 + [grad] * 4,
+        grid_spec=pltpu.PrefetchScalarGridSpec(
+            num_scalar_prefetch=1,
+            grid=(count // blocks,),
+            in_specs=[whole, whole] + [weight_spec(slot) for slot in range(blocks)],
+            out_specs=[half] * 4 + [grad_block] * 4,
+        ),
         compiler_params=pltpu.CompilerParams(
             dimension_semantics=("arbitrary",), vmem_limit_bytes=60 * 1024 * 1024
         ),
@@ -390,7 +403,7 @@
             flops=12 * tokens * D * count * rows, transcendentals=0, bytes_accessed=32 * 1024 * 1024
         ),
         name="ffn",
-    )(mixed, cot, weights)
+    )(order, mixed, cot, *([weights] * blocks))
 
 
 def soft(q, k):
@@ -471,7 +484,10 @@
     attended_ref,
     part_a,
     part_b,
-    grad_ref,
+    own_ref,
+    near_ref,
+    far_x_ref,
+    far_y_ref,
     grads_s,
     mat_s,
 ):
@@ -497,9 +513,24 @@
     projected = grads_s[...].astype(jnp.bfloat16)
     mat_s[: 3 * HEAD] = dot_tn(projected, normed)
     mat_s[3 * HEAD :] = dot_tn(attended_ref[0], low)
-    which = meta_ref[0]
-    grad_ref[which, 0] = mat_s[: 2 * HEAD].astype(jnp.bfloat16)
-    grad_ref[1 - which, 0] = mat_s[2 * HEAD :].astype(jnp.bfloat16)
+    first = meta_ref[0] == 0
+    query_key = mat_s[: 2 * HEAD]
+    value_out = mat_s[2 * HEAD :]
+    own_ref[0] = jnp.where(first, query_key, value_out).astype(jnp.bfloat16)
+    other = jnp.where(first, value_out, query_key).astype(jnp.bfloat16)
+
+    @pl.when(step < 4)
+    def _():
+        near_ref[0] = other
+
+    @pl.when((step >= 4) & (step < 6))
+    def _():
+        far_x_ref[0] = other
+
+    @pl.when(step >= 6)
+    def _():
+        far_y_ref[0] = other
+
     add = dot_nn(projected[:, : 2 * HEAD], qk_ref[0, 0]) + dot_nn(
         projected[:, 2 * HEAD :], vo_ref[0, 0, :HEAD]
     )
@@ -516,13 +547,23 @@
         out_shape=[
             jax.ShapeDtypeStruct((tokens // 2, D), jnp.float32),
             jax.ShapeDtypeStruct((tokens // 2, D), jnp.float32),
-            jax.ShapeDtypeStruct((2, heads, rows, D), jnp.bfloat16),
+            jax.ShapeDtypeStruct((heads, rows, D), jnp.bfloat16),
+            jax.ShapeDtypeStruct((4, rows, D), jnp.bfloat16),
+            jax.ShapeDtypeStruct((2, rows, D), jnp.bfloat16),
+            jax.ShapeDtypeStruct((2, rows, D), jnp.bfloat16),
         ],
         grid_spec=pltpu.PrefetchScalarGridSpec(
             num_scalar_prefetch=1,
             grid=(heads,),
             in_specs=[whole, whole, qk, vo, qkv, att],
-            out_specs=[half, half, pl.BlockSpec((2, 1, rows, D), lambda s, m: (0, s, 0, 0))],
+            out_specs=[
+                half,
+                half,
+                pl.BlockSpec((1, rows, D), lambda s, m: (s, 0, 0)),
+                pl.BlockSpec((1, rows, D), lambda s, m: (jnp.minimum(s, 3), 0, 0)),
+                pl.BlockSpec((1, rows, D), lambda s, m: (jnp.clip(s - 4, 0, 1), 0, 0)),
+                pl.BlockSpec((1, rows, D), lambda s, m: (jnp.clip(s - 6, 0, 1), 0, 0)),
+            ],
             scratch_shapes=[
                 pltpu.VMEM((tokens, 3 * HEAD), jnp.float32),
                 pltpu.VMEM((2 * rows, D), jnp.float32),
@@ -603,9 +644,6 @@
     def over_y(value):
         return send(value, lambda x, c, z, y: (x, c, z, 1 - y))
 
-    def over_z(value, step):
-        return send(value, lambda x, c, z, y: (x, c, (z + step) % ZS, y))
-
     def xor_z(value, bit):
         return send(value, lambda x, c, z, y: (x, c, z ^ bit, y))
 
@@ -621,46 +659,107 @@
     def padded(own):
         return jnp.pad(own, ((0, PAD - SEQ), (0, 0)))
 
-    def shifted(line, sign=1):
-        return [pick(line, (zi + sign * step) % ZS, 0) for step in range(ZS)]
-
-    def canonical(blocks, sign=1):
-        stacked = jnp.stack(blocks)
-        out = []
-        for number in range(narrow_count):
-            step = (sign * (zi - number // 2)) % ZS
-            out.append(pick(pick(stacked, step, 0), yi ^ (number % 2), 0))
-        return jnp.stack(out)
+    distances = [0]
+    bit = ZS // 2
+    while bit:
+        distances += [distance ^ bit for distance in distances]
+        bit //= 2
+
+    def gather_z(block):
+        line = block[None]
+        bit = ZS // 2
+        while bit:
+            line = jnp.concatenate([line, xor_z(line, bit)])
+            bit //= 2
+        return line
+
+    order = jnp.stack(
+        [(zi ^ distance) * 2 + (yi ^ j) for j in range(2) for distance in distances]
+    ).astype(jnp.int32)
+
+    def canonical(blocks):
+        def exchange(table, flag, bit, width):
+            return [
+                jnp.where(flag == 0, table[index], table[index ^ bit]) for index in range(width)
+            ]
+
+        table = [None] * narrow_count
+        for place, distance in enumerate(distances):
+            for j in range(2):
+                table[distance * 2 + j] = blocks[j * ZS + place]
+        bit = 1
+        while bit < narrow_count:
+            table = exchange(table, (narrow_index // bit) % 2, bit, narrow_count)
+            bit *= 2
+        return table
 
     def split_y(array):
         grid = array.reshape((ZS, YS) + array.shape[1:])
         return pick(grid, yi, 1), pick(grid, 1 - yi, 1)
 
     def z_pieces(near, far):
-        both = jnp.stack([near, far])
-        return [pick(both, (zi + step) % ZS, 1) for step in range(ZS)]
+        return [
+            jnp.concatenate([pick(near, zi ^ distance, 0), pick(far, zi ^ distance, 0)], axis=-1)
+            for distance in distances
+        ]
 
     def z_line(pieces):
-        return [pieces[0]] + [over_z(pieces[step], step) for step in range(1, ZS)]
+        return [pieces[0]] + [
+            xor_z(piece, distance) for piece, distance in zip(pieces[1:], distances[1:])
+        ]
+
+    def halves_z(total):
+        return total[: ZS // 2], total[ZS // 2 :]
 
     half = ZS // 2
     meta = xi.astype(jnp.int32)[None]
     is_first = ci == 0
 
+    def in_order(pair, other_core):
+        four = jnp.stack([pair, other_core])
+        return jnp.stack(
+            [pick(pick(four, c ^ ci, 0), x ^ xi, 0) for c in range(2) for x in range(2)]
+        )
+
+    def all_narrow(value):
+        value = value + over_y(value)
+        bit = 1
+        while bit < ZS:
+            value = value + xor_z(value, bit)
+            bit *= 2
+        return value
+
+    def columns(array):
+        size = D // wide_count
+        return lax.dynamic_slice_in_dim(array, wide_index * size, size, array.ndim - 1)
+
+    def statistics(grad, old):
+        squares = grad * grad + EPS_SQUARE
+        new = DECAY * old + (1.0 - DECAY) * (jnp.sum(squares, axis=1) / D)
+        old_sum = jnp.where(lax.broadcasted_iota(jnp.int32, (D,), 0) == 0, jnp.sum(old), 0.0)
+        sums = [
+            jnp.sum(squares, axis=0),
+            jnp.sum(grad * grad * (1.0 / new)[:, None], axis=0),
+            old_sum,
+        ]
+        return new, sums
+
+    def step_of(grad, new, totals, old_wide, rows_all, row_along_wide):
+        wide_mean = totals[0] / rows_all
+        wide_new = DECAY * old_wide + (1.0 - DECAY) * wide_mean
+        if row_along_wide:
+            row_mean = jnp.mean(wide_new)
+        else:
+            row_mean = DECAY * (totals[2][0] / rows_all) + (1.0 - DECAY) * jnp.mean(wide_mean)
+        square_total = jnp.sum(totals[1] / wide_new) * row_mean
+        ratio = jnp.sqrt(square_total / (rows_all * D)) / CLIP_LEVEL
+        factor = -(STEP_RATE * jnp.sqrt(row_mean) / jnp.maximum(1.0, ratio))
+        step = grad * lax.rsqrt(new)[:, None] * (lax.rsqrt(wide_new) * factor)[None, :]
+        return wide_new, ratio, step
+
     mine = jnp.where(is_first, stream, skip_in)
     given = core(jnp.where(is_first, skip_in, stream))
     skip_block = pick(pick(skip_weight, ci, 0).reshape(2, feat // 2, D), xi, 0)
-    skip_line = jnp.stack(z_line([skip_block] * ZS))
-    tokens = jnp.stack([mine, given]).reshape(2, narrow_count, SEQ, feat).transpose(1, 0, 2, 3)
-    token_near, token_give = split_y(tokens)
-    token_far = over_y(token_give)
-
-    skip_line, token_far, cotangent, qkv_weight, out_weight = tie(
-        skip_line, token_far, cotangent, qkv_weight, out_weight
-    )
-    token_blocks = z_line(z_pieces(token_near, token_far))
-    skip_beside = over_y(skip_line)
-    skip_across = over_x(skip_line)
     attn_rows = jnp.concatenate(
         [
             pick(qkv_weight.transpose(1, 2, 0).reshape(3, 2, half_head, D), ci, 1),
@@ -668,16 +767,49 @@
         ]
     ).reshape(2, 2 * half_head, D)
     attn_block = pick(attn_rows, xi, 0)
-    cot_near, cot_give = split_y(cotangent.reshape(narrow_count, SEQ, feat))
-
-    *token_blocks, skip_beside, skip_across, attn_block, cot_give = tie(
-        *token_blocks, skip_beside, skip_across, attn_block, cot_give
-    )
-    attn_line = jnp.stack(z_line([attn_block] * ZS))
+    skip_two = xor_z(skip_block, 2)
+    attn_two = xor_z(attn_block, 2)
+    tokens = jnp.concatenate([mine, given, cotangent], axis=1).reshape(narrow_count, SEQ, 3 * feat)
+    token_near, token_give = split_y(tokens)
+    token_far = over_y(token_give)
+    skip_two, attn_two, token_near = tie(skip_two, attn_two, token_near)
+    skip_line = jnp.stack([skip_block, skip_two])
+    attn_line = jnp.stack([attn_block, attn_two])
+    skip_line = jnp.concatenate([skip_line, xor_z(skip_line, 1)])
+    attn_line = jnp.concatenate([attn_line, xor_z(attn_line, 1)])
+
+    token_blocks = z_line(z_pieces(token_near, token_far))
+    skip_beside = over_y(skip_line)
+    skip_across = over_x(skip_line)
+    ffn_block = jnp.stack(
+        [
+            lax.dynamic_slice_in_dim(up_weight, (ci * 2 + xi) * quarter, quarter, 1).T,
+            lax.dynamic_slice_in_dim(down_weight, (ci * 2 + xi) * quarter, quarter, 0),
+        ]
+    )
+
+    skip_beside, skip_across, attn_line = tie(skip_beside, skip_across, attn_line)
     skip_corner = jnp.concatenate([over_x(skip_beside[:half]), over_y(skip_across[half:])])
-    cot_far = over_y(cot_give)
-    flat = jnp.concatenate([block[j] for j in range(2) for block in token_blocks], axis=-1)
-    flat = jnp.pad(flat, ((0, 0), (0, PAD - SEQ), (0, 0))).reshape(2 * PAD, D)
+    attn_beside = over_y(attn_line)
+    attn_across = over_x(attn_line)
+
+    *token_blocks, skip_corner, ffn_block = tie(*token_blocks, skip_corner, ffn_block)
+    ffn_full = lax.all_gather(ffn_block[None], "narrow", tiled=True)
+    parts = [
+        [
+            block[:, (3 * j + kind) * feat : (3 * j + kind + 1) * feat]
+            for j in range(2)
+            for block in token_blocks
+        ]
+        for kind in range(3)
+    ]
+    flat = jnp.concatenate(
+        [padded(jnp.concatenate(parts[kind], axis=1)) for kind in range(2)]
+    )
+    flat, attn_beside, attn_across = tie(flat, attn_beside, attn_across)
+    attn_corner_x = over_x(attn_beside[:half])
+    attn_corner_y = over_y(attn_across[half:])
+    cot_own = jnp.concatenate(canonical(parts[2]), axis=1)
     skip_near = jnp.concatenate([skip_line, skip_beside])
     skip_away = jnp.concatenate([skip_across, skip_corner])
     skip_mat = jnp.where(
@@ -685,18 +817,6 @@
         jnp.stack([skip_near, skip_away], axis=1),
         jnp.stack([skip_away, skip_near], axis=1),
     ).reshape(D, D)
-    ffn_block = jnp.stack(
-        [
-            lax.dynamic_slice_in_dim(up_weight, (ci * 2 + xi) * quarter, quarter, 1).T,
-            lax.dynamic_slice_in_dim(down_weight, (ci * 2 + xi) * quarter, quarter, 0),
-        ]
-    )
-
-    attn_line, cot_far, skip_mat, ffn_block = tie(attn_line, cot_far, skip_mat, ffn_block)
-    attn_beside = over_y(attn_line)
-    attn_across = over_x(attn_line)
-    cot_blocks = z_line(z_pieces(cot_near, cot_far))
-    ffn_full = lax.all_gather(ffn_block[None], "narrow", tiled=True)
 
     def both_images(own):
         own = padded(own)
@@ -710,11 +830,8 @@
     unit_one, inverse_one = unit_parts(hidden_in)
     normed = both_images((unit_one * norm_gain[0] + norm_bias[0]).astype(bf16))
 
-    normed, attn_beside, attn_across, *cot_blocks = tie(
-        normed, attn_beside, attn_across, *cot_blocks
-    )
-    attn_corner = jnp.concatenate([over_x(attn_beside[:half]), over_y(attn_across[half:])])
-    cot_own = canonical(cot_blocks).transpose(1, 0, 2).reshape(SEQ, D)
+    attn_corner = jnp.concatenate([attn_corner_x, attn_corner_y])
+    normed, cot_own, attn_corner = tie(normed, cot_own, attn_corner)
     cot_pair = padded(cot_own)
     cot_pair = jnp.concatenate([cot_pair, over_x(cot_pair)])
     attn_full = jnp.stack(
@@ -732,13 +849,17 @@
     mixed = jnp.concatenate([mixed_pair, core(mixed_pair)])
     cot = jnp.concatenate([cot_pair, core(cot_pair)])
 
-    down_a, down_b, mixed_a, mixed_b, ffn_grad = ffn(mixed, cot, ffn_full)
+    down_a, down_b, mixed_a, mixed_b, up_near, up_give, down_near, down_give = ffn(
+        order, mixed, cot, ffn_full
+    )
     mixed_sum = mixed_a + core(mixed_b)
     mixed_far = over_x(mixed_sum[PAD:].astype(bf16))
-    ffn_near, ffn_give = split_y(ffn_grad)
-    ffn_far = over_y(ffn_give)
-
-    mixed_far, down_b = tie(mixed_far, down_b)
+    ffn_far_down = over_y(down_give)
+
+    mixed_far, ffn_far_down, down_b, up_give = tie(mixed_far, ffn_far_down, down_b, up_give)
+    ffn_far_up = over_y(up_give)
+    ffn_down, ffn_down_give = halves_z(add_low(down_near, ffn_far_down))
+    ffn_down_one = xor_z(ffn_down_give, 1)
     down_sum = down_a + core(down_b)
     down_far = over_x(down_sum[PAD:].astype(bf16))
     back_middle, gain_two, bias_two = norm_back_own(
@@ -749,215 +870,185 @@
     )
     grad_middle = cot_own.astype(f32) + back_middle
     middle_low = both_images(grad_middle.astype(bf16))
-    normed_a, normed_b, attn_grad = attn_backward(
+    normed_a, normed_b, own, other_near, other_x, other_y = attn_backward(
         meta, normed, middle_low, attn_full, qkv_kept, attended
     )
 
-    normed_b, ffn_far, down_far = tie(normed_b, ffn_far, down_far)
-    own, other = attn_grad[0], attn_grad[1]
-    attn_from_x = over_x(other[ZS : ZS + half])
-    attn_from_y = over_y(other[ZS + half :])
-    ffn_total = add_low(ffn_near, ffn_far)
-    ffn_pieces = z_line(shifted(ffn_total))
+    normed_b, ffn_far_up, ffn_down_one, down_far = tie(
+        normed_b, ffn_far_up, ffn_down_one, down_far
+    )
+    attn_from_x = over_x(other_x)
+    attn_from_y = over_y(other_y)
+    ffn_up, ffn_up_give = halves_z(add_low(up_near, ffn_far_up))
+    ffn_up_one = xor_z(ffn_up_give, 1)
+    ffn_down = add_low(ffn_down, ffn_down_one)
+    ffn_down_two = xor_z(ffn_down[1], 2)
     block_own = (middle + (down_sum[:PAD] + down_far.astype(f32))[:SEQ]).astype(bf16)
-    block_near, block_give = split_y(
-        block_own.reshape(SEQ, narrow_count, feat).transpose(1, 0, 2)
-    )
-    block_far = over_y(block_give)
     back_hidden, gain_one, bias_one = norm_back_own(
         unit_one, inverse_one, core_sum(normed_a, normed_b), norm_gain[0]
     )
     hidden_low = both_images((grad_middle + back_hidden).astype(bf16))
 
-    hidden_low, attn_from_x, attn_from_y, block_far = tie(
-        hidden_low, attn_from_x, attn_from_y, block_far
-    )
-    attn_beside = over_y(
-        jnp.concatenate([add_low(own[ZS : ZS + half], attn_from_x), own[ZS + half :]])
-    )
-    attn_across = over_x(
-        jnp.concatenate([other[:half], add_low(other[half:ZS], attn_from_y)])
-    )
     grad_skip = matmul(flat, hidden_low, "rc,rd->cd").astype(bf16)
     grad_skip = grad_skip.reshape(narrow_count, 2, feat // 2, D)
     skip_own, skip_other = pick(grad_skip, xi, 1), pick(grad_skip, 1 - xi, 1)
-    token_grad = matmul(hidden_low, skip_mat, "rd,cd->rc").astype(bf16)
-    kept_grads = token_grad.reshape(2, PAD, 2, ZS, feat)[:, :SEQ].transpose(2, 3, 0, 1, 4)
-
-    attn_beside, attn_across, skip_own, skip_other, kept_grads, *ffn_pieces = tie(
-        attn_beside, attn_across, skip_own, skip_other, kept_grads, *ffn_pieces
-    )
     skip_from_x = over_x(skip_other[ZS : ZS + half])
     skip_from_y = over_y(skip_other[ZS + half :])
-    attn_total = (
-        own[:ZS].astype(f32) + attn_beside.astype(f32) + attn_across.astype(f32)
-    ).astype(bf16)
-    attn_pieces = [attn_total[0]] + [over_z(attn_total[step], -step) for step in range(1, ZS)]
-    grads_far = over_y(kept_grads[1])
-    ffn_own = sum(piece.astype(f32) for piece in ffn_pieces).astype(bf16)
+    token_grad = matmul(hidden_low, skip_mat, "rd,cd->rc").astype(bf16)
+    block_pieces = jnp.stack(jnp.split(block_own, narrow_count, axis=1))
+
+    def back_piece(slot):
+        columns_of = slice(slot * feat, (slot + 1) * feat)
+        return jnp.concatenate(
+            [
+                token_grad[:SEQ, columns_of],
+                token_grad[PAD : PAD + SEQ, columns_of],
+                pick(block_pieces, order[slot], 0),
+            ],
+            axis=1,
+        )
+
+    back_near = [back_piece(slot) for slot in range(ZS)]
+    back_give = jnp.stack([back_piece(slot) for slot in range(ZS, narrow_count)])
+
+    attn_from_x, attn_from_y, back_give, ffn_up_one, ffn_down_two = tie(
+        attn_from_x, attn_from_y, back_give, ffn_up_one, ffn_down_two
+    )
+    back_far = over_y(back_give)
+    attn_across = over_x(
+        jnp.concatenate([other_near[:half], add_low(other_near[half:], attn_from_y)])
+    )
+    attn_beside = over_y(
+        jnp.concatenate([add_low(own[ZS : ZS + half], attn_from_x), own[ZS + half :]])
+    )
+    ffn_up = add_low(ffn_up, ffn_up_one)
+    ffn_up_two = xor_z(ffn_up[1], 2)
+
+    skip_from_x, skip_from_y, back_far = tie(skip_from_x, skip_from_y, back_far)
+    skip_near_sum = add_low(skip_own[ZS : ZS + half], skip_from_x)
+    skip_far_sum = add_low(skip_other[half:ZS], skip_from_y)
+    back_pieces = [
+        jnp.concatenate([back_near[place], back_far[place]], axis=1) for place in range(ZS)
+    ]
+    back_blocks = z_line(back_pieces)
+
+    attn_beside, attn_across, ffn_up_two = tie(attn_beside, attn_across, ffn_up_two)
+    attn_total, attn_give = halves_z(
+        (own[:ZS].astype(f32) + attn_beside.astype(f32) + attn_across.astype(f32)).astype(bf16)
+    )
+    attn_one = xor_z(attn_give, 1)
+    skip_across = over_x(jnp.concatenate([skip_other[:half], skip_far_sum]))
+    skip_beside = over_y(jnp.concatenate([skip_near_sum, skip_own[ZS + half :]]))
+    ffn_own = jnp.stack([add_low(ffn_up[0], ffn_up_two), add_low(ffn_down[0], ffn_down_two)])
     ffn_x = over_x(ffn_own)
 
-    skip_from_x, skip_from_y, grads_far, ffn_x = tie(skip_from_x, skip_from_y, grads_far, ffn_x)
-    skip_beside = over_y(
-        jnp.concatenate(
-            [add_low(skip_own[ZS : ZS + half], skip_from_x), skip_own[ZS + half :]]
-        )
-    )
-    skip_across = over_x(
-        jnp.concatenate([skip_other[:half], add_low(skip_other[half:ZS], skip_from_y)])
-    )
-    returned = jnp.stack([kept_grads[0], grads_far])
-    backs = [returned[:, 0]] + [over_z(returned[:, step], -step) for step in range(1, ZS)]
+    attn_one, ffn_x = tie(attn_one, ffn_x)
+    attn_total = add_low(attn_total, attn_one)
+    attn_two = xor_z(attn_total[1], 2)
     ffn_pair = jnp.stack([ffn_own, ffn_x])
     ffn_core = core(ffn_pair)
 
-    skip_beside, skip_across, ffn_core, *attn_pieces = tie(
-        skip_beside, skip_across, ffn_core, *attn_pieces
-    )
-    skip_total = (
-        skip_own[:ZS].astype(f32) + skip_beside.astype(f32) + skip_across.astype(f32)
-    ).astype(bf16)
-    skip_pieces = [skip_total[0]] + [over_z(skip_total[step], -step) for step in range(1, ZS)]
-    attn_own = sum(piece.astype(f32) for piece in attn_pieces).astype(bf16)
-    attn_x = over_x(attn_own)
-    block_blocks = z_line(z_pieces(block_near, block_far))
-
-    *backs, attn_x = tie(*backs, attn_x)
-    attn_pair = jnp.stack([attn_own, attn_x])
-    attn_core = core(attn_pair)
-    ordered = canonical(backs, -1)
-    grad_mine = ordered[:, 0].reshape(rows_local, feat)
-    grad_given = core(ordered[:, 1].reshape(rows_local, feat))
+    ffn_all = in_order(ffn_pair, ffn_core).astype(f32)
+    grad_up_rows = ffn_all[:, 0].reshape(hidden, D)
+    grad_down = ffn_all[:, 1].reshape(hidden, D)
+    new_col_up, up_sums = statistics(grad_up_rows, col_up)
+    new_row_down, down_sums = statistics(grad_down, row_down)
+    ffn_totals = all_narrow(jnp.stack(up_sums + down_sums))
+
+    skip_beside, skip_across, ffn_totals, *back_blocks = tie(
+        skip_beside, skip_across, ffn_totals, *back_blocks
+    )
+    new_row_up, ratio_up, step_up = step_of(
+        grad_up_rows, new_col_up, ffn_totals[:3], row_up, hidden * narrow_count, True
+    )
+    new_col_down, ratio_down, step_down = step_of(
+        grad_down, new_row_down, ffn_totals[3:], col_down, hidden * narrow_count, False
+    )
+    new_up = up_weight.astype(f32) + step_up.T
+    new_down = down_weight.astype(f32) + step_down
+    grad_up_out = columns(grad_up_rows).T
+    grad_down_out = columns(grad_down)
+    skip_total, skip_give = halves_z(
+        (skip_own[:ZS].astype(f32) + skip_beside.astype(f32) + skip_across.astype(f32)).astype(
+            bf16
+        )
+    )
+    skip_one = xor_z(skip_give, 1)
+    back = [block[:, j * 3 * feat : (j + 1) * 3 * feat] for j in range(2) for block in back_blocks]
+    back = jnp.concatenate(canonical(back), axis=0)
+    grad_mine = back[:, :feat]
+    grad_given = core(back[:, feat : 2 * feat])
+    block_out = back[:, 2 * feat :]
+
+    attn_two, skip_one, grad_given, block_out, new_up, new_down, grad_up_out, grad_down_out = tie(
+        attn_two, skip_one, grad_given, block_out, new_up, new_down, grad_up_out, grad_down_out
+    )
+    attn_own = add_low(attn_total[0], attn_two)
+    skip_total = add_low(skip_total, skip_one)
+    skip_two = xor_z(skip_total[1], 2)
     grad_stream = jnp.where(is_first, grad_mine, grad_given).astype(f32)
     grad_skip_in = jnp.where(is_first, grad_given, grad_mine).astype(f32)
-    block_out = canonical(block_blocks).reshape(rows_local, feat)
-    skip_last = sum(piece.astype(f32) for piece in skip_pieces).astype(bf16)
-    skip_pair = jnp.stack([skip_last, over_x(skip_last)])
-    skip_core = core(skip_pair)
-
-    def in_order(pair, other_core):
-        four = jnp.stack([pair, other_core])
-        return jnp.stack(
-            [pick(pick(four, c ^ ci, 0), x ^ xi, 0) for c in range(2) for x in range(2)]
-        )
-
-    ffn_all = in_order(ffn_pair, ffn_core)
-    up_all = ffn_all[:, 0].reshape(hidden, D)
-    down_all = ffn_all[:, 1].reshape(hidden, D)
-    attn_all = in_order(attn_pair, attn_core).reshape(2, 4, half_head, D)
-    skip_all = in_order(skip_pair, skip_core).reshape(2, feat, D)
-    qkv_all = attn_all[:, :3].transpose(1, 0, 2, 3).reshape(3, feat, D)
-    out_all = attn_all[:, 3].reshape(feat, D)
-
-    def all_narrow(value):
-        value = value + over_y(value)
-        bit = 1
-        while bit < ZS:
-            value = value + xor_z(value, bit)
-            bit *= 2
-        return value
+
+    grad_stream, grad_skip_in, skip_two = tie(grad_stream, grad_skip_in, skip_two)
+    last_own = jnp.concatenate([attn_own, add_low(skip_total[0], skip_two)])
+    last_pair = jnp.stack([last_own, over_x(last_own)])
+    last_all = in_order(last_pair, core(last_pair)).astype(f32)
+    attn_rows_all = 2 * half_head
+    attn_all = last_all[:, :attn_rows_all].reshape(2, 4, half_head, D)
+    grad_skip_rows = last_all[:, attn_rows_all:].reshape(2 * feat, D)
+    grad_qkv_rows = attn_all[:, :3].transpose(1, 0, 2, 3).reshape(3 * feat, D)
+    grad_out = attn_all[:, 3].reshape(feat, D)
 
     norm_sums = jnp.stack([gain_one, gain_two, bias_one, bias_two])
     norm_sums = norm_sums + core(norm_sums)
     norm_sums = norm_sums + over_x(norm_sums)
-
-    grads = [
-        skip_all.reshape(-1, D).astype(f32),
-        qkv_all.reshape(-1, D).astype(f32),
-        out_all.astype(f32),
-        up_all.astype(f32),
-        down_all.astype(f32),
-    ]
-    old_wide = (col_skip, row_qkv, col_out, row_up, col_down)
-    old_narrow = (row_skip.reshape(-1), col_qkv.reshape(-1), row_out, col_up, row_down)
-    row_along_wide = (False, True, False, True, False)
-    wide_counts = (2 * D, 3 * D, D, FF, FF)
-    entry_counts = (2 * D * D, 3 * D * D, D * D, D * FF, FF * D)
-    new_narrow = []
-    sums = []
-    for number in range(5):
-        grad = grads[number]
-        squares = grad * grad + EPS_SQUARE
-        narrow_new = DECAY * old_narrow[number] + (1.0 - DECAY) * (jnp.sum(squares, axis=1) / D)
-        new_narrow.append(narrow_new)
-        old_sum = jnp.zeros((D,), f32).at[0].set(jnp.sum(old_narrow[number]))
-        sums.append(
-            jnp.stack(
-                [
-                    jnp.sum(squares, axis=0),
-                    jnp.sum(grad * grad * (1.0 / narrow_new)[:, None], axis=0),
-                    old_sum,
-                ]
-            )
-        )
-    early = all_narrow(jnp.concatenate([sums[number] for number in range(1, 5)]))
-    late = all_narrow(jnp.concatenate([sums[0], norm_sums]))
-    totals = [late[:3]] + [early[3 * number : 3 * number + 3] for number in range(4)]
-    gain_total = late[3:5]
-    bias_total = late[5:7]
-
-    new_wide = []
-    steps = []
-    ratios = []
-    for number in range(5):
-        wide_mean = totals[number][0] / wide_counts[number]
-        wide_new = DECAY * old_wide[number] + (1.0 - DECAY) * wide_mean
-        if row_along_wide[number]:
-            row_mean = jnp.mean(wide_new)
-        else:
-            row_mean = DECAY * (totals[number][2][0] / wide_counts[number]) + (
-                1.0 - DECAY
-            ) * jnp.mean(wide_mean)
-        square_total = jnp.sum(totals[number][1] / wide_new) * row_mean
-        ratio = jnp.sqrt(square_total / entry_counts[number]) / CLIP_LEVEL
-        ratios.append(ratio)
-        factor = -(STEP_RATE * jnp.sqrt(row_mean) / jnp.maximum(1.0, ratio))
-        step = (
-            grads[number]
-            * lax.rsqrt(new_narrow[number])[:, None]
-            * (lax.rsqrt(wide_new) * factor)[None, :]
-        )
-        new_wide.append(wide_new)
-        steps.append(step)
-    clip_ratio = jnp.stack(ratios)
-
-    def columns(array):
-        size = D // wide_count
-        return lax.dynamic_slice_in_dim(array, wide_index * size, size, array.ndim - 1)
-
-    new_skip = skip_weight.astype(f32) + steps[0].reshape(2, feat, D)
-    new_qkv = qkv_weight.astype(f32) + steps[1].reshape(3, feat, D).transpose(2, 0, 1)
-    new_up = up_weight.astype(f32) + steps[3].T
-    new_down = down_weight.astype(f32) + steps[4]
+    new_row_skip, skip_sums = statistics(grad_skip_rows, row_skip.reshape(-1))
+    new_col_qkv, qkv_sums = statistics(grad_qkv_rows, col_qkv.reshape(-1))
+    new_row_out, out_sums = statistics(grad_out, row_out)
+    totals = all_narrow(jnp.concatenate([jnp.stack(skip_sums + qkv_sums + out_sums), norm_sums]))
+    gain_total = totals[9:11]
+    bias_total = totals[11:13]
+    new_col_skip, ratio_skip, step_skip = step_of(
+        grad_skip_rows, new_row_skip, totals[:3], col_skip, 2 * D, False
+    )
+    new_row_qkv, ratio_qkv, step_qkv = step_of(
+        grad_qkv_rows, new_col_qkv, totals[3:6], row_qkv, 3 * D, True
+    )
+    new_col_out, ratio_out, step_out = step_of(
+        grad_out, new_row_out, totals[6:9], col_out, D, False
+    )
+    clip_ratio = jnp.stack([ratio_skip, ratio_qkv, ratio_out, ratio_up, ratio_down])
+    new_skip = skip_weight.astype(f32) + step_skip.reshape(2, feat, D)
+    new_qkv = qkv_weight.astype(f32) + step_qkv.reshape(3, feat, D).transpose(2, 0, 1)
     new_second_gain, gain_step = plain_update(gain_total, second_gain)
     new_second_bias, bias_step = plain_update(bias_total, second_bias)
     return (
         block_out,
         grad_stream,
         grad_skip_in,
-        columns(grads[0]).reshape(2, feat, -1),
-        columns(grads[1]).reshape(3, feat, -1).transpose(2, 0, 1),
-        columns(grads[2]),
-        columns(grads[3]).T,
-        columns(grads[4]),
+        columns(grad_skip_rows).reshape(2, feat, -1),
+        columns(grad_qkv_rows).reshape(3, feat, -1).transpose(2, 0, 1),
+        columns(grad_out),
+        grad_up_out,
+        grad_down_out,
         gain_total,
         bias_total,
-        new_narrow[0].reshape(2, feat),
-        new_wide[0],
-        new_wide[1],
-        new_narrow[1].reshape(3, feat),
-        new_narrow[2],
-        new_wide[2],
-        new_wide[3],
-        new_narrow[3],
-        new_narrow[4],
-        new_wide[4],
+        new_row_skip.reshape(2, feat),
+        new_col_skip,
+        new_row_qkv,
+        new_col_qkv.reshape(3, feat),
+        new_row_out,
+        new_col_out,
+        new_row_up,
+        new_col_up,
+        new_row_down,
+        new_col_down,
         new_second_gain,
         new_second_bias[0],
         new_second_bias[1],
         new_skip,
         new_qkv,
-        steps[2],
+        step_out,
         new_up,
         new_down,
         gain_step,

time: 725 us -> 627 us (0.86)
  starting transfers between devices: 154 us -> 58.4 us
  waiting for transfers between devices: 266 us -> 232 us
  local copies, waits for them, and re-layouts: 73.4 us -> 95.1 us
    ppermute x78 -> x66, starting transfers between devices: 154 us -> 58.3 us  [send(): return lax.ppermute(value, axes, perm(move))]
    ppermute x78 -> x66, waiting for transfers between devices: 266 us -> 227 us  [send(): return lax.ppermute(value, axes, perm(move))]
    concatenate x2 -> x6, local copies, waits for them, and re-layouts: 0.82 us -> 14.2 us  [the longest x1 5.01 us: chips(): back = jnp.concatenate(canonical(back), axis=0)]
    slice x11 -> x20, local copies, waits for them, and re-layouts: 9.92 us -> 22.3 us  [the longest x2 3.93 us: back_piece(): token_grad[:SEQ, columns_of]]
    select_n x0 -> x10, other arithmetic: none -> 10.9 us  [the longest x6 7.62 us: exchange(): jnp.where(flag == 0, table[index], table[index ^ bit])]
    optimization_barrier x0 -> x6, local copies, waits for them, and re-layouts: none -> 10.5 us  [tie(): return lax.optimization_barrier(values)]
    concatenate x4 -> x17, other arithmetic: 2.62 us -> 11.9 us  [the longest x4 4.09 us: chips(): jnp.concatenate([back_near[place], back_far[place]], axis=1)]
    squeeze x3 -> x0, other arithmetic: 8.8 us -> none  [the longest x1 4.85 us: chips(): returned[:, step]]
  transfers between devices with their start and end apart: 79 -> 67, of which waited for: 36 -> 33; matrix products, arithmetic and copies ran while one was open for 19% -> 26% of each run, Pallas kernels for 8% -> 9%
where the time goes in v3:
time: 627 us; the launch traced here: 615 us
  waiting for transfers between devices  232 us (37%)
  other arithmetic  100 us (16%)
  Pallas kernels  96.2 us (15%)
  local copies, waits for them, and re-layouts  95.1 us (15%)
  starting transfers between devices  58.4 us (9%)
  between operations  26.7 us (4%)
  matrix products  6.36 us (1%)
    ppermute x66, waiting for transfers between devices, send(): return lax.ppermute(value, axes, perm(move))  227 us
    ppermute x66, starting transfers between devices, send(): return lax.ppermute(value, axes, perm(move))  58.3 us
    pallas_call x1, Pallas kernels, attn_backward(): pl.pallas_call(attn_backward_kernel, out_shape=[jax.ShapeDtypeStruct((tok...  38.6 us
    pallas_call x1, Pallas kernels, ffn(): pl.pallas_call(ffn_kernel, out_shape=[part] * 4 + [grad] * 4, grid_spec=p...  38.4 us
    pallas_call x1, Pallas kernels, attn_forward(): pl.pallas_call(attn_forward_kernel, out_shape=[jax.ShapeDtypeStruct((toke...  19.2 us
    unnamed x205, local copies, waits for them, and re-layouts  12.9 us
  transfers between devices with their start and end apart: 67, of which 33 were waited for; matrix products, arithmetic and copies ran while one was open for 26% of the time, Pallas kernels for 9%

profile of v3, /device:TPU:0, one launch (start us, length us, event | category | flops | bytes accessed | tf_op | source)
XLA Modules:
  0.0 614.5 jit_solution(16242394206567580404)
XLA Ops:
  7.3 2.3 broadcast_select_fusion.1
  11.0 3.6 collective-permute-start.1
  20.7 2.4 copy.195
  23.1 2.0 reshape_reshape.3
  26.2 11.3 %collective-permute-done = bf16[72,1152]{1,0:T(8,128)(2,1)S(1)} collective-permute-done((bf16[72,1152]{1,0:T(8,128)(2,1)}, bf16[72,1152]{1,0:T(8,128)(2,1)S(1)}, u32[]{:S(2)}, u32[]{:S(2)}) %collective-permute-start) | collective-permute-done | bytes 165920 | tf_op jit(solution)/shard_map/ppermute | solution.py:636
  37.5 1.9 pad_maximum_fusion.24
  45.7 17.8 %collective-permute-done.7 = bf16[2,72,1152]{2,1,0:T(8,128)(2,1)S(1)} collective-permute-done((bf16[2,72,1152]{2,1,0:T(8,128)(2,1)S(1)}, bf16[2,72,1152]{2,1,0:T(8,128)(2,1)S(1)}, u32[]{:S(2)}, u32[]{:S(2)}) %collective-permute-start.7) | collective-permute-done | bytes 331808 | tf_op jit(solution)/shard_map/ppermute | solution.py:636
  69.7 4.8 constant_dynamic-slice_fusion.5
  74.7 3.6 collective-permute-start.6
  79.7 2.4 collective-permute-done.8
  85.5 4.8 collective-permute-done.11
  93.9 5.8 collective-permute-done.5
  99.7 16.4 %collective-permute-done.4 = bf16[258,864]{1,0:T(8,128)(2,1)S(1)} collective-permute-done((bf16[258,864]{1,0:T(8,128)(2,1)S(1)}, bf16[258,864]{1,0:T(8,128)(2,1)S(1)}, u32[]{:S(2)}, u32[]{:S(2)}) %collective-permute-start.4) | collective-permute-done | bytes 445856 | tf_op jit(solution)/shard_map/ppermute | solution.py:636
  119.7 2.4 concatenate.133
  122.1 2.3 concatenate.134
  127.1 1.9 fusion.87
  133.7 2.1 concatenate.139
  145.3 9.3 %collective-permute-done.17 = bf16[2,144,1152]{2,1,0:T(8,128)(2,1)S(1)} collective-permute-done((bf16[2,144,1152]{2,1,0:T(8,128)(2,1)S(1)}, bf16[2,144,1152]{2,1,0:T(8,128)(2,1)S(1)}, u32[]{:S(2)}, u32[]{:S(2)}) %collective-permute-start.17) | collective-permute-done | bytes 663584 | tf_op jit(solution)/shard_map/ppermute | solution.py:636
  154.6 8.4 %collective-permute-done.18 = bf16[2,144,1152]{2,1,0:T(8,128)(2,1)S(1)} collective-permute-done((bf16[2,144,1152]{2,1,0:T(8,128)(2,1)S(1)}, bf16[2,144,1152]{2,1,0:T(8,128)(2,1)S(1)}, u32[]{:S(2)}, u32[]{:S(2)}) %collective-permute-start.18) | collective-permute-done | bytes 663584 | tf_op jit(solution)/shard_map/ppermute | solution.py:636
  167.0 19.2 %attn_forward.1 = (f32[272,1152]{1,0:T(8,128)S(1)}, f32[272,1152]{1,0:T(8,128)S(1)}, bf16[8,544,216]{2,1,0:T(8,128)(2,1)S(1)}, bf16[8,544,72]{2,1,0:T(8,128)(2,1)S(1)}) custom-call(s32[1]{0:T(128)} %bitcast.meta_ref, bf16[544,1152]{1,0:T(8,128)(2,1)S(1)} %pad_maximum_fusion.12.normed_ref, bf16[2,8,144,1152]{3,2,1,0:T(8,128)(2,1)S(1)} %pad_maximum_fusion.qk_ref.vo_ref, ...), custom_call_target="tpu_custom_call" | custom-call | flops 2887778304 | bytes 16777216 | tf_op jit(solution)/shard_map/attn_forward/pallas_call | solution.py:451
  187.5 3.0 collective-permute-done.20
  192.5 15.6 %collective-permute-done.21 = bf16[272,1152]{1,0:T(8,128)(2,1)S(1)} collective-permute-done((bf16[272,1152]{1,0:T(8,128)(2,1)S(1)}, bf16[272,1152]{1,0:T(8,128)(2,1)S(1)}, u32[]{:S(2)}, u32[]{:S(2)}) %collective-permute-start.21) | collective-permute-done | bytes 626720 | tf_op jit(solution)/shard_map/ppermute | solution.py:636
  210.7 3.4 pad_maximum_fusion.2.cot_ref
  214.1 2.9 pad_maximum_fusion.1.mixed_ref
  217.0 4.3 all-gather.3.cloned.1.call-done
  221.3 38.4 %ffn.1 = (f32[544,1152]{1,0:T(8,128)}, f32[544,1152]{1,0:T(8,128)}, f32[544,1152]{1,0:T(8,128)}, f32[544,1152]{1,0:T(8,128)}, bf16[4,144,1152]{2,1,0:T(8,128)(2,...) custom-call(s32[8]{0:T(128)} %stack.264.order_ref, ...), custom_call_target="tpu_custom_call" | custom-call | flops 17326669824 | bytes 33554432 | tf_op jit(solution)/shard_map/ffn/pallas_call | solution.py:390
  260.4 4.3 collective-permute-done.24
  264.7 2.1 add.501
  269.9 21.6 %collective-permute-done.26 = bf16[4,144,1152]{2,1,0:T(8,128)(2,1)S(1)} collective-permute-done((bf16[4,144,1152]{2,1,0:T(8,128)(2,1)}, bf16[4,144,1152]{2,1,0:T(8,128)(2,1)S(1)}, u32[]{:S(2)}, u32[]{:S(2)}) %collective-permute-start.26) | collective-permute-done | bytes 1327136 | tf_op jit(solution)/shard_map/ppermute | solution.py:636
  298.9 2.0 add.505
  303.7 38.6 %attn_backward.1 = (f32[272,1152]{1,0:T(8,128)S(1)}, f32[272,1152]{1,0:T(8,128)S(1)}, bf16[8,144,1152]{2,1,0:T(8,128)(2,1)}, bf16[4,144,1152]{2,1,0:T(8,128)(2,1...) custom-call(s32[1]{0:T(128)} %bitcast.meta_ref, ...), custom_call_target="tpu_custom_call" | custom-call | flops 5775556608 | bytes 25165824 | tf_op jit(solution)/shard_map/attn_backward/pallas_call | solution.py:545
  356.5 2.4 convolution_convert_fusion
  362.3 2.0 convolution_convert_fusion.1
  367.7 6.5 %collective-permute-done.36 = bf16[2,144,1152]{2,1,0:T(8,128)(2,1)S(1)} collective-permute-done((bf16[2,144,1152]{2,1,0:T(8,128)(2,1)S(1)}, bf16[2,144,1152]{2,1,0:T(8,128)(2,1)S(1)}, u32[]{:S(2)}, u32[]{:S(2)}) %collective-permute-start.36) | collective-permute-done | bytes 663584 | tf_op jit(solution)/shard_map/ppermute | solution.py:636
  379.0 15.7 %collective-permute-done.40 = bf16[144,1152]{1,0:T(8,128)(2,1)S(1)} collective-permute-done((bf16[144,1152]{1,0:T(8,128)(2,1)S(1)}, bf16[144,1152]{1,0:T(8,128)(2,1)S(1)}, u32[]{:S(2)}, u32[]{:S(2)}) %collective-permute-start.40) | collective-permute-done | bytes 331808 | tf_op jit(solution)/shard_map/ppermute | solution.py:636
  396.1 10.5 %collective-permute-done.39 = bf16[4,144,1152]{2,1,0:T(8,128)(2,1)S(1)} collective-permute-done((bf16[4,144,1152]{2,1,0:T(8,128)(2,1)S(1)}, bf16[4,144,1152]{2,1,0:T(8,128)(2,1)S(1)}, u32[]{:S(2)}, u32[]{:S(2)}) %collective-permute-start.39) | collective-permute-done | bytes 1327136 | tf_op jit(solution)/shard_map/ppermute | solution.py:636
  406.6 3.4 collective-permute-done.38
  415.6 2.0 copy.209
  419.3 11.9 %collective-permute-done.46 = bf16[4,258,432]{2,0,1:T(4,128)(2,1)S(1)} collective-permute-done((bf16[4,258,432]{2,0,1:T(4,128)(2,1)}, bf16[4,258,432]{2,0,1:T(4,128)(2,1)S(1)}, u32[]{:S(2)}, u32[]{:S(2)}) %collective-permute-start.46) | collective-permute-done | bytes 891680 | tf_op jit(solution)/shard_map/ppermute | solution.py:636
  432.4 2.4 copy.208
  442.0 3.1 collective-permute-start.53
  457.0 3.5 multiply_reduce_fusion
  463.5 2.5 collective-permute-done.50
  467.3 2.6 collective-permute-done.51
  469.9 2.3 collective-permute-start.52
  473.0 6.4 %collective-permute-done.52 = f32[6,1152]{1,0:T(8,128)S(1)} collective-permute-done((f32[6,1152]{1,0:T(8,128)S(1)}, f32[6,1152]{1,0:T(8,128)S(1)}, u32[]{:S(2)}, u32[]{:S(2)}) %collective-permute-start.52) | collective-permute-done | bytes 27680 | tf_op jit(solution)/shard_map/ppermute | solution.py:636
  480.0 2.9 fusion.78
  485.8 8.4 %collective-permute-done.47 = bf16[4,72,1152]{2,1,0:T(8,128)(2,1)} collective-permute-done((bf16[4,72,1152]{2,1,0:T(8,128)(2,1)}, bf16[4,72,1152]{2,1,0:T(8,128)(2,1)}, u32[]{:S(2)}, u32[]{:S(2)}) %collective-permute-start.47) | collective-permute-done | bytes 663584 | tf_op jit(solution)/shard_map/ppermute | solution.py:636
  500.1 2.1 copy.220
  503.3 2.1 copy.224
  505.5 2.0 broadcast_select_fusion.18
  509.8 5.0 concatenate.161
  514.8 2.3 fusion.80
  517.1 1.9 fusion.11
  519.5 2.0 multiply_add_fusion
  521.4 1.9 bitcast_add_fusion
  523.4 5.8 collective-permute-done.56
  530.0 2.7 select_convert_fusion
  533.7 5.7 collective-permute-done.58
  541.1 11.8 %collective-permute-done.59 = bf16[216,1152]{1,0:T(8,128)(2,1)S(1)} collective-permute-done((bf16[216,1152]{1,0:T(8,128)(2,1)S(1)}, bf16[216,1152]{1,0:T(8,128)(2,1)S(1)}, u32[]{:S(2)}, u32[]{:S(2)}) %collective-permute-start.59) | collective-permute-done | bytes 497696 | tf_op jit(solution)/shard_map/ppermute | solution.py:636
  557.8 2.3 collective-permute-done.62
  562.5 1.9 fusion.34
  581.4 3.3 collective-permute-done.64
  586.0 4.3 collective-permute-done.65
  (536 shorter events, 180.9 us)
Async XLA Ops:
  7.2 214.1 %all-gather.3.cloned.1.call-start = ((), (), s32[]{:S(2)}) async-start(), calls=%async_computation | async-start | bytes 5971968 | tf_op jit(solution)/shard_map/all_gather | solution.py:797
  9.6 9.7 %collective-permute-start.2 = (bf16[2064,144]{0,1:T(8,128)(2,1)}, bf16[2064,144]{0,1:T(8,128)(2,1)}, u32[]{:S(2)}, u32[]{:S(2)}) collective-permute-start(bf16[2064,144]{0,1:T(8,128)(2,1)} %get-tuple-element.557), channel_id=1, source_target_pairs={{0,8},{1,9},{2,10},{3,11},{4,12},{5,13},{6,14},{7,15},{8,0},{9,1},... | collective-permute-start | bytes 1783304 | tf_op jit(solution)/shard_map/ppermute | solution.py:636
  11.0 26.5 %collective-permute-start.1 = (bf16[144,1152]{1,0:T(8,128)(2,1)}, bf16[144,1152]{1,0:T(8,128)(2,1)}, u32[]{:S(2)}, u32[]{:S(2)}) collective-permute-start(bf16[144,1152]{1,0:T(8,128)(2,1)} %fusion.93), channel_id=1, source_target_pairs={{0,4},{1,5},{2,6},{3,7},{4,0},{5,1},{6,2},{7,3},{8,12},{9,13},{10,... | collective-permute-start | bytes 995336 | tf_op jit(solution)/shard_map/ppermute | solution.py:636
  15.3 22.2 %collective-permute-start = (bf16[72,1152]{1,0:T(8,128)(2,1)}, bf16[72,1152]{1,0:T(8,128)(2,1)S(1)}, u32[]{:S(2)}, u32[]{:S(2)}) collective-permute-start(bf16[72,1152]{1,0:T(8,128)(2,1)} %fusion.94), channel_id=1, source_target_pairs={{0,4},{1,5},{2,6},{3,7},{4,0},{5,1},{6,2},{7,3},{8,12},{9,13},{10,... | collective-permute-start | bytes 497672 | tf_op jit(solution)/shard_map/ppermute | solution.py:636
  39.4 27.1 %collective-permute-start.10 = (bf16[2,144,1152]{2,1,0:T(8,128)(2,1)}, bf16[2,144,1152]{2,1,0:T(8,128)(2,1)}, u32[]{:S(2)}, u32[]{:S(2)}) collective-permute-start(bf16[2,144,1152]{2,1,0:T(8,128)(2,1)} %pad_maximum_fusion.24), channel_id=1, source_target_pairs={{0,2},{1,3},{2,0},{3,1},{4,6},{5,7},{6,4},{7,5},{8,10},{9,11},{10,... | collective-permute-start | bytes 1990664 | tf_op jit(solution)/shard_map/ppermute | solution.py:636
  40.3 23.2 %collective-permute-start.7 = (bf16[2,72,1152]{2,1,0:T(8,128)(2,1)S(1)}, bf16[2,72,1152]{2,1,0:T(8,128)(2,1)S(1)}, u32[]{:S(2)}, u32[]{:S(2)}) collective-permute-start(bf16[2,72,1152]{2,1,0:T(8,128)(2,1)S(1)} %pad_maximum_fusion.39), channel_id=1, source_target_pairs={{0,2},{1,3},{2,0},{3,1},{4,6},{5,7},{6,4},{7,5},{8,10},{9,11},{10,... | collective-permute-start | bytes 995336 | tf_op jit(solution)/shard_map/ppermute | solution.py:636
  43.1 26.6 %collective-permute-start.3 = (bf16[4,258,432]{2,0,1:T(4,128)(2,1)}, bf16[4,258,432]{2,0,1:T(4,128)(2,1)}, u32[]{:S(2)}, u32[]{:S(2)}) collective-permute-start(bf16[4,258,432]{2,0,1:T(4,128)(2,1)} %copy.196), channel_id=1, source_target_pairs={{0,1},{1,0},{2,3},{3,2},{4,5},{5,4},{6,7},{7,6},{8,9},{9,8},{10,11... | collective-permute-start | bytes 2674952 | tf_op jit(solution)/shard_map/ppermute | solution.py:636
  63.6 18.5 %collective-permute-start.8 = (bf16[4,72,1152]{2,1,0:T(8,128)(2,1)S(1)}, bf16[4,72,1152]{2,1,0:T(8,128)(2,1)S(1)}, u32[]{:S(2)}, u32[]{:S(2)}) collective-permute-start(bf16[4,72,1152]{2,1,0:T(8,128)(2,1)S(1)} %pad_maximum_fusion.23), channel_id=1, source_target_pairs={{0,1},{1,0},{2,3},{3,2},{4,5},{5,4},{6,7},{7,6},{8,9},{9,8},{10,11... | collective-permute-start | bytes 1990664 | tf_op jit(solution)/shard_map/ppermute | solution.py:636
  65.0 17.1 %collective-permute-start.9 = (bf16[4,72,1152]{2,1,0:T(8,128)(2,1)S(1)}, bf16[4,72,1152]{2,1,0:T(8,128)(2,1)S(1)}, u32[]{:S(2)}, u32[]{:S(2)}) collective-permute-start(bf16[4,72,1152]{2,1,0:T(8,128)(2,1)S(1)} %pad_maximum_fusion.23), channel_id=1, source_target_pairs={{0,16},{1,17},{2,18},{3,19},{4,20},{5,21},{6,22},{7,23},{8,24},{9,... | collective-permute-start | bytes 1990664 | tf_op jit(solution)/shard_map/ppermute | solution.py:636
  74.7 19.3 %collective-permute-start.6 = (bf16[258,864]{1,0:T(8,128)(2,1)S(1)}, bf16[258,864]{1,0:T(8,128)(2,1)S(1)}, u32[]{:S(2)}, u32[]{:S(2)}) collective-permute-start(bf16[258,864]{1,0:T(8,128)(2,1)S(1)} %pad_maximum_fusion.35), channel_id=1, source_target_pairs={{0,6},{1,7},{2,4},{3,5},{4,2},{5,3},{6,0},{7,1},{8,14},{9,15},{10,... | collective-permute-start | bytes 1337480 | tf_op jit(solution)/shard_map/ppermute | solution.py:636
  78.5 21.2 %collective-permute-start.5 = (bf16[258,864]{1,0:T(8,128)(2,1)S(1)}, bf16[258,864]{1,0:T(8,128)(2,1)S(1)}, u32[]{:S(2)}, u32[]{:S(2)}) collective-permute-start(bf16[258,864]{1,0:T(8,128)(2,1)S(1)} %pad_maximum_fusion.34), channel_id=1, source_target_pairs={{0,2},{1,3},{2,0},{3,1},{4,6},{5,7},{6,4},{7,5},{8,10},{9,11},{10,... | collective-permute-start | bytes 1337480 | tf_op jit(solution)/shard_map/ppermute | solution.py:636
  78.7 37.4 %collective-permute-start.4 = (bf16[258,864]{1,0:T(8,128)(2,1)S(1)}, bf16[258,864]{1,0:T(8,128)(2,1)S(1)}, u32[]{:S(2)}, u32[]{:S(2)}) collective-permute-start(bf16[258,864]{1,0:T(8,128)(2,1)S(1)} %pad_maximum_fusion.33), channel_id=1, source_target_pairs={{0,4},{1,5},{2,6},{3,7},{4,0},{5,1},{6,2},{7,3},{8,12},{9,13},{10,... | collective-permute-start | bytes 1337480 | tf_op jit(solution)/shard_map/ppermute | solution.py:636
  82.2 8.2 %collective-permute-start.11 = (bf16[2,72,1152]{2,1,0:T(8,128)(2,1)S(1)}, bf16[2,72,1152]{2,1,0:T(8,128)(2,1)S(1)}, u32[]{:S(2)}, u32[]{:S(2)}) collective-permute-start(bf16[2,72,1152]{2,1,0:T(8,128)(2,1)S(1)} %slice.421), channel_id=1, source_target_pairs={{0,16},{1,17},{2,18},{3,19},{4,20},{5,21},{6,22},{7,23},{8,24},{9,... | collective-permute-start | bytes 995336 | tf_op jit(solution)/shard_map/ppermute | solution.py:636
  83.6 8.5 %collective-permute-start.12 = (bf16[2,72,1152]{2,1,0:T(8,128)(2,1)S(1)}, bf16[2,72,1152]{2,1,0:T(8,128)(2,1)S(1)}, u32[]{:S(2)}, u32[]{:S(2)}) collective-permute-start(bf16[2,72,1152]{2,1,0:T(8,128)(2,1)S(1)} %slice.422), channel_id=1, source_target_pairs={{0,1},{1,0},{2,3},{3,2},{4,5},{5,4},{6,7},{7,6},{8,9},{9,8},{10,11... | collective-permute-start | bytes 995336 | tf_op jit(solution)/shard_map/ppermute | solution.py:636
  90.4 36.6 %collective-permute-start.13 = (bf16[4,144,1152]{2,1,0:T(8,128)(2,1)S(1)}, bf16[4,144,1152]{2,1,0:T(8,128)(2,1)}, u32[]{:S(2)}, u32[]{:S(2)}) collective-permute-start(bf16[4,144,1152]{2,1,0:T(8,128)(2,1)S(1)} %pad_maximum_fusion.7), channel_id=1, source_target_pairs={{0,1},{1,0},{2,3},{3,2},{4,5},{5,4},{6,7},{7,6},{8,9},{9,8},{10,11... | collective-permute-start | bytes 3981320 | tf_op jit(solution)/shard_map/ppermute | solution.py:636
  92.1 34.9 %collective-permute-start.14 = (bf16[4,144,1152]{2,1,0:T(8,128)(2,1)S(1)}, bf16[4,144,1152]{2,1,0:T(8,128)(2,1)}, u32[]{:S(2)}, u32[]{:S(2)}) collective-permute-start(bf16[4,144,1152]{2,1,0:T(8,128)(2,1)S(1)} %pad_maximum_fusion.7), channel_id=1, source_target_pairs={{0,16},{1,17},{2,18},{3,19},{4,20},{5,21},{6,22},{7,23},{8,24},{9,... | collective-permute-start | bytes 3981320 | tf_op jit(solution)/shard_map/ppermute | solution.py:636
  130.3 11.1 %collective-permute-start.15 = (f32[272,1152]{1,0:T(8,128)}, f32[272,1152]{1,0:T(8,128)}, u32[]{:S(2)}, u32[]{:S(2)}) collective-permute-start(f32[272,1152]{1,0:T(8,128)} %get-tuple-element.518), channel_id=1, source_target_pairs={{0,8},{1,9},{2,10},{3,11},{4,12},{5,13},{6,14},{7,15},{8,0},{9,1},... | collective-permute-start | bytes 3760136 | tf_op jit(solution)/shard_map/ppermute | solution.py:636
  137.2 17.4 %collective-permute-start.17 = (bf16[2,144,1152]{2,1,0:T(8,128)(2,1)S(1)}, bf16[2,144,1152]{2,1,0:T(8,128)(2,1)S(1)}, u32[]{:S(2)}, u32[]{:S(2)}) collective-permute-start(bf16[2,144,1152]{2,1,0:T(8,128)(2,1)S(1)} %slice.452), channel_id=1, source_target_pairs={{0,16},{1,17},{2,18},{3,19},{4,20},{5,21},{6,22},{7,23},{8,24},{9,... | collective-permute-start | bytes 1990664 | tf_op jit(solution)/shard_map/ppermute | solution.py:636
  139.8 23.2 %collective-permute-start.18 = (bf16[2,144,1152]{2,1,0:T(8,128)(2,1)S(1)}, bf16[2,144,1152]{2,1,0:T(8,128)(2,1)S(1)}, u32[]{:S(2)}, u32[]{:S(2)}) collective-permute-start(bf16[2,144,1152]{2,1,0:T(8,128)(2,1)S(1)} %slice.453), channel_id=1, source_target_pairs={{0,1},{1,0},{2,3},{3,2},{4,5},{5,4},{6,7},{7,6},{8,9},{9,8},{10,11... | collective-permute-start | bytes 1990664 | tf_op jit(solution)/shard_map/ppermute | solution.py:636
  143.7 19.5 %collective-permute-start.16 = (bf16[272,1152]{1,0:T(8,128)(2,1)S(1)}, bf16[272,1152]{1,0:T(8,128)(2,1)S(1)}, u32[]{:S(2)}, u32[]{:S(2)}) collective-permute-start(bf16[272,1152]{1,0:T(8,128)(2,1)S(1)} %pad.24), channel_id=1, source_target_pairs={{0,8},{1,9},{2,10},{3,11},{4,12},{5,13},{6,14},{7,15},{8,0},{9,1},... | collective-permute-start | bytes 1880072 | tf_op jit(solution)/shard_map/ppermute | solution.py:636
  163.3 22.9 %collective-permute-start.19 = (bf16[272,1152]{1,0:T(8,128)(2,1)S(1)}, bf16[272,1152]{1,0:T(8,128)(2,1)S(1)}, u32[]{:S(2)}, u32[]{:S(2)}) collective-permute-start(bf16[272,1152]{1,0:T(8,128)(2,1)S(1)} %pad.25), channel_id=1, source_target_pairs={{0,16},{1,17},{2,18},{3,19},{4,20},{5,21},{6,22},{7,23},{8,24},{9,... | collective-permute-start | bytes 1880072 | tf_op jit(solution)/shard_map/ppermute | solution.py:636
  191.9 16.2 %collective-permute-start.21 = (bf16[272,1152]{1,0:T(8,128)(2,1)S(1)}, bf16[272,1152]{1,0:T(8,128)(2,1)S(1)}, u32[]{:S(2)}, u32[]{:S(2)}) collective-permute-start(bf16[272,1152]{1,0:T(8,128)(2,1)S(1)} %pad.26), channel_id=1, source_target_pairs={{0,16},{1,17},{2,18},{3,19},{4,20},{5,21},{6,22},{7,23},{8,24},{9,... | collective-permute-start | bytes 1880072 | tf_op jit(solution)/shard_map/ppermute | solution.py:636
  192.5 18.2 %collective-permute-start.23 = (bf16[544,1152]{1,0:T(8,128)(2,1)}, bf16[544,1152]{1,0:T(8,128)(2,1)}, u32[]{:S(2)}, u32[]{:S(2)}) collective-permute-start(bf16[544,1152]{1,0:T(8,128)(2,1)} %pad_maximum_fusion.13), channel_id=1, source_target_pairs={{0,8},{1,9},{2,10},{3,11},{4,12},{5,13},{6,14},{7,15},{8,0},{9,1},... | collective-permute-start | bytes 3760136 | tf_op jit(solution)/shard_map/ppermute | solution.py:636
  210.1 4.0 collective-permute-start.22
  259.7 5.0 collective-permute-start.24
  259.8 31.8 %collective-permute-start.26 = (bf16[4,144,1152]{2,1,0:T(8,128)(2,1)}, bf16[4,144,1152]{2,1,0:T(8,128)(2,1)S(1)}, u32[]{:S(2)}, u32[]{:S(2)}) collective-permute-start(bf16[4,144,1152]{2,1,0:T(8,128)(2,1)} %get-tuple-element.132), channel_id=1, source_target_pairs={{0,1},{1,0},{2,3},{3,2},{4,5},{5,4},{6,7},{7,6},{8,9},{9,8},{10,11... | collective-permute-start | bytes 3981320 | tf_op jit(solution)/shard_map/ppermute | solution.py:636
  268.4 23.2 %collective-permute-start.25 = (bf16[272,1152]{1,0:T(8,128)(2,1)S(1)}, bf16[272,1152]{1,0:T(8,128)(2,1)S(1)}, u32[]{:S(2)}, u32[]{:S(2)}) collective-permute-start(bf16[272,1152]{1,0:T(8,128)(2,1)S(1)} %slice.764), channel_id=1, source_target_pairs={{0,16},{1,17},{2,18},{3,19},{4,20},{5,21},{6,22},{7,23},{8,24},{9,... | collective-permute-start | bytes 1880072 | tf_op jit(solution)/shard_map/ppermute | solution.py:636
  292.7 5.4 collective-permute-start.32
  296.1 6.5 %collective-permute-start.27 = (bf16[272,1152]{1,0:T(8,128)(2,1)S(1)}, bf16[272,1152]{1,0:T(8,128)(2,1)S(1)}, u32[]{:S(2)}, u32[]{:S(2)}) collective-permute-start(bf16[272,1152]{1,0:T(8,128)(2,1)S(1)} %pad.27), channel_id=1, source_target_pairs={{0,8},{1,9},{2,10},{3,11},{4,12},{5,13},{6,14},{7,15},{8,0},{9,1},... | collective-permute-start | bytes 1880072 | tf_op jit(solution)/shard_map/ppermute | solution.py:636
  296.7 50.1 %collective-permute-start.30 = (bf16[4,144,1152]{2,1,0:T(8,128)(2,1)}, bf16[4,144,1152]{2,1,0:T(8,128)(2,1)}, u32[]{:S(2)}, u32[]{:S(2)}) collective-permute-start(bf16[4,144,1152]{2,1,0:T(8,128)(2,1)} %get-tuple-element.143), channel_id=1, source_target_pairs={{0,1},{1,0},{2,3},{3,2},{4,5},{5,4},{6,7},{7,6},{8,9},{9,8},{10,11... | collective-permute-start | bytes 3981320 | tf_op jit(solution)/shard_map/ppermute | solution.py:636
  297.6 49.1 %collective-permute-start.31 = (bf16[2,144,1152]{2,1,0:T(8,128)(2,1)S(1)}, bf16[2,144,1152]{2,1,0:T(8,128)(2,1)S(1)}, u32[]{:S(2)}, u32[]{:S(2)}) collective-permute-start(bf16[2,144,1152]{2,1,0:T(8,128)(2,1)S(1)} %slice.560), channel_id=1, source_target_pairs={{0,2},{1,3},{2,0},{3,1},{4,6},{5,7},{6,4},{7,5},{8,10},{9,11},{10,... | collective-permute-start | bytes 1990664 | tf_op jit(solution)/shard_map/ppermute | solution.py:636
  301.0 45.7 %collective-permute-start.33 = (bf16[272,1152]{1,0:T(8,128)(2,1)S(1)}, bf16[272,1152]{1,0:T(8,128)(2,1)S(1)}, u32[]{:S(2)}, u32[]{:S(2)}) collective-permute-start(bf16[272,1152]{1,0:T(8,128)(2,1)S(1)} %slice.763), channel_id=1, source_target_pairs={{0,16},{1,17},{2,18},{3,19},{4,20},{5,21},{6,22},{7,23},{8,24},{9,... | collective-permute-start | bytes 1880072 | tf_op jit(solution)/shard_map/ppermute | solution.py:636
  342.3 24.7 %collective-permute-start.28 = (bf16[2,144,1152]{2,1,0:T(8,128)(2,1)S(1)}, bf16[2,144,1152]{2,1,0:T(8,128)(2,1)S(1)}, u32[]{:S(2)}, u32[]{:S(2)}) collective-permute-start(bf16[2,144,1152]{2,1,0:T(8,128)(2,1)S(1)} %get-tuple-element.139), channel_id=1, source_target_pairs={{0,16},{1,17},{2,18},{3,19},{4,20},{5,21},{6,22},{7,23},{8,24},{9,... | collective-permute-start | bytes 1990664 | tf_op jit(solution)/shard_map/ppermute | solution.py:636
  343.0 24.7 %collective-permute-start.29 = (bf16[2,144,1152]{2,1,0:T(8,128)(2,1)S(1)}, bf16[2,144,1152]{2,1,0:T(8,128)(2,1)S(1)}, u32[]{:S(2)}, u32[]{:S(2)}) collective-permute-start(bf16[2,144,1152]{2,1,0:T(8,128)(2,1)S(1)} %get-tuple-element.140), channel_id=1, source_target_pairs={{0,1},{1,0},{2,3},{3,2},{4,5},{5,4},{6,7},{7,6},{8,9},{9,8},{10,11... | collective-permute-start | bytes 1990664 | tf_op jit(solution)/shard_map/ppermute | solution.py:636
  346.8 5.6 collective-permute-start.34
  347.0 20.6 %collective-permute-start.37 = (bf16[144,1152]{1,0:T(8,128)(2,1)S(1)}, bf16[144,1152]{1,0:T(8,128)(2,1)S(1)}, u32[]{:S(2)}, u32[]{:S(2)}) collective-permute-start(bf16[144,1152]{1,0:T(8,128)(2,1)S(1)} %slice_bitcast_fusion.7), channel_id=1, source_target_pairs={{0,4},{1,5},{2,6},{3,7},{4,0},{5,1},{6,2},{7,3},{8,12},{9,13},{10,... | collective-permute-start | bytes 995336 | tf_op jit(solution)/shard_map/ppermute | solution.py:636
  350.3 23.9 %collective-permute-start.36 = (bf16[2,144,1152]{2,1,0:T(8,128)(2,1)S(1)}, bf16[2,144,1152]{2,1,0:T(8,128)(2,1)S(1)}, u32[]{:S(2)}, u32[]{:S(2)}) collective-permute-start(bf16[2,144,1152]{2,1,0:T(8,128)(2,1)S(1)} %slice.575), channel_id=1, source_target_pairs={{0,2},{1,3},{2,0},{3,1},{4,6},{5,7},{6,4},{7,5},{8,10},{9,11},{10,... | collective-permute-start | bytes 1990664 | tf_op jit(solution)/shard_map/ppermute | solution.py:636
  360.8 58.5 %collective-permute-start.44 = (bf16[2,72,1152]{2,1,0:T(8,128)(2,1)}, bf16[2,72,1152]{2,1,0:T(8,128)(2,1)}, u32[]{:S(2)}, u32[]{:S(2)}) collective-permute-start(bf16[2,72,1152]{2,1,0:T(8,128)(2,1)} %get-tuple-element.511), channel_id=1, source_target_pairs={{0,16},{1,17},{2,18},{3,19},{4,20},{5,21},{6,22},{7,23},{8,24},{9,... | collective-permute-start | bytes 995336 | tf_op jit(solution)/shard_map/ppermute | solution.py:636
  367.1 52.3 %collective-permute-start.45 = (bf16[2,72,1152]{2,1,0:T(8,128)(2,1)}, bf16[2,72,1152]{2,1,0:T(8,128)(2,1)}, u32[]{:S(2)}, u32[]{:S(2)}) collective-permute-start(bf16[2,72,1152]{2,1,0:T(8,128)(2,1)} %get-tuple-element.510), channel_id=1, source_target_pairs={{0,1},{1,0},{2,3},{3,2},{4,5},{5,4},{6,7},{7,6},{8,9},{9,8},{10,11... | collective-permute-start | bytes 995336 | tf_op jit(solution)/shard_map/ppermute | solution.py:636
  376.0 30.6 %collective-permute-start.39 = (bf16[4,144,1152]{2,1,0:T(8,128)(2,1)S(1)}, bf16[4,144,1152]{2,1,0:T(8,128)(2,1)S(1)}, u32[]{:S(2)}, u32[]{:S(2)}) collective-permute-start(bf16[4,144,1152]{2,1,0:T(8,128)(2,1)S(1)} %pad_maximum_fusion.10), channel_id=1, source_target_pairs={{0,16},{1,17},{2,18},{3,19},{4,20},{5,21},{6,22},{7,23},{8,24},{9,... | collective-permute-start | bytes 3981320 | tf_op jit(solution)/shard_map/ppermute | solution.py:636
  378.0 32.1 %collective-permute-start.38 = (bf16[4,144,1152]{2,1,0:T(8,128)(2,1)S(1)}, bf16[4,144,1152]{2,1,0:T(8,128)(2,1)S(1)}, u32[]{:S(2)}, u32[]{:S(2)}) collective-permute-start(bf16[4,144,1152]{2,1,0:T(8,128)(2,1)S(1)} %pad_maximum_fusion.9), channel_id=1, source_target_pairs={{0,1},{1,0},{2,3},{3,2},{4,5},{5,4},{6,7},{7,6},{8,9},{9,8},{10,11... | collective-permute-start | bytes 3981320 | tf_op jit(solution)/shard_map/ppermute | solution.py:636
  378.8 15.9 %collective-permute-start.40 = (bf16[144,1152]{1,0:T(8,128)(2,1)S(1)}, bf16[144,1152]{1,0:T(8,128)(2,1)S(1)}, u32[]{:S(2)}, u32[]{:S(2)}) collective-permute-start(bf16[144,1152]{1,0:T(8,128)(2,1)S(1)} %slice_bitcast_fusion.6), channel_id=1, source_target_pairs={{0,4},{1,5},{2,6},{3,7},{4,0},{5,1},{6,2},{7,3},{8,12},{9,13},{10,... | collective-permute-start | bytes 995336 | tf_op jit(solution)/shard_map/ppermute | solution.py:636
  394.7 36.5 %collective-permute-start.46 = (bf16[4,258,432]{2,0,1:T(4,128)(2,1)}, bf16[4,258,432]{2,0,1:T(4,128)(2,1)S(1)}, u32[]{:S(2)}, u32[]{:S(2)}) collective-permute-start(bf16[4,258,432]{2,0,1:T(4,128)(2,1)} %copy.203), channel_id=1, source_target_pairs={{0,1},{1,0},{2,3},{3,2},{4,5},{5,4},{6,7},{7,6},{8,9},{9,8},{10,11... | collective-permute-start | bytes 2674952 | tf_op jit(solution)/shard_map/ppermute | solution.py:636
  411.1 28.4 %collective-permute-start.42 = (bf16[2,144,1152]{2,1,0:T(8,128)(2,1)}, bf16[2,144,1152]{2,1,0:T(8,128)(2,1)}, u32[]{:S(2)}, u32[]{:S(2)}) collective-permute-start(bf16[2,144,1152]{2,1,0:T(8,128)(2,1)} %get-tuple-element.580), channel_id=1, source_target_pairs={{0,16},{1,17},{2,18},{3,19},{4,20},{5,21},{6,22},{7,23},{8,24},{9,... | collective-permute-start | bytes 1990664 | tf_op jit(solution)/shard_map/ppermute | solution.py:636
  414.0 25.5 %collective-permute-start.41 = (bf16[2,144,1152]{2,1,0:T(8,128)(2,1)}, bf16[2,144,1152]{2,1,0:T(8,128)(2,1)}, u32[]{:S(2)}, u32[]{:S(2)}) collective-permute-start(bf16[2,144,1152]{2,1,0:T(8,128)(2,1)} %slice.581), channel_id=1, source_target_pairs={{0,2},{1,3},{2,0},{3,1},{4,6},{5,7},{6,4},{7,5},{8,10},{9,11},{10,... | collective-permute-start | bytes 1990664 | tf_op jit(solution)/shard_map/ppermute | solution.py:636
  437.2 48.5 %collective-permute-start.55 = (bf16[258,864]{1,0:T(8,128)(2,1)}, bf16[258,864]{1,0:T(8,128)(2,1)}, u32[]{:S(2)}, u32[]{:S(2)}) collective-permute-start(bf16[258,864]{1,0:T(8,128)(2,1)} %pad_maximum_fusion.38), channel_id=1, source_target_pairs={{0,6},{1,7},{2,4},{3,5},{4,2},{5,3},{6,0},{7,1},{8,14},{9,15},{10,... | collective-permute-start | bytes 1337480 | tf_op jit(solution)/shard_map/ppermute | solution.py:636
  439.5 46.3 %collective-permute-start.54 = (bf16[258,864]{1,0:T(8,128)(2,1)}, bf16[258,864]{1,0:T(8,128)(2,1)}, u32[]{:S(2)}, u32[]{:S(2)}) collective-permute-start(bf16[258,864]{1,0:T(8,128)(2,1)} %pad_maximum_fusion.37), channel_id=1, source_target_pairs={{0,2},{1,3},{2,0},{3,1},{4,6},{5,7},{6,4},{7,5},{8,10},{9,11},{10,... | collective-permute-start | bytes 1337480 | tf_op jit(solution)/shard_map/ppermute | solution.py:636
  440.8 10.1 %collective-permute-start.49 = (bf16[2,2,144,1152]{3,2,1,0:T(8,128)(2,1)S(1)}, bf16[2,2,144,1152]{3,2,1,0:T(8,128)(2,1)S(1)}, u32[]{:S(2)}, u32[]{:S(2)}) collective-permute-start(bf16[2,2,144,1152]{3,2,1,0:T(8,128)(2,1)S(1)} %get-tuple-element.538), channel_id=1, source_target_pairs={{0,8},{1,9},{2,10},{3,11},{4,12},{5,13},{6,14},{7,15},{8,0},{9,1},... | collective-permute-start | bytes 3981320 | tf_op jit(solution)/shard_map/ppermute | solution.py:636
  442.0 43.7 %collective-permute-start.53 = (bf16[258,864]{1,0:T(8,128)(2,1)}, bf16[258,864]{1,0:T(8,128)(2,1)S(1)}, u32[]{:S(2)}, u32[]{:S(2)}) collective-permute-start(bf16[258,864]{1,0:T(8,128)(2,1)} %pad_maximum_fusion.36), channel_id=1, source_target_pairs={{0,4},{1,5},{2,6},{3,7},{4,0},{5,1},{6,2},{7,3},{8,12},{9,13},{10,... | collective-permute-start | bytes 1337480 | tf_op jit(solution)/shard_map/ppermute | solution.py:636
  447.5 38.2 %collective-permute-start.48 = (bf16[4,72,1152]{2,1,0:T(8,128)(2,1)}, bf16[4,72,1152]{2,1,0:T(8,128)(2,1)}, u32[]{:S(2)}, u32[]{:S(2)}) collective-permute-start(bf16[4,72,1152]{2,1,0:T(8,128)(2,1)} %pad_maximum_fusion.29), channel_id=1, source_target_pairs={{0,16},{1,17},{2,18},{3,19},{4,20},{5,21},{6,22},{7,23},{8,24},{9,... | collective-permute-start | bytes 1990664 | tf_op jit(solution)/shard_map/ppermute | solution.py:636
  461.9 4.0 collective-permute-start.50
  466.0 4.0 collective-permute-start.51
  469.9 9.5 %collective-permute-start.52 = (f32[6,1152]{1,0:T(8,128)S(1)}, f32[6,1152]{1,0:T(8,128)S(1)}, u32[]{:S(2)}, u32[]{:S(2)}) collective-permute-start(f32[6,1152]{1,0:T(8,128)S(1)} %add.534), channel_id=1, source_target_pairs={{0,4},{1,5},{2,6},{3,7},{4,0},{5,1},{6,2},{7,3},{8,12},{9,13},{10,... | collective-permute-start | bytes 82952 | tf_op jit(solution)/shard_map/ppermute | solution.py:636
  479.5 14.7 %collective-permute-start.47 = (bf16[4,72,1152]{2,1,0:T(8,128)(2,1)}, bf16[4,72,1152]{2,1,0:T(8,128)(2,1)}, u32[]{:S(2)}, u32[]{:S(2)}) collective-permute-start(bf16[4,72,1152]{2,1,0:T(8,128)(2,1)} %pad_maximum_fusion.28), channel_id=1, source_target_pairs={{0,1},{1,0},{2,3},{3,2},{4,5},{5,4},{6,7},{7,6},{8,9},{9,8},{10,11... | collective-permute-start | bytes 1990664 | tf_op jit(solution)/shard_map/ppermute | solution.py:636
  485.7 37.7 %collective-permute-start.43 = (bf16[144,1152]{1,0:T(8,128)(2,1)}, bf16[144,1152]{1,0:T(8,128)(2,1)}, u32[]{:S(2)}, u32[]{:S(2)}) collective-permute-start(bf16[144,1152]{1,0:T(8,128)(2,1)} %slice_bitcast_fusion.3), channel_id=1, source_target_pairs={{0,4},{1,5},{2,6},{3,7},{4,0},{5,1},{6,2},{7,3},{8,12},{9,13},{10,... | collective-permute-start | bytes 995336 | tf_op jit(solution)/shard_map/ppermute | solution.py:636
  517.1 12.1 %collective-permute-start.57 = (bf16[2064,144]{0,1:T(8,128)(2,1)S(1)}, bf16[2064,144]{0,1:T(8,128)(2,1)S(1)}, u32[]{:S(2)}, u32[]{:S(2)}) collective-permute-start(bf16[2064,144]{0,1:T(8,128)(2,1)S(1)} %get-tuple-element.531), channel_id=1, source_target_pairs={{0,8},{1,9},{2,10},{3,11},{4,12},{5,13},{6,14},{7,15},{8,0},{9,1},... | collective-permute-start | bytes 1783304 | tf_op jit(solution)/shard_map/ppermute | solution.py:636
  519.0 10.1 %collective-permute-start.56 = (bf16[2,72,1152]{2,1,0:T(8,128)(2,1)S(1)}, bf16[2,72,1152]{2,1,0:T(8,128)(2,1)S(1)}, u32[]{:S(2)}, u32[]{:S(2)}) collective-permute-start(bf16[2,72,1152]{2,1,0:T(8,128)(2,1)S(1)} %slice.599), channel_id=1, source_target_pairs={{0,2},{1,3},{2,0},{3,1},{4,6},{5,7},{6,4},{7,5},{8,10},{9,11},{10,... | collective-permute-start | bytes 995336 | tf_op jit(solution)/shard_map/ppermute | solution.py:636
  529.3 10.2 %collective-permute-start.58 = (bf16[72,1152]{1,0:T(8,128)(2,1)S(1)}, bf16[72,1152]{1,0:T(8,128)(2,1)S(1)}, u32[]{:S(2)}, u32[]{:S(2)}) collective-permute-start(bf16[72,1152]{1,0:T(8,128)(2,1)S(1)} %slice_bitcast_fusion.12), channel_id=1, source_target_pairs={{0,4},{1,5},{2,6},{3,7},{4,0},{5,1},{6,2},{7,3},{8,12},{9,13},{10,... | collective-permute-start | bytes 497672 | tf_op jit(solution)/shard_map/ppermute | solution.py:636
  539.6 13.3 %collective-permute-start.59 = (bf16[216,1152]{1,0:T(8,128)(2,1)S(1)}, bf16[216,1152]{1,0:T(8,128)(2,1)S(1)}, u32[]{:S(2)}, u32[]{:S(2)}) collective-permute-start(bf16[216,1152]{1,0:T(8,128)(2,1)S(1)} %get-tuple-element.588), channel_id=1, source_target_pairs={{0,16},{1,17},{2,18},{3,19},{4,20},{5,21},{6,22},{7,23},{8,24},{9,... | collective-permute-start | bytes 1493000 | tf_op jit(solution)/shard_map/ppermute | solution.py:636
  554.0 8.5 %collective-permute-start.60 = (bf16[2,216,1152]{2,1,0:T(8,128)(2,1)}, bf16[2,216,1152]{2,1,0:T(8,128)(2,1)}, u32[]{:S(2)}, u32[]{:S(2)}) collective-permute-start(bf16[2,216,1152]{2,1,0:T(8,128)(2,1)} %get-tuple-element.577), channel_id=1, source_target_pairs={{0,8},{1,9},{2,10},{3,11},{4,12},{5,13},{6,14},{7,15},{8,0},{9,1},... | collective-permute-start | bytes 2985992 | tf_op jit(solution)/shard_map/ppermute | solution.py:636
  556.3 3.8 collective-permute-start.62
  575.9 4.4 collective-permute-start.63
  580.3 4.4 collective-permute-start.64
  584.7 5.5 collective-permute-start.65
  (100 other events, 696.1 us)
Sparse Core Ops, SparseCore 0:
  130.6 90.7 all-gather.2

commit v4 on v3

--- a/solution.py
+++ b/solution.py
@@ -368,7 +368,10 @@
         @pl.when(step == j)
         def _():
             grads[j][...] = grad_up.reshape(grads[j].shape)
-            grads[2 + j][...] = grad_down.reshape(grads[j].shape)
+
+    down_rows = grad_down.reshape((2,) + grads[2].shape[1:])
+    grads[2][0] = down_rows[0]
+    grads[3][0] = down_rows[1]
 
     accumulate(step, (mixed_a, mixed_b), dot_nn(grad_up_in, up))
     accumulate(step, (down_a, down_b), dot_nn(activation, down))
@@ -387,14 +390,16 @@
     grad_block = pl.BlockSpec((blocks, rows, D), lambda t, m: (0, 0, 0))
     part = jax.ShapeDtypeStruct((tokens // 2, D), jnp.float32)
     grad = jax.ShapeDtypeStruct((blocks, rows, D), jnp.bfloat16)
+    turn_block = pl.BlockSpec((1, blocks // 2, rows, D), lambda t, m: (t, 0, 0, 0))
+    turn = jax.ShapeDtypeStruct((2, blocks // 2, rows, D), jnp.bfloat16)
     return pl.pallas_call(
         ffn_kernel,
-        out_shape=[part] * 4 + [grad] * 4,
+        out_shape=[part] * 4 + [grad] * 2 + [turn] * 2,
         grid_spec=pltpu.PrefetchScalarGridSpec(
             num_scalar_prefetch=1,
             grid=(count // blocks,),
             in_specs=[whole, whole] + [weight_spec(slot) for slot in range(blocks)],
-            out_specs=[half] * 4 + [grad_block] * 4,
+            out_specs=[half] * 4 + [grad_block] * 2 + [turn_block] * 2,
         ),
         compiler_params=pltpu.CompilerParams(
             dimension_semantics=("arbitrary",), vmem_limit_bytes=60 * 1024 * 1024
@@ -414,33 +419,48 @@
     return exponent / jnp.sum(exponent, axis=-1, keepdims=True)
 
 
+GROUP = 4
+
+
+def head_weights(qk_ref, vo_ref):
+    qk = [qk_ref[0, head] for head in range(GROUP)]
+    v = [vo_ref[0, head, :HEAD] for head in range(GROUP)]
+    out = [vo_ref[0, head, HEAD:] for head in range(GROUP)]
+    return jnp.concatenate(qk + v, axis=0), jnp.concatenate(out, axis=0)
+
+
+def head_columns(head):
+    first = 2 * HEAD * head
+    value = 2 * HEAD * GROUP + HEAD * head
+    return (
+        slice(first, first + HEAD),
+        slice(first + HEAD, first + 2 * HEAD),
+        slice(value, value + HEAD),
+    )
+
+
 def attn_forward_kernel(meta_ref, normed_ref, qk_ref, vo_ref, part_a, part_b, qkv_ref, attended_ref):
     step = pl.program_id(0)
-    normed = normed_ref[...]
-    qk = dot_nt(normed, qk_ref[0, 0])
-    v_all = dot_nt(normed, vo_ref[0, 0, :HEAD])
-    out_weight = vo_ref[0, 0, HEAD:]
-    qkv_ref[0, :, : 2 * HEAD] = qk.astype(jnp.bfloat16)
-    qkv_ref[0, :, 2 * HEAD :] = v_all.astype(jnp.bfloat16)
-    for image in range(2):
-        rows = slice(image * PAD, (image + 1) * PAD)
-        q = qk[rows, :HEAD].astype(jnp.bfloat16)
-        k = qk[rows, HEAD:].astype(jnp.bfloat16)
-        v = v_all[rows].astype(jnp.bfloat16)
-        probs = soft(q, k).astype(jnp.bfloat16)
-        attended_ref[0, rows] = dot_nn(probs, v).astype(jnp.bfloat16)
-    add = dot_nn(attended_ref[0], out_weight)
-
-    accumulate(step, (part_a, part_b), add)
+    weights, out_weight = head_weights(qk_ref, vo_ref)
+    qkv_ref[0] = dot_nt(normed_ref[...], weights).astype(jnp.bfloat16)
+    for head in range(GROUP):
+        q_at, k_at, v_at = head_columns(head)
+        for image in range(2):
+            rows = slice(image * PAD, (image + 1) * PAD)
+            probs = soft(qkv_ref[0, rows, q_at], qkv_ref[0, rows, k_at]).astype(jnp.bfloat16)
+            attended_ref[0, rows, HEAD * head : HEAD * (head + 1)] = dot_nn(
+                probs, qkv_ref[0, rows, v_at]
+            ).astype(jnp.bfloat16)
+    accumulate(step, (part_a, part_b), dot_nn(attended_ref[0], out_weight))
 
 
 def attn_specs(rows, tokens):
     whole = pl.BlockSpec((tokens, D), lambda s, m: (0, 0))
     half = pl.BlockSpec((tokens // 2, D), lambda s, m: (0, 0))
-    qk = pl.BlockSpec((1, 1, rows, D), lambda s, m: (m[0], s, 0, 0))
-    vo = pl.BlockSpec((1, 1, rows, D), lambda s, m: (1 - m[0], s, 0, 0))
-    qkv = pl.BlockSpec((1, tokens, 3 * HEAD), lambda s, m: (s, 0, 0))
-    att = pl.BlockSpec((1, tokens, HEAD), lambda s, m: (s, 0, 0))
+    qk = pl.BlockSpec((1, GROUP, rows, D), lambda s, m: (m[0], s, 0, 0))
+    vo = pl.BlockSpec((1, GROUP, rows, D), lambda s, m: (1 - m[0], s, 0, 0))
+    qkv = pl.BlockSpec((1, tokens, 3 * HEAD * GROUP), lambda s, m: (s, 0, 0))
+    att = pl.BlockSpec((1, tokens, HEAD * GROUP), lambda s, m: (s, 0, 0))
     return whole, half, qk, vo, qkv, att
 
 
@@ -453,23 +473,19 @@
         out_shape=[
             jax.ShapeDtypeStruct((tokens // 2, D), jnp.float32),
             jax.ShapeDtypeStruct((tokens // 2, D), jnp.float32),
-            jax.ShapeDtypeStruct((heads, tokens, 3 * HEAD), jnp.bfloat16),
-            jax.ShapeDtypeStruct((heads, tokens, HEAD), jnp.bfloat16),
+            jax.ShapeDtypeStruct((heads // GROUP, tokens, 3 * HEAD * GROUP), jnp.bfloat16),
+            jax.ShapeDtypeStruct((heads // GROUP, tokens, HEAD * GROUP), jnp.bfloat16),
         ],
         grid_spec=pltpu.PrefetchScalarGridSpec(
             num_scalar_prefetch=1,
-            grid=(heads,),
+            grid=(heads // GROUP,),
             in_specs=[whole, qk, vo],
             out_specs=[half, half, qkv, att],
         ),
         compiler_params=pltpu.CompilerParams(
-            dimension_semantics=("arbitrary",), vmem_limit_bytes=40 * 1024 * 1024
+            dimension_semantics=("arbitrary",), vmem_limit_bytes=48 * 1024 * 1024
         ),
-        cost_estimate=pl.CostEstimate(
-            flops=2 * tokens * D * heads * 2 * rows,
-            transcendentals=0,
-            bytes_accessed=16 * 1024 * 1024,
-        ),
+        cost_estimate=pl.CostEstimate(flops=0, transcendentals=0, bytes_accessed=1024 * 1024),
         name="attn_forward",
     )(meta, normed, weights, weights)
 
@@ -489,59 +505,62 @@
     far_x_ref,
     far_y_ref,
     grads_s,
-    mat_s,
+    out_s,
 ):
     step = pl.program_id(0)
     normed = normed_ref[...]
     low = low_ref[...]
-    out_weight = vo_ref[0, 0, HEAD:]
-    grad_attended = dot_nt(low, out_weight)
-    for image in range(2):
-        rows = slice(image * PAD, (image + 1) * PAD)
-        q = qkv_ref[0, rows, :HEAD]
-        k = qkv_ref[0, rows, HEAD : 2 * HEAD]
-        v = qkv_ref[0, rows, 2 * HEAD :]
-        grad = grad_attended[rows].astype(jnp.bfloat16)
-        probs = soft(q, k)
-        grad_v = dot_tn(probs.astype(jnp.bfloat16), grad)
-        grad_probs = dot_nt(grad, v)
-        inner = jnp.sum(probs * grad_probs, axis=-1, keepdims=True)
-        grad_scores = (probs * (grad_probs - inner) * (1.0 / math.sqrt(HEAD))).astype(jnp.bfloat16)
-        grads_s[rows, :HEAD] = dot_nn(grad_scores, k)
-        grads_s[rows, HEAD : 2 * HEAD] = dot_tn(grad_scores, q)
-        grads_s[rows, 2 * HEAD :] = grad_v
-    projected = grads_s[...].astype(jnp.bfloat16)
-    mat_s[: 3 * HEAD] = dot_tn(projected, normed)
-    mat_s[3 * HEAD :] = dot_tn(attended_ref[0], low)
+    weights, out_weight = head_weights(qk_ref, vo_ref)
+    out_s[...] = dot_nt(low, out_weight).astype(jnp.bfloat16)
+    for head in range(GROUP):
+        q_at, k_at, v_at = head_columns(head)
+        for image in range(2):
+            rows = slice(image * PAD, (image + 1) * PAD)
+            q = qkv_ref[0, rows, q_at]
+            k = qkv_ref[0, rows, k_at]
+            v = qkv_ref[0, rows, v_at]
+            grad = out_s[rows, HEAD * head : HEAD * (head + 1)]
+            probs = soft(q, k)
+            grads_s[rows, v_at] = dot_tn(probs.astype(jnp.bfloat16), grad).astype(jnp.bfloat16)
+            grad_probs = dot_nt(grad, v)
+            inner = jnp.sum(probs * grad_probs, axis=-1, keepdims=True)
+            grad_scores = (probs * (grad_probs - inner) * (1.0 / math.sqrt(HEAD))).astype(
+                jnp.bfloat16
+            )
+            grads_s[rows, q_at] = dot_nn(grad_scores, k).astype(jnp.bfloat16)
+            grads_s[rows, k_at] = dot_tn(grad_scores, q).astype(jnp.bfloat16)
+    projected = grads_s[...]
+    accumulate(step, (part_a, part_b), dot_nn(projected, weights))
+    mats = dot_tn(projected, normed)
+    outs = dot_tn(attended_ref[0], low)
     first = meta_ref[0] == 0
-    query_key = mat_s[: 2 * HEAD]
-    value_out = mat_s[2 * HEAD :]
-    own_ref[0] = jnp.where(first, query_key, value_out).astype(jnp.bfloat16)
-    other = jnp.where(first, value_out, query_key).astype(jnp.bfloat16)
-
-    @pl.when(step < 4)
-    def _():
-        near_ref[0] = other
-
-    @pl.when((step >= 4) & (step < 6))
-    def _():
-        far_x_ref[0] = other
-
-    @pl.when(step >= 6)
-    def _():
-        far_y_ref[0] = other
-
-    add = dot_nn(projected[:, : 2 * HEAD], qk_ref[0, 0]) + dot_nn(
-        projected[:, 2 * HEAD :], vo_ref[0, 0, :HEAD]
-    )
-
-    accumulate(step, (part_a, part_b), add)
+    for head in range(GROUP):
+        q_at, k_at, v_at = head_columns(head)
+        query_key = mats[q_at.start : k_at.stop]
+        value_out = jnp.concatenate([mats[v_at], outs[HEAD * head : HEAD * (head + 1)]], axis=0)
+        own_ref[head] = jnp.where(first, query_key, value_out).astype(jnp.bfloat16)
+        other = jnp.where(first, value_out, query_key).astype(jnp.bfloat16)
+
+        @pl.when(step == 0)
+        def _():
+            near_ref[head] = other
+
+        @pl.when(step == 1)
+        def _():
+            if head < 2:
+                far_x_ref[head] = other
+            else:
+                far_y_ref[head - 2] = other
 
 
 def attn_backward(meta, normed, low, weights, qkv_kept, attended):
     heads, rows = weights.shape[1:3]
     tokens = normed.shape[0]
     whole, half, qk, vo, qkv, att = attn_specs(rows, tokens)
+
+    def fixed(size):
+        return pl.BlockSpec((size, rows, D), lambda s, m: (0, 0, 0))
+
     return pl.pallas_call(
         attn_backward_kernel,
         out_shape=[
@@ -554,23 +573,23 @@
         ],
         grid_spec=pltpu.PrefetchScalarGridSpec(
             num_scalar_prefetch=1,
-            grid=(heads,),
+            grid=(heads // GROUP,),
             in_specs=[whole, whole, qk, vo, qkv, att],
             out_specs=[
                 half,
                 half,
-                pl.BlockSpec((1, rows, D), lambda s, m: (s, 0, 0)),
-                pl.BlockSpec((1, rows, D), lambda s, m: (jnp.minimum(s, 3), 0, 0)),
-                pl.BlockSpec((1, rows, D), lambda s, m: (jnp.clip(s - 4, 0, 1), 0, 0)),
-                pl.BlockSpec((1, rows, D), lambda s, m: (jnp.clip(s - 6, 0, 1), 0, 0)),
+                pl.BlockSpec((GROUP, rows, D), lambda s, m: (s, 0, 0)),
+                fixed(4),
+                fixed(2),
+                fixed(2),
             ],
             scratch_shapes=[
-                pltpu.VMEM((tokens, 3 * HEAD), jnp.float32),
-                pltpu.VMEM((2 * rows, D), jnp.float32),
+                pltpu.VMEM((tokens, 3 * HEAD * GROUP), jnp.bfloat16),
+                pltpu.VMEM((tokens, HEAD * GROUP), jnp.bfloat16),
             ],
         ),
         compiler_params=pltpu.CompilerParams(
-            dimension_semantics=("arbitrary",), vmem_limit_bytes=48 * 1024 * 1024
+            dimension_semantics=("arbitrary",), vmem_limit_bytes=56 * 1024 * 1024
         ),
         cost_estimate=pl.CostEstimate(
             flops=4 * tokens * D * heads * 2 * rows,
@@ -579,6 +598,172 @@
         ),
         name="attn_backward",
     )(meta, normed, low, weights, weights, qkv_kept, attended)
+
+
+def by_narrow(blocks, flag_refs):
+    table = [None] * 8
+    for place, distance in enumerate((0, 2, 1, 3)):
+        for j in range(2):
+            table[distance * 2 + j] = blocks[j * 4 + place]
+    for number, flag in enumerate(flag_refs):
+        bit = 1 << number
+        table = [jnp.where(flag == 0, table[i], table[i ^ bit]) for i in range(8)]
+    return table
+
+
+def by_slot(blocks, flag_refs):
+    table = list(blocks)
+    for number, flag in enumerate(flag_refs):
+        bit = 1 << number
+        table = [jnp.where(flag == 0, table[i], table[i ^ bit]) for i in range(8)]
+    return [table[distance * 2 + j] for j in range(2) for distance in (0, 2, 1, 3)]
+
+
+def take_kernel(flags_ref, *refs):
+    blocks, (mine_ref, give_ref, cot_ref) = refs[:4], refs[4:]
+    width = blocks[0].shape[1] // 6
+    rows = blocks[0].shape[0]
+    first = flags_ref[3] == 0
+    for ref in (mine_ref, give_ref, cot_ref):
+        ref[rows - 2 :] = jnp.zeros((ref.shape[0] - rows + 2, ref.shape[1]), ref.dtype)
+    cots = []
+    for j in range(2):
+        for place in range(4):
+            slot = j * 4 + place
+            columns = slice(slot * width, (slot + 1) * width)
+            one, two, three = [
+                blocks[place][:, (3 * j + kind) * width : (3 * j + kind + 1) * width]
+                for kind in range(3)
+            ]
+            mine_ref[:rows, columns] = jnp.where(first, one, two)
+            give_ref[:rows, columns] = jnp.where(first, two, one)
+            cots.append(three)
+    for number, piece in enumerate(by_narrow(cots, [flags_ref[i] for i in range(3)])):
+        cot_ref[:rows, number * width : (number + 1) * width] = piece
+
+
+def take_tokens(flags, blocks):
+    out = jax.ShapeDtypeStruct((PAD, D), jnp.bfloat16)
+    full = pl.BlockSpec(memory_space=pltpu.VMEM)
+    return pl.pallas_call(
+        take_kernel,
+        out_shape=[out] * 3,
+        in_specs=[pl.BlockSpec(memory_space=pltpu.SMEM)] + [full] * 4,
+        out_specs=[full] * 3,
+        compiler_params=pltpu.CompilerParams(vmem_limit_bytes=24 * 1024 * 1024),
+        cost_estimate=pl.CostEstimate(flops=0, transcendentals=0, bytes_accessed=4 * 1024 * 1024),
+        name="take_tokens",
+    )(flags, *blocks)
+
+
+def give_kernel(flags_ref, kept_ref, other_ref, block_ref, near_ref, far_ref):
+    rows = near_ref.shape[1]
+    width = near_ref.shape[2] // 3
+    first = flags_ref[3] == 0
+    parts = [block_ref[:rows, n * width : (n + 1) * width] for n in range(8)]
+    parts = by_slot(parts, [flags_ref[i] for i in range(3)])
+    for slot in range(8):
+        columns = slice(slot * width, (slot + 1) * width)
+        kept = kept_ref[:rows, columns]
+        other = other_ref[:rows, columns]
+        target = (near_ref, far_ref)[slot // 4]
+        target[slot % 4, :, :width] = jnp.where(first, kept, other)
+        target[slot % 4, :, width : 2 * width] = jnp.where(first, other, kept)
+        target[slot % 4, :, 2 * width :] = parts[slot]
+
+
+def give_tokens(flags, kept, other, block):
+    out = jax.ShapeDtypeStruct((4, SEQ, 3 * (D // 8)), jnp.bfloat16)
+    full = pl.BlockSpec(memory_space=pltpu.VMEM)
+    return pl.pallas_call(
+        give_kernel,
+        out_shape=[out] * 2,
+        in_specs=[pl.BlockSpec(memory_space=pltpu.SMEM)] + [full] * 3,
+        out_specs=[full] * 2,
+        compiler_params=pltpu.CompilerParams(vmem_limit_bytes=24 * 1024 * 1024),
+        cost_estimate=pl.CostEstimate(flops=0, transcendentals=0, bytes_accessed=4 * 1024 * 1024),
+        name="give_tokens",
+    )(flags, kept, other, block)
+
+
+def join_kernel(near_ref, far_ref, *out_refs):
+    width = near_ref.shape[2]
+    for place, ref in enumerate(out_refs):
+        ref[:, :width] = near_ref[place]
+        ref[:, width:] = far_ref[place]
+
+
+def join_lanes(near, far):
+    count, rows, width = near.shape
+    full = pl.BlockSpec(memory_space=pltpu.VMEM)
+    return pl.pallas_call(
+        join_kernel,
+        out_shape=[jax.ShapeDtypeStruct((rows, 2 * width), near.dtype)] * count,
+        in_specs=[full] * 2,
+        out_specs=[full] * count,
+        compiler_params=pltpu.CompilerParams(vmem_limit_bytes=24 * 1024 * 1024),
+        cost_estimate=pl.CostEstimate(flops=0, transcendentals=0, bytes_accessed=4 * 1024 * 1024),
+        name="join_lanes",
+    )(near, far)
+def pack_kernel(flags_ref, stream_ref, skip_ref, cot_ref, near_ref, give_ref):
+    rows = near_ref.shape[1]
+    pieces = []
+    for number in range(8):
+        at = slice(number * rows, (number + 1) * rows)
+        piece = jnp.concatenate([stream_ref[:, at], skip_ref[:, at], cot_ref[:, at]], axis=0)
+        pieces.append(piece.T)
+    pieces = by_slot(pieces, [flags_ref[i] for i in range(3)])
+    for place in range(4):
+        near_ref[place] = pieces[place]
+        give_ref[place] = pieces[4 + place]
+
+
+def pack_tokens(flags, stream, skip_in, cotangent):
+    out = jax.ShapeDtypeStruct((4, SEQ, 3 * stream.shape[0]), stream.dtype)
+    full = pl.BlockSpec(memory_space=pltpu.VMEM)
+    return pl.pallas_call(
+        pack_kernel,
+        out_shape=[out] * 2,
+        in_specs=[pl.BlockSpec(memory_space=pltpu.SMEM)] + [full] * 3,
+        out_specs=[full] * 2,
+        compiler_params=pltpu.CompilerParams(vmem_limit_bytes=24 * 1024 * 1024),
+        cost_estimate=pl.CostEstimate(flops=0, transcendentals=0, bytes_accessed=4 * 1024 * 1024),
+        name="pack_tokens",
+    )(flags, stream, skip_in, cotangent)
+
+
+def back_kernel(flags_ref, *refs):
+    blocks, (stream_ref, skip_ref, block_ref) = refs[:4], refs[4:]
+    width = stream_ref.shape[0]
+    rows = blocks[0].shape[0]
+    pieces = [
+        blocks[place][:, 3 * j * width : 3 * (j + 1) * width] for j in range(2) for place in range(4)
+    ]
+    for number, piece in enumerate(by_narrow(pieces, [flags_ref[i] for i in range(3)])):
+        at = slice(number * rows, (number + 1) * rows)
+        turned = piece.T
+        stream_ref[:, at] = turned[:width].astype(jnp.float32)
+        skip_ref[:, at] = turned[width : 2 * width].astype(jnp.float32)
+        block_ref[:, at] = turned[2 * width :]
+
+
+def back_tokens(flags, blocks):
+    rows, width = blocks[0].shape
+    shape = (width // 6, 8 * rows)
+    full = pl.BlockSpec(memory_space=pltpu.VMEM)
+    return pl.pallas_call(
+        back_kernel,
+        out_shape=[
+            jax.ShapeDtypeStruct(shape, jnp.float32),
+            jax.ShapeDtypeStruct(shape, jnp.float32),
+            jax.ShapeDtypeStruct(shape, jnp.bfloat16),
+        ],
+        in_specs=[pl.BlockSpec(memory_space=pltpu.SMEM)] + [full] * 4,
+        out_specs=[full] * 3,
+        compiler_params=pltpu.CompilerParams(vmem_limit_bytes=24 * 1024 * 1024),
+        cost_estimate=pl.CostEstimate(flops=0, transcendentals=0, bytes_accessed=8 * 1024 * 1024),
+        name="back_tokens",
+    )(flags, *blocks)
 
 
 def chips(
@@ -731,9 +916,10 @@
 
     def columns(array):
         size = D // wide_count
-        return lax.dynamic_slice_in_dim(array, wide_index * size, size, array.ndim - 1)
+        return lax.dynamic_slice_in_dim(array, wide_index * size, size, array.ndim - 1).astype(f32)
 
     def statistics(grad, old):
+        grad = grad.astype(f32)
         squares = grad * grad + EPS_SQUARE
         new = DECAY * old + (1.0 - DECAY) * (jnp.sum(squares, axis=1) / D)
         old_sum = jnp.where(lax.broadcasted_iota(jnp.int32, (D,), 0) == 0, jnp.sum(old), 0.0)
@@ -754,11 +940,11 @@
         square_total = jnp.sum(totals[1] / wide_new) * row_mean
         ratio = jnp.sqrt(square_total / (rows_all * D)) / CLIP_LEVEL
         factor = -(STEP_RATE * jnp.sqrt(row_mean) / jnp.maximum(1.0, ratio))
-        step = grad * lax.rsqrt(new)[:, None] * (lax.rsqrt(wide_new) * factor)[None, :]
+        step = grad.astype(f32) * lax.rsqrt(new)[:, None] * (lax.rsqrt(wide_new) * factor)[None, :]
         return wide_new, ratio, step
 
-    mine = jnp.where(is_first, stream, skip_in)
-    given = core(jnp.where(is_first, skip_in, stream))
+    flags = jnp.stack([yi, zi % 2, zi // 2, ci]).astype(jnp.int32)
+    token_near, token_give = pack_tokens(flags, stream.T, skip_in.T, cotangent.T)
     skip_block = pick(pick(skip_weight, ci, 0).reshape(2, feat // 2, D), xi, 0)
     attn_rows = jnp.concatenate(
         [
@@ -767,18 +953,17 @@
         ]
     ).reshape(2, 2 * half_head, D)
     attn_block = pick(attn_rows, xi, 0)
+    skip_block, attn_block, token_give = tie(skip_block, attn_block, token_give)
+    token_far = over_y(token_give)
     skip_two = xor_z(skip_block, 2)
     attn_two = xor_z(attn_block, 2)
-    tokens = jnp.concatenate([mine, given, cotangent], axis=1).reshape(narrow_count, SEQ, 3 * feat)
-    token_near, token_give = split_y(tokens)
-    token_far = over_y(token_give)
-    skip_two, attn_two, token_near = tie(skip_two, attn_two, token_near)
     skip_line = jnp.stack([skip_block, skip_two])
     attn_line = jnp.stack([attn_block, attn_two])
     skip_line = jnp.concatenate([skip_line, xor_z(skip_line, 1)])
     attn_line = jnp.concatenate([attn_line, xor_z(attn_line, 1)])
 
-    token_blocks = z_line(z_pieces(token_near, token_far))
+    token_far, up_weight, down_weight = tie(token_far, up_weight, down_weight)
+    token_blocks = z_line(join_lanes(token_near, token_far))
     skip_beside = over_y(skip_line)
     skip_across = over_x(skip_line)
     ffn_block = jnp.stack(
@@ -793,23 +978,12 @@
     attn_beside = over_y(attn_line)
     attn_across = over_x(attn_line)
 
-    *token_blocks, skip_corner, ffn_block = tie(*token_blocks, skip_corner, ffn_block)
     ffn_full = lax.all_gather(ffn_block[None], "narrow", tiled=True)
-    parts = [
-        [
-            block[:, (3 * j + kind) * feat : (3 * j + kind + 1) * feat]
-            for j in range(2)
-            for block in token_blocks
-        ]
-        for kind in range(3)
-    ]
-    flat = jnp.concatenate(
-        [padded(jnp.concatenate(parts[kind], axis=1)) for kind in range(2)]
-    )
-    flat, attn_beside, attn_across = tie(flat, attn_beside, attn_across)
+    mine, give, cot_pad = take_tokens(flags, token_blocks)
+    flat = jnp.concatenate([mine, core(give)])
+    cot_own = cot_pad[:SEQ]
     attn_corner_x = over_x(attn_beside[:half])
     attn_corner_y = over_y(attn_across[half:])
-    cot_own = jnp.concatenate(canonical(parts[2]), axis=1)
     skip_near = jnp.concatenate([skip_line, skip_beside])
     skip_away = jnp.concatenate([skip_across, skip_corner])
     skip_mat = jnp.where(
@@ -831,9 +1005,8 @@
     normed = both_images((unit_one * norm_gain[0] + norm_bias[0]).astype(bf16))
 
     attn_corner = jnp.concatenate([attn_corner_x, attn_corner_y])
-    normed, cot_own, attn_corner = tie(normed, cot_own, attn_corner)
-    cot_pair = padded(cot_own)
-    cot_pair = jnp.concatenate([cot_pair, over_x(cot_pair)])
+    normed, cot_pad, attn_corner = tie(normed, cot_pad, attn_corner)
+    cot_pair = jnp.concatenate([cot_pad, over_x(cot_pad)])
     attn_full = jnp.stack(
         [
             jnp.concatenate([attn_line, attn_beside]),
@@ -854,12 +1027,10 @@
     )
     mixed_sum = mixed_a + core(mixed_b)
     mixed_far = over_x(mixed_sum[PAD:].astype(bf16))
-    ffn_far_down = over_y(down_give)
-
-    mixed_far, ffn_far_down, down_b, up_give = tie(mixed_far, ffn_far_down, down_b, up_give)
     ffn_far_up = over_y(up_give)
-    ffn_down, ffn_down_give = halves_z(add_low(down_near, ffn_far_down))
-    ffn_down_one = xor_z(ffn_down_give, 1)
+    ffn_down_one = xor_z(down_give, 1)
+
+    mixed_far, down_b = tie(mixed_far, down_b)
     down_sum = down_a + core(down_b)
     down_far = over_x(down_sum[PAD:].astype(bf16))
     back_middle, gain_two, bias_two = norm_back_own(
@@ -879,41 +1050,28 @@
     )
     attn_from_x = over_x(other_x)
     attn_from_y = over_y(other_y)
+    ffn_down = add_low(down_near, ffn_down_one)
+    ffn_down_two = xor_z(ffn_down[:, 1], 2)
     ffn_up, ffn_up_give = halves_z(add_low(up_near, ffn_far_up))
     ffn_up_one = xor_z(ffn_up_give, 1)
-    ffn_down = add_low(ffn_down, ffn_down_one)
-    ffn_down_two = xor_z(ffn_down[1], 2)
     block_own = (middle + (down_sum[:PAD] + down_far.astype(f32))[:SEQ]).astype(bf16)
     back_hidden, gain_one, bias_one = norm_back_own(
         unit_one, inverse_one, core_sum(normed_a, normed_b), norm_gain[0]
     )
     hidden_low = both_images((grad_middle + back_hidden).astype(bf16))
-
+    token_grad = matmul(hidden_low, skip_mat, "rd,cd->rc").astype(bf16)
+    back_near, back_give = give_tokens(
+        flags, token_grad[:PAD], core(token_grad[PAD:]), padded(block_own)
+    )
     grad_skip = matmul(flat, hidden_low, "rc,rd->cd").astype(bf16)
     grad_skip = grad_skip.reshape(narrow_count, 2, feat // 2, D)
     skip_own, skip_other = pick(grad_skip, xi, 1), pick(grad_skip, 1 - xi, 1)
+
+    attn_from_x, attn_from_y, back_give, skip_other = tie(
+        attn_from_x, attn_from_y, back_give, skip_other
+    )
     skip_from_x = over_x(skip_other[ZS : ZS + half])
     skip_from_y = over_y(skip_other[ZS + half :])
-    token_grad = matmul(hidden_low, skip_mat, "rd,cd->rc").astype(bf16)
-    block_pieces = jnp.stack(jnp.split(block_own, narrow_count, axis=1))
-
-    def back_piece(slot):
-        columns_of = slice(slot * feat, (slot + 1) * feat)
-        return jnp.concatenate(
-            [
-                token_grad[:SEQ, columns_of],
-                token_grad[PAD : PAD + SEQ, columns_of],
-                pick(block_pieces, order[slot], 0),
-            ],
-            axis=1,
-        )
-
-    back_near = [back_piece(slot) for slot in range(ZS)]
-    back_give = jnp.stack([back_piece(slot) for slot in range(ZS, narrow_count)])
-
-    attn_from_x, attn_from_y, back_give, ffn_up_one, ffn_down_two = tie(
-        attn_from_x, attn_from_y, back_give, ffn_up_one, ffn_down_two
-    )
     back_far = over_y(back_give)
     attn_across = over_x(
         jnp.concatenate([other_near[:half], add_low(other_near[half:], attn_from_y)])
@@ -921,93 +1079,92 @@
     attn_beside = over_y(
         jnp.concatenate([add_low(own[ZS : ZS + half], attn_from_x), own[ZS + half :]])
     )
+
+    skip_from_x, skip_from_y, ffn_down_two, ffn_up_one = tie(
+        skip_from_x, skip_from_y, ffn_down_two, ffn_up_one
+    )
     ffn_up = add_low(ffn_up, ffn_up_one)
     ffn_up_two = xor_z(ffn_up[1], 2)
-
-    skip_from_x, skip_from_y, back_far = tie(skip_from_x, skip_from_y, back_far)
-    skip_near_sum = add_low(skip_own[ZS : ZS + half], skip_from_x)
-    skip_far_sum = add_low(skip_other[half:ZS], skip_from_y)
-    back_pieces = [
-        jnp.concatenate([back_near[place], back_far[place]], axis=1) for place in range(ZS)
-    ]
-    back_blocks = z_line(back_pieces)
-
-    attn_beside, attn_across, ffn_up_two = tie(attn_beside, attn_across, ffn_up_two)
+    ffn_down = add_low(ffn_down[:, 0], ffn_down_two)
+    ffn_down_far = over_y(ffn_down[1])
+    skip_across = over_x(
+        jnp.concatenate([skip_other[:half], add_low(skip_other[half:ZS], skip_from_y)])
+    )
+    skip_beside = over_y(
+        jnp.concatenate([add_low(skip_own[ZS : ZS + half], skip_from_x), skip_own[ZS + half :]])
+    )
+    back_blocks = z_line(join_lanes(back_near, back_far))
+
+    attn_beside, attn_across, ffn_up_two, ffn_down_far = tie(
+        attn_beside, attn_across, ffn_up_two, ffn_down_far
+    )
     attn_total, attn_give = halves_z(
         (own[:ZS].astype(f32) + attn_beside.astype(f32) + attn_across.astype(f32)).astype(bf16)
     )
     attn_one = xor_z(attn_give, 1)
-    skip_across = over_x(jnp.concatenate([skip_other[:half], skip_far_sum]))
-    skip_beside = over_y(jnp.concatenate([skip_near_sum, skip_own[ZS + half :]]))
-    ffn_own = jnp.stack([add_low(ffn_up[0], ffn_up_two), add_low(ffn_down[0], ffn_down_two)])
+    ffn_own = jnp.stack([add_low(ffn_up[0], ffn_up_two), add_low(ffn_down[0], ffn_down_far)])
     ffn_x = over_x(ffn_own)
 
     attn_one, ffn_x = tie(attn_one, ffn_x)
     attn_total = add_low(attn_total, attn_one)
     attn_two = xor_z(attn_total[1], 2)
     ffn_pair = jnp.stack([ffn_own, ffn_x])
-    ffn_core = core(ffn_pair)
-
-    ffn_all = in_order(ffn_pair, ffn_core).astype(f32)
+    (ffn_all,) = tie(in_order(ffn_pair, core(ffn_pair)))
     grad_up_rows = ffn_all[:, 0].reshape(hidden, D)
     grad_down = ffn_all[:, 1].reshape(hidden, D)
     new_col_up, up_sums = statistics(grad_up_rows, col_up)
     new_row_down, down_sums = statistics(grad_down, row_down)
-    ffn_totals = all_narrow(jnp.stack(up_sums + down_sums))
-
-    skip_beside, skip_across, ffn_totals, *back_blocks = tie(
-        skip_beside, skip_across, ffn_totals, *back_blocks
-    )
-    new_row_up, ratio_up, step_up = step_of(
-        grad_up_rows, new_col_up, ffn_totals[:3], row_up, hidden * narrow_count, True
-    )
-    new_col_down, ratio_down, step_down = step_of(
-        grad_down, new_row_down, ffn_totals[3:], col_down, hidden * narrow_count, False
-    )
-    new_up = up_weight.astype(f32) + step_up.T
-    new_down = down_weight.astype(f32) + step_down
-    grad_up_out = columns(grad_up_rows).T
-    grad_down_out = columns(grad_down)
+
+    skip_beside, skip_across, *ffn_sums = tie(skip_beside, skip_across, *up_sums, *down_sums)
     skip_total, skip_give = halves_z(
         (skip_own[:ZS].astype(f32) + skip_beside.astype(f32) + skip_across.astype(f32)).astype(
             bf16
         )
     )
     skip_one = xor_z(skip_give, 1)
-    back = [block[:, j * 3 * feat : (j + 1) * 3 * feat] for j in range(2) for block in back_blocks]
-    back = jnp.concatenate(canonical(back), axis=0)
-    grad_mine = back[:, :feat]
-    grad_given = core(back[:, feat : 2 * feat])
-    block_out = back[:, 2 * feat :]
-
-    attn_two, skip_one, grad_given, block_out, new_up, new_down, grad_up_out, grad_down_out = tie(
-        attn_two, skip_one, grad_given, block_out, new_up, new_down, grad_up_out, grad_down_out
-    )
+
+    attn_two, skip_one, *back_blocks = tie(attn_two, skip_one, *back_blocks)
     attn_own = add_low(attn_total[0], attn_two)
+    attn_x = over_x(attn_own)
     skip_total = add_low(skip_total, skip_one)
     skip_two = xor_z(skip_total[1], 2)
-    grad_stream = jnp.where(is_first, grad_mine, grad_given).astype(f32)
-    grad_skip_in = jnp.where(is_first, grad_given, grad_mine).astype(f32)
-
-    grad_stream, grad_skip_in, skip_two = tie(grad_stream, grad_skip_in, skip_two)
-    last_own = jnp.concatenate([attn_own, add_low(skip_total[0], skip_two)])
-    last_pair = jnp.stack([last_own, over_x(last_own)])
-    last_all = in_order(last_pair, core(last_pair)).astype(f32)
-    attn_rows_all = 2 * half_head
-    attn_all = last_all[:, :attn_rows_all].reshape(2, 4, half_head, D)
-    grad_skip_rows = last_all[:, attn_rows_all:].reshape(2 * feat, D)
+    grad_stream, grad_skip_in, block_out = [
+        part.T for part in back_tokens(flags, back_blocks)
+    ]
+    attn_pair = jnp.stack([attn_own, attn_x])
+    (attn_all,) = tie(in_order(attn_pair, core(attn_pair)))
+    attn_all = attn_all.reshape(2, 4, half_head, D)
     grad_qkv_rows = attn_all[:, :3].transpose(1, 0, 2, 3).reshape(3 * feat, D)
     grad_out = attn_all[:, 3].reshape(feat, D)
+    new_col_qkv, qkv_sums = statistics(grad_qkv_rows, col_qkv.reshape(-1))
+    new_row_out, out_sums = statistics(grad_out, row_out)
+    grad_up_out = columns(grad_up_rows).T
+    grad_down_out = columns(grad_down)
+
+    grad_stream, grad_skip_in, block_out, grad_up_out, grad_down_out, skip_two, *sums = tie(
+        grad_stream,
+        grad_skip_in,
+        block_out,
+        grad_up_out,
+        grad_down_out,
+        skip_two,
+        *qkv_sums,
+        *out_sums,
+    )
+    skip_last = add_low(skip_total[0], skip_two)
+    skip_pair = jnp.stack([skip_last, over_x(skip_last)])
+    (skip_all,) = tie(in_order(skip_pair, core(skip_pair)))
+    grad_skip_rows = skip_all.reshape(2 * feat, D)
 
     norm_sums = jnp.stack([gain_one, gain_two, bias_one, bias_two])
     norm_sums = norm_sums + core(norm_sums)
     norm_sums = norm_sums + over_x(norm_sums)
     new_row_skip, skip_sums = statistics(grad_skip_rows, row_skip.reshape(-1))
-    new_col_qkv, qkv_sums = statistics(grad_qkv_rows, col_qkv.reshape(-1))
-    new_row_out, out_sums = statistics(grad_out, row_out)
-    totals = all_narrow(jnp.concatenate([jnp.stack(skip_sums + qkv_sums + out_sums), norm_sums]))
-    gain_total = totals[9:11]
-    bias_total = totals[11:13]
+    totals = all_narrow(
+        jnp.concatenate([jnp.stack(skip_sums + sums + list(ffn_sums)), norm_sums])
+    )
+    gain_total = totals[15:17]
+    bias_total = totals[17:19]
     new_col_skip, ratio_skip, step_skip = step_of(
         grad_skip_rows, new_row_skip, totals[:3], col_skip, 2 * D, False
     )
@@ -1017,6 +1174,14 @@
     new_col_out, ratio_out, step_out = step_of(
         grad_out, new_row_out, totals[6:9], col_out, D, False
     )
+    new_row_up, ratio_up, step_up = step_of(
+        grad_up_rows, new_col_up, totals[9:12], row_up, hidden * narrow_count, True
+    )
+    new_col_down, ratio_down, step_down = step_of(
+        grad_down, new_row_down, totals[12:15], col_down, hidden * narrow_count, False
+    )
+    new_up = up_weight.astype(f32) + step_up.T
+    new_down = down_weight.astype(f32) + step_down
     clip_ratio = jnp.stack([ratio_skip, ratio_qkv, ratio_out, ratio_up, ratio_down])
     new_skip = skip_weight.astype(f32) + step_skip.reshape(2, feat, D)
     new_qkv = qkv_weight.astype(f32) + step_qkv.reshape(3, feat, D).transpose(2, 0, 1)

time: 627 us -> 553 us (0.88)
  local copies, waits for them, and re-layouts: 95.1 us -> 35.5 us
  other arithmetic: 100 us -> 86.1 us
  starting transfers between devices: 58.4 us -> 68.9 us
    ppermute x66 -> x65, waiting for transfers between devices: 227 us -> 212 us  [send(): return lax.ppermute(value, axes, perm(move))]
    concatenate x6 -> x2, local copies, waits for them, and re-layouts: 14.2 us -> 0.34 us  [the longest x1 0.26 us: chips(): jnp.concatenate([jnp.stack(skip_sums + sums + list(ffn_sums)), norm_sums])]
    pallas_call x1 -> x7, Pallas kernels: 38.4 us -> 50.8 us  [the longest x1 38.3 us: ffn(): pl.pallas_call(ffn_kernel, out_shape=[part] * 4 + [grad] * 2 + [turn] * 2...]
    slice x9 -> x4, local copies, waits for them, and re-layouts: 12.5 us -> 0.24 us  [the longest x1 0.1 us: chips(): token_grad[PAD:]]
    ppermute x66 -> x65, starting transfers between devices: 58.3 us -> 68.9 us  [send(): return lax.ppermute(value, axes, perm(move))]
    select_n x7 -> x0, other arithmetic: 9.92 us -> none  [the longest x6 7.62 us: exchange(): jnp.where(flag == 0, table[index], table[index ^ bit])]
    all_gather x1, waiting for transfers between devices: 4.32 us -> 14.1 us  [chips(): ffn_full = lax.all_gather(ffn_block[None], 'narrow', tiled=True)]
    concatenate x14 -> x3, other arithmetic: 11.5 us -> 3.05 us  [the longest x1 1.23 us: chips(): cot_pair = jnp.concatenate([cot_pad, over_x(cot_pad)])]
  transfers between devices with their start and end apart: 67 -> 66, of which waited for: 33 -> 28; matrix products, arithmetic and copies ran while one was open for 26% -> 17% of each run, Pallas kernels for 9% -> 10%
where the time goes in v4:
time: 553 us; the launch traced here: 546 us
  waiting for transfers between devices  226 us (41%)
  Pallas kernels  96.6 us (17%)
  other arithmetic  86.1 us (16%)
  starting transfers between devices  68.9 us (12%)
  local copies, waits for them, and re-layouts  35.5 us (6%)
  between operations  26.8 us (5%)
  matrix products  6.37 us (1%)
    ppermute x65, waiting for transfers between devices, send(): return lax.ppermute(value, axes, perm(move))  212 us
    ppermute x65, starting transfers between devices, send(): return lax.ppermute(value, axes, perm(move))  68.9 us
    pallas_call x1, Pallas kernels, ffn(): pl.pallas_call(ffn_kernel, out_shape=[part] * 4 + [grad] * 2 + [turn] * 2...  38.3 us
    pallas_call x1, Pallas kernels, attn_backward(): pl.pallas_call(attn_backward_kernel, out_shape=[jax.ShapeDtypeStruct((tok...  31.1 us
    pallas_call x1, Pallas kernels, attn_forward(): pl.pallas_call(attn_forward_kernel, out_shape=[jax.ShapeDtypeStruct((toke...  14.7 us
    all_gather x1, waiting for transfers between devices, chips(): ffn_full = lax.all_gather(ffn_block[None], 'narrow', tiled=True)  14.1 us
  transfers between devices with their start and end apart: 66, of which 28 were waited for; matrix products, arithmetic and copies ran while one was open for 17% of the time, Pallas kernels for 10%

profile of v4, /device:TPU:0, one launch (start us, length us, event | category | flops | bytes accessed | tf_op | source)
XLA Modules:
  0.0 546.2 jit_solution(9974770187941960446)
XLA Ops:
  10.2 2.2 pack_tokens.1
  12.4 4.1 collective-permute-start.5
  16.6 15.6 %collective-permute-done.5 = bf16[72,1152]{1,0:T(8,128)(2,1)S(1)} collective-permute-done((bf16[72,1152]{1,0:T(8,128)(2,1)S(1)}, bf16[72,1152]{1,0:T(8,128)(2,1)S(1)}, u32[]{:S(2)}, u32[]{:S(2)}) %collective-permute-start.5) | collective-permute-done | bytes 165920 | tf_op jit(solution)/shard_map/ppermute | solution.py:821
  33.9 1.9 collective-permute-start
  35.8 2.9 collective-permute-done.9
  40.3 5.5 %collective-permute-done.6 = bf16[2,72,1152]{2,1,0:T(8,128)(2,1)S(1)} collective-permute-done((bf16[2,72,1152]{2,1,0:T(8,128)(2,1)S(1)}, bf16[2,72,1152]{2,1,0:T(8,128)(2,1)S(1)}, u32[]{:S(2)}, u32[]{:S(2)}) %collective-permute-start.6) | collective-permute-done | bytes 331808 | tf_op jit(solution)/shard_map/ppermute | solution.py:821
  49.7 10.7 %collective-permute-done = bf16[4,258,432]{2,0,1:T(4,128)(2,1)} collective-permute-done((bf16[4,258,432]{2,0,1:T(4,128)(2,1)}, bf16[4,258,432]{2,0,1:T(4,128)(2,1)}, u32[]{:S(2)}, u32[]{:S(2)}) %collective-permute-start) | collective-permute-done | bytes 891680 | tf_op jit(solution)/shard_map/ppermute | solution.py:821
  62.3 3.4 collective-permute-start.1
  68.5 4.8 collective-permute-done.7
  75.9 1.6 collective-permute-start.12
  78.7 10.0 %collective-permute-done.1.refs_1_ = bf16[258,864]{1,0:T(8,128)(2,1)S(1)} collective-permute-done((bf16[258,864]{1,0:T(8,128)(2,1)S(1)}, bf16[258,864]{1,0:T(8,128)(2,1)S(1)}, u32[]{:S(2)}, u32[]{:S(2)}) %collective-permute-start.1) | collective-permute-done | bytes 445856 | tf_op jit(solution)/shard_map/ppermute | solution.py:821
  88.7 7.3 %collective-permute-start.15 = (bf16[4,144,1152]{2,1,0:T(8,128)(2,1)S(1)}, bf16[4,144,1152]{2,1,0:T(8,128)(2,1)}, u32[]{:S(2)}, u32[]{:S(2)}) collective-permute-start(bf16[4,144,1152]{2,1,0:T(8,128)(2,1)S(1)} %pad_maximum_fusion.4), channel_id=1, source_target_pairs={{0,1},{1,0},{2,3},{3,2},{4,5},{5,4},{6,7},{7,6},{8,9},{9,8},{10,11... | collective-permute-start | bytes 3981320 | tf_op jit(solution)/shard_map/ppermute | solution.py:821
  97.5 2.6 take_tokens.1
  102.4 1.9 fusion.83
  108.7 11.0 %collective-permute-done.15 = bf16[4,144,1152]{2,1,0:T(8,128)(2,1)} collective-permute-done((bf16[4,144,1152]{2,1,0:T(8,128)(2,1)S(1)}, bf16[4,144,1152]{2,1,0:T(8,128)(2,1)}, u32[]{:S(2)}, u32[]{:S(2)}) %collective-permute-start.15) | collective-permute-done | bytes 1327136 | tf_op jit(solution)/shard_map/ppermute | solution.py:821
  120.9 2.9 collective-permute-start.16
  126.6 1.6 fusion.77
  128.9 1.6 maximum_bitcast_fusion
  130.5 5.7 %collective-permute-done.16 = bf16[2,144,1152]{2,1,0:T(8,128)(2,1)S(1)} collective-permute-done((bf16[2,144,1152]{2,1,0:T(8,128)(2,1)S(1)}, bf16[2,144,1152]{2,1,0:T(8,128)(2,1)S(1)}, u32[]{:S(2)}, u32[]{:S(2)}) %collective-permute-start.16) | collective-permute-done | bytes 663584 | tf_op jit(solution)/shard_map/ppermute | solution.py:821
  136.3 4.5 collective-permute-done.18
  141.1 1.8 collective-permute-start.19
  142.9 1.6 maximum_bitcast_fusion.1
  144.4 2.9 pad_maximum_fusion.qk_ref.vo_ref
  147.3 14.7 %attn_forward.1 = (f32[272,1152]{1,0:T(8,128)S(1)}, f32[272,1152]{1,0:T(8,128)S(1)}, bf16[2,544,864]{2,1,0:T(8,128)(2,1)}, bf16[2,544,288]{2,1,0:T(8,128)(2,1)S(1)}) custom-call(s32[1]{0:T(128)} %bitcast.4.meta_ref, bf16[544,1152]{1,0:T(8,128)(2,1)S(1)} %pad_maximum_fusion.10.normed_ref, bf16[2,8,144,1152]{3,2,1,0:T(8,128)(2,1)} %pad_maximum_fusion.qk_ref.vo_ref, ...), custom_call_target="tpu_custom_call" | custom-call | bytes 1048576 | tf_op jit(solution)/shard_map/attn_forward/pallas_call | solution.py:471
  163.3 3.0 collective-permute-done.20
  167.7 15.8 %collective-permute-done.21 = bf16[272,1152]{1,0:T(8,128)(2,1)S(1)} collective-permute-done((bf16[272,1152]{1,0:T(8,128)(2,1)S(1)}, bf16[272,1152]{1,0:T(8,128)(2,1)S(1)}, u32[]{:S(2)}, u32[]{:S(2)}) %collective-permute-start.21) | collective-permute-done | bytes 626720 | tf_op jit(solution)/shard_map/ppermute | solution.py:821
  185.2 3.4 pad_maximum_fusion.3.cot_ref
  188.6 3.0 pad_maximum_fusion.2.mixed_ref
  191.6 14.1 %all-gather.3.cloned.1.call-done = bf16[16,144,1152]{2,1,0:T(8,128)(2,1)} async-done(((bf16[2,144,1152]{2,1,0:T(8,128)(2,1)}), bf16[16,144,1152]{2,1,0:T(8,128)(2,1)}) %all-gather.3.cloned.1.call-update) | async-done | bytes 5308432 | tf_op jit(solution)/shard_map/all_gather | solution.py:981
  205.7 38.3 %ffn.1 = (f32[544,1152]{1,0:T(8,128)}, f32[544,1152]{1,0:T(8,128)}, f32[544,1152]{1,0:T(8,128)}, f32[544,1152]{1,0:T(8,128)}, bf16[4,144,1152]{2,1,0:T(8,128)(2,...) custom-call(s32[8]{0:T(128)} %stack.275.order_ref, ...), custom_call_target="tpu_custom_call" | custom-call | flops 17326669824 | bytes 33554432 | tf_op jit(solution)/shard_map/ffn/pallas_call | solution.py:395
  244.1 4.9 collective-permute-done.24
  249.0 2.3 add.446
  252.9 14.7 %collective-permute-done.25 = bf16[272,1152]{1,0:T(8,128)(2,1)S(1)} collective-permute-done((bf16[272,1152]{1,0:T(8,128)(2,1)S(1)}, bf16[272,1152]{1,0:T(8,128)(2,1)S(1)}, u32[]{:S(2)}, u32[]{:S(2)}) %collective-permute-start.25) | collective-permute-done | bytes 626720 | tf_op jit(solution)/shard_map/ppermute | solution.py:821
  270.6 1.8 collective-permute-done.31
  275.4 31.1 %attn_backward.1 = (f32[272,1152]{1,0:T(8,128)}, f32[272,1152]{1,0:T(8,128)}, bf16[8,144,1152]{2,1,0:T(8,128)(2,1)}, bf16[4,144,1152]{2,1,0:T(8,128)(2,1)}, bf16...) custom-call(s32[1]{0:T(128)} %bitcast.4.meta_ref, bf16[544,1152]{1,0:T(8,128)(2,1)} %copy-done.2, ...), custom_call_target="tpu_custom_call" | custom-call | flops 5775556608 | bytes 25165824 | tf_op jit(solution)/shard_map/attn_backward/pallas_call | solution.py:564
  312.8 1.7 add_convert_fusion.2
  315.9 2.0 multiply_reduce_fusion.5
  319.2 1.8 add_convert_fusion.1
  321.0 1.6 collective-permute-start.40
  322.6 2.0 convolution_convert_fusion.1
  325.9 2.4 convolution_convert_fusion
  328.8 2.2 give_tokens.1
  336.1 3.2 collective-permute-done.41
  340.7 12.2 %collective-permute-done.40 = bf16[2,144,1152]{2,1,0:T(8,128)(2,1)S(1)} collective-permute-done((bf16[2,144,1152]{2,1,0:T(8,128)(2,1)S(1)}, bf16[2,144,1152]{2,1,0:T(8,128)(2,1)S(1)}, u32[]{:S(2)}, u32[]{:S(2)}) %collective-permute-start.40) | collective-permute-done | bytes 663584 | tf_op jit(solution)/shard_map/ppermute | solution.py:821
  355.6 21.4 %collective-permute-done.43 = bf16[144,1152]{1,0:T(8,128)(2,1)S(1)} collective-permute-done((bf16[144,1152]{1,0:T(8,128)(2,1)S(1)}, bf16[144,1152]{1,0:T(8,128)(2,1)S(1)}, u32[]{:S(2)}, u32[]{:S(2)}) %collective-permute-start.43) | collective-permute-done | bytes 331808 | tf_op jit(solution)/shard_map/ppermute | solution.py:821
  383.5 13.2 %collective-permute-done.45 = bf16[2,144,1152]{2,1,0:T(8,128)(2,1)S(1)} collective-permute-done((bf16[2,144,1152]{2,1,0:T(8,128)(2,1)S(1)}, bf16[2,144,1152]{2,1,0:T(8,128)(2,1)S(1)}, u32[]{:S(2)}, u32[]{:S(2)}) %collective-permute-start.45) | collective-permute-done | bytes 663584 | tf_op jit(solution)/shard_map/ppermute | solution.py:821
  398.5 2.3 collective-permute-done.51
  409.7 3.6 multiply_reduce_fusion
  417.8 2.3 multiply_reduce_fusion.1
  420.1 2.1 collective-permute-start.54
  422.5 1.7 fusion.8
  424.2 2.1 collective-permute-start.50
  427.0 11.9 %collective-permute-done.52.refs_1_ = bf16[258,864]{1,0:T(8,128)(2,1)S(1)} collective-permute-done((bf16[258,864]{1,0:T(8,128)(2,1)S(1)}, bf16[258,864]{1,0:T(8,128)(2,1)S(1)}, u32[]{:S(2)}, u32[]{:S(2)}) %collective-permute-start.52) | collective-permute-done | bytes 445856 | tf_op jit(solution)/shard_map/ppermute | solution.py:821
  440.2 17.4 %collective-permute-done.46 = bf16[144,1152]{1,0:T(8,128)(2,1)S(1)} collective-permute-done((bf16[144,1152]{1,0:T(8,128)(2,1)S(1)}, bf16[144,1152]{1,0:T(8,128)(2,1)S(1)}, u32[]{:S(2)}, u32[]{:S(2)}) %collective-permute-start.46) | collective-permute-done | bytes 331808 | tf_op jit(solution)/shard_map/ppermute | solution.py:821
  460.7 6.5 %collective-permute-done.56 = bf16[144,1152]{1,0:T(8,128)(2,1)S(1)} collective-permute-done((bf16[144,1152]{1,0:T(8,128)(2,1)S(1)}, bf16[144,1152]{1,0:T(8,128)(2,1)S(1)}, u32[]{:S(2)}, u32[]{:S(2)}) %collective-permute-start.56) | collective-permute-done | bytes 331808 | tf_op jit(solution)/shard_map/ppermute | solution.py:821
  467.6 4.8 back_tokens.1
  479.5 5.3 collective-permute-done.58
  492.7 3.1 copy.92
  498.2 1.7 collective-permute-start.63
  503.4 2.7 collective-permute-start.64
  507.1 4.0 collective-permute-done.64
  527.9 3.5 multiply_add_fusion
  531.4 2.0 bitcast_add_fusion
  535.2 1.6 bitcast_add_fusion.1
  (449 shorter events, 122.1 us)
Async XLA Ops:
  7.2 198.5 %all-gather.3.cloned.1.call-start = ((), (), s32[]{:S(2)}) async-start(), calls=%async_computation | async-start | bytes 5971968 | tf_op jit(solution)/shard_map/all_gather | solution.py:981
  12.4 19.8 %collective-permute-start.5 = (bf16[72,1152]{1,0:T(8,128)(2,1)S(1)}, bf16[72,1152]{1,0:T(8,128)(2,1)S(1)}, u32[]{:S(2)}, u32[]{:S(2)}) collective-permute-start(bf16[72,1152]{1,0:T(8,128)(2,1)S(1)} %dynamic-slice_bitcast_fusion.7), channel_id=1, source_target_pairs={{0,4},{1,5},{2,6},{3,7},{4,0},{5,1},{6,2},{7,3},{8,12},{9,13},{10,... | collective-permute-start | bytes 497672 | tf_op jit(solution)/shard_map/ppermute | solution.py:821
  16.5 22.1 %collective-permute-start.9 = (bf16[144,1152]{1,0:T(8,128)(2,1)S(1)}, bf16[144,1152]{1,0:T(8,128)(2,1)S(1)}, u32[]{:S(2)}, u32[]{:S(2)}) collective-permute-start(bf16[144,1152]{1,0:T(8,128)(2,1)S(1)} %copy-done.21), channel_id=1, source_target_pairs={{0,4},{1,5},{2,6},{3,7},{4,0},{5,1},{6,2},{7,3},{8,12},{9,13},{10,... | collective-permute-start | bytes 995336 | tf_op jit(solution)/shard_map/ppermute | solution.py:821
  32.3 13.4 %collective-permute-start.6 = (bf16[2,72,1152]{2,1,0:T(8,128)(2,1)S(1)}, bf16[2,72,1152]{2,1,0:T(8,128)(2,1)S(1)}, u32[]{:S(2)}, u32[]{:S(2)}) collective-permute-start(bf16[2,72,1152]{2,1,0:T(8,128)(2,1)S(1)} %pad_maximum_fusion.26), channel_id=1, source_target_pairs={{0,2},{1,3},{2,0},{3,1},{4,6},{5,7},{6,4},{7,5},{8,10},{9,11},{10,... | collective-permute-start | bytes 995336 | tf_op jit(solution)/shard_map/ppermute | solution.py:821
  33.9 26.6 %collective-permute-start = (bf16[4,258,432]{2,0,1:T(4,128)(2,1)}, bf16[4,258,432]{2,0,1:T(4,128)(2,1)}, u32[]{:S(2)}, u32[]{:S(2)}) collective-permute-start(bf16[4,258,432]{2,0,1:T(4,128)(2,1)} %copy.80), channel_id=1, source_target_pairs={{0,1},{1,0},{2,3},{3,2},{4,5},{5,4},{6,7},{7,6},{8,9},{9,8},{10,11... | collective-permute-start | bytes 2674952 | tf_op jit(solution)/shard_map/ppermute | solution.py:821
  39.6 26.1 %collective-permute-start.10 = (bf16[2,144,1152]{2,1,0:T(8,128)(2,1)}, bf16[2,144,1152]{2,1,0:T(8,128)(2,1)}, u32[]{:S(2)}, u32[]{:S(2)}) collective-permute-start(bf16[2,144,1152]{2,1,0:T(8,128)(2,1)} %pad_maximum_fusion.19), channel_id=1, source_target_pairs={{0,2},{1,3},{2,0},{3,1},{4,6},{5,7},{6,4},{7,5},{8,10},{9,11},{10,... | collective-permute-start | bytes 1990664 | tf_op jit(solution)/shard_map/ppermute | solution.py:821
  46.7 26.6 %collective-permute-start.7 = (bf16[4,72,1152]{2,1,0:T(8,128)(2,1)}, bf16[4,72,1152]{2,1,0:T(8,128)(2,1)}, u32[]{:S(2)}, u32[]{:S(2)}) collective-permute-start(bf16[4,72,1152]{2,1,0:T(8,128)(2,1)} %pad_maximum_fusion.18), channel_id=1, source_target_pairs={{0,1},{1,0},{2,3},{3,2},{4,5},{5,4},{6,7},{7,6},{8,9},{9,8},{10,11... | collective-permute-start | bytes 1990664 | tf_op jit(solution)/shard_map/ppermute | solution.py:821
  48.2 25.1 %collective-permute-start.8 = (bf16[4,72,1152]{2,1,0:T(8,128)(2,1)}, bf16[4,72,1152]{2,1,0:T(8,128)(2,1)S(1)}, u32[]{:S(2)}, u32[]{:S(2)}) collective-permute-start(bf16[4,72,1152]{2,1,0:T(8,128)(2,1)} %pad_maximum_fusion.18), channel_id=1, source_target_pairs={{0,16},{1,17},{2,18},{3,19},{4,20},{5,21},{6,22},{7,23},{8,24},{9,... | collective-permute-start | bytes 1990664 | tf_op jit(solution)/shard_map/ppermute | solution.py:821
  62.3 26.4 %collective-permute-start.1 = (bf16[258,864]{1,0:T(8,128)(2,1)S(1)}, bf16[258,864]{1,0:T(8,128)(2,1)S(1)}, u32[]{:S(2)}, u32[]{:S(2)}) collective-permute-start(bf16[258,864]{1,0:T(8,128)(2,1)S(1)} %get-tuple-element.132), channel_id=1, source_target_pairs={{0,4},{1,5},{2,6},{3,7},{4,0},{5,1},{6,2},{7,3},{8,12},{9,13},{10,... | collective-permute-start | bytes 1337480 | tf_op jit(solution)/shard_map/ppermute | solution.py:821
  65.7 30.4 %collective-permute-start.2 = (bf16[258,864]{1,0:T(8,128)(2,1)S(1)}, bf16[258,864]{1,0:T(8,128)(2,1)S(1)}, u32[]{:S(2)}, u32[]{:S(2)}) collective-permute-start(bf16[258,864]{1,0:T(8,128)(2,1)S(1)} %get-tuple-element.133), channel_id=1, source_target_pairs={{0,2},{1,3},{2,0},{3,1},{4,6},{5,7},{6,4},{7,5},{8,10},{9,11},{10,... | collective-permute-start | bytes 1337480 | tf_op jit(solution)/shard_map/ppermute | solution.py:821
  65.7 31.9 %collective-permute-start.3 = (bf16[258,864]{1,0:T(8,128)(2,1)S(1)}, bf16[258,864]{1,0:T(8,128)(2,1)S(1)}, u32[]{:S(2)}, u32[]{:S(2)}) collective-permute-start(bf16[258,864]{1,0:T(8,128)(2,1)S(1)} %get-tuple-element.134), channel_id=1, source_target_pairs={{0,6},{1,7},{2,4},{3,5},{4,2},{5,3},{6,0},{7,1},{8,14},{9,15},{10,... | collective-permute-start | bytes 1337480 | tf_op jit(solution)/shard_map/ppermute | solution.py:821
  74.3 26.0 %collective-permute-start.11 = (bf16[2,72,1152]{2,1,0:T(8,128)(2,1)S(1)}, bf16[2,72,1152]{2,1,0:T(8,128)(2,1)S(1)}, u32[]{:S(2)}, u32[]{:S(2)}) collective-permute-start(bf16[2,72,1152]{2,1,0:T(8,128)(2,1)S(1)} %slice.249), channel_id=1, source_target_pairs={{0,16},{1,17},{2,18},{3,19},{4,20},{5,21},{6,22},{7,23},{8,24},{9,... | collective-permute-start | bytes 995336 | tf_op jit(solution)/shard_map/ppermute | solution.py:821
  75.9 24.4 %collective-permute-start.12 = (bf16[2,72,1152]{2,1,0:T(8,128)(2,1)S(1)}, bf16[2,72,1152]{2,1,0:T(8,128)(2,1)S(1)}, u32[]{:S(2)}, u32[]{:S(2)}) collective-permute-start(bf16[2,72,1152]{2,1,0:T(8,128)(2,1)S(1)} %slice.250), channel_id=1, source_target_pairs={{0,1},{1,0},{2,3},{3,2},{4,5},{5,4},{6,7},{7,6},{8,9},{9,8},{10,11... | collective-permute-start | bytes 995336 | tf_op jit(solution)/shard_map/ppermute | solution.py:821
  88.7 31.0 %collective-permute-start.15 = (bf16[4,144,1152]{2,1,0:T(8,128)(2,1)S(1)}, bf16[4,144,1152]{2,1,0:T(8,128)(2,1)}, u32[]{:S(2)}, u32[]{:S(2)}) collective-permute-start(bf16[4,144,1152]{2,1,0:T(8,128)(2,1)S(1)} %pad_maximum_fusion.4), channel_id=1, source_target_pairs={{0,1},{1,0},{2,3},{3,2},{4,5},{5,4},{6,7},{7,6},{8,9},{9,8},{10,11... | collective-permute-start | bytes 3981320 | tf_op jit(solution)/shard_map/ppermute | solution.py:821
  96.1 29.0 %collective-permute-start.17 = (bf16[4,144,1152]{2,1,0:T(8,128)(2,1)S(1)}, bf16[4,144,1152]{2,1,0:T(8,128)(2,1)}, u32[]{:S(2)}, u32[]{:S(2)}) collective-permute-start(bf16[4,144,1152]{2,1,0:T(8,128)(2,1)S(1)} %pad_maximum_fusion.4), channel_id=1, source_target_pairs={{0,16},{1,17},{2,18},{3,19},{4,20},{5,21},{6,22},{7,23},{8,24},{9,... | collective-permute-start | bytes 3981320 | tf_op jit(solution)/shard_map/ppermute | solution.py:821
  105.5 21.1 %collective-permute-start.13 = (f32[272,1152]{1,0:T(8,128)}, f32[272,1152]{1,0:T(8,128)}, u32[]{:S(2)}, u32[]{:S(2)}) collective-permute-start(f32[272,1152]{1,0:T(8,128)} %get-tuple-element.427), channel_id=1, source_target_pairs={{0,8},{1,9},{2,10},{3,11},{4,12},{5,13},{6,14},{7,15},{8,0},{9,1},... | collective-permute-start | bytes 3760136 | tf_op jit(solution)/shard_map/ppermute | solution.py:821
  120.9 15.4 %collective-permute-start.16 = (bf16[2,144,1152]{2,1,0:T(8,128)(2,1)S(1)}, bf16[2,144,1152]{2,1,0:T(8,128)(2,1)S(1)}, u32[]{:S(2)}, u32[]{:S(2)}) collective-permute-start(bf16[2,144,1152]{2,1,0:T(8,128)(2,1)S(1)} %slice.325), channel_id=1, source_target_pairs={{0,16},{1,17},{2,18},{3,19},{4,20},{5,21},{6,22},{7,23},{8,24},{9,... | collective-permute-start | bytes 1990664 | tf_op jit(solution)/shard_map/ppermute | solution.py:821
  126.2 14.6 %collective-permute-start.18 = (bf16[2,144,1152]{2,1,0:T(8,128)(2,1)S(1)}, bf16[2,144,1152]{2,1,0:T(8,128)(2,1)S(1)}, u32[]{:S(2)}, u32[]{:S(2)}) collective-permute-start(bf16[2,144,1152]{2,1,0:T(8,128)(2,1)S(1)} %slice.326), channel_id=1, source_target_pairs={{0,1},{1,0},{2,3},{3,2},{4,5},{5,4},{6,7},{7,6},{8,9},{9,8},{10,11... | collective-permute-start | bytes 1990664 | tf_op jit(solution)/shard_map/ppermute | solution.py:821
  128.9 12.1 %collective-permute-start.14 = (bf16[272,1152]{1,0:T(8,128)(2,1)S(1)}, bf16[272,1152]{1,0:T(8,128)(2,1)S(1)}, u32[]{:S(2)}, u32[]{:S(2)}) collective-permute-start(bf16[272,1152]{1,0:T(8,128)(2,1)S(1)} %pad.16), channel_id=1, source_target_pairs={{0,8},{1,9},{2,10},{3,11},{4,12},{5,13},{6,14},{7,15},{8,0},{9,1},... | collective-permute-start | bytes 1880072 | tf_op jit(solution)/shard_map/ppermute | solution.py:821
  141.1 21.0 %collective-permute-start.19 = (bf16[272,1152]{1,0:T(8,128)(2,1)S(1)}, bf16[272,1152]{1,0:T(8,128)(2,1)S(1)}, u32[]{:S(2)}, u32[]{:S(2)}) collective-permute-start(bf16[272,1152]{1,0:T(8,128)(2,1)S(1)} %get-tuple-element.147), channel_id=1, source_target_pairs={{0,16},{1,17},{2,18},{3,19},{4,20},{5,21},{6,22},{7,23},{8,24},{9,... | collective-permute-start | bytes 1880072 | tf_op jit(solution)/shard_map/ppermute | solution.py:821
  163.3 3.0 collective-permute-start.20
  167.2 16.2 %collective-permute-start.21 = (bf16[272,1152]{1,0:T(8,128)(2,1)S(1)}, bf16[272,1152]{1,0:T(8,128)(2,1)S(1)}, u32[]{:S(2)}, u32[]{:S(2)}) collective-permute-start(bf16[272,1152]{1,0:T(8,128)(2,1)S(1)} %pad.17), channel_id=1, source_target_pairs={{0,16},{1,17},{2,18},{3,19},{4,20},{5,21},{6,22},{7,23},{8,24},{9,... | collective-permute-start | bytes 1880072 | tf_op jit(solution)/shard_map/ppermute | solution.py:821
  167.7 17.5 %collective-permute-start.23 = (bf16[544,1152]{1,0:T(8,128)(2,1)}, bf16[544,1152]{1,0:T(8,128)(2,1)}, u32[]{:S(2)}, u32[]{:S(2)}) collective-permute-start(bf16[544,1152]{1,0:T(8,128)(2,1)} %pad_maximum_fusion.11), channel_id=1, source_target_pairs={{0,8},{1,9},{2,10},{3,11},{4,12},{5,13},{6,14},{7,15},{8,0},{9,1},... | collective-permute-start | bytes 3760136 | tf_op jit(solution)/shard_map/ppermute | solution.py:821
  184.6 4.0 collective-permute-start.22
  244.0 5.0 collective-permute-start.24
  251.4 16.2 %collective-permute-start.25 = (bf16[272,1152]{1,0:T(8,128)(2,1)S(1)}, bf16[272,1152]{1,0:T(8,128)(2,1)S(1)}, u32[]{:S(2)}, u32[]{:S(2)}) collective-permute-start(bf16[272,1152]{1,0:T(8,128)(2,1)S(1)} %slice.494), channel_id=1, source_target_pairs={{0,16},{1,17},{2,18},{3,19},{4,20},{5,21},{6,22},{7,23},{8,24},{9,... | collective-permute-start | bytes 1880072 | tf_op jit(solution)/shard_map/ppermute | solution.py:821
  267.6 4.7 collective-permute-start.31
  269.1 5.1 collective-permute-start.26
  269.7 36.8 %collective-permute-start.29 = (bf16[4,144,1152]{2,1,0:T(8,128)(2,1)}, bf16[4,144,1152]{2,1,0:T(8,128)(2,1)}, u32[]{:S(2)}, u32[]{:S(2)}) collective-permute-start(bf16[4,144,1152]{2,1,0:T(8,128)(2,1)} %get-tuple-element.163), channel_id=1, source_target_pairs={{0,1},{1,0},{2,3},{3,2},{4,5},{5,4},{6,7},{7,6},{8,9},{9,8},{10,11... | collective-permute-start | bytes 3981320 | tf_op jit(solution)/shard_map/ppermute | solution.py:821
  270.2 36.2 %collective-permute-start.30 = (bf16[2,2,144,1152]{3,2,1,0:T(8,128)(2,1)}, bf16[2,2,144,1152]{3,2,1,0:T(8,128)(2,1)}, u32[]{:S(2)}, u32[]{:S(2)}) collective-permute-start(bf16[2,2,144,1152]{3,2,1,0:T(8,128)(2,1)} %get-tuple-element.164), channel_id=1, source_target_pairs={{0,2},{1,3},{2,0},{3,1},{4,6},{5,7},{6,4},{7,5},{8,10},{9,11},{10,... | collective-permute-start | bytes 3981320 | tf_op jit(solution)/shard_map/ppermute | solution.py:821
  272.7 33.8 %collective-permute-start.32 = (bf16[272,1152]{1,0:T(8,128)(2,1)S(1)}, bf16[272,1152]{1,0:T(8,128)(2,1)S(1)}, u32[]{:S(2)}, u32[]{:S(2)}) collective-permute-start(bf16[272,1152]{1,0:T(8,128)(2,1)S(1)} %slice.493), channel_id=1, source_target_pairs={{0,16},{1,17},{2,18},{3,19},{4,20},{5,21},{6,22},{7,23},{8,24},{9,... | collective-permute-start | bytes 1880072 | tf_op jit(solution)/shard_map/ppermute | solution.py:821
  306.5 9.0 %collective-permute-start.33 = (f32[272,1152]{1,0:T(8,128)}, f32[272,1152]{1,0:T(8,128)}, u32[]{:S(2)}, u32[]{:S(2)}) collective-permute-start(f32[272,1152]{1,0:T(8,128)} %get-tuple-element.167), channel_id=1, source_target_pairs={{0,8},{1,9},{2,10},{3,11},{4,12},{5,13},{6,14},{7,15},{8,0},{9,1},... | collective-permute-start | bytes 3760136 | tf_op jit(solution)/shard_map/ppermute | solution.py:821
  306.7 24.3 %collective-permute-start.27 = (bf16[2,144,1152]{2,1,0:T(8,128)(2,1)}, bf16[2,144,1152]{2,1,0:T(8,128)(2,1)S(1)}, u32[]{:S(2)}, u32[]{:S(2)}) collective-permute-start(bf16[2,144,1152]{2,1,0:T(8,128)(2,1)} %get-tuple-element.159), channel_id=1, source_target_pairs={{0,16},{1,17},{2,18},{3,19},{4,20},{5,21},{6,22},{7,23},{8,24},{9,... | collective-permute-start | bytes 1990664 | tf_op jit(solution)/shard_map/ppermute | solution.py:821
  307.4 23.6 %collective-permute-start.28 = (bf16[2,144,1152]{2,1,0:T(8,128)(2,1)}, bf16[2,144,1152]{2,1,0:T(8,128)(2,1)S(1)}, u32[]{:S(2)}, u32[]{:S(2)}) collective-permute-start(bf16[2,144,1152]{2,1,0:T(8,128)(2,1)} %get-tuple-element.160), channel_id=1, source_target_pairs={{0,1},{1,0},{2,3},{3,2},{4,5},{5,4},{6,7},{7,6},{8,9},{9,8},{10,11... | collective-permute-start | bytes 1990664 | tf_op jit(solution)/shard_map/ppermute | solution.py:821
  314.7 24.6 %collective-permute-start.41 = (bf16[2,144,1152]{2,1,0:T(8,128)(2,1)S(1)}, bf16[2,144,1152]{2,1,0:T(8,128)(2,1)S(1)}, u32[]{:S(2)}, u32[]{:S(2)}) collective-permute-start(bf16[2,144,1152]{2,1,0:T(8,128)(2,1)S(1)} %slice.343), channel_id=1, source_target_pairs={{0,2},{1,3},{2,0},{3,1},{4,6},{5,7},{6,4},{7,5},{8,10},{9,11},{10,... | collective-permute-start | bytes 1990664 | tf_op jit(solution)/shard_map/ppermute | solution.py:821
  318.4 4.2 collective-permute-start.34
  321.0 31.9 %collective-permute-start.40 = (bf16[2,144,1152]{2,1,0:T(8,128)(2,1)S(1)}, bf16[2,144,1152]{2,1,0:T(8,128)(2,1)S(1)}, u32[]{:S(2)}, u32[]{:S(2)}) collective-permute-start(bf16[2,144,1152]{2,1,0:T(8,128)(2,1)S(1)} %slice_bitcast_fusion.3), channel_id=1, source_target_pairs={{0,4},{1,5},{2,6},{3,7},{4,0},{5,1},{6,2},{7,3},{8,12},{9,13},{10,... | collective-permute-start | bytes 1990664 | tf_op jit(solution)/shard_map/ppermute | solution.py:821
  324.8 4.0 collective-permute-start.35
  331.1 21.8 %collective-permute-start.38 = (bf16[2,72,1152]{2,1,0:T(8,128)(2,1)S(1)}, bf16[2,72,1152]{2,1,0:T(8,128)(2,1)S(1)}, u32[]{:S(2)}, u32[]{:S(2)}) collective-permute-start(bf16[2,72,1152]{2,1,0:T(8,128)(2,1)S(1)} %get-tuple-element.438), channel_id=1, source_target_pairs={{0,16},{1,17},{2,18},{3,19},{4,20},{5,21},{6,22},{7,23},{8,24},{9,... | collective-permute-start | bytes 995336 | tf_op jit(solution)/shard_map/ppermute | solution.py:821
  332.4 20.5 %collective-permute-start.39 = (bf16[2,72,1152]{2,1,0:T(8,128)(2,1)S(1)}, bf16[2,72,1152]{2,1,0:T(8,128)(2,1)S(1)}, u32[]{:S(2)}, u32[]{:S(2)}) collective-permute-start(bf16[2,72,1152]{2,1,0:T(8,128)(2,1)S(1)} %get-tuple-element.437), channel_id=1, source_target_pairs={{0,1},{1,0},{2,3},{3,2},{4,5},{5,4},{6,7},{7,6},{8,9},{9,8},{10,11... | collective-permute-start | bytes 995336 | tf_op jit(solution)/shard_map/ppermute | solution.py:821
  334.2 44.3 %collective-permute-start.37 = (bf16[4,144,1152]{2,1,0:T(8,128)(2,1)S(1)}, bf16[4,144,1152]{2,1,0:T(8,128)(2,1)S(1)}, u32[]{:S(2)}, u32[]{:S(2)}) collective-permute-start(bf16[4,144,1152]{2,1,0:T(8,128)(2,1)S(1)} %pad_maximum_fusion.7), channel_id=1, source_target_pairs={{0,16},{1,17},{2,18},{3,19},{4,20},{5,21},{6,22},{7,23},{8,24},{9,... | collective-permute-start | bytes 3981320 | tf_op jit(solution)/shard_map/ppermute | solution.py:821
  339.3 39.2 %collective-permute-start.36 = (bf16[4,144,1152]{2,1,0:T(8,128)(2,1)S(1)}, bf16[4,144,1152]{2,1,0:T(8,128)(2,1)S(1)}, u32[]{:S(2)}, u32[]{:S(2)}) collective-permute-start(bf16[4,144,1152]{2,1,0:T(8,128)(2,1)S(1)} %pad_maximum_fusion.6), channel_id=1, source_target_pairs={{0,1},{1,0},{2,3},{3,2},{4,5},{5,4},{6,7},{7,6},{8,9},{9,8},{10,11... | collective-permute-start | bytes 3981320 | tf_op jit(solution)/shard_map/ppermute | solution.py:821
  353.1 23.9 %collective-permute-start.43 = (bf16[144,1152]{1,0:T(8,128)(2,1)S(1)}, bf16[144,1152]{1,0:T(8,128)(2,1)S(1)}, u32[]{:S(2)}, u32[]{:S(2)}) collective-permute-start(bf16[144,1152]{1,0:T(8,128)(2,1)S(1)} %slice_bitcast_fusion.9), channel_id=1, source_target_pairs={{0,1},{1,0},{2,3},{3,2},{4,5},{5,4},{6,7},{7,6},{8,9},{9,8},{10,11... | collective-permute-start | bytes 995336 | tf_op jit(solution)/shard_map/ppermute | solution.py:821
  354.8 23.6 %collective-permute-start.42 = (bf16[144,1152]{1,0:T(8,128)(2,1)S(1)}, bf16[144,1152]{1,0:T(8,128)(2,1)S(1)}, u32[]{:S(2)}, u32[]{:S(2)}) collective-permute-start(bf16[144,1152]{1,0:T(8,128)(2,1)S(1)} %slice_bitcast_fusion.10), channel_id=1, source_target_pairs={{0,4},{1,5},{2,6},{3,7},{4,0},{5,1},{6,2},{7,3},{8,12},{9,13},{10,... | collective-permute-start | bytes 995336 | tf_op jit(solution)/shard_map/ppermute | solution.py:821
  354.9 69.2 %collective-permute-start.60 = (f32[4,1152]{1,0:T(4,128)S(1)}, f32[4,1152]{1,0:T(4,128)S(1)}, u32[]{:S(2)}, u32[]{:S(2)}) collective-permute-start(f32[4,1152]{1,0:T(4,128)S(1)} %pad_maximum_fusion.28), channel_id=1, source_target_pairs={{0,8},{1,9},{2,10},{3,11},{4,12},{5,13},{6,14},{7,15},{8,0},{9,1},... | collective-permute-start | bytes 55304 | tf_op jit(solution)/shard_map/ppermute | solution.py:821
  377.0 23.9 %collective-permute-start.51 = (bf16[4,258,432]{2,0,1:T(4,128)(2,1)S(1)}, bf16[4,258,432]{2,0,1:T(4,128)(2,1)S(1)}, u32[]{:S(2)}, u32[]{:S(2)}) collective-permute-start(bf16[4,258,432]{2,0,1:T(4,128)(2,1)S(1)} %copy.87), channel_id=1, source_target_pairs={{0,1},{1,0},{2,3},{3,2},{4,5},{5,4},{6,7},{7,6},{8,9},{9,8},{10,11... | collective-permute-start | bytes 2674952 | tf_op jit(solution)/shard_map/ppermute | solution.py:821
  378.7 17.9 %collective-permute-start.45 = (bf16[2,144,1152]{2,1,0:T(8,128)(2,1)S(1)}, bf16[2,144,1152]{2,1,0:T(8,128)(2,1)S(1)}, u32[]{:S(2)}, u32[]{:S(2)}) collective-permute-start(bf16[2,144,1152]{2,1,0:T(8,128)(2,1)S(1)} %get-tuple-element.448), channel_id=1, source_target_pairs={{0,16},{1,17},{2,18},{3,19},{4,20},{5,21},{6,22},{7,23},{8,24},{9,... | collective-permute-start | bytes 1990664 | tf_op jit(solution)/shard_map/ppermute | solution.py:821
  380.5 16.2 %collective-permute-start.44 = (bf16[2,144,1152]{2,1,0:T(8,128)(2,1)S(1)}, bf16[2,144,1152]{2,1,0:T(8,128)(2,1)S(1)}, u32[]{:S(2)}, u32[]{:S(2)}) collective-permute-start(bf16[2,144,1152]{2,1,0:T(8,128)(2,1)S(1)} %slice.348), channel_id=1, source_target_pairs={{0,2},{1,3},{2,0},{3,1},{4,6},{5,7},{6,4},{7,5},{8,10},{9,11},{10,... | collective-permute-start | bytes 1990664 | tf_op jit(solution)/shard_map/ppermute | solution.py:821
  382.2 37.9 %collective-permute-start.48 = (bf16[4,72,1152]{2,1,0:T(8,128)(2,1)}, bf16[4,72,1152]{2,1,0:T(8,128)(2,1)}, u32[]{:S(2)}, u32[]{:S(2)}) collective-permute-start(bf16[4,72,1152]{2,1,0:T(8,128)(2,1)} %pad_maximum_fusion.23), channel_id=1, source_target_pairs={{0,16},{1,17},{2,18},{3,19},{4,20},{5,21},{6,22},{7,23},{8,24},{9,... | collective-permute-start | bytes 1990664 | tf_op jit(solution)/shard_map/ppermute | solution.py:821
  396.9 6.0 %collective-permute-start.49 = (bf16[2,2,144,1152]{3,2,1,0:T(8,128)(2,1)S(1)}, bf16[2,2,144,1152]{3,2,1,0:T(8,128)(2,1)S(1)}, u32[]{:S(2)}, u32[]{:S(2)}) collective-permute-start(bf16[2,2,144,1152]{3,2,1,0:T(8,128)(2,1)S(1)} %get-tuple-element.434), channel_id=1, source_target_pairs={{0,8},{1,9},{2,10},{3,11},{4,12},{5,13},{6,14},{7,15},{8,0},{9,1},... | collective-permute-start | bytes 3981320 | tf_op jit(solution)/shard_map/ppermute | solution.py:821
  398.0 24.2 %collective-permute-start.47 = (bf16[4,72,1152]{2,1,0:T(8,128)(2,1)}, bf16[4,72,1152]{2,1,0:T(8,128)(2,1)}, u32[]{:S(2)}, u32[]{:S(2)}) collective-permute-start(bf16[4,72,1152]{2,1,0:T(8,128)(2,1)} %pad_maximum_fusion.22), channel_id=1, source_target_pairs={{0,1},{1,0},{2,3},{3,2},{4,5},{5,4},{6,7},{7,6},{8,9},{9,8},{10,11... | collective-permute-start | bytes 1990664 | tf_op jit(solution)/shard_map/ppermute | solution.py:821
  401.4 37.4 %collective-permute-start.52 = (bf16[258,864]{1,0:T(8,128)(2,1)S(1)}, bf16[258,864]{1,0:T(8,128)(2,1)S(1)}, u32[]{:S(2)}, u32[]{:S(2)}) collective-permute-start(bf16[258,864]{1,0:T(8,128)(2,1)S(1)} %get-tuple-element.193), channel_id=1, source_target_pairs={{0,4},{1,5},{2,6},{3,7},{4,0},{5,1},{6,2},{7,3},{8,12},{9,13},{10,... | collective-permute-start | bytes 1337480 | tf_op jit(solution)/shard_map/ppermute | solution.py:821
  402.9 37.3 %collective-permute-start.53 = (bf16[258,864]{1,0:T(8,128)(2,1)S(1)}, bf16[258,864]{1,0:T(8,128)(2,1)S(1)}, u32[]{:S(2)}, u32[]{:S(2)}) collective-permute-start(bf16[258,864]{1,0:T(8,128)(2,1)S(1)} %get-tuple-element.194), channel_id=1, source_target_pairs={{0,2},{1,3},{2,0},{3,1},{4,6},{5,7},{6,4},{7,5},{8,10},{9,11},{10,... | collective-permute-start | bytes 1337480 | tf_op jit(solution)/shard_map/ppermute | solution.py:821
  420.1 20.1 %collective-permute-start.54 = (bf16[258,864]{1,0:T(8,128)(2,1)S(1)}, bf16[258,864]{1,0:T(8,128)(2,1)S(1)}, u32[]{:S(2)}, u32[]{:S(2)}) collective-permute-start(bf16[258,864]{1,0:T(8,128)(2,1)S(1)} %get-tuple-element.195), channel_id=1, source_target_pairs={{0,6},{1,7},{2,4},{3,5},{4,2},{5,3},{6,0},{7,1},{8,14},{9,15},{10,... | collective-permute-start | bytes 1337480 | tf_op jit(solution)/shard_map/ppermute | solution.py:821
  422.2 35.5 %collective-permute-start.46 = (bf16[144,1152]{1,0:T(8,128)(2,1)S(1)}, bf16[144,1152]{1,0:T(8,128)(2,1)S(1)}, u32[]{:S(2)}, u32[]{:S(2)}) collective-permute-start(bf16[144,1152]{1,0:T(8,128)(2,1)S(1)} %slice_bitcast_fusion.6), channel_id=1, source_target_pairs={{0,4},{1,5},{2,6},{3,7},{4,0},{5,1},{6,2},{7,3},{8,12},{9,13},{10,... | collective-permute-start | bytes 995336 | tf_op jit(solution)/shard_map/ppermute | solution.py:821
  424.2 33.5 %collective-permute-start.50 = (bf16[2,72,1152]{2,1,0:T(8,128)(2,1)S(1)}, bf16[2,72,1152]{2,1,0:T(8,128)(2,1)S(1)}, u32[]{:S(2)}, u32[]{:S(2)}) collective-permute-start(bf16[2,72,1152]{2,1,0:T(8,128)(2,1)S(1)} %slice.356), channel_id=1, source_target_pairs={{0,2},{1,3},{2,0},{3,1},{4,6},{5,7},{6,4},{7,5},{8,10},{9,11},{10,... | collective-permute-start | bytes 995336 | tf_op jit(solution)/shard_map/ppermute | solution.py:821
  438.8 39.8 %collective-permute-start.61 = (f32[4,1152]{1,0:T(4,128)}, f32[4,1152]{1,0:T(4,128)}, u32[]{:S(2)}, u32[]{:S(2)}) collective-permute-start(f32[4,1152]{1,0:T(4,128)} %fusion.60), channel_id=1, source_target_pairs={{0,16},{1,17},{2,18},{3,19},{4,20},{5,21},{6,22},{7,23},{8,24},{9,... | collective-permute-start | bytes 55304 | tf_op jit(solution)/shard_map/ppermute | solution.py:821
  457.8 9.4 %collective-permute-start.56 = (bf16[144,1152]{1,0:T(8,128)(2,1)S(1)}, bf16[144,1152]{1,0:T(8,128)(2,1)S(1)}, u32[]{:S(2)}, u32[]{:S(2)}) collective-permute-start(bf16[144,1152]{1,0:T(8,128)(2,1)S(1)} %fusion.23), channel_id=1, source_target_pairs={{0,16},{1,17},{2,18},{3,19},{4,20},{5,21},{6,22},{7,23},{8,24},{9,... | collective-permute-start | bytes 995336 | tf_op jit(solution)/shard_map/ppermute | solution.py:821
  467.3 5.1 collective-permute-start.57
  467.5 10.3 %collective-permute-start.55 = (bf16[72,1152]{1,0:T(8,128)(2,1)S(1)}, bf16[72,1152]{1,0:T(8,128)(2,1)S(1)}, u32[]{:S(2)}, u32[]{:S(2)}) collective-permute-start(bf16[72,1152]{1,0:T(8,128)(2,1)S(1)} %slice_bitcast_fusion.12), channel_id=1, source_target_pairs={{0,4},{1,5},{2,6},{3,7},{4,0},{5,1},{6,2},{7,3},{8,12},{9,13},{10,... | collective-permute-start | bytes 497672 | tf_op jit(solution)/shard_map/ppermute | solution.py:821
  478.1 6.7 %collective-permute-start.58 = (bf16[72,1152]{1,0:T(8,128)(2,1)S(1)}, bf16[72,1152]{1,0:T(8,128)(2,1)S(1)}, u32[]{:S(2)}, u32[]{:S(2)}) collective-permute-start(bf16[72,1152]{1,0:T(8,128)(2,1)S(1)} %fusion.40), channel_id=1, source_target_pairs={{0,16},{1,17},{2,18},{3,19},{4,20},{5,21},{6,22},{7,23},{8,24},{9,... | collective-permute-start | bytes 497672 | tf_op jit(solution)/shard_map/ppermute | solution.py:821
  490.3 7.9 %collective-permute-start.62 = (f32[19,1152]{1,0:T(8,128)S(1)}, f32[19,1152]{1,0:T(8,128)S(1)}, u32[]{:S(2)}, u32[]{:S(2)}) collective-permute-start(f32[19,1152]{1,0:T(8,128)S(1)} %concatenate.87), channel_id=1, source_target_pairs={{0,1},{1,0},{2,3},{3,2},{4,5},{5,4},{6,7},{7,6},{8,9},{9,8},{10,11... | collective-permute-start | bytes 262664 | tf_op jit(solution)/shard_map/ppermute | solution.py:821
  498.2 5.2 collective-permute-start.63
  503.4 7.7 %collective-permute-start.64 = (f32[19,1152]{1,0:T(8,128)S(1)}, f32[19,1152]{1,0:T(8,128)S(1)}, u32[]{:S(2)}, u32[]{:S(2)}) collective-permute-start(f32[19,1152]{1,0:T(8,128)S(1)} %add.492), channel_id=1, source_target_pairs={{0,4},{1,5},{2,6},{3,7},{4,0},{5,1},{6,2},{7,3},{8,12},{9,13},{10,... | collective-permute-start | bytes 262664 | tf_op jit(solution)/shard_map/ppermute | solution.py:821
  (79 other events, 679.6 us)
Sparse Core Ops, SparseCore 0:
  108.8 96.9 all-gather.2

commit v5 on v4

--- a/solution.py
+++ b/solution.py
@@ -348,67 +348,103 @@
             ref[...] += value[number * size : (number + 1) * size]
 
 
-def ffn_kernel(order_ref, mixed_ref, cot_ref, *refs):
-    blocks = 4
-    weights, (down_a, down_b, mixed_a, mixed_b), grads = refs[:blocks], refs[blocks : blocks + 4], refs[blocks + 4 :]
-    step = pl.program_id(0)
-    mixed = mixed_ref[...]
-    cot = cot_ref[...]
+def ffn_first_kernel(order_ref, mixed_ref, cot_ref, *refs):
+    weights, (mixed_a, mixed_b, act_ref, grad_ref) = refs[:4], refs[4:]
     up = jnp.concatenate([ref[0, 0] for ref in weights], axis=0)
     down = jnp.concatenate([ref[0, 1] for ref in weights], axis=0)
-    up_input = dot_nt(mixed, up)
+    up_input = dot_nt(mixed_ref[...], up)
     gate = 0.5 * (1.0 + lax.erf(up_input * (1.0 / math.sqrt(2.0))))
-    activation = (up_input * gate).astype(jnp.bfloat16)
+    act_ref[0] = (up_input * gate).astype(jnp.bfloat16)
     slope = gate + up_input * (jnp.exp(-0.5 * up_input * up_input) * (1.0 / math.sqrt(2.0 * math.pi)))
-    grad_up_in = (dot_nt(cot, down) * slope).astype(jnp.bfloat16)
-    grad_up = dot_tn(grad_up_in, mixed).astype(jnp.bfloat16)
-    grad_down = dot_tn(activation, cot).astype(jnp.bfloat16)
-    for j in range(2):
+    grad = (dot_nt(cot_ref[...], down) * slope).astype(jnp.bfloat16)
+    grad_ref[0] = grad
+    accumulate(pl.program_id(0), (mixed_a, mixed_b), dot_nn(grad, up))
+
+
+def ffn_second_kernel(order_ref, mixed_ref, cot_ref, act_ref, grad_ref, *refs):
+    weights, (down_a, down_b, up_near, up_far, down_near, down_far) = refs[:4], refs[4:]
+    step = pl.program_id(0)
+    down = jnp.concatenate([ref[0, 0] for ref in weights], axis=0)
+    grad_up = dot_tn(grad_ref[0], mixed_ref[...]).astype(jnp.bfloat16)
+    grad_down = dot_tn(act_ref[0], cot_ref[...]).astype(jnp.bfloat16)
+    for j, ref in enumerate((up_near, up_far)):
 
         @pl.when(step == j)
         def _():
-            grads[j][...] = grad_up.reshape(grads[j].shape)
-
-    down_rows = grad_down.reshape((2,) + grads[2].shape[1:])
-    grads[2][0] = down_rows[0]
-    grads[3][0] = down_rows[1]
-
-    accumulate(step, (mixed_a, mixed_b), dot_nn(grad_up_in, up))
-    accumulate(step, (down_a, down_b), dot_nn(activation, down))
-
-
-def ffn(order, mixed, cot, weights):
+            ref[...] = grad_up.reshape(ref.shape)
+
+    halves = grad_down.reshape((2,) + down_near.shape[1:])
+    down_near[0] = halves[0]
+    down_far[0] = halves[1]
+    accumulate(step, (down_a, down_b), dot_nn(act_ref[0], down))
+
+
+def ffn_specs(tokens, rows):
+    whole = pl.BlockSpec((tokens, D), lambda t, m: (0, 0))
+    half = pl.BlockSpec((tokens // 2, D), lambda t, m: (0, 0))
+    units = pl.BlockSpec((1, tokens, 4 * rows), lambda t, m: (t, 0, 0))
+    return whole, half, units
+
+
+def ffn_first(order, mixed, cot, weights):
     count, _, rows, _ = weights.shape
     tokens = mixed.shape[0]
-    blocks = 4
-    whole = pl.BlockSpec((tokens, D), lambda t, m: (0, 0))
-    half = pl.BlockSpec((tokens // 2, D), lambda t, m: (0, 0))
+    whole, half, units = ffn_specs(tokens, rows)
 
     def weight_spec(slot):
-        return pl.BlockSpec((1, 2, rows, D), lambda t, m: (m[blocks * t + slot], 0, 0, 0))
-
-    grad_block = pl.BlockSpec((blocks, rows, D), lambda t, m: (0, 0, 0))
+        return pl.BlockSpec((1, 2, rows, D), lambda t, m: (m[4 * t + slot], 0, 0, 0))
+
     part = jax.ShapeDtypeStruct((tokens // 2, D), jnp.float32)
-    grad = jax.ShapeDtypeStruct((blocks, rows, D), jnp.bfloat16)
-    turn_block = pl.BlockSpec((1, blocks // 2, rows, D), lambda t, m: (t, 0, 0, 0))
-    turn = jax.ShapeDtypeStruct((2, blocks // 2, rows, D), jnp.bfloat16)
+    hidden = jax.ShapeDtypeStruct((count // 4, tokens, 4 * rows), jnp.bfloat16)
     return pl.pallas_call(
-        ffn_kernel,
-        out_shape=[part] * 4 + [grad] * 2 + [turn] * 2,
+        ffn_first_kernel,
+        out_shape=[part] * 2 + [hidden] * 2,
         grid_spec=pltpu.PrefetchScalarGridSpec(
             num_scalar_prefetch=1,
-            grid=(count // blocks,),
-            in_specs=[whole, whole] + [weight_spec(slot) for slot in range(blocks)],
-            out_specs=[half] * 4 + [grad_block] * 2 + [turn_block] * 2,
+            grid=(count // 4,),
+            in_specs=[whole, whole] + [weight_spec(slot) for slot in range(4)],
+            out_specs=[half] * 2 + [units] * 2,
         ),
         compiler_params=pltpu.CompilerParams(
-            dimension_semantics=("arbitrary",), vmem_limit_bytes=60 * 1024 * 1024
+            dimension_semantics=("arbitrary",), vmem_limit_bytes=56 * 1024 * 1024
         ),
         cost_estimate=pl.CostEstimate(
-            flops=12 * tokens * D * count * rows, transcendentals=0, bytes_accessed=32 * 1024 * 1024
+            flops=6 * tokens * D * count * rows, transcendentals=0, bytes_accessed=24 * 1024 * 1024
         ),
-        name="ffn",
-    )(order, mixed, cot, *([weights] * blocks))
+        name="ffn_first",
+    )(order, mixed, cot, *([weights] * 4))
+
+
+def ffn_second(order, mixed, cot, act, grad, weights):
+    count, _, rows, _ = weights.shape
+    tokens = mixed.shape[0]
+    whole, half, units = ffn_specs(tokens, rows)
+
+    def weight_spec(slot):
+        return pl.BlockSpec((1, 1, rows, D), lambda t, m: (m[4 * t + slot], 1, 0, 0))
+
+    part = jax.ShapeDtypeStruct((tokens // 2, D), jnp.float32)
+    side = jax.ShapeDtypeStruct((4, rows, D), jnp.bfloat16)
+    turn = jax.ShapeDtypeStruct((2, 2, rows, D), jnp.bfloat16)
+    side_block = pl.BlockSpec((4, rows, D), lambda t, m: (0, 0, 0))
+    turn_block = pl.BlockSpec((1, 2, rows, D), lambda t, m: (t, 0, 0, 0))
+    return pl.pallas_call(
+        ffn_second_kernel,
+        out_shape=[part] * 2 + [side] * 2 + [turn] * 2,
+        grid_spec=pltpu.PrefetchScalarGridSpec(
+            num_scalar_prefetch=1,
+            grid=(count // 4,),
+            in_specs=[whole, whole, units, units] + [weight_spec(slot) for slot in range(4)],
+            out_specs=[half] * 2 + [side_block] * 2 + [turn_block] * 2,
+        ),
+        compiler_params=pltpu.CompilerParams(
+            dimension_semantics=("arbitrary",), vmem_limit_bytes=56 * 1024 * 1024
+        ),
+        cost_estimate=pl.CostEstimate(
+            flops=6 * tokens * D * count * rows, transcendentals=0, bytes_accessed=24 * 1024 * 1024
+        ),
+        name="ffn_second",
+    )(order, mixed, cot, act, grad, *([weights] * 4))
 
 
 def soft(q, k):
@@ -922,26 +958,20 @@
         grad = grad.astype(f32)
         squares = grad * grad + EPS_SQUARE
         new = DECAY * old + (1.0 - DECAY) * (jnp.sum(squares, axis=1) / D)
-        old_sum = jnp.where(lax.broadcasted_iota(jnp.int32, (D,), 0) == 0, jnp.sum(old), 0.0)
-        sums = [
-            jnp.sum(squares, axis=0),
-            jnp.sum(grad * grad * (1.0 / new)[:, None], axis=0),
-            old_sum,
-        ]
-        return new, sums
-
-    def step_of(grad, new, totals, old_wide, rows_all, row_along_wide):
-        wide_mean = totals[0] / rows_all
-        wide_new = DECAY * old_wide + (1.0 - DECAY) * wide_mean
-        if row_along_wide:
-            row_mean = jnp.mean(wide_new)
-        else:
-            row_mean = DECAY * (totals[2][0] / rows_all) + (1.0 - DECAY) * jnp.mean(wide_mean)
-        square_total = jnp.sum(totals[1] / wide_new) * row_mean
-        ratio = jnp.sqrt(square_total / (rows_all * D)) / CLIP_LEVEL
-        factor = -(STEP_RATE * jnp.sqrt(row_mean) / jnp.maximum(1.0, ratio))
-        step = grad.astype(f32) * lax.rsqrt(new)[:, None] * (lax.rsqrt(wide_new) * factor)[None, :]
-        return wide_new, ratio, step
+        return new, jnp.sum(squares, axis=0), jnp.sum(grad * grad * (1.0 / new)[:, None], axis=0)
+
+    def step_of(grad, new, scale):
+        return grad.astype(f32) * lax.rsqrt(new)[:, None] * scale[None, :]
+
+    old_wide = jnp.stack([col_skip, row_qkv, col_out, row_up, col_down])
+    lane = lax.broadcasted_iota(jnp.int32, (1, D), 1)
+    old_sums = (
+        jnp.where(lane == 0, jnp.sum(row_skip), 0.0)
+        + jnp.where(lane == 2, jnp.sum(row_out), 0.0)
+        + jnp.where(lane == 4, jnp.sum(row_down), 0.0)
+    )
+    rows_all = jnp.array([[2 * D], [3 * D], [D], [FF], [FF]], f32)
+    along_wide = jnp.array([[False], [True], [False], [True], [False]])
 
     flags = jnp.stack([yi, zi % 2, zi // 2, ci]).astype(jnp.int32)
     token_near, token_give = pack_tokens(flags, stream.T, skip_in.T, cotangent.T)
@@ -1022,11 +1052,13 @@
     mixed = jnp.concatenate([mixed_pair, core(mixed_pair)])
     cot = jnp.concatenate([cot_pair, core(cot_pair)])
 
-    down_a, down_b, mixed_a, mixed_b, up_near, up_give, down_near, down_give = ffn(
-        order, mixed, cot, ffn_full
-    )
+    mixed_a, mixed_b, act, act_grad = ffn_first(order, mixed, cot, ffn_full)
     mixed_sum = mixed_a + core(mixed_b)
     mixed_far = over_x(mixed_sum[PAD:].astype(bf16))
+    mixed_sum, act = tie(mixed_sum, act)
+    down_a, down_b, up_near, up_give, down_near, down_give = ffn_second(
+        order, mixed, cot, act, act_grad, ffn_full
+    )
     ffn_far_up = over_y(up_give)
     ffn_down_one = xor_z(down_give, 1)
 
@@ -1045,13 +1077,13 @@
         meta, normed, middle_low, attn_full, qkv_kept, attended
     )
 
-    normed_b, ffn_far_up, ffn_down_one, down_far = tie(
-        normed_b, ffn_far_up, ffn_down_one, down_far
+    normed_b, ffn_far_up, ffn_down_one, down_far, other_x, other_y = tie(
+        normed_b, ffn_far_up, ffn_down_one, down_far, other_x, other_y
     )
     attn_from_x = over_x(other_x)
     attn_from_y = over_y(other_y)
     ffn_down = add_low(down_near, ffn_down_one)
-    ffn_down_two = xor_z(ffn_down[:, 1], 2)
+    ffn_down_far = over_y(ffn_down[1])
     ffn_up, ffn_up_give = halves_z(add_low(up_near, ffn_far_up))
     ffn_up_one = xor_z(ffn_up_give, 1)
     block_own = (middle + (down_sum[:PAD] + down_far.astype(f32))[:SEQ]).astype(bf16)
@@ -1059,6 +1091,7 @@
         unit_one, inverse_one, core_sum(normed_a, normed_b), norm_gain[0]
     )
     hidden_low = both_images((grad_middle + back_hidden).astype(bf16))
+    hidden_low, attn_from_x, attn_from_y = tie(hidden_low, attn_from_x, attn_from_y)
     token_grad = matmul(hidden_low, skip_mat, "rd,cd->rc").astype(bf16)
     back_near, back_give = give_tokens(
         flags, token_grad[:PAD], core(token_grad[PAD:]), padded(block_own)
@@ -1067,122 +1100,119 @@
     grad_skip = grad_skip.reshape(narrow_count, 2, feat // 2, D)
     skip_own, skip_other = pick(grad_skip, xi, 1), pick(grad_skip, 1 - xi, 1)
 
-    attn_from_x, attn_from_y, back_give, skip_other = tie(
-        attn_from_x, attn_from_y, back_give, skip_other
-    )
+    attn_from_x, attn_from_y, ffn_down_far, ffn_up_one, back_give, skip_own, skip_other = tie(
+        attn_from_x, attn_from_y, ffn_down_far, ffn_up_one, back_give, skip_own, skip_other
+    )
+    back_far = over_y(back_give)
     skip_from_x = over_x(skip_other[ZS : ZS + half])
     skip_from_y = over_y(skip_other[ZS + half :])
-    back_far = over_y(back_give)
     attn_across = over_x(
         jnp.concatenate([other_near[:half], add_low(other_near[half:], attn_from_y)])
     )
-    attn_beside = over_y(
-        jnp.concatenate([add_low(own[ZS : ZS + half], attn_from_x), own[ZS + half :]])
-    )
-
-    skip_from_x, skip_from_y, ffn_down_two, ffn_up_one = tie(
-        skip_from_x, skip_from_y, ffn_down_two, ffn_up_one
-    )
-    ffn_up = add_low(ffn_up, ffn_up_one)
-    ffn_up_two = xor_z(ffn_up[1], 2)
-    ffn_down = add_low(ffn_down[:, 0], ffn_down_two)
-    ffn_down_far = over_y(ffn_down[1])
-    skip_across = over_x(
-        jnp.concatenate([skip_other[:half], add_low(skip_other[half:ZS], skip_from_y)])
-    )
-    skip_beside = over_y(
-        jnp.concatenate([add_low(skip_own[ZS : ZS + half], skip_from_x), skip_own[ZS + half :]])
-    )
+    attn_far = jnp.concatenate([add_low(own[ZS : ZS + half], attn_from_x), own[ZS + half :]])
+    ffn_both = jnp.stack([add_low(ffn_up, ffn_up_one), add_low(ffn_down[0], ffn_down_far)])
+    ffn_two = xor_z(ffn_both[:, 1], 2)
+
+    back_far, skip_from_x, skip_from_y, attn_across, ffn_two, attn_far = tie(
+        back_far, skip_from_x, skip_from_y, attn_across, ffn_two, attn_far
+    )
+    attn_beside = over_y(attn_far)
     back_blocks = z_line(join_lanes(back_near, back_far))
-
-    attn_beside, attn_across, ffn_up_two, ffn_down_far = tie(
-        attn_beside, attn_across, ffn_up_two, ffn_down_far
+    ffn_own = add_low(ffn_both[:, 0], ffn_two)
+    ffn_x = over_x(ffn_own)
+    skip_give_x = jnp.concatenate([skip_other[:half], add_low(skip_other[half:ZS], skip_from_y)])
+    skip_give_y = jnp.concatenate(
+        [add_low(skip_own[ZS : ZS + half], skip_from_x), skip_own[ZS + half :]]
+    )
+
+    attn_beside, back_blocks, ffn_x, skip_give_x, skip_give_y = tie(
+        attn_beside, back_blocks, ffn_x, skip_give_x, skip_give_y
     )
     attn_total, attn_give = halves_z(
         (own[:ZS].astype(f32) + attn_beside.astype(f32) + attn_across.astype(f32)).astype(bf16)
     )
     attn_one = xor_z(attn_give, 1)
-    ffn_own = jnp.stack([add_low(ffn_up[0], ffn_up_two), add_low(ffn_down[0], ffn_down_far)])
-    ffn_x = over_x(ffn_own)
-
-    attn_one, ffn_x = tie(attn_one, ffn_x)
+    skip_across = over_x(skip_give_x)
+    skip_beside = over_y(skip_give_y)
+    ffn_pair = jnp.stack([ffn_own, ffn_x])
+    ffn_core = core(ffn_pair)
+    back_out = back_tokens(flags, back_blocks)
+    (ffn_all,) = tie(in_order(ffn_pair, ffn_core))
+    grad_up_rows = ffn_all[:, 0].reshape(hidden, D)
+    grad_down = ffn_all[:, 1].reshape(hidden, D)
+    new_col_up, *up_sums = statistics(grad_up_rows, col_up)
+    new_row_down, *down_sums = statistics(grad_down, row_down)
+    ffn_sums = list(up_sums) + list(down_sums)
+
+    attn_one, skip_across, skip_beside, ffn_sums, back_out = tie(
+        attn_one, skip_across, skip_beside, ffn_sums, back_out
+    )
     attn_total = add_low(attn_total, attn_one)
     attn_two = xor_z(attn_total[1], 2)
-    ffn_pair = jnp.stack([ffn_own, ffn_x])
-    (ffn_all,) = tie(in_order(ffn_pair, core(ffn_pair)))
-    grad_up_rows = ffn_all[:, 0].reshape(hidden, D)
-    grad_down = ffn_all[:, 1].reshape(hidden, D)
-    new_col_up, up_sums = statistics(grad_up_rows, col_up)
-    new_row_down, down_sums = statistics(grad_down, row_down)
-
-    skip_beside, skip_across, *ffn_sums = tie(skip_beside, skip_across, *up_sums, *down_sums)
     skip_total, skip_give = halves_z(
         (skip_own[:ZS].astype(f32) + skip_beside.astype(f32) + skip_across.astype(f32)).astype(
             bf16
         )
     )
     skip_one = xor_z(skip_give, 1)
-
-    attn_two, skip_one, *back_blocks = tie(attn_two, skip_one, *back_blocks)
+    grad_stream, grad_skip_in, block_out = [part.T for part in back_out]
+
+    attn_two, skip_one = tie(attn_two, skip_one)
     attn_own = add_low(attn_total[0], attn_two)
     attn_x = over_x(attn_own)
     skip_total = add_low(skip_total, skip_one)
     skip_two = xor_z(skip_total[1], 2)
-    grad_stream, grad_skip_in, block_out = [
-        part.T for part in back_tokens(flags, back_blocks)
-    ]
+    grad_up_out = columns(grad_up_rows).T
+    grad_down_out = columns(grad_down)
+
+    attn_x, skip_two, grad_up_out, grad_down_out = tie(
+        attn_x, skip_two, grad_up_out, grad_down_out
+    )
+    skip_last = add_low(skip_total[0], skip_two)
+    skip_x = over_x(skip_last)
     attn_pair = jnp.stack([attn_own, attn_x])
     (attn_all,) = tie(in_order(attn_pair, core(attn_pair)))
     attn_all = attn_all.reshape(2, 4, half_head, D)
     grad_qkv_rows = attn_all[:, :3].transpose(1, 0, 2, 3).reshape(3 * feat, D)
     grad_out = attn_all[:, 3].reshape(feat, D)
-    new_col_qkv, qkv_sums = statistics(grad_qkv_rows, col_qkv.reshape(-1))
-    new_row_out, out_sums = statistics(grad_out, row_out)
-    grad_up_out = columns(grad_up_rows).T
-    grad_down_out = columns(grad_down)
-
-    grad_stream, grad_skip_in, block_out, grad_up_out, grad_down_out, skip_two, *sums = tie(
-        grad_stream,
-        grad_skip_in,
-        block_out,
-        grad_up_out,
-        grad_down_out,
-        skip_two,
-        *qkv_sums,
-        *out_sums,
-    )
-    skip_last = add_low(skip_total[0], skip_two)
-    skip_pair = jnp.stack([skip_last, over_x(skip_last)])
+    new_col_qkv, *qkv_sums = statistics(grad_qkv_rows, col_qkv.reshape(-1))
+    new_row_out, *out_sums = statistics(grad_out, row_out)
+
+    skip_x, *sums = tie(skip_x, *qkv_sums, *out_sums)
+    skip_pair = jnp.stack([skip_last, skip_x])
     (skip_all,) = tie(in_order(skip_pair, core(skip_pair)))
     grad_skip_rows = skip_all.reshape(2 * feat, D)
 
     norm_sums = jnp.stack([gain_one, gain_two, bias_one, bias_two])
     norm_sums = norm_sums + core(norm_sums)
     norm_sums = norm_sums + over_x(norm_sums)
-    new_row_skip, skip_sums = statistics(grad_skip_rows, row_skip.reshape(-1))
+    new_row_skip, *skip_sums = statistics(grad_skip_rows, row_skip.reshape(-1))
+    sums = list(skip_sums) + sums + list(ffn_sums)
     totals = all_narrow(
-        jnp.concatenate([jnp.stack(skip_sums + sums + list(ffn_sums)), norm_sums])
-    )
-    gain_total = totals[15:17]
-    bias_total = totals[17:19]
-    new_col_skip, ratio_skip, step_skip = step_of(
-        grad_skip_rows, new_row_skip, totals[:3], col_skip, 2 * D, False
-    )
-    new_row_qkv, ratio_qkv, step_qkv = step_of(
-        grad_qkv_rows, new_col_qkv, totals[3:6], row_qkv, 3 * D, True
-    )
-    new_col_out, ratio_out, step_out = step_of(
-        grad_out, new_row_out, totals[6:9], col_out, D, False
-    )
-    new_row_up, ratio_up, step_up = step_of(
-        grad_up_rows, new_col_up, totals[9:12], row_up, hidden * narrow_count, True
-    )
-    new_col_down, ratio_down, step_down = step_of(
-        grad_down, new_row_down, totals[12:15], col_down, hidden * narrow_count, False
-    )
+        jnp.concatenate([jnp.stack(sums[0::2] + sums[1::2]), norm_sums, old_sums])
+    )
+    gain_total = totals[10:12]
+    bias_total = totals[12:14]
+    wide_mean = totals[:5] / rows_all
+    new_wide = DECAY * old_wide + (1.0 - DECAY) * wide_mean
+    row_mean = jnp.where(
+        along_wide,
+        jnp.mean(new_wide, axis=1, keepdims=True),
+        DECAY * (totals[14, :5].reshape(5, 1) / rows_all)
+        + (1.0 - DECAY) * jnp.mean(wide_mean, axis=1, keepdims=True),
+    )
+    square_total = jnp.sum(totals[5:10] / new_wide, axis=1, keepdims=True) * row_mean
+    ratios = jnp.sqrt(square_total / (rows_all * D)) / CLIP_LEVEL
+    scales = lax.rsqrt(new_wide) * (-(STEP_RATE * jnp.sqrt(row_mean) / jnp.maximum(1.0, ratios)))
+    new_col_skip, new_row_qkv, new_col_out, new_row_up, new_col_down = new_wide
+    clip_ratio = ratios[:, 0]
+    step_skip = step_of(grad_skip_rows, new_row_skip, scales[0])
+    step_qkv = step_of(grad_qkv_rows, new_col_qkv, scales[1])
+    step_out = step_of(grad_out, new_row_out, scales[2])
+    step_up = step_of(grad_up_rows, new_col_up, scales[3])
+    step_down = step_of(grad_down, new_row_down, scales[4])
     new_up = up_weight.astype(f32) + step_up.T
     new_down = down_weight.astype(f32) + step_down
-    clip_ratio = jnp.stack([ratio_skip, ratio_qkv, ratio_out, ratio_up, ratio_down])
     new_skip = skip_weight.astype(f32) + step_skip.reshape(2, feat, D)
     new_qkv = qkv_weight.astype(f32) + step_qkv.reshape(3, feat, D).transpose(2, 0, 1)
     new_second_gain, gain_step = plain_update(gain_total, second_gain)

time: 553 us -> 537 us (0.971)
  waiting for transfers between devices: 226 us -> 209 us
  between operations: 26.8 us -> 17.5 us
  starting transfers between devices: 68.9 us -> 76 us
  other arithmetic: 86.1 us -> 79.5 us
  Pallas kernels: 96.6 us -> 103 us
    ppermute x65 -> x64, waiting for transfers between devices: 212 us -> 197 us  [send(): return lax.ppermute(value, axes, perm(move))]
    ppermute x65 -> x64, starting transfers between devices: 68.9 us -> 75.9 us  [send(): return lax.ppermute(value, axes, perm(move))]
    pallas_call x1 -> x2, Pallas kernels: 38.3 us -> 44 us  [the longest x1 22.7 us: ffn_second(): pl.pallas_call(ffn_second_kernel, out_shape=[part] * 2 + [side] * 2 + [tu...]
    unnamed x155 -> x146, local copies, waits for them, and re-layouts: 10.9 us -> 14.4 us
  transfers between devices with their start and end apart: 66 -> 65, of which waited for: 28 -> 30; matrix products, arithmetic and copies ran while one was open for 17% -> 17% of each run, Pallas kernels for 10% -> 15%
where the time goes in v5:
time: 537 us; the launch traced here: 531 us
  waiting for transfers between devices  209 us (39%)
  Pallas kernels  103 us (19%)
  other arithmetic  79.5 us (15%)
  starting transfers between devices  76 us (14%)
  local copies, waits for them, and re-layouts  39.7 us (7%)
  between operations  17.5 us (3%)
  matrix products  6.36 us (1%)
    ppermute x64, waiting for transfers between devices, send(): return lax.ppermute(value, axes, perm(move))  197 us
    ppermute x64, starting transfers between devices, send(): return lax.ppermute(value, axes, perm(move))  75.9 us
    pallas_call x1, Pallas kernels, attn_backward(): pl.pallas_call(attn_backward_kernel, out_shape=[jax.ShapeDtypeStruct((tok...  31.1 us
    pallas_call x1, Pallas kernels, ffn_second(): pl.pallas_call(ffn_second_kernel, out_shape=[part] * 2 + [side] * 2 + [tu...  22.7 us
    pallas_call x1, Pallas kernels, ffn_first(): pl.pallas_call(ffn_first_kernel, out_shape=[part] * 2 + [hidden] * 2, gri...  21.3 us
    pallas_call x1, Pallas kernels, attn_forward(): pl.pallas_call(attn_forward_kernel, out_shape=[jax.ShapeDtypeStruct((toke...  14.7 us
    unnamed x146, local copies, waits for them, and re-layouts  14.4 us
    all_gather x1, waiting for transfers between devices, chips(): ffn_full = lax.all_gather(ffn_block[None], 'narrow', tiled=True)  12.6 us
  transfers between devices with their start and end apart: 65, of which 30 were waited for; matrix products, arithmetic and copies ran while one was open for 17% of the time, Pallas kernels for 15%

profile of v5, /device:TPU:0, one launch (start us, length us, event | category | flops | bytes accessed | tf_op | source)
XLA Modules:
  0.0 530.8 jit_solution(4110995521035813443)
XLA Ops:
  10.2 2.2 pack_tokens.1
  12.4 4.1 collective-permute-start.5
  16.6 15.6 %collective-permute-done.5 = bf16[72,1152]{1,0:T(8,128)(2,1)S(1)} collective-permute-done((bf16[72,1152]{1,0:T(8,128)(2,1)S(1)}, bf16[72,1152]{1,0:T(8,128)(2,1)S(1)}, u32[]{:S(2)}, u32[]{:S(2)}) %collective-permute-start.5) | collective-permute-done | bytes 165920 | tf_op jit(solution)/shard_map/ppermute | solution.py:857
  33.9 1.9 collective-permute-start
  35.8 2.9 collective-permute-done.9
  40.3 5.5 %collective-permute-done.6 = bf16[2,72,1152]{2,1,0:T(8,128)(2,1)S(1)} collective-permute-done((bf16[2,72,1152]{2,1,0:T(8,128)(2,1)S(1)}, bf16[2,72,1152]{2,1,0:T(8,128)(2,1)S(1)}, u32[]{:S(2)}, u32[]{:S(2)}) %collective-permute-start.6) | collective-permute-done | bytes 331808 | tf_op jit(solution)/shard_map/ppermute | solution.py:857
  49.7 10.7 %collective-permute-done = bf16[4,258,432]{2,0,1:T(4,128)(2,1)} collective-permute-done((bf16[4,258,432]{2,0,1:T(4,128)(2,1)}, bf16[4,258,432]{2,0,1:T(4,128)(2,1)}, u32[]{:S(2)}, u32[]{:S(2)}) %collective-permute-start) | collective-permute-done | bytes 891680 | tf_op jit(solution)/shard_map/ppermute | solution.py:857
  62.3 3.4 collective-permute-start.1
  68.5 4.8 collective-permute-done.7
  78.7 10.0 %collective-permute-done.1.refs_1_ = bf16[258,864]{1,0:T(8,128)(2,1)S(1)} collective-permute-done((bf16[258,864]{1,0:T(8,128)(2,1)S(1)}, bf16[258,864]{1,0:T(8,128)(2,1)S(1)}, u32[]{:S(2)}, u32[]{:S(2)}) %collective-permute-start.1) | collective-permute-done | bytes 445856 | tf_op jit(solution)/shard_map/ppermute | solution.py:857
  88.7 7.3 %collective-permute-start.15 = (bf16[4,144,1152]{2,1,0:T(8,128)(2,1)S(1)}, bf16[4,144,1152]{2,1,0:T(8,128)(2,1)}, u32[]{:S(2)}, u32[]{:S(2)}) collective-permute-start(bf16[4,144,1152]{2,1,0:T(8,128)(2,1)S(1)} %pad_maximum_fusion.3), channel_id=1, source_target_pairs={{0,1},{1,0},{2,3},{3,2},{4,5},{5,4},{6,7},{7,6},{8,9},{9,8},{10,11... | collective-permute-start | bytes 3981320 | tf_op jit(solution)/shard_map/ppermute | solution.py:857
  97.5 2.6 take_tokens.1
  102.4 1.9 fusion.85
  108.7 11.0 %collective-permute-done.15 = bf16[4,144,1152]{2,1,0:T(8,128)(2,1)} collective-permute-done((bf16[4,144,1152]{2,1,0:T(8,128)(2,1)S(1)}, bf16[4,144,1152]{2,1,0:T(8,128)(2,1)}, u32[]{:S(2)}, u32[]{:S(2)}) %collective-permute-start.15) | collective-permute-done | bytes 1327136 | tf_op jit(solution)/shard_map/ppermute | solution.py:857
  120.9 2.9 collective-permute-start.16
  130.5 5.7 %collective-permute-done.16 = bf16[2,144,1152]{2,1,0:T(8,128)(2,1)S(1)} collective-permute-done((bf16[2,144,1152]{2,1,0:T(8,128)(2,1)S(1)}, bf16[2,144,1152]{2,1,0:T(8,128)(2,1)S(1)}, u32[]{:S(2)}, u32[]{:S(2)}) %collective-permute-start.16) | collective-permute-done | bytes 663584 | tf_op jit(solution)/shard_map/ppermute | solution.py:857
  136.3 4.5 collective-permute-done.18
  141.1 1.8 collective-permute-start.19
  144.4 2.9 pad_maximum_fusion.qk_ref.vo_ref
  147.3 14.7 %attn_forward.1 = (f32[272,1152]{1,0:T(8,128)S(1)}, f32[272,1152]{1,0:T(8,128)S(1)}, bf16[2,544,864]{2,1,0:T(8,128)(2,1)}, bf16[2,544,288]{2,1,0:T(8,128)(2,1)S(1)}) custom-call(s32[1]{0:T(128)} %bitcast.meta_ref, bf16[544,1152]{1,0:T(8,128)(2,1)S(1)} %pad_maximum_fusion.9.normed_ref, bf16[2,8,144,1152]{3,2,1,0:T(8,128)(2,1)} %pad_maximum_fusion.qk_ref.vo_ref, ...), custom_call_target="tpu_custom_call" | custom-call | bytes 1048576 | tf_op jit(solution)/shard_map/attn_forward/pallas_call | solution.py:507
  163.3 3.0 collective-permute-done.20
  167.7 15.8 %collective-permute-done.21 = bf16[272,1152]{1,0:T(8,128)(2,1)S(1)} collective-permute-done((bf16[272,1152]{1,0:T(8,128)(2,1)S(1)}, bf16[272,1152]{1,0:T(8,128)(2,1)S(1)}, u32[]{:S(2)}, u32[]{:S(2)}) %collective-permute-start.21) | collective-permute-done | bytes 626720 | tf_op jit(solution)/shard_map/ppermute | solution.py:857
  185.3 2.5 constant_dynamic-update-slice_fusion.3
  187.7 2.5 constant_dynamic-update-slice_fusion.2.cot_ref
  190.2 2.9 pad_maximum_fusion.2.mixed_ref
  193.1 12.6 %all-gather.3.cloned.1.call-done = bf16[16,144,1152]{2,1,0:T(8,128)(2,1)} async-done(((bf16[2,144,1152]{2,1,0:T(8,128)(2,1)}), bf16[16,144,1152]{2,1,0:T(8,128)(2,1)}) %all-gather.3.cloned.1.call-update) | async-done | bytes 5308432 | tf_op jit(solution)/shard_map/all_gather | solution.py:1011
  205.7 21.3 %ffn_first.1 = (f32[544,1152]{1,0:T(8,128)}, f32[544,1152]{1,0:T(8,128)}, bf16[2,1088,576]{2,1,0:T(8,128)(2,1)}, bf16[2,1088,576]{2,1,0:T(8,128)(2,1)}) custom-call(s32[8]{0:T(128)} %stack.262.order_ref, bf16[1088,1152]{1,0:T(8,128)(2,1)} %pad_maximum_fusion.2.mixed_ref, bf16[1088,1152]{1,0:T(8,128)(2,1)} %constant_dynamic-update-slice_fusion.2.cot_ref, ...), custom_call_target="tpu_custom_call" | custom-call | flops 8663334912 | bytes 25165824 | tf_op jit(solution)/shard_map/ffn_first/pallas_call | solution.py:399
  227.0 4.9 collective-permute-done.24
  232.0 2.1 add.448
  235.7 22.7 %ffn_second.1 = (f32[544,1152]{1,0:T(8,128)}, f32[544,1152]{1,0:T(8,128)}, bf16[4,144,1152]{2,1,0:T(8,128)(2,1)}, bf16[4,144,1152]{2,1,0:T(8,128)(2,1)}, bf16[2,...) custom-call(s32[8]{0:T(128)} %stack.262.order_ref, bf16[1088,1152]{1,0:T(8,128)(2,1)} %pad_maximum_fusion.2.mixed_ref, ...), custom_call_target="tpu_custom_call" | custom-call | flops 8663334912 | bytes 25165824 | tf_op jit(solution)/shard_map/ffn_second/pallas_call | solution.py:431
  261.5 2.0 collective-permute-done.29
  265.6 31.1 %attn_backward.1 = (f32[272,1152]{1,0:T(8,128)}, f32[272,1152]{1,0:T(8,128)}, bf16[8,144,1152]{2,1,0:T(8,128)(2,1)}, bf16[4,144,1152]{2,1,0:T(8,128)(2,1)}, bf16...) custom-call(s32[1]{0:T(128)} %bitcast.meta_ref, bf16[544,1152]{1,0:T(8,128)(2,1)} %copy-done.2, ...), custom_call_target="tpu_custom_call" | custom-call | flops 5775556608 | bytes 25165824 | tf_op jit(solution)/shard_map/attn_backward/pallas_call | solution.py:600
  302.7 1.7 add_convert_fusion.1
  305.7 1.9 multiply_reduce_fusion.5
  309.0 1.6 add_convert_fusion.2
  312.4 4.3 collective-permute-done.33
  316.7 1.9 collective-permute-done.34
  318.6 2.0 convolution_convert_fusion.1
  321.9 2.4 convolution_convert_fusion
  324.5 2.2 give_tokens.1
  326.8 5.3 collective-permute-done.35
  340.7 31.0 %collective-permute-done.39 = bf16[2,72,1152]{2,1,0:T(8,128)(2,1)S(1)} collective-permute-done((bf16[2,72,1152]{2,1,0:T(8,128)(2,1)S(1)}, bf16[2,72,1152]{2,1,0:T(8,128)(2,1)S(1)}, u32[]{:S(2)}, u32[]{:S(2)}) %collective-permute-start.39) | collective-permute-done | bytes 331808 | tf_op jit(solution)/shard_map/ppermute | solution.py:857
  377.2 2.2 collective-permute-start.46
  381.2 25.7 %collective-permute-done.44.refs_1_ = bf16[258,864]{1,0:T(8,128)(2,1)S(1)} collective-permute-done((bf16[258,864]{1,0:T(8,128)(2,1)S(1)}, bf16[258,864]{1,0:T(8,128)(2,1)S(1)}, u32[]{:S(2)}, u32[]{:S(2)}) %collective-permute-start.44) | collective-permute-done | bytes 445856 | tf_op jit(solution)/shard_map/ppermute | solution.py:857
  407.0 1.7 pad_maximum_fusion.7
  409.6 2.0 collective-permute-done.59
  413.1 2.6 add_convert_fusion
  417.7 10.5 %collective-permute-start.48 = (bf16[2,144,1152]{2,1,0:T(8,128)(2,1)}, bf16[2,144,1152]{2,1,0:T(8,128)(2,1)}, u32[]{:S(2)}, u32[]{:S(2)}) collective-permute-start(bf16[2,144,1152]{2,1,0:T(8,128)(2,1)} %slice.285), channel_id=1, source_target_pairs={{0,2},{1,3},{2,0},{3,1},{4,6},{5,7},{6,4},{7,5},{8,10},{9,11},{10,... | collective-permute-start | bytes 1990664 | tf_op jit(solution)/shard_map/ppermute | solution.py:857
  429.9 4.8 back_tokens.1
  434.7 2.4 fusion.21
  440.1 1.7 multiply_reduce_fusion
  445.1 1.6 add_convert_fusion.4
  448.4 2.1 collective-permute-start.52
  450.7 9.3 %collective-permute-done.53 = bf16[2,72,1152]{2,1,0:T(8,128)(2,1)S(1)} collective-permute-done((bf16[2,72,1152]{2,1,0:T(8,128)(2,1)S(1)}, bf16[2,72,1152]{2,1,0:T(8,128)(2,1)S(1)}, u32[]{:S(2)}, u32[]{:S(2)}) %collective-permute-start.53) | collective-permute-done | bytes 331808 | tf_op jit(solution)/shard_map/ppermute | solution.py:857
  460.1 5.1 collective-permute-done.52
  465.4 3.3 collective-permute-start.54
  469.2 5.7 %collective-permute-done.55 = bf16[72,1152]{1,0:T(8,128)(2,1)S(1)} collective-permute-done((bf16[72,1152]{1,0:T(8,128)(2,1)S(1)}, bf16[72,1152]{1,0:T(8,128)(2,1)S(1)}, u32[]{:S(2)}, u32[]{:S(2)}) %collective-permute-start.55) | collective-permute-done | bytes 165920 | tf_op jit(solution)/shard_map/ppermute | solution.py:857
  490.6 1.9 fusion.51
  495.1 3.0 copy.86
  500.1 2.4 collective-permute-done.62
  504.7 3.6 collective-permute-done.63
  513.3 3.5 multiply_add_fusion
  516.8 2.0 bitcast_add_fusion
  520.4 1.6 bitcast_add_fusion.1
  (429 shorter events, 120.4 us)
Async XLA Ops:
  7.2 198.5 %all-gather.3.cloned.1.call-start = ((), (), s32[]{:S(2)}) async-start(), calls=%async_computation | async-start | bytes 5971968 | tf_op jit(solution)/shard_map/all_gather | solution.py:1011
  12.4 19.8 %collective-permute-start.5 = (bf16[72,1152]{1,0:T(8,128)(2,1)S(1)}, bf16[72,1152]{1,0:T(8,128)(2,1)S(1)}, u32[]{:S(2)}, u32[]{:S(2)}) collective-permute-start(bf16[72,1152]{1,0:T(8,128)(2,1)S(1)} %dynamic-slice_bitcast_fusion.6), channel_id=1, source_target_pairs={{0,4},{1,5},{2,6},{3,7},{4,0},{5,1},{6,2},{7,3},{8,12},{9,13},{10,... | collective-permute-start | bytes 497672 | tf_op jit(solution)/shard_map/ppermute | solution.py:857
  16.5 22.1 %collective-permute-start.9 = (bf16[144,1152]{1,0:T(8,128)(2,1)S(1)}, bf16[144,1152]{1,0:T(8,128)(2,1)S(1)}, u32[]{:S(2)}, u32[]{:S(2)}) collective-permute-start(bf16[144,1152]{1,0:T(8,128)(2,1)S(1)} %copy-done.21), channel_id=1, source_target_pairs={{0,4},{1,5},{2,6},{3,7},{4,0},{5,1},{6,2},{7,3},{8,12},{9,13},{10,... | collective-permute-start | bytes 995336 | tf_op jit(solution)/shard_map/ppermute | solution.py:857
  32.3 13.4 %collective-permute-start.6 = (bf16[2,72,1152]{2,1,0:T(8,128)(2,1)S(1)}, bf16[2,72,1152]{2,1,0:T(8,128)(2,1)S(1)}, u32[]{:S(2)}, u32[]{:S(2)}) collective-permute-start(bf16[2,72,1152]{2,1,0:T(8,128)(2,1)S(1)} %pad_maximum_fusion.23), channel_id=1, source_target_pairs={{0,2},{1,3},{2,0},{3,1},{4,6},{5,7},{6,4},{7,5},{8,10},{9,11},{10,... | collective-permute-start | bytes 995336 | tf_op jit(solution)/shard_map/ppermute | solution.py:857
  33.9 26.6 %collective-permute-start = (bf16[4,258,432]{2,0,1:T(4,128)(2,1)}, bf16[4,258,432]{2,0,1:T(4,128)(2,1)}, u32[]{:S(2)}, u32[]{:S(2)}) collective-permute-start(bf16[4,258,432]{2,0,1:T(4,128)(2,1)} %copy.76), channel_id=1, source_target_pairs={{0,1},{1,0},{2,3},{3,2},{4,5},{5,4},{6,7},{7,6},{8,9},{9,8},{10,11... | collective-permute-start | bytes 2674952 | tf_op jit(solution)/shard_map/ppermute | solution.py:857
  39.6 26.1 %collective-permute-start.10 = (bf16[2,144,1152]{2,1,0:T(8,128)(2,1)}, bf16[2,144,1152]{2,1,0:T(8,128)(2,1)}, u32[]{:S(2)}, u32[]{:S(2)}) collective-permute-start(bf16[2,144,1152]{2,1,0:T(8,128)(2,1)} %pad_maximum_fusion.17), channel_id=1, source_target_pairs={{0,2},{1,3},{2,0},{3,1},{4,6},{5,7},{6,4},{7,5},{8,10},{9,11},{10,... | collective-permute-start | bytes 1990664 | tf_op jit(solution)/shard_map/ppermute | solution.py:857
  46.7 26.6 %collective-permute-start.7 = (bf16[4,72,1152]{2,1,0:T(8,128)(2,1)}, bf16[4,72,1152]{2,1,0:T(8,128)(2,1)}, u32[]{:S(2)}, u32[]{:S(2)}) collective-permute-start(bf16[4,72,1152]{2,1,0:T(8,128)(2,1)} %pad_maximum_fusion.16), channel_id=1, source_target_pairs={{0,1},{1,0},{2,3},{3,2},{4,5},{5,4},{6,7},{7,6},{8,9},{9,8},{10,11... | collective-permute-start | bytes 1990664 | tf_op jit(solution)/shard_map/ppermute | solution.py:857
  48.2 25.1 %collective-permute-start.8 = (bf16[4,72,1152]{2,1,0:T(8,128)(2,1)}, bf16[4,72,1152]{2,1,0:T(8,128)(2,1)S(1)}, u32[]{:S(2)}, u32[]{:S(2)}) collective-permute-start(bf16[4,72,1152]{2,1,0:T(8,128)(2,1)} %pad_maximum_fusion.16), channel_id=1, source_target_pairs={{0,16},{1,17},{2,18},{3,19},{4,20},{5,21},{6,22},{7,23},{8,24},{9,... | collective-permute-start | bytes 1990664 | tf_op jit(solution)/shard_map/ppermute | solution.py:857
  62.3 26.4 %collective-permute-start.1 = (bf16[258,864]{1,0:T(8,128)(2,1)S(1)}, bf16[258,864]{1,0:T(8,128)(2,1)S(1)}, u32[]{:S(2)}, u32[]{:S(2)}) collective-permute-start(bf16[258,864]{1,0:T(8,128)(2,1)S(1)} %get-tuple-element.143), channel_id=1, source_target_pairs={{0,4},{1,5},{2,6},{3,7},{4,0},{5,1},{6,2},{7,3},{8,12},{9,13},{10,... | collective-permute-start | bytes 1337480 | tf_op jit(solution)/shard_map/ppermute | solution.py:857
  65.7 30.4 %collective-permute-start.2 = (bf16[258,864]{1,0:T(8,128)(2,1)S(1)}, bf16[258,864]{1,0:T(8,128)(2,1)S(1)}, u32[]{:S(2)}, u32[]{:S(2)}) collective-permute-start(bf16[258,864]{1,0:T(8,128)(2,1)S(1)} %get-tuple-element.144), channel_id=1, source_target_pairs={{0,2},{1,3},{2,0},{3,1},{4,6},{5,7},{6,4},{7,5},{8,10},{9,11},{10,... | collective-permute-start | bytes 1337480 | tf_op jit(solution)/shard_map/ppermute | solution.py:857
  65.7 31.9 %collective-permute-start.3 = (bf16[258,864]{1,0:T(8,128)(2,1)S(1)}, bf16[258,864]{1,0:T(8,128)(2,1)S(1)}, u32[]{:S(2)}, u32[]{:S(2)}) collective-permute-start(bf16[258,864]{1,0:T(8,128)(2,1)S(1)} %get-tuple-element.145), channel_id=1, source_target_pairs={{0,6},{1,7},{2,4},{3,5},{4,2},{5,3},{6,0},{7,1},{8,14},{9,15},{10,... | collective-permute-start | bytes 1337480 | tf_op jit(solution)/shard_map/ppermute | solution.py:857
  74.3 26.0 %collective-permute-start.11 = (bf16[2,72,1152]{2,1,0:T(8,128)(2,1)S(1)}, bf16[2,72,1152]{2,1,0:T(8,128)(2,1)S(1)}, u32[]{:S(2)}, u32[]{:S(2)}) collective-permute-start(bf16[2,72,1152]{2,1,0:T(8,128)(2,1)S(1)} %slice.196), channel_id=1, source_target_pairs={{0,16},{1,17},{2,18},{3,19},{4,20},{5,21},{6,22},{7,23},{8,24},{9,... | collective-permute-start | bytes 995336 | tf_op jit(solution)/shard_map/ppermute | solution.py:857
  75.9 24.4 %collective-permute-start.12 = (bf16[2,72,1152]{2,1,0:T(8,128)(2,1)S(1)}, bf16[2,72,1152]{2,1,0:T(8,128)(2,1)S(1)}, u32[]{:S(2)}, u32[]{:S(2)}) collective-permute-start(bf16[2,72,1152]{2,1,0:T(8,128)(2,1)S(1)} %slice.197), channel_id=1, source_target_pairs={{0,1},{1,0},{2,3},{3,2},{4,5},{5,4},{6,7},{7,6},{8,9},{9,8},{10,11... | collective-permute-start | bytes 995336 | tf_op jit(solution)/shard_map/ppermute | solution.py:857
  88.7 31.0 %collective-permute-start.15 = (bf16[4,144,1152]{2,1,0:T(8,128)(2,1)S(1)}, bf16[4,144,1152]{2,1,0:T(8,128)(2,1)}, u32[]{:S(2)}, u32[]{:S(2)}) collective-permute-start(bf16[4,144,1152]{2,1,0:T(8,128)(2,1)S(1)} %pad_maximum_fusion.3), channel_id=1, source_target_pairs={{0,1},{1,0},{2,3},{3,2},{4,5},{5,4},{6,7},{7,6},{8,9},{9,8},{10,11... | collective-permute-start | bytes 3981320 | tf_op jit(solution)/shard_map/ppermute | solution.py:857
  96.1 29.0 %collective-permute-start.17 = (bf16[4,144,1152]{2,1,0:T(8,128)(2,1)S(1)}, bf16[4,144,1152]{2,1,0:T(8,128)(2,1)}, u32[]{:S(2)}, u32[]{:S(2)}) collective-permute-start(bf16[4,144,1152]{2,1,0:T(8,128)(2,1)S(1)} %pad_maximum_fusion.3), channel_id=1, source_target_pairs={{0,16},{1,17},{2,18},{3,19},{4,20},{5,21},{6,22},{7,23},{8,24},{9,... | collective-permute-start | bytes 3981320 | tf_op jit(solution)/shard_map/ppermute | solution.py:857
  100.2 2.1 collective-permute-start.4
  105.5 21.1 %collective-permute-start.13 = (f32[272,1152]{1,0:T(8,128)}, f32[272,1152]{1,0:T(8,128)}, u32[]{:S(2)}, u32[]{:S(2)}) collective-permute-start(f32[272,1152]{1,0:T(8,128)} %get-tuple-element.440), channel_id=1, source_target_pairs={{0,8},{1,9},{2,10},{3,11},{4,12},{5,13},{6,14},{7,15},{8,0},{9,1},... | collective-permute-start | bytes 3760136 | tf_op jit(solution)/shard_map/ppermute | solution.py:857
  120.9 15.4 %collective-permute-start.16 = (bf16[2,144,1152]{2,1,0:T(8,128)(2,1)S(1)}, bf16[2,144,1152]{2,1,0:T(8,128)(2,1)S(1)}, u32[]{:S(2)}, u32[]{:S(2)}) collective-permute-start(bf16[2,144,1152]{2,1,0:T(8,128)(2,1)S(1)} %slice.264), channel_id=1, source_target_pairs={{0,16},{1,17},{2,18},{3,19},{4,20},{5,21},{6,22},{7,23},{8,24},{9,... | collective-permute-start | bytes 1990664 | tf_op jit(solution)/shard_map/ppermute | solution.py:857
  126.2 14.6 %collective-permute-start.18 = (bf16[2,144,1152]{2,1,0:T(8,128)(2,1)S(1)}, bf16[2,144,1152]{2,1,0:T(8,128)(2,1)S(1)}, u32[]{:S(2)}, u32[]{:S(2)}) collective-permute-start(bf16[2,144,1152]{2,1,0:T(8,128)(2,1)S(1)} %slice.265), channel_id=1, source_target_pairs={{0,1},{1,0},{2,3},{3,2},{4,5},{5,4},{6,7},{7,6},{8,9},{9,8},{10,11... | collective-permute-start | bytes 1990664 | tf_op jit(solution)/shard_map/ppermute | solution.py:857
  128.9 12.1 %collective-permute-start.14 = (bf16[272,1152]{1,0:T(8,128)(2,1)S(1)}, bf16[272,1152]{1,0:T(8,128)(2,1)S(1)}, u32[]{:S(2)}, u32[]{:S(2)}) collective-permute-start(bf16[272,1152]{1,0:T(8,128)(2,1)S(1)} %pad.16), channel_id=1, source_target_pairs={{0,8},{1,9},{2,10},{3,11},{4,12},{5,13},{6,14},{7,15},{8,0},{9,1},... | collective-permute-start | bytes 1880072 | tf_op jit(solution)/shard_map/ppermute | solution.py:857
  141.1 21.0 %collective-permute-start.19 = (bf16[272,1152]{1,0:T(8,128)(2,1)S(1)}, bf16[272,1152]{1,0:T(8,128)(2,1)S(1)}, u32[]{:S(2)}, u32[]{:S(2)}) collective-permute-start(bf16[272,1152]{1,0:T(8,128)(2,1)S(1)} %get-tuple-element.158), channel_id=1, source_target_pairs={{0,16},{1,17},{2,18},{3,19},{4,20},{5,21},{6,22},{7,23},{8,24},{9,... | collective-permute-start | bytes 1880072 | tf_op jit(solution)/shard_map/ppermute | solution.py:857
  163.3 3.0 collective-permute-start.20
  167.3 16.2 %collective-permute-start.21 = (bf16[272,1152]{1,0:T(8,128)(2,1)S(1)}, bf16[272,1152]{1,0:T(8,128)(2,1)S(1)}, u32[]{:S(2)}, u32[]{:S(2)}) collective-permute-start(bf16[272,1152]{1,0:T(8,128)(2,1)S(1)} %pad.17), channel_id=1, source_target_pairs={{0,16},{1,17},{2,18},{3,19},{4,20},{5,21},{6,22},{7,23},{8,24},{9,... | collective-permute-start | bytes 1880072 | tf_op jit(solution)/shard_map/ppermute | solution.py:857
  167.7 20.0 %collective-permute-start.23 = (bf16[544,1152]{1,0:T(8,128)(2,1)}, bf16[544,1152]{1,0:T(8,128)(2,1)}, u32[]{:S(2)}, u32[]{:S(2)}) collective-permute-start(bf16[544,1152]{1,0:T(8,128)(2,1)} %pad_maximum_fusion.10), channel_id=1, source_target_pairs={{0,8},{1,9},{2,10},{3,11},{4,12},{5,13},{6,14},{7,15},{8,0},{9,1},... | collective-permute-start | bytes 3760136 | tf_op jit(solution)/shard_map/ppermute | solution.py:857
  184.6 5.6 %collective-permute-start.22 = (bf16[544,1152]{1,0:T(8,128)(2,1)}, bf16[544,1152]{1,0:T(8,128)(2,1)}, u32[]{:S(2)}, u32[]{:S(2)}) collective-permute-start(bf16[544,1152]{1,0:T(8,128)(2,1)} %pad_maximum_fusion.11), channel_id=1, source_target_pairs={{0,8},{1,9},{2,10},{3,11},{4,12},{5,13},{6,14},{7,15},{8,0},{9,1},... | collective-permute-start | bytes 3760136 | tf_op jit(solution)/shard_map/ppermute | solution.py:857
  227.0 5.0 collective-permute-start.24
  234.2 24.2 %collective-permute-start.25 = (bf16[272,1152]{1,0:T(8,128)(2,1)S(1)}, bf16[272,1152]{1,0:T(8,128)(2,1)S(1)}, u32[]{:S(2)}, u32[]{:S(2)}) collective-permute-start(bf16[272,1152]{1,0:T(8,128)(2,1)S(1)} %slice.424), channel_id=1, source_target_pairs={{0,16},{1,17},{2,18},{3,19},{4,20},{5,21},{6,22},{7,23},{8,24},{9,... | collective-permute-start | bytes 1880072 | tf_op jit(solution)/shard_map/ppermute | solution.py:857
  258.4 5.0 collective-permute-start.29
  260.0 4.4 collective-permute-start.26
  260.5 36.1 %collective-permute-start.27 = (bf16[4,144,1152]{2,1,0:T(8,128)(2,1)}, bf16[4,144,1152]{2,1,0:T(8,128)(2,1)}, u32[]{:S(2)}, u32[]{:S(2)}) collective-permute-start(bf16[4,144,1152]{2,1,0:T(8,128)(2,1)} %get-tuple-element.176), channel_id=1, source_target_pairs={{0,1},{1,0},{2,3},{3,2},{4,5},{5,4},{6,7},{7,6},{8,9},{9,8},{10,11... | collective-permute-start | bytes 3981320 | tf_op jit(solution)/shard_map/ppermute | solution.py:857
  261.1 35.5 %collective-permute-start.28 = (bf16[2,2,144,1152]{3,2,1,0:T(8,128)(2,1)S(1)}, bf16[2,2,144,1152]{3,2,1,0:T(8,128)(2,1)}, u32[]{:S(2)}, u32[]{:S(2)}) collective-permute-start(bf16[2,2,144,1152]{3,2,1,0:T(8,128)(2,1)S(1)} %copy-done.68), channel_id=1, source_target_pairs={{0,2},{1,3},{2,0},{3,1},{4,6},{5,7},{6,4},{7,5},{8,10},{9,11},{10,... | collective-permute-start | bytes 3981320 | tf_op jit(solution)/shard_map/ppermute | solution.py:857
  263.8 32.9 %collective-permute-start.30 = (bf16[272,1152]{1,0:T(8,128)(2,1)S(1)}, bf16[272,1152]{1,0:T(8,128)(2,1)S(1)}, u32[]{:S(2)}, u32[]{:S(2)}) collective-permute-start(bf16[272,1152]{1,0:T(8,128)(2,1)S(1)} %slice.423), channel_id=1, source_target_pairs={{0,16},{1,17},{2,18},{3,19},{4,20},{5,21},{6,22},{7,23},{8,24},{9,... | collective-permute-start | bytes 1880072 | tf_op jit(solution)/shard_map/ppermute | solution.py:857
  296.7 8.5 %collective-permute-start.31 = (f32[272,1152]{1,0:T(8,128)}, f32[272,1152]{1,0:T(8,128)}, u32[]{:S(2)}, u32[]{:S(2)}) collective-permute-start(f32[272,1152]{1,0:T(8,128)} %get-tuple-element.182), channel_id=1, source_target_pairs={{0,8},{1,9},{2,10},{3,11},{4,12},{5,13},{6,14},{7,15},{8,0},{9,1},... | collective-permute-start | bytes 3760136 | tf_op jit(solution)/shard_map/ppermute | solution.py:857
  299.5 17.2 %collective-permute-start.33 = (bf16[2,144,1152]{2,1,0:T(8,128)(2,1)S(1)}, bf16[2,144,1152]{2,1,0:T(8,128)(2,1)S(1)}, u32[]{:S(2)}, u32[]{:S(2)}) collective-permute-start(bf16[2,144,1152]{2,1,0:T(8,128)(2,1)S(1)} %copy-done.70), channel_id=1, source_target_pairs={{0,16},{1,17},{2,18},{3,19},{4,20},{5,21},{6,22},{7,23},{8,24},{9,... | collective-permute-start | bytes 1990664 | tf_op jit(solution)/shard_map/ppermute | solution.py:857
  300.8 17.7 %collective-permute-start.34 = (bf16[2,144,1152]{2,1,0:T(8,128)(2,1)S(1)}, bf16[2,144,1152]{2,1,0:T(8,128)(2,1)S(1)}, u32[]{:S(2)}, u32[]{:S(2)}) collective-permute-start(bf16[2,144,1152]{2,1,0:T(8,128)(2,1)S(1)} %copy-done.69), channel_id=1, source_target_pairs={{0,1},{1,0},{2,3},{3,2},{4,5},{5,4},{6,7},{7,6},{8,9},{9,8},{10,11... | collective-permute-start | bytes 1990664 | tf_op jit(solution)/shard_map/ppermute | solution.py:857
  304.5 22.3 %collective-permute-start.36 = (bf16[2,144,1152]{2,1,0:T(8,128)(2,1)S(1)}, bf16[2,144,1152]{2,1,0:T(8,128)(2,1)S(1)}, u32[]{:S(2)}, u32[]{:S(2)}) collective-permute-start(bf16[2,144,1152]{2,1,0:T(8,128)(2,1)S(1)} %slice.275), channel_id=1, source_target_pairs={{0,2},{1,3},{2,0},{3,1},{4,6},{5,7},{6,4},{7,5},{8,10},{9,11},{10,... | collective-permute-start | bytes 1990664 | tf_op jit(solution)/shard_map/ppermute | solution.py:857
  308.2 4.0 collective-permute-start.32
  310.7 21.3 %collective-permute-start.35 = (bf16[2,144,1152]{2,1,0:T(8,128)(2,1)S(1)}, bf16[2,144,1152]{2,1,0:T(8,128)(2,1)S(1)}, u32[]{:S(2)}, u32[]{:S(2)}) collective-permute-start(bf16[2,144,1152]{2,1,0:T(8,128)(2,1)S(1)} %slice_bitcast_fusion.2), channel_id=1, source_target_pairs={{0,1},{1,0},{2,3},{3,2},{4,5},{5,4},{6,7},{7,6},{8,9},{9,8},{10,11... | collective-permute-start | bytes 1990664 | tf_op jit(solution)/shard_map/ppermute | solution.py:857
  320.7 3.9 collective-permute-start.37
  332.5 39.2 %collective-permute-start.42 = (bf16[2,144,1152]{2,1,0:T(8,128)(2,1)S(1)}, bf16[2,144,1152]{2,1,0:T(8,128)(2,1)S(1)}, u32[]{:S(2)}, u32[]{:S(2)}) collective-permute-start(bf16[2,144,1152]{2,1,0:T(8,128)(2,1)S(1)} %fusion.17), channel_id=1, source_target_pairs={{0,4},{1,5},{2,6},{3,7},{4,0},{5,1},{6,2},{7,3},{8,12},{9,13},{10,... | collective-permute-start | bytes 1990664 | tf_op jit(solution)/shard_map/ppermute | solution.py:857
  334.4 37.3 %collective-permute-start.41 = (bf16[4,144,1152]{2,1,0:T(8,128)(2,1)S(1)}, bf16[4,144,1152]{2,1,0:T(8,128)(2,1)S(1)}, u32[]{:S(2)}, u32[]{:S(2)}) collective-permute-start(bf16[4,144,1152]{2,1,0:T(8,128)(2,1)S(1)} %pad_maximum_fusion.5), channel_id=1, source_target_pairs={{0,16},{1,17},{2,18},{3,19},{4,20},{5,21},{6,22},{7,23},{8,24},{9,... | collective-permute-start | bytes 3981320 | tf_op jit(solution)/shard_map/ppermute | solution.py:857
  335.6 36.1 %collective-permute-start.38 = (bf16[4,258,432]{2,0,1:T(4,128)(2,1)S(1)}, bf16[4,258,432]{2,0,1:T(4,128)(2,1)S(1)}, u32[]{:S(2)}, u32[]{:S(2)}) collective-permute-start(bf16[4,258,432]{2,0,1:T(4,128)(2,1)S(1)} %copy.78), channel_id=1, source_target_pairs={{0,1},{1,0},{2,3},{3,2},{4,5},{5,4},{6,7},{7,6},{8,9},{9,8},{10,11... | collective-permute-start | bytes 2674952 | tf_op jit(solution)/shard_map/ppermute | solution.py:857
  336.3 35.4 %collective-permute-start.39 = (bf16[2,72,1152]{2,1,0:T(8,128)(2,1)S(1)}, bf16[2,72,1152]{2,1,0:T(8,128)(2,1)S(1)}, u32[]{:S(2)}, u32[]{:S(2)}) collective-permute-start(bf16[2,72,1152]{2,1,0:T(8,128)(2,1)S(1)} %get-tuple-element.451), channel_id=1, source_target_pairs={{0,16},{1,17},{2,18},{3,19},{4,20},{5,21},{6,22},{7,23},{8,24},{9,... | collective-permute-start | bytes 995336 | tf_op jit(solution)/shard_map/ppermute | solution.py:857
  337.8 33.9 %collective-permute-start.40 = (bf16[2,72,1152]{2,1,0:T(8,128)(2,1)S(1)}, bf16[2,72,1152]{2,1,0:T(8,128)(2,1)S(1)}, u32[]{:S(2)}, u32[]{:S(2)}) collective-permute-start(bf16[2,72,1152]{2,1,0:T(8,128)(2,1)S(1)} %get-tuple-element.450), channel_id=1, source_target_pairs={{0,1},{1,0},{2,3},{3,2},{4,5},{5,4},{6,7},{7,6},{8,9},{9,8},{10,11... | collective-permute-start | bytes 995336 | tf_op jit(solution)/shard_map/ppermute | solution.py:857
  372.8 34.1 %collective-permute-start.47 = (bf16[2,144,1152]{2,1,0:T(8,128)(2,1)S(1)}, bf16[2,144,1152]{2,1,0:T(8,128)(2,1)S(1)}, u32[]{:S(2)}, u32[]{:S(2)}) collective-permute-start(bf16[2,144,1152]{2,1,0:T(8,128)(2,1)S(1)} %fusion.7), channel_id=1, source_target_pairs={{0,16},{1,17},{2,18},{3,19},{4,20},{5,21},{6,22},{7,23},{8,24},{9,... | collective-permute-start | bytes 1990664 | tf_op jit(solution)/shard_map/ppermute | solution.py:857
  373.2 33.7 %collective-permute-start.43 = (bf16[4,144,1152]{2,1,0:T(8,128)(2,1)S(1)}, bf16[4,144,1152]{2,1,0:T(8,128)(2,1)S(1)}, u32[]{:S(2)}, u32[]{:S(2)}) collective-permute-start(bf16[4,144,1152]{2,1,0:T(8,128)(2,1)S(1)} %pad_maximum_fusion.6), channel_id=1, source_target_pairs={{0,1},{1,0},{2,3},{3,2},{4,5},{5,4},{6,7},{7,6},{8,9},{9,8},{10,11... | collective-permute-start | bytes 3981320 | tf_op jit(solution)/shard_map/ppermute | solution.py:857
  374.9 31.9 %collective-permute-start.44 = (bf16[258,864]{1,0:T(8,128)(2,1)S(1)}, bf16[258,864]{1,0:T(8,128)(2,1)S(1)}, u32[]{:S(2)}, u32[]{:S(2)}) collective-permute-start(bf16[258,864]{1,0:T(8,128)(2,1)S(1)} %get-tuple-element.205), channel_id=1, source_target_pairs={{0,4},{1,5},{2,6},{3,7},{4,0},{5,1},{6,2},{7,3},{8,12},{9,13},{10,... | collective-permute-start | bytes 1337480 | tf_op jit(solution)/shard_map/ppermute | solution.py:857
  376.4 30.5 %collective-permute-start.45 = (bf16[258,864]{1,0:T(8,128)(2,1)S(1)}, bf16[258,864]{1,0:T(8,128)(2,1)S(1)}, u32[]{:S(2)}, u32[]{:S(2)}) collective-permute-start(bf16[258,864]{1,0:T(8,128)(2,1)S(1)} %get-tuple-element.206), channel_id=1, source_target_pairs={{0,2},{1,3},{2,0},{3,1},{4,6},{5,7},{6,4},{7,5},{8,10},{9,11},{10,... | collective-permute-start | bytes 1337480 | tf_op jit(solution)/shard_map/ppermute | solution.py:857
  377.2 29.7 %collective-permute-start.46 = (bf16[258,864]{1,0:T(8,128)(2,1)S(1)}, bf16[258,864]{1,0:T(8,128)(2,1)S(1)}, u32[]{:S(2)}, u32[]{:S(2)}) collective-permute-start(bf16[258,864]{1,0:T(8,128)(2,1)S(1)} %get-tuple-element.207), channel_id=1, source_target_pairs={{0,6},{1,7},{2,4},{3,5},{4,2},{5,3},{6,0},{7,1},{8,14},{9,15},{10,... | collective-permute-start | bytes 1337480 | tf_op jit(solution)/shard_map/ppermute | solution.py:857
  408.8 25.9 %collective-permute-start.51 = (bf16[2,2,144,1152]{3,2,1,0:T(8,128)(2,1)}, bf16[2,2,144,1152]{3,2,1,0:T(8,128)(2,1)}, u32[]{:S(2)}, u32[]{:S(2)}) collective-permute-start(bf16[2,2,144,1152]{3,2,1,0:T(8,128)(2,1)} %get-tuple-element.447), channel_id=1, source_target_pairs={{0,8},{1,9},{2,10},{3,11},{4,12},{5,13},{6,14},{7,15},{8,0},{9,1},... | collective-permute-start | bytes 3981320 | tf_op jit(solution)/shard_map/ppermute | solution.py:857
  408.9 2.7 collective-permute-start.59
  411.6 64.4 %collective-permute-start.60 = (f32[4,1152]{1,0:T(4,128)S(1)}, f32[4,1152]{1,0:T(4,128)}, u32[]{:S(2)}, u32[]{:S(2)}) collective-permute-start(f32[4,1152]{1,0:T(4,128)S(1)} %fusion.63), channel_id=1, source_target_pairs={{0,16},{1,17},{2,18},{3,19},{4,20},{5,21},{6,22},{7,23},{8,24},{9,... | collective-permute-start | bytes 55304 | tf_op jit(solution)/shard_map/ppermute | solution.py:857
  417.7 26.0 %collective-permute-start.48 = (bf16[2,144,1152]{2,1,0:T(8,128)(2,1)}, bf16[2,144,1152]{2,1,0:T(8,128)(2,1)}, u32[]{:S(2)}, u32[]{:S(2)}) collective-permute-start(bf16[2,144,1152]{2,1,0:T(8,128)(2,1)} %slice.285), channel_id=1, source_target_pairs={{0,2},{1,3},{2,0},{3,1},{4,6},{5,7},{6,4},{7,5},{8,10},{9,11},{10,... | collective-permute-start | bytes 1990664 | tf_op jit(solution)/shard_map/ppermute | solution.py:857
  428.2 16.9 %collective-permute-start.49 = (bf16[4,72,1152]{2,1,0:T(8,128)(2,1)}, bf16[4,72,1152]{2,1,0:T(8,128)(2,1)}, u32[]{:S(2)}, u32[]{:S(2)}) collective-permute-start(bf16[4,72,1152]{2,1,0:T(8,128)(2,1)} %pad_maximum_fusion.19), channel_id=1, source_target_pairs={{0,16},{1,17},{2,18},{3,19},{4,20},{5,21},{6,22},{7,23},{8,24},{9,... | collective-permute-start | bytes 1990664 | tf_op jit(solution)/shard_map/ppermute | solution.py:857
  428.5 16.7 %collective-permute-start.50 = (bf16[4,72,1152]{2,1,0:T(8,128)(2,1)}, bf16[4,72,1152]{2,1,0:T(8,128)(2,1)}, u32[]{:S(2)}, u32[]{:S(2)}) collective-permute-start(bf16[4,72,1152]{2,1,0:T(8,128)(2,1)} %pad_maximum_fusion.20), channel_id=1, source_target_pairs={{0,1},{1,0},{2,3},{3,2},{4,5},{5,4},{6,7},{7,6},{8,9},{9,8},{10,11... | collective-permute-start | bytes 1990664 | tf_op jit(solution)/shard_map/ppermute | solution.py:857
  446.8 13.3 %collective-permute-start.53 = (bf16[2,72,1152]{2,1,0:T(8,128)(2,1)S(1)}, bf16[2,72,1152]{2,1,0:T(8,128)(2,1)S(1)}, u32[]{:S(2)}, u32[]{:S(2)}) collective-permute-start(bf16[2,72,1152]{2,1,0:T(8,128)(2,1)S(1)} %slice.291), channel_id=1, source_target_pairs={{0,2},{1,3},{2,0},{3,1},{4,6},{5,7},{6,4},{7,5},{8,10},{9,11},{10,... | collective-permute-start | bytes 995336 | tf_op jit(solution)/shard_map/ppermute | solution.py:857
  448.4 16.8 %collective-permute-start.52 = (bf16[144,1152]{1,0:T(8,128)(2,1)S(1)}, bf16[144,1152]{1,0:T(8,128)(2,1)S(1)}, u32[]{:S(2)}, u32[]{:S(2)}) collective-permute-start(bf16[144,1152]{1,0:T(8,128)(2,1)S(1)} %slice_bitcast_fusion.4), channel_id=1, source_target_pairs={{0,4},{1,5},{2,6},{3,7},{4,0},{5,1},{6,2},{7,3},{8,12},{9,13},{10,... | collective-permute-start | bytes 995336 | tf_op jit(solution)/shard_map/ppermute | solution.py:857
  465.4 9.6 %collective-permute-start.54 = (bf16[144,1152]{1,0:T(8,128)(2,1)S(1)}, bf16[144,1152]{1,0:T(8,128)(2,1)S(1)}, u32[]{:S(2)}, u32[]{:S(2)}) collective-permute-start(bf16[144,1152]{1,0:T(8,128)(2,1)S(1)} %fusion.27), channel_id=1, source_target_pairs={{0,16},{1,17},{2,18},{3,19},{4,20},{5,21},{6,22},{7,23},{8,24},{9,... | collective-permute-start | bytes 995336 | tf_op jit(solution)/shard_map/ppermute | solution.py:857
  468.7 6.3 %collective-permute-start.55 = (bf16[72,1152]{1,0:T(8,128)(2,1)S(1)}, bf16[72,1152]{1,0:T(8,128)(2,1)S(1)}, u32[]{:S(2)}, u32[]{:S(2)}) collective-permute-start(bf16[72,1152]{1,0:T(8,128)(2,1)S(1)} %slice_bitcast_fusion.5), channel_id=1, source_target_pairs={{0,4},{1,5},{2,6},{3,7},{4,0},{5,1},{6,2},{7,3},{8,12},{9,13},{10,... | collective-permute-start | bytes 497672 | tf_op jit(solution)/shard_map/ppermute | solution.py:857
  475.9 5.3 collective-permute-start.57
  478.0 7.0 %collective-permute-start.56 = (bf16[72,1152]{1,0:T(8,128)(2,1)}, bf16[72,1152]{1,0:T(8,128)(2,1)}, u32[]{:S(2)}, u32[]{:S(2)}) collective-permute-start(bf16[72,1152]{1,0:T(8,128)(2,1)} %fusion.39), channel_id=1, source_target_pairs={{0,16},{1,17},{2,18},{3,19},{4,20},{5,21},{6,22},{7,23},{8,24},{9,... | collective-permute-start | bytes 497672 | tf_op jit(solution)/shard_map/ppermute | solution.py:857
  492.7 5.4 %collective-permute-start.61 = (f32[15,1152]{1,0:T(8,128)S(1)}, f32[15,1152]{1,0:T(8,128)S(1)}, u32[]{:S(2)}, u32[]{:S(2)}) collective-permute-start(f32[15,1152]{1,0:T(8,128)S(1)} %concatenate.87), channel_id=1, source_target_pairs={{0,1},{1,0},{2,3},{3,2},{4,5},{5,4},{6,7},{7,6},{8,9},{9,8},{10,11... | collective-permute-start | bytes 207368 | tf_op jit(solution)/shard_map/ppermute | solution.py:857
  498.1 4.4 collective-permute-start.62
  502.5 5.8 %collective-permute-start.63 = (f32[15,1152]{1,0:T(8,128)S(1)}, f32[15,1152]{1,0:T(8,128)S(1)}, u32[]{:S(2)}, u32[]{:S(2)}) collective-permute-start(f32[15,1152]{1,0:T(8,128)S(1)} %add.495), channel_id=1, source_target_pairs={{0,4},{1,5},{2,6},{3,7},{4,0},{5,1},{6,2},{7,3},{8,12},{9,13},{10,... | collective-permute-start | bytes 207368 | tf_op jit(solution)/shard_map/ppermute | solution.py:857
  (73 other events, 406.3 us)
Sparse Core Ops, SparseCore 0:
  108.8 96.9 all-gather.2

commit v6 on v5

--- a/solution.py
+++ b/solution.py
@@ -348,25 +348,42 @@
             ref[...] += value[number * size : (number + 1) * size]
 
 
-def ffn_first_kernel(order_ref, mixed_ref, cot_ref, *refs):
-    weights, (mixed_a, mixed_b, act_ref, grad_ref) = refs[:4], refs[4:]
+def all_four(refs):
+    return jnp.concatenate([ref[...] for ref in refs], axis=0)
+
+
+def ffn_first_kernel(order_ref, *refs):
+    mixed, cot, weights, parts, (act_ref, grad_ref) = (
+        all_four(refs[:4]),
+        all_four(refs[4:8]),
+        refs[8:12],
+        refs[12:16],
+        refs[16:],
+    )
     up = jnp.concatenate([ref[0, 0] for ref in weights], axis=0)
     down = jnp.concatenate([ref[0, 1] for ref in weights], axis=0)
-    up_input = dot_nt(mixed_ref[...], up)
+    up_input = dot_nt(mixed, up)
     gate = 0.5 * (1.0 + lax.erf(up_input * (1.0 / math.sqrt(2.0))))
     act_ref[0] = (up_input * gate).astype(jnp.bfloat16)
     slope = gate + up_input * (jnp.exp(-0.5 * up_input * up_input) * (1.0 / math.sqrt(2.0 * math.pi)))
-    grad = (dot_nt(cot_ref[...], down) * slope).astype(jnp.bfloat16)
+    grad = (dot_nt(cot, down) * slope).astype(jnp.bfloat16)
     grad_ref[0] = grad
-    accumulate(pl.program_id(0), (mixed_a, mixed_b), dot_nn(grad, up))
-
-
-def ffn_second_kernel(order_ref, mixed_ref, cot_ref, act_ref, grad_ref, *refs):
-    weights, (down_a, down_b, up_near, up_far, down_near, down_far) = refs[:4], refs[4:]
+    accumulate(pl.program_id(0), parts, dot_nn(grad, up))
+
+
+def ffn_second_kernel(order_ref, *refs):
+    mixed, cot, (act_ref, grad_ref), weights, parts, (up_near, up_far, down_near, down_far) = (
+        all_four(refs[:4]),
+        all_four(refs[4:8]),
+        refs[8:10],
+        refs[10:14],
+        refs[14:18],
+        refs[18:],
+    )
     step = pl.program_id(0)
     down = jnp.concatenate([ref[0, 0] for ref in weights], axis=0)
-    grad_up = dot_tn(grad_ref[0], mixed_ref[...]).astype(jnp.bfloat16)
-    grad_down = dot_tn(act_ref[0], cot_ref[...]).astype(jnp.bfloat16)
+    grad_up = dot_tn(grad_ref[0], mixed).astype(jnp.bfloat16)
+    grad_down = dot_tn(act_ref[0], cot).astype(jnp.bfloat16)
     for j, ref in enumerate((up_near, up_far)):
 
         @pl.when(step == j)
@@ -376,34 +393,33 @@
     halves = grad_down.reshape((2,) + down_near.shape[1:])
     down_near[0] = halves[0]
     down_far[0] = halves[1]
-    accumulate(step, (down_a, down_b), dot_nn(act_ref[0], down))
+    accumulate(step, parts, dot_nn(act_ref[0], down))
 
 
 def ffn_specs(tokens, rows):
-    whole = pl.BlockSpec((tokens, D), lambda t, m: (0, 0))
-    half = pl.BlockSpec((tokens // 2, D), lambda t, m: (0, 0))
+    image = pl.BlockSpec((tokens // 4, D), lambda t, m: (0, 0))
     units = pl.BlockSpec((1, tokens, 4 * rows), lambda t, m: (t, 0, 0))
-    return whole, half, units
+    return image, units
 
 
 def ffn_first(order, mixed, cot, weights):
     count, _, rows, _ = weights.shape
-    tokens = mixed.shape[0]
-    whole, half, units = ffn_specs(tokens, rows)
+    tokens = 4 * mixed[0].shape[0]
+    image, units = ffn_specs(tokens, rows)
 
     def weight_spec(slot):
         return pl.BlockSpec((1, 2, rows, D), lambda t, m: (m[4 * t + slot], 0, 0, 0))
 
-    part = jax.ShapeDtypeStruct((tokens // 2, D), jnp.float32)
+    part = jax.ShapeDtypeStruct((tokens // 4, D), jnp.float32)
     hidden = jax.ShapeDtypeStruct((count // 4, tokens, 4 * rows), jnp.bfloat16)
-    return pl.pallas_call(
+    *parts, act, grad = pl.pallas_call(
         ffn_first_kernel,
-        out_shape=[part] * 2 + [hidden] * 2,
+        out_shape=[part] * 4 + [hidden] * 2,
         grid_spec=pltpu.PrefetchScalarGridSpec(
             num_scalar_prefetch=1,
             grid=(count // 4,),
-            in_specs=[whole, whole] + [weight_spec(slot) for slot in range(4)],
-            out_specs=[half] * 2 + [units] * 2,
+            in_specs=[image] * 8 + [weight_spec(slot) for slot in range(4)],
+            out_specs=[image] * 4 + [units] * 2,
         ),
         compiler_params=pltpu.CompilerParams(
             dimension_semantics=("arbitrary",), vmem_limit_bytes=56 * 1024 * 1024
@@ -412,30 +428,31 @@
             flops=6 * tokens * D * count * rows, transcendentals=0, bytes_accessed=24 * 1024 * 1024
         ),
         name="ffn_first",
-    )(order, mixed, cot, *([weights] * 4))
+    )(order, *mixed, *cot, *([weights] * 4))
+    return parts, act, grad
 
 
 def ffn_second(order, mixed, cot, act, grad, weights):
     count, _, rows, _ = weights.shape
-    tokens = mixed.shape[0]
-    whole, half, units = ffn_specs(tokens, rows)
+    tokens = 4 * mixed[0].shape[0]
+    image, units = ffn_specs(tokens, rows)
 
     def weight_spec(slot):
         return pl.BlockSpec((1, 1, rows, D), lambda t, m: (m[4 * t + slot], 1, 0, 0))
 
-    part = jax.ShapeDtypeStruct((tokens // 2, D), jnp.float32)
+    part = jax.ShapeDtypeStruct((tokens // 4, D), jnp.float32)
     side = jax.ShapeDtypeStruct((4, rows, D), jnp.bfloat16)
     turn = jax.ShapeDtypeStruct((2, 2, rows, D), jnp.bfloat16)
     side_block = pl.BlockSpec((4, rows, D), lambda t, m: (0, 0, 0))
     turn_block = pl.BlockSpec((1, 2, rows, D), lambda t, m: (t, 0, 0, 0))
-    return pl.pallas_call(
+    *outs, up_near, up_far, down_near, down_far = pl.pallas_call(
         ffn_second_kernel,
-        out_shape=[part] * 2 + [side] * 2 + [turn] * 2,
+        out_shape=[part] * 4 + [side] * 2 + [turn] * 2,
         grid_spec=pltpu.PrefetchScalarGridSpec(
             num_scalar_prefetch=1,
             grid=(count // 4,),
-            in_specs=[whole, whole, units, units] + [weight_spec(slot) for slot in range(4)],
-            out_specs=[half] * 2 + [side_block] * 2 + [turn_block] * 2,
+            in_specs=[image] * 8 + [units, units] + [weight_spec(slot) for slot in range(4)],
+            out_specs=[image] * 4 + [side_block] * 2 + [turn_block] * 2,
         ),
         compiler_params=pltpu.CompilerParams(
             dimension_semantics=("arbitrary",), vmem_limit_bytes=56 * 1024 * 1024
@@ -444,7 +461,8 @@
             flops=6 * tokens * D * count * rows, transcendentals=0, bytes_accessed=24 * 1024 * 1024
         ),
         name="ffn_second",
-    )(order, mixed, cot, act, grad, *([weights] * 4))
+    )(order, *mixed, *cot, act, grad, *([weights] * 4))
+    return outs, up_near, up_far, down_near, down_far
 
 
 def soft(q, k):
@@ -475,10 +493,16 @@
     )
 
 
-def attn_forward_kernel(meta_ref, normed_ref, qk_ref, vo_ref, part_a, part_b, qkv_ref, attended_ref):
+def both(first_ref, second_ref):
+    return jnp.concatenate([first_ref[...], second_ref[...]], axis=0)
+
+
+def attn_forward_kernel(
+    meta_ref, normed_a, normed_b, qk_ref, vo_ref, part_a, part_b, qkv_ref, attended_ref
+):
     step = pl.program_id(0)
     weights, out_weight = head_weights(qk_ref, vo_ref)
-    qkv_ref[0] = dot_nt(normed_ref[...], weights).astype(jnp.bfloat16)
+    qkv_ref[0] = dot_nt(both(normed_a, normed_b), weights).astype(jnp.bfloat16)
     for head in range(GROUP):
         q_at, k_at, v_at = head_columns(head)
         for image in range(2):
@@ -502,7 +526,7 @@
 
 def attn_forward(meta, normed, weights):
     heads, rows = weights.shape[1:3]
-    tokens = normed.shape[0]
+    tokens = 2 * normed[0].shape[0]
     whole, half, qk, vo, qkv, att = attn_specs(rows, tokens)
     return pl.pallas_call(
         attn_forward_kernel,
@@ -515,7 +539,7 @@
         grid_spec=pltpu.PrefetchScalarGridSpec(
             num_scalar_prefetch=1,
             grid=(heads // GROUP,),
-            in_specs=[whole, qk, vo],
+            in_specs=[half, half, qk, vo],
             out_specs=[half, half, qkv, att],
         ),
         compiler_params=pltpu.CompilerParams(
@@ -523,13 +547,15 @@
         ),
         cost_estimate=pl.CostEstimate(flops=0, transcendentals=0, bytes_accessed=1024 * 1024),
         name="attn_forward",
-    )(meta, normed, weights, weights)
+    )(meta, *normed, weights, weights)
 
 
 def attn_backward_kernel(
     meta_ref,
-    normed_ref,
-    low_ref,
+    normed_first,
+    normed_second,
+    low_first,
+    low_second,
     qk_ref,
     vo_ref,
     qkv_ref,
@@ -544,8 +570,8 @@
     out_s,
 ):
     step = pl.program_id(0)
-    normed = normed_ref[...]
-    low = low_ref[...]
+    normed = both(normed_first, normed_second)
+    low = both(low_first, low_second)
     weights, out_weight = head_weights(qk_ref, vo_ref)
     out_s[...] = dot_nt(low, out_weight).astype(jnp.bfloat16)
     for head in range(GROUP):
@@ -591,7 +617,7 @@
 
 def attn_backward(meta, normed, low, weights, qkv_kept, attended):
     heads, rows = weights.shape[1:3]
-    tokens = normed.shape[0]
+    tokens = 2 * normed[0].shape[0]
     whole, half, qk, vo, qkv, att = attn_specs(rows, tokens)
 
     def fixed(size):
@@ -610,7 +636,7 @@
         grid_spec=pltpu.PrefetchScalarGridSpec(
             num_scalar_prefetch=1,
             grid=(heads // GROUP,),
-            in_specs=[whole, whole, qk, vo, qkv, att],
+            in_specs=[half, half, half, half, qk, vo, qkv, att],
             out_specs=[
                 half,
                 half,
@@ -633,7 +659,7 @@
             bytes_accessed=24 * 1024 * 1024,
         ),
         name="attn_backward",
-    )(meta, normed, low, weights, weights, qkv_kept, attended)
+    )(meta, *normed, *low, weights, weights, qkv_kept, attended)
 
 
 def by_narrow(blocks, flag_refs):
@@ -1008,9 +1034,10 @@
     attn_beside = over_y(attn_line)
     attn_across = over_x(attn_line)
 
+    token_blocks, ffn_block = tie(token_blocks, ffn_block)
     ffn_full = lax.all_gather(ffn_block[None], "narrow", tiled=True)
     mine, give, cot_pad = take_tokens(flags, token_blocks)
-    flat = jnp.concatenate([mine, core(give)])
+    flat = (mine, core(give))
     cot_own = cot_pad[:SEQ]
     attn_corner_x = over_x(attn_beside[:half])
     attn_corner_y = over_y(attn_across[half:])
@@ -1024,19 +1051,19 @@
 
     def both_images(own):
         own = padded(own)
-        return jnp.concatenate([own, core(own)])
+        return own, core(own)
 
     def core_sum(kept, given):
         return (kept + core(given))[:SEQ]
 
-    skip_part = matmul(flat, skip_mat, "rc,cd->rd")
-    hidden_in = core_sum(skip_part[:PAD], skip_part[PAD:])
+    skip_give = matmul(flat[1], skip_mat, "rc,cd->rd")
+    hidden_in = core_sum(matmul(flat[0], skip_mat, "rc,cd->rd"), skip_give)
     unit_one, inverse_one = unit_parts(hidden_in)
     normed = both_images((unit_one * norm_gain[0] + norm_bias[0]).astype(bf16))
 
     attn_corner = jnp.concatenate([attn_corner_x, attn_corner_y])
     normed, cot_pad, attn_corner = tie(normed, cot_pad, attn_corner)
-    cot_pair = jnp.concatenate([cot_pad, over_x(cot_pad)])
+    cot_pair = (cot_pad, over_x(cot_pad))
     attn_full = jnp.stack(
         [
             jnp.concatenate([attn_line, attn_beside]),
@@ -1048,27 +1075,28 @@
     middle = hidden_in + core_sum(attn_a, attn_b)
     unit_two, inverse_two = unit_parts(middle)
     mixed_own = padded((unit_two * norm_gain[1] + norm_bias[1]).astype(bf16))
-    mixed_pair = jnp.concatenate([mixed_own, over_x(mixed_own)])
-    mixed = jnp.concatenate([mixed_pair, core(mixed_pair)])
-    cot = jnp.concatenate([cot_pair, core(cot_pair)])
-
-    mixed_a, mixed_b, act, act_grad = ffn_first(order, mixed, cot, ffn_full)
-    mixed_sum = mixed_a + core(mixed_b)
-    mixed_far = over_x(mixed_sum[PAD:].astype(bf16))
-    mixed_sum, act = tie(mixed_sum, act)
-    down_a, down_b, up_near, up_give, down_near, down_give = ffn_second(
+    mixed_far = over_x(mixed_own)
+    mixed = (mixed_own, mixed_far, core(mixed_own), core(mixed_far))
+    cot = (*cot_pair, core(cot_pair[0]), core(cot_pair[1]))
+
+    mixed_parts, act, act_grad = ffn_first(order, mixed, cot, ffn_full)
+    mixed_far = mixed_parts[1] + core(mixed_parts[3])
+    mixed_far, act = tie(mixed_far, act)
+    mixed_far = over_x(mixed_far.astype(bf16))
+    mixed_sum = mixed_parts[0] + core(mixed_parts[2])
+    down_parts, up_near, up_give, down_near, down_give = ffn_second(
         order, mixed, cot, act, act_grad, ffn_full
     )
     ffn_far_up = over_y(up_give)
     ffn_down_one = xor_z(down_give, 1)
 
-    mixed_far, down_b = tie(mixed_far, down_b)
-    down_sum = down_a + core(down_b)
-    down_far = over_x(down_sum[PAD:].astype(bf16))
+    mixed_far, down_parts = tie(mixed_far, down_parts)
+    down_far = over_x((down_parts[1] + core(down_parts[3])).astype(bf16))
+    down_sum = down_parts[0] + core(down_parts[2])
     back_middle, gain_two, bias_two = norm_back_own(
         unit_two,
         inverse_two,
-        (mixed_sum[:PAD] + mixed_far.astype(f32))[:SEQ],
+        (mixed_sum + mixed_far.astype(f32))[:SEQ],
         norm_gain[1],
     )
     grad_middle = cot_own.astype(f32) + back_middle
@@ -1086,22 +1114,27 @@
     ffn_down_far = over_y(ffn_down[1])
     ffn_up, ffn_up_give = halves_z(add_low(up_near, ffn_far_up))
     ffn_up_one = xor_z(ffn_up_give, 1)
-    block_own = (middle + (down_sum[:PAD] + down_far.astype(f32))[:SEQ]).astype(bf16)
+    block_own = (middle + (down_sum + down_far.astype(f32))[:SEQ]).astype(bf16)
     back_hidden, gain_one, bias_one = norm_back_own(
         unit_one, inverse_one, core_sum(normed_a, normed_b), norm_gain[0]
     )
     hidden_low = both_images((grad_middle + back_hidden).astype(bf16))
-    hidden_low, attn_from_x, attn_from_y = tie(hidden_low, attn_from_x, attn_from_y)
-    token_grad = matmul(hidden_low, skip_mat, "rd,cd->rc").astype(bf16)
+    hidden_low, attn_from_x = tie(hidden_low, attn_from_x)
+    token_grads = [matmul(low, skip_mat, "rd,cd->rc").astype(bf16) for low in hidden_low]
     back_near, back_give = give_tokens(
-        flags, token_grad[:PAD], core(token_grad[PAD:]), padded(block_own)
-    )
-    grad_skip = matmul(flat, hidden_low, "rc,rd->cd").astype(bf16)
+        flags, token_grads[0], core(token_grads[1]), padded(block_own)
+    )
+    grad_skip = matmul(
+        jnp.concatenate(flat), jnp.concatenate(hidden_low), "rc,rd->cd"
+    ).astype(bf16)
     grad_skip = grad_skip.reshape(narrow_count, 2, feat // 2, D)
     skip_own, skip_other = pick(grad_skip, xi, 1), pick(grad_skip, 1 - xi, 1)
 
-    attn_from_x, attn_from_y, ffn_down_far, ffn_up_one, back_give, skip_own, skip_other = tie(
-        attn_from_x, attn_from_y, ffn_down_far, ffn_up_one, back_give, skip_own, skip_other
+    norm_sums = jnp.stack([gain_one, gain_two, bias_one, bias_two])
+    norm_sums = norm_sums + core(norm_sums)
+
+    attn_from_y, ffn_down_far, ffn_up_one, back_give, skip_own, skip_other, norm_sums = tie(
+        attn_from_y, ffn_down_far, ffn_up_one, back_give, skip_own, skip_other, norm_sums
     )
     back_far = over_y(back_give)
     skip_from_x = over_x(skip_other[ZS : ZS + half])
@@ -1157,7 +1190,10 @@
     skip_one = xor_z(skip_give, 1)
     grad_stream, grad_skip_in, block_out = [part.T for part in back_out]
 
-    attn_two, skip_one = tie(attn_two, skip_one)
+    norm_far = over_x(norm_sums)
+
+    attn_two, skip_one, norm_far = tie(attn_two, skip_one, norm_far)
+    norm_sums = norm_sums + norm_far
     attn_own = add_low(attn_total[0], attn_two)
     attn_x = over_x(attn_own)
     skip_total = add_low(skip_total, skip_one)
@@ -1183,9 +1219,6 @@
     (skip_all,) = tie(in_order(skip_pair, core(skip_pair)))
     grad_skip_rows = skip_all.reshape(2 * feat, D)
 
-    norm_sums = jnp.stack([gain_one, gain_two, bias_one, bias_two])
-    norm_sums = norm_sums + core(norm_sums)
-    norm_sums = norm_sums + over_x(norm_sums)
     new_row_skip, *skip_sums = statistics(grad_skip_rows, row_skip.reshape(-1))
     sums = list(skip_sums) + sums + list(ffn_sums)
     totals = all_narrow(

time: 537 us -> 525 us (0.978)
  other arithmetic: 79.5 us -> 73.9 us
    all_gather x1, waiting for transfers between devices: 12.6 us -> 0.01 us  [chips(): ffn_full = lax.all_gather(ffn_block[None], 'narrow', tiled=True)]
    ppermute x64 -> x68, waiting for transfers between devices: 197 us -> 207 us  [send(): return lax.ppermute(value, axes, perm(move))]
    concatenate x6 -> x0, other arithmetic: 6.69 us -> none  [the longest x1 2.94 us: chips(): mixed = jnp.concatenate([mixed_pair, core(mixed_pair)])]
    unnamed x146 -> x172, local copies, waits for them, and re-layouts: 14.4 us -> 10.6 us
    ppermute x64 -> x68, starting transfers between devices: 75.9 us -> 73.1 us  [send(): return lax.ppermute(value, axes, perm(move))]
  transfers between devices with their start and end apart: 65 -> 69, of which waited for: 30 -> 30; matrix products, arithmetic and copies ran while one was open for 17% -> 16% of each run, Pallas kernels for 15% -> 15%
where the time goes in v6:
time: 525 us; the launch traced here: 518 us
  waiting for transfers between devices  207 us (39%)
  Pallas kernels  103 us (20%)
  other arithmetic  73.9 us (14%)
  starting transfers between devices  73.2 us (14%)
  local copies, waits for them, and re-layouts  36.6 us (7%)
  between operations  17.6 us (3%)
  matrix products  6.8 us (1%)
    ppermute x68, waiting for transfers between devices, send(): return lax.ppermute(value, axes, perm(move))  207 us
    ppermute x68, starting transfers between devices, send(): return lax.ppermute(value, axes, perm(move))  73.1 us
    pallas_call x1, Pallas kernels, attn_backward(): pl.pallas_call(attn_backward_kernel, out_shape=[jax.ShapeDtypeStruct((tok...  31.2 us
    pallas_call x1, Pallas kernels, ffn_second(): pl.pallas_call(ffn_second_kernel, out_shape=[part] * 4 + [side] * 2 + [tu...  22.6 us
    pallas_call x1, Pallas kernels, ffn_first(): pl.pallas_call(ffn_first_kernel, out_shape=[part] * 4 + [hidden] * 2, gri...  21.3 us
    pallas_call x1, Pallas kernels, attn_forward(): pl.pallas_call(attn_forward_kernel, out_shape=[jax.ShapeDtypeStruct((toke...  14.7 us
    unnamed x172, local copies, waits for them, and re-layouts  10.6 us
  transfers between devices with their start and end apart: 69, of which 30 were waited for; matrix products, arithmetic and copies ran while one was open for 16% of the time, Pallas kernels for 15%

profile of v6, /device:TPU:0, one launch (start us, length us, event | category | flops | bytes accessed | tf_op | source)
XLA Modules:
  0.0 518.3 jit_solution(2549791009152043124)
XLA Ops:
  11.6 2.2 pack_tokens.1
  13.9 4.1 collective-permute-start.4
  21.3 12.4 %collective-permute-done.4 = bf16[72,1152]{1,0:T(8,128)(2,1)S(1)} collective-permute-done((bf16[72,1152]{1,0:T(8,128)(2,1)S(1)}, bf16[72,1152]{1,0:T(8,128)(2,1)S(1)}, u32[]{:S(2)}, u32[]{:S(2)}) %collective-permute-start.4) | collective-permute-done | bytes 165920 | tf_op jit(solution)/shard_map/ppermute | solution.py:883
  33.8 6.2 %collective-permute-done.8 = bf16[144,1152]{1,0:T(8,128)(2,1)S(1)} collective-permute-done((bf16[144,1152]{1,0:T(8,128)(2,1)S(1)}, bf16[144,1152]{1,0:T(8,128)(2,1)S(1)}, u32[]{:S(2)}, u32[]{:S(2)}) %collective-permute-start.8) | collective-permute-done | bytes 331808 | tf_op jit(solution)/shard_map/ppermute | solution.py:883
  40.9 6.3 %collective-permute-done.5 = bf16[2,72,1152]{2,1,0:T(8,128)(2,1)S(1)} collective-permute-done((bf16[2,72,1152]{2,1,0:T(8,128)(2,1)S(1)}, bf16[2,72,1152]{2,1,0:T(8,128)(2,1)S(1)}, u32[]{:S(2)}, u32[]{:S(2)}) %collective-permute-start.5) | collective-permute-done | bytes 331808 | tf_op jit(solution)/shard_map/ppermute | solution.py:883
  47.3 1.6 collective-permute-start.6
  54.6 2.5 collective-permute-start.2
  59.1 5.2 collective-permute-done.9
  68.4 2.1 collective-permute-start.11
  71.2 2.4 collective-permute-start.10
  74.5 3.5 collective-permute-done.1.refs_1_
  78.6 13.2 %collective-permute-done.2.refs_2_ = bf16[258,864]{1,0:T(8,128)(2,1)S(1)} collective-permute-done((bf16[258,864]{1,0:T(8,128)(2,1)S(1)}, bf16[258,864]{1,0:T(8,128)(2,1)S(1)}, u32[]{:S(2)}, u32[]{:S(2)}) %collective-permute-start.2) | collective-permute-done | bytes 445856 | tf_op jit(solution)/shard_map/ppermute | solution.py:883
  94.7 2.6 take_tokens.1
  97.5 1.6 maximum_bitcast_fusion.3
  103.2 6.5 %collective-permute-done.17 = bf16[4,144,1152]{2,1,0:T(8,128)(2,1)} collective-permute-done((bf16[4,144,1152]{2,1,0:T(8,128)(2,1)}, bf16[4,144,1152]{2,1,0:T(8,128)(2,1)}, u32[]{:S(2)}, u32[]{:S(2)}) %collective-permute-start.17) | collective-permute-done | bytes 1327136 | tf_op jit(solution)/shard_map/ppermute | solution.py:883
  111.2 20.0 %collective-permute-done.15 = bf16[4,144,1152]{2,1,0:T(8,128)(2,1)} collective-permute-done((bf16[4,144,1152]{2,1,0:T(8,128)(2,1)}, bf16[4,144,1152]{2,1,0:T(8,128)(2,1)}, u32[]{:S(2)}, u32[]{:S(2)}) %collective-permute-start.15) | collective-permute-done | bytes 1327136 | tf_op jit(solution)/shard_map/ppermute | solution.py:883
  132.3 1.6 collective-permute-start.16
  136.1 1.9 maximum_bitcast_fusion
  138.0 12.8 %collective-permute-done.18 = bf16[2,144,1152]{2,1,0:T(8,128)(2,1)S(1)} collective-permute-done((bf16[2,144,1152]{2,1,0:T(8,128)(2,1)S(1)}, bf16[2,144,1152]{2,1,0:T(8,128)(2,1)S(1)}, u32[]{:S(2)}, u32[]{:S(2)}) %collective-permute-start.18) | collective-permute-done | bytes 663584 | tf_op jit(solution)/shard_map/ppermute | solution.py:883
  152.4 1.6 maximum_bitcast_fusion.1
  154.0 2.9 pad_maximum_fusion.qk_ref.vo_ref
  156.9 14.7 %attn_forward.1 = (f32[272,1152]{1,0:T(8,128)S(1)}, f32[272,1152]{1,0:T(8,128)S(1)}, bf16[2,544,864]{2,1,0:T(8,128)(2,1)}, bf16[2,544,288]{2,1,0:T(8,128)(2,1)S(1)}) custom-call(s32[1]{0:T(128)} %bitcast.meta_ref, bf16[272,1152]{1,0:T(8,128)(2,1)S(1)} %pad.16.normed_a.normed_first, bf16[272,1152]{1,0:T(8,128)(2,1)S(1)} %collective-permute-done.14.normed_b.normed_second, ...), custom_call_target="tpu_custom_call" | custom-call | bytes 1048576 | tf_op jit(solution)/shard_map/attn_forward/pallas_call | solution.py:531
  171.7 2.9 collective-permute-done.20
  177.6 15.2 %collective-permute-done.21.refs_1_ = bf16[272,1152]{1,0:T(8,128)(2,1)} collective-permute-done((bf16[272,1152]{1,0:T(8,128)(2,1)}, bf16[272,1152]{1,0:T(8,128)(2,1)}, u32[]{:S(2)}, u32[]{:S(2)}) %collective-permute-start.21) | collective-permute-done | bytes 626720 | tf_op jit(solution)/shard_map/ppermute | solution.py:883
  193.5 1.8 collective-permute-done.23.refs_3_
  195.3 21.3 %ffn_first.1 = (f32[272,1152]{1,0:T(8,128)}, f32[272,1152]{1,0:T(8,128)}, f32[272,1152]{1,0:T(8,128)}, f32[272,1152]{1,0:T(8,128)}, bf16[2,1088,576]{2,1,0:T(8,128)(2,1)}, /*index=5*/bf16[2,1088,576]{2,1,0:T(8,128)(2,1)}) custom-call(s32[8]{0:T(128)} %stack.265.order_ref, bf16[272,1152]{1,0:T(8,128)(2,1)} %pad.17.refs_0_, ...), custom_call_target="tpu_custom_call" | custom-call | flops 8663334912 | bytes 25165824 | tf_op jit(solution)/shard_map/ffn_first/pallas_call | solution.py:415
  217.1 2.7 collective-permute-done.27
  222.1 22.6 %ffn_second.1 = (f32[272,1152]{1,0:T(8,128)}, f32[272,1152]{1,0:T(8,128)}, f32[272,1152]{1,0:T(8,128)}, f32[272,1152]{1,0:T(8,128)}, bf16[4,144,1152]{2,1,0:T(8,...) custom-call(s32[8]{0:T(128)} %stack.265.order_ref, ...), custom_call_target="tpu_custom_call" | custom-call | flops 8663334912 | bytes 25165824 | tf_op jit(solution)/shard_map/ffn_second/pallas_call | solution.py:448
  244.6 2.6 collective-permute-start.30
  252.7 31.2 %attn_backward.1 = (f32[272,1152]{1,0:T(8,128)}, f32[272,1152]{1,0:T(8,128)}, bf16[8,144,1152]{2,1,0:T(8,128)(2,1)}, bf16[4,144,1152]{2,1,0:T(8,128)(2,1)}, bf16...) custom-call(s32[1]{0:T(128)} %bitcast.meta_ref, bf16[272,1152]{1,0:T(8,128)(2,1)} %copy-done.2, ...), custom_call_target="tpu_custom_call" | custom-call | flops 5775556608 | bytes 25165824 | tf_op jit(solution)/shard_map/attn_backward/pallas_call | solution.py:626
  287.0 1.7 add_convert_fusion.2
  288.8 1.7 collective-permute-start.35
  294.7 1.8 add_convert_fusion.1
  296.6 2.1 collective-permute-start.36
  298.7 8.6 %collective-permute-done.39 = bf16[2,144,1152]{2,1,0:T(8,128)(2,1)S(1)} collective-permute-done((bf16[2,144,1152]{2,1,0:T(8,128)(2,1)S(1)}, bf16[2,144,1152]{2,1,0:T(8,128)(2,1)S(1)}, u32[]{:S(2)}, u32[]{:S(2)}) %collective-permute-start.39) | collective-permute-done | bytes 663584 | tf_op jit(solution)/shard_map/ppermute | solution.py:883
  309.7 2.4 convolution_convert_fusion
  312.4 2.2 give_tokens.1
  314.6 3.5 collective-permute-done.35
  320.0 1.7 collective-permute-start.45
  323.8 4.3 collective-permute-start.47
  329.9 20.9 %collective-permute-done.45 = bf16[2,72,1152]{2,1,0:T(8,128)(2,1)S(1)} collective-permute-done((bf16[2,72,1152]{2,1,0:T(8,128)(2,1)S(1)}, bf16[2,72,1152]{2,1,0:T(8,128)(2,1)S(1)}, u32[]{:S(2)}, u32[]{:S(2)}) %collective-permute-start.45) | collective-permute-done | bytes 331808 | tf_op jit(solution)/shard_map/ppermute | solution.py:883
  350.9 5.0 collective-permute-done.47
  357.9 1.7 collective-permute-start.48
  360.2 4.3 collective-permute-start.49
  369.0 17.6 %collective-permute-done.49.refs_1_ = bf16[258,864]{1,0:T(8,128)(2,1)S(1)} collective-permute-done((bf16[258,864]{1,0:T(8,128)(2,1)S(1)}, bf16[258,864]{1,0:T(8,128)(2,1)S(1)}, u32[]{:S(2)}, u32[]{:S(2)}) %collective-permute-start.49) | collective-permute-done | bytes 445856 | tf_op jit(solution)/shard_map/ppermute | solution.py:883
  386.6 8.7 %collective-permute-done.50.refs_2_ = bf16[258,864]{1,0:T(8,128)(2,1)S(1)} collective-permute-done((bf16[258,864]{1,0:T(8,128)(2,1)S(1)}, bf16[258,864]{1,0:T(8,128)(2,1)S(1)}, u32[]{:S(2)}, u32[]{:S(2)}) %collective-permute-start.50) | collective-permute-done | bytes 445856 | tf_op jit(solution)/shard_map/ppermute | solution.py:883
  395.3 1.8 pad_maximum_fusion.6
  397.4 2.6 add_convert_fusion
  402.0 9.6 %collective-permute-start.53 = (bf16[2,144,1152]{2,1,0:T(8,128)(2,1)}, bf16[2,144,1152]{2,1,0:T(8,128)(2,1)}, u32[]{:S(2)}, u32[]{:S(2)}) collective-permute-start(bf16[2,144,1152]{2,1,0:T(8,128)(2,1)} %slice.246), channel_id=1, source_target_pairs={{0,2},{1,3},{2,0},{3,1},{4,6},{5,7},{6,4},{7,5},{8,10},{9,11},{10,... | collective-permute-start | bytes 1990664 | tf_op jit(solution)/shard_map/ppermute | solution.py:883
  411.6 1.6 collective-permute-start.54
  413.7 4.7 back_tokens.1
  418.4 2.4 fusion.29
  434.0 1.8 collective-permute-start.58
  436.0 11.9 %collective-permute-done.57 = bf16[144,1152]{1,0:T(8,128)(2,1)S(1)} collective-permute-done((bf16[144,1152]{1,0:T(8,128)(2,1)S(1)}, bf16[144,1152]{1,0:T(8,128)(2,1)S(1)}, u32[]{:S(2)}, u32[]{:S(2)}) %collective-permute-start.57) | collective-permute-done | bytes 331808 | tf_op jit(solution)/shard_map/ppermute | solution.py:883
  451.0 7.7 %collective-permute-done.61 = bf16[72,1152]{1,0:T(8,128)(2,1)S(1)} collective-permute-done((bf16[72,1152]{1,0:T(8,128)(2,1)S(1)}, bf16[72,1152]{1,0:T(8,128)(2,1)S(1)}, u32[]{:S(2)}, u32[]{:S(2)}) %collective-permute-start.61) | collective-permute-done | bytes 165920 | tf_op jit(solution)/shard_map/ppermute | solution.py:883
  462.5 1.6 fusion.47
  477.3 1.9 fusion.59
  480.8 3.1 copy.86
  485.0 3.4 collective-permute-done.66
  489.8 4.2 collective-permute-done.67
  498.9 1.9 multiply_multiply_fusion
  500.9 3.5 bitcast_add_fusion
  504.4 2.0 multiply_add_fusion
  508.7 1.6 bitcast_add_fusion.1
  (450 shorter events, 116.8 us)
Async XLA Ops:
  7.2 188.0 %all-gather.3.cloned.1.call-start = ((), (), s32[]{:S(2)}) async-start(), calls=%async_computation | async-start | bytes 5971968 | tf_op jit(solution)/shard_map/all_gather | solution.py:1038
  13.9 19.8 %collective-permute-start.4 = (bf16[72,1152]{1,0:T(8,128)(2,1)S(1)}, bf16[72,1152]{1,0:T(8,128)(2,1)S(1)}, u32[]{:S(2)}, u32[]{:S(2)}) collective-permute-start(bf16[72,1152]{1,0:T(8,128)(2,1)S(1)} %dynamic-slice_bitcast_fusion.6), channel_id=1, source_target_pairs={{0,4},{1,5},{2,6},{3,7},{4,0},{5,1},{6,2},{7,3},{8,12},{9,13},{10,... | collective-permute-start | bytes 497672 | tf_op jit(solution)/shard_map/ppermute | solution.py:883
  19.5 30.9 %collective-permute-start = (bf16[4,258,432]{2,0,1:T(4,128)(2,1)}, bf16[4,258,432]{2,0,1:T(4,128)(2,1)}, u32[]{:S(2)}, u32[]{:S(2)}) collective-permute-start(bf16[4,258,432]{2,0,1:T(4,128)(2,1)} %copy.76), channel_id=1, source_target_pairs={{0,1},{1,0},{2,3},{3,2},{4,5},{5,4},{6,7},{7,6},{8,9},{9,8},{10,11... | collective-permute-start | bytes 2674952 | tf_op jit(solution)/shard_map/ppermute | solution.py:883
  21.0 19.1 %collective-permute-start.8 = (bf16[144,1152]{1,0:T(8,128)(2,1)S(1)}, bf16[144,1152]{1,0:T(8,128)(2,1)S(1)}, u32[]{:S(2)}, u32[]{:S(2)}) collective-permute-start(bf16[144,1152]{1,0:T(8,128)(2,1)S(1)} %dynamic-slice_bitcast_fusion.5), channel_id=1, source_target_pairs={{0,4},{1,5},{2,6},{3,7},{4,0},{5,1},{6,2},{7,3},{8,12},{9,13},{10,... | collective-permute-start | bytes 995336 | tf_op jit(solution)/shard_map/ppermute | solution.py:883
  33.8 13.4 %collective-permute-start.5 = (bf16[2,72,1152]{2,1,0:T(8,128)(2,1)S(1)}, bf16[2,72,1152]{2,1,0:T(8,128)(2,1)S(1)}, u32[]{:S(2)}, u32[]{:S(2)}) collective-permute-start(bf16[2,72,1152]{2,1,0:T(8,128)(2,1)S(1)} %pad_maximum_fusion.17), channel_id=1, source_target_pairs={{0,2},{1,3},{2,0},{3,1},{4,6},{5,7},{6,4},{7,5},{8,10},{9,11},{10,... | collective-permute-start | bytes 995336 | tf_op jit(solution)/shard_map/ppermute | solution.py:883
  40.2 24.0 %collective-permute-start.9 = (bf16[2,144,1152]{2,1,0:T(8,128)(2,1)S(1)}, bf16[2,144,1152]{2,1,0:T(8,128)(2,1)S(1)}, u32[]{:S(2)}, u32[]{:S(2)}) collective-permute-start(bf16[2,144,1152]{2,1,0:T(8,128)(2,1)S(1)} %pad_maximum_fusion.12), channel_id=1, source_target_pairs={{0,2},{1,3},{2,0},{3,1},{4,6},{5,7},{6,4},{7,5},{8,10},{9,11},{10,... | collective-permute-start | bytes 1990664 | tf_op jit(solution)/shard_map/ppermute | solution.py:883
  47.3 19.4 %collective-permute-start.6 = (bf16[4,72,1152]{2,1,0:T(8,128)(2,1)S(1)}, bf16[4,72,1152]{2,1,0:T(8,128)(2,1)S(1)}, u32[]{:S(2)}, u32[]{:S(2)}) collective-permute-start(bf16[4,72,1152]{2,1,0:T(8,128)(2,1)S(1)} %pad_maximum_fusion.11), channel_id=1, source_target_pairs={{0,1},{1,0},{2,3},{3,2},{4,5},{5,4},{6,7},{7,6},{8,9},{9,8},{10,11... | collective-permute-start | bytes 1990664 | tf_op jit(solution)/shard_map/ppermute | solution.py:883
  48.9 17.8 %collective-permute-start.7 = (bf16[4,72,1152]{2,1,0:T(8,128)(2,1)S(1)}, bf16[4,72,1152]{2,1,0:T(8,128)(2,1)S(1)}, u32[]{:S(2)}, u32[]{:S(2)}) collective-permute-start(bf16[4,72,1152]{2,1,0:T(8,128)(2,1)S(1)} %pad_maximum_fusion.11), channel_id=1, source_target_pairs={{0,16},{1,17},{2,18},{3,19},{4,20},{5,21},{6,22},{7,23},{8,24},{9,... | collective-permute-start | bytes 1990664 | tf_op jit(solution)/shard_map/ppermute | solution.py:883
  53.0 25.1 %collective-permute-start.1 = (bf16[258,864]{1,0:T(8,128)(2,1)}, bf16[258,864]{1,0:T(8,128)(2,1)S(1)}, u32[]{:S(2)}, u32[]{:S(2)}) collective-permute-start(bf16[258,864]{1,0:T(8,128)(2,1)} %get-tuple-element.158), channel_id=1, source_target_pairs={{0,4},{1,5},{2,6},{3,7},{4,0},{5,1},{6,2},{7,3},{8,12},{9,13},{10,... | collective-permute-start | bytes 1337480 | tf_op jit(solution)/shard_map/ppermute | solution.py:883
  54.6 37.2 %collective-permute-start.2 = (bf16[258,864]{1,0:T(8,128)(2,1)S(1)}, bf16[258,864]{1,0:T(8,128)(2,1)S(1)}, u32[]{:S(2)}, u32[]{:S(2)}) collective-permute-start(bf16[258,864]{1,0:T(8,128)(2,1)S(1)} %get-tuple-element.159), channel_id=1, source_target_pairs={{0,2},{1,3},{2,0},{3,1},{4,6},{5,7},{6,4},{7,5},{8,10},{9,11},{10,... | collective-permute-start | bytes 1337480 | tf_op jit(solution)/shard_map/ppermute | solution.py:883
  64.2 29.1 %collective-permute-start.3 = (bf16[258,864]{1,0:T(8,128)(2,1)S(1)}, bf16[258,864]{1,0:T(8,128)(2,1)S(1)}, u32[]{:S(2)}, u32[]{:S(2)}) collective-permute-start(bf16[258,864]{1,0:T(8,128)(2,1)S(1)} %get-tuple-element.160), channel_id=1, source_target_pairs={{0,6},{1,7},{2,4},{3,5},{4,2},{5,3},{6,0},{7,1},{8,14},{9,15},{10,... | collective-permute-start | bytes 1337480 | tf_op jit(solution)/shard_map/ppermute | solution.py:883
  68.4 29.1 %collective-permute-start.11 = (bf16[2,72,1152]{2,1,0:T(8,128)(2,1)}, bf16[2,72,1152]{2,1,0:T(8,128)(2,1)}, u32[]{:S(2)}, u32[]{:S(2)}) collective-permute-start(bf16[2,72,1152]{2,1,0:T(8,128)(2,1)} %slice.171), channel_id=1, source_target_pairs={{0,1},{1,0},{2,3},{3,2},{4,5},{5,4},{6,7},{7,6},{8,9},{9,8},{10,11... | collective-permute-start | bytes 995336 | tf_op jit(solution)/shard_map/ppermute | solution.py:883
  71.2 26.3 %collective-permute-start.10 = (bf16[2,72,1152]{2,1,0:T(8,128)(2,1)}, bf16[2,72,1152]{2,1,0:T(8,128)(2,1)}, u32[]{:S(2)}, u32[]{:S(2)}) collective-permute-start(bf16[2,72,1152]{2,1,0:T(8,128)(2,1)} %slice.170), channel_id=1, source_target_pairs={{0,16},{1,17},{2,18},{3,19},{4,20},{5,21},{6,22},{7,23},{8,24},{9,... | collective-permute-start | bytes 995336 | tf_op jit(solution)/shard_map/ppermute | solution.py:883
  78.0 31.6 %collective-permute-start.17 = (bf16[4,144,1152]{2,1,0:T(8,128)(2,1)}, bf16[4,144,1152]{2,1,0:T(8,128)(2,1)}, u32[]{:S(2)}, u32[]{:S(2)}) collective-permute-start(bf16[4,144,1152]{2,1,0:T(8,128)(2,1)} %pad_maximum_fusion.2), channel_id=1, source_target_pairs={{0,16},{1,17},{2,18},{3,19},{4,20},{5,21},{6,22},{7,23},{8,24},{9,... | collective-permute-start | bytes 3981320 | tf_op jit(solution)/shard_map/ppermute | solution.py:883
  91.7 39.4 %collective-permute-start.15 = (bf16[4,144,1152]{2,1,0:T(8,128)(2,1)}, bf16[4,144,1152]{2,1,0:T(8,128)(2,1)}, u32[]{:S(2)}, u32[]{:S(2)}) collective-permute-start(bf16[4,144,1152]{2,1,0:T(8,128)(2,1)} %pad_maximum_fusion.2), channel_id=1, source_target_pairs={{0,1},{1,0},{2,3},{3,2},{4,5},{5,4},{6,7},{7,6},{8,9},{9,8},{10,11... | collective-permute-start | bytes 3981320 | tf_op jit(solution)/shard_map/ppermute | solution.py:883
  97.4 3.1 collective-permute-start.12
  101.7 32.2 %collective-permute-start.13 = (f32[272,1152]{1,0:T(8,128)S(1)}, f32[272,1152]{1,0:T(8,128)S(1)}, u32[]{:S(2)}, u32[]{:S(2)}) collective-permute-start(f32[272,1152]{1,0:T(8,128)S(1)} %fusion.93), channel_id=1, source_target_pairs={{0,8},{1,9},{2,10},{3,11},{4,12},{5,13},{6,14},{7,15},{8,0},{9,1},... | collective-permute-start | bytes 3760136 | tf_op jit(solution)/shard_map/ppermute | solution.py:883
  110.8 40.0 %collective-permute-start.18 = (bf16[2,144,1152]{2,1,0:T(8,128)(2,1)S(1)}, bf16[2,144,1152]{2,1,0:T(8,128)(2,1)S(1)}, u32[]{:S(2)}, u32[]{:S(2)}) collective-permute-start(bf16[2,144,1152]{2,1,0:T(8,128)(2,1)S(1)} %slice.229), channel_id=1, source_target_pairs={{0,1},{1,0},{2,3},{3,2},{4,5},{5,4},{6,7},{7,6},{8,9},{9,8},{10,11... | collective-permute-start | bytes 1990664 | tf_op jit(solution)/shard_map/ppermute | solution.py:883
  132.3 18.6 %collective-permute-start.16 = (bf16[2,144,1152]{2,1,0:T(8,128)(2,1)S(1)}, bf16[2,144,1152]{2,1,0:T(8,128)(2,1)S(1)}, u32[]{:S(2)}, u32[]{:S(2)}) collective-permute-start(bf16[2,144,1152]{2,1,0:T(8,128)(2,1)S(1)} %slice.228), channel_id=1, source_target_pairs={{0,16},{1,17},{2,18},{3,19},{4,20},{5,21},{6,22},{7,23},{8,24},{9,... | collective-permute-start | bytes 1990664 | tf_op jit(solution)/shard_map/ppermute | solution.py:883
  134.8 16.1 %collective-permute-start.14 = (bf16[272,1152]{1,0:T(8,128)(2,1)S(1)}, bf16[272,1152]{1,0:T(8,128)(2,1)S(1)}, u32[]{:S(2)}, u32[]{:S(2)}) collective-permute-start(bf16[272,1152]{1,0:T(8,128)(2,1)S(1)} %pad.16.normed_a.normed_first), channel_id=1, source_target_pairs={{0,8},{1,9},{2,10},{3,11},{4,12},{5,13},{6,14},{7,15},{8,0},{9,1},... | collective-permute-start | bytes 1880072 | tf_op jit(solution)/shard_map/ppermute | solution.py:883
  151.0 20.6 %collective-permute-start.19 = (bf16[272,1152]{1,0:T(8,128)(2,1)S(1)}, bf16[272,1152]{1,0:T(8,128)(2,1)}, u32[]{:S(2)}, u32[]{:S(2)}) collective-permute-start(bf16[272,1152]{1,0:T(8,128)(2,1)S(1)} %get-tuple-element.182.refs_4_), channel_id=1, source_target_pairs={{0,16},{1,17},{2,18},{3,19},{4,20},{5,21},{6,22},{7,23},{8,24},{9,... | collective-permute-start | bytes 1880072 | tf_op jit(solution)/shard_map/ppermute | solution.py:883
  176.4 16.5 %collective-permute-start.21 = (bf16[272,1152]{1,0:T(8,128)(2,1)}, bf16[272,1152]{1,0:T(8,128)(2,1)}, u32[]{:S(2)}, u32[]{:S(2)}) collective-permute-start(bf16[272,1152]{1,0:T(8,128)(2,1)} %pad.17.refs_0_), channel_id=1, source_target_pairs={{0,16},{1,17},{2,18},{3,19},{4,20},{5,21},{6,22},{7,23},{8,24},{9,... | collective-permute-start | bytes 1880072 | tf_op jit(solution)/shard_map/ppermute | solution.py:883
  177.1 16.4 %collective-permute-start.24 = (bf16[272,1152]{1,0:T(8,128)(2,1)S(1)}, bf16[272,1152]{1,0:T(8,128)(2,1)}, u32[]{:S(2)}, u32[]{:S(2)}) collective-permute-start(bf16[272,1152]{1,0:T(8,128)(2,1)S(1)} %get-tuple-element.182.refs_4_), channel_id=1, source_target_pairs={{0,8},{1,9},{2,10},{3,11},{4,12},{5,13},{6,14},{7,15},{8,0},{9,1},... | collective-permute-start | bytes 1880072 | tf_op jit(solution)/shard_map/ppermute | solution.py:883
  177.1 16.4 %collective-permute-start.25 = (bf16[272,1152]{1,0:T(8,128)(2,1)}, bf16[272,1152]{1,0:T(8,128)(2,1)}, u32[]{:S(2)}, u32[]{:S(2)}) collective-permute-start(bf16[272,1152]{1,0:T(8,128)(2,1)} %collective-permute-done.19.refs_5_), channel_id=1, source_target_pairs={{0,8},{1,9},{2,10},{3,11},{4,12},{5,13},{6,14},{7,15},{8,0},{9,1},... | collective-permute-start | bytes 1880072 | tf_op jit(solution)/shard_map/ppermute | solution.py:883
  177.6 15.9 %collective-permute-start.22 = (bf16[272,1152]{1,0:T(8,128)(2,1)}, bf16[272,1152]{1,0:T(8,128)(2,1)}, u32[]{:S(2)}, u32[]{:S(2)}) collective-permute-start(bf16[272,1152]{1,0:T(8,128)(2,1)} %pad.17.refs_0_), channel_id=1, source_target_pairs={{0,8},{1,9},{2,10},{3,11},{4,12},{5,13},{6,14},{7,15},{8,0},{9,1},... | collective-permute-start | bytes 1880072 | tf_op jit(solution)/shard_map/ppermute | solution.py:883
  216.6 3.2 collective-permute-start.27
  216.8 30.5 %collective-permute-start.26 = (f32[272,1152]{1,0:T(8,128)}, f32[272,1152]{1,0:T(8,128)S(1)}, u32[]{:S(2)}, u32[]{:S(2)}) collective-permute-start(f32[272,1152]{1,0:T(8,128)} %get-tuple-element.186), channel_id=1, source_target_pairs={{0,8},{1,9},{2,10},{3,11},{4,12},{5,13},{6,14},{7,15},{8,0},{9,1},... | collective-permute-start | bytes 3760136 | tf_op jit(solution)/shard_map/ppermute | solution.py:883
  221.3 25.9 %collective-permute-start.28 = (bf16[272,1152]{1,0:T(8,128)(2,1)S(1)}, bf16[272,1152]{1,0:T(8,128)(2,1)S(1)}, u32[]{:S(2)}, u32[]{:S(2)}) collective-permute-start(bf16[272,1152]{1,0:T(8,128)(2,1)S(1)} %add.455), channel_id=1, source_target_pairs={{0,16},{1,17},{2,18},{3,19},{4,20},{5,21},{6,22},{7,23},{8,24},{9,... | collective-permute-start | bytes 1880072 | tf_op jit(solution)/shard_map/ppermute | solution.py:883
  244.6 41.7 %collective-permute-start.30 = (bf16[4,144,1152]{2,1,0:T(8,128)(2,1)}, bf16[4,144,1152]{2,1,0:T(8,128)(2,1)}, u32[]{:S(2)}, u32[]{:S(2)}) collective-permute-start(bf16[4,144,1152]{2,1,0:T(8,128)(2,1)} %get-tuple-element.202), channel_id=1, source_target_pairs={{0,1},{1,0},{2,3},{3,2},{4,5},{5,4},{6,7},{7,6},{8,9},{9,8},{10,11... | collective-permute-start | bytes 3981320 | tf_op jit(solution)/shard_map/ppermute | solution.py:883
  247.2 39.1 %collective-permute-start.31 = (bf16[2,2,144,1152]{3,2,1,0:T(8,128)(2,1)}, bf16[2,2,144,1152]{3,2,1,0:T(8,128)(2,1)}, u32[]{:S(2)}, u32[]{:S(2)}) collective-permute-start(bf16[2,2,144,1152]{3,2,1,0:T(8,128)(2,1)} %get-tuple-element.203), channel_id=1, source_target_pairs={{0,2},{1,3},{2,0},{3,1},{4,6},{5,7},{6,4},{7,5},{8,10},{9,11},{10,... | collective-permute-start | bytes 3981320 | tf_op jit(solution)/shard_map/ppermute | solution.py:883
  247.2 3.2 collective-permute-start.32
  251.4 35.0 %collective-permute-start.33 = (bf16[272,1152]{1,0:T(8,128)(2,1)}, bf16[272,1152]{1,0:T(8,128)(2,1)}, u32[]{:S(2)}, u32[]{:S(2)}) collective-permute-start(bf16[272,1152]{1,0:T(8,128)(2,1)} %add_convert_fusion.8), channel_id=1, source_target_pairs={{0,16},{1,17},{2,18},{3,19},{4,20},{5,21},{6,22},{7,23},{8,24},{9,... | collective-permute-start | bytes 1880072 | tf_op jit(solution)/shard_map/ppermute | solution.py:883
  252.6 38.7 %collective-permute-start.41 = (f32[272,1152]{1,0:T(8,128)}, f32[272,1152]{1,0:T(8,128)S(1)}, u32[]{:S(2)}, u32[]{:S(2)}) collective-permute-start(f32[272,1152]{1,0:T(8,128)} %get-tuple-element.219), channel_id=1, source_target_pairs={{0,8},{1,9},{2,10},{3,11},{4,12},{5,13},{6,14},{7,15},{8,0},{9,1},... | collective-permute-start | bytes 3760136 | tf_op jit(solution)/shard_map/ppermute | solution.py:883
  286.3 28.3 %collective-permute-start.34 = (bf16[2,144,1152]{2,1,0:T(8,128)(2,1)}, bf16[2,144,1152]{2,1,0:T(8,128)(2,1)S(1)}, u32[]{:S(2)}, u32[]{:S(2)}) collective-permute-start(bf16[2,144,1152]{2,1,0:T(8,128)(2,1)} %get-tuple-element.208), channel_id=1, source_target_pairs={{0,1},{1,0},{2,3},{3,2},{4,5},{5,4},{6,7},{7,6},{8,9},{9,8},{10,11... | collective-permute-start | bytes 1990664 | tf_op jit(solution)/shard_map/ppermute | solution.py:883
  286.6 6.1 %collective-permute-start.37 = (f32[272,1152]{1,0:T(8,128)S(1)}, f32[272,1152]{1,0:T(8,128)S(1)}, u32[]{:S(2)}, u32[]{:S(2)}) collective-permute-start(f32[272,1152]{1,0:T(8,128)S(1)} %copy-done.81), channel_id=1, source_target_pairs={{0,8},{1,9},{2,10},{3,11},{4,12},{5,13},{6,14},{7,15},{8,0},{9,1},... | collective-permute-start | bytes 3760136 | tf_op jit(solution)/shard_map/ppermute | solution.py:883
  288.8 29.4 %collective-permute-start.35 = (bf16[2,144,1152]{2,1,0:T(8,128)(2,1)S(1)}, bf16[2,144,1152]{2,1,0:T(8,128)(2,1)S(1)}, u32[]{:S(2)}, u32[]{:S(2)}) collective-permute-start(bf16[2,144,1152]{2,1,0:T(8,128)(2,1)S(1)} %slice_bitcast_fusion.2), channel_id=1, source_target_pairs={{0,1},{1,0},{2,3},{3,2},{4,5},{5,4},{6,7},{7,6},{8,9},{9,8},{10,11... | collective-permute-start | bytes 1990664 | tf_op jit(solution)/shard_map/ppermute | solution.py:883
  290.5 16.8 %collective-permute-start.39 = (bf16[2,144,1152]{2,1,0:T(8,128)(2,1)S(1)}, bf16[2,144,1152]{2,1,0:T(8,128)(2,1)S(1)}, u32[]{:S(2)}, u32[]{:S(2)}) collective-permute-start(bf16[2,144,1152]{2,1,0:T(8,128)(2,1)S(1)} %copy-done.82), channel_id=1, source_target_pairs={{0,16},{1,17},{2,18},{3,19},{4,20},{5,21},{6,22},{7,23},{8,24},{9,... | collective-permute-start | bytes 1990664 | tf_op jit(solution)/shard_map/ppermute | solution.py:883
  293.9 13.4 %collective-permute-start.38 = (bf16[272,1152]{1,0:T(8,128)(2,1)S(1)}, bf16[272,1152]{1,0:T(8,128)(2,1)S(1)}, u32[]{:S(2)}, u32[]{:S(2)}) collective-permute-start(bf16[272,1152]{1,0:T(8,128)(2,1)S(1)} %pad.19), channel_id=1, source_target_pairs={{0,8},{1,9},{2,10},{3,11},{4,12},{5,13},{6,14},{7,15},{8,0},{9,1},... | collective-permute-start | bytes 1880072 | tf_op jit(solution)/shard_map/ppermute | solution.py:883
  296.6 21.6 %collective-permute-start.36 = (bf16[2,144,1152]{2,1,0:T(8,128)(2,1)S(1)}, bf16[2,144,1152]{2,1,0:T(8,128)(2,1)S(1)}, u32[]{:S(2)}, u32[]{:S(2)}) collective-permute-start(bf16[2,144,1152]{2,1,0:T(8,128)(2,1)S(1)} %slice.236), channel_id=1, source_target_pairs={{0,2},{1,3},{2,0},{3,1},{4,6},{5,7},{6,4},{7,5},{8,10},{9,11},{10,... | collective-permute-start | bytes 1990664 | tf_op jit(solution)/shard_map/ppermute | solution.py:883
  308.5 3.9 collective-permute-start.40
  318.7 37.1 %collective-permute-start.43 = (bf16[4,258,432]{2,0,1:T(4,128)(2,1)S(1)}, bf16[4,258,432]{2,0,1:T(4,128)(2,1)S(1)}, u32[]{:S(2)}, u32[]{:S(2)}) collective-permute-start(bf16[4,258,432]{2,0,1:T(4,128)(2,1)S(1)} %copy.78), channel_id=1, source_target_pairs={{0,1},{1,0},{2,3},{3,2},{4,5},{5,4},{6,7},{7,6},{8,9},{9,8},{10,11... | collective-permute-start | bytes 2674952 | tf_op jit(solution)/shard_map/ppermute | solution.py:883
  319.1 10.8 %collective-permute-start.44 = (bf16[2,72,1152]{2,1,0:T(8,128)(2,1)S(1)}, bf16[2,72,1152]{2,1,0:T(8,128)(2,1)S(1)}, u32[]{:S(2)}, u32[]{:S(2)}) collective-permute-start(bf16[2,72,1152]{2,1,0:T(8,128)(2,1)S(1)} %get-tuple-element.480), channel_id=1, source_target_pairs={{0,16},{1,17},{2,18},{3,19},{4,20},{5,21},{6,22},{7,23},{8,24},{9,... | collective-permute-start | bytes 995336 | tf_op jit(solution)/shard_map/ppermute | solution.py:883
  320.0 30.9 %collective-permute-start.45 = (bf16[2,72,1152]{2,1,0:T(8,128)(2,1)S(1)}, bf16[2,72,1152]{2,1,0:T(8,128)(2,1)S(1)}, u32[]{:S(2)}, u32[]{:S(2)}) collective-permute-start(bf16[2,72,1152]{2,1,0:T(8,128)(2,1)S(1)} %get-tuple-element.479), channel_id=1, source_target_pairs={{0,1},{1,0},{2,3},{3,2},{4,5},{5,4},{6,7},{7,6},{8,9},{9,8},{10,11... | collective-permute-start | bytes 995336 | tf_op jit(solution)/shard_map/ppermute | solution.py:883
  322.0 34.8 %collective-permute-start.46 = (bf16[4,144,1152]{2,1,0:T(8,128)(2,1)S(1)}, bf16[4,144,1152]{2,1,0:T(8,128)(2,1)S(1)}, u32[]{:S(2)}, u32[]{:S(2)}) collective-permute-start(bf16[4,144,1152]{2,1,0:T(8,128)(2,1)S(1)} %pad_maximum_fusion.4), channel_id=1, source_target_pairs={{0,16},{1,17},{2,18},{3,19},{4,20},{5,21},{6,22},{7,23},{8,24},{9,... | collective-permute-start | bytes 3981320 | tf_op jit(solution)/shard_map/ppermute | solution.py:883
  323.8 32.1 %collective-permute-start.47 = (bf16[2,144,1152]{2,1,0:T(8,128)(2,1)S(1)}, bf16[2,144,1152]{2,1,0:T(8,128)(2,1)S(1)}, u32[]{:S(2)}, u32[]{:S(2)}) collective-permute-start(bf16[2,144,1152]{2,1,0:T(8,128)(2,1)S(1)} %fusion.25), channel_id=1, source_target_pairs={{0,4},{1,5},{2,6},{3,7},{4,0},{5,1},{6,2},{7,3},{8,12},{9,13},{10,... | collective-permute-start | bytes 1990664 | tf_op jit(solution)/shard_map/ppermute | solution.py:883
  357.9 37.4 %collective-permute-start.48 = (bf16[4,144,1152]{2,1,0:T(8,128)(2,1)S(1)}, bf16[4,144,1152]{2,1,0:T(8,128)(2,1)S(1)}, u32[]{:S(2)}, u32[]{:S(2)}) collective-permute-start(bf16[4,144,1152]{2,1,0:T(8,128)(2,1)S(1)} %pad_maximum_fusion.5), channel_id=1, source_target_pairs={{0,1},{1,0},{2,3},{3,2},{4,5},{5,4},{6,7},{7,6},{8,9},{9,8},{10,11... | collective-permute-start | bytes 3981320 | tf_op jit(solution)/shard_map/ppermute | solution.py:883
  360.2 26.4 %collective-permute-start.49 = (bf16[258,864]{1,0:T(8,128)(2,1)S(1)}, bf16[258,864]{1,0:T(8,128)(2,1)S(1)}, u32[]{:S(2)}, u32[]{:S(2)}) collective-permute-start(bf16[258,864]{1,0:T(8,128)(2,1)S(1)} %get-tuple-element.233), channel_id=1, source_target_pairs={{0,4},{1,5},{2,6},{3,7},{4,0},{5,1},{6,2},{7,3},{8,12},{9,13},{10,... | collective-permute-start | bytes 1337480 | tf_op jit(solution)/shard_map/ppermute | solution.py:883
  364.4 30.9 %collective-permute-start.50 = (bf16[258,864]{1,0:T(8,128)(2,1)S(1)}, bf16[258,864]{1,0:T(8,128)(2,1)S(1)}, u32[]{:S(2)}, u32[]{:S(2)}) collective-permute-start(bf16[258,864]{1,0:T(8,128)(2,1)S(1)} %get-tuple-element.234), channel_id=1, source_target_pairs={{0,2},{1,3},{2,0},{3,1},{4,6},{5,7},{6,4},{7,5},{8,10},{9,11},{10,... | collective-permute-start | bytes 1337480 | tf_op jit(solution)/shard_map/ppermute | solution.py:883
  364.4 30.9 %collective-permute-start.51 = (bf16[258,864]{1,0:T(8,128)(2,1)S(1)}, bf16[258,864]{1,0:T(8,128)(2,1)S(1)}, u32[]{:S(2)}, u32[]{:S(2)}) collective-permute-start(bf16[258,864]{1,0:T(8,128)(2,1)S(1)} %get-tuple-element.235), channel_id=1, source_target_pairs={{0,6},{1,7},{2,4},{3,5},{4,2},{5,3},{6,0},{7,1},{8,14},{9,15},{10,... | collective-permute-start | bytes 1337480 | tf_op jit(solution)/shard_map/ppermute | solution.py:883
  366.4 28.9 %collective-permute-start.52 = (bf16[2,144,1152]{2,1,0:T(8,128)(2,1)S(1)}, bf16[2,144,1152]{2,1,0:T(8,128)(2,1)S(1)}, u32[]{:S(2)}, u32[]{:S(2)}) collective-permute-start(bf16[2,144,1152]{2,1,0:T(8,128)(2,1)S(1)} %fusion.7), channel_id=1, source_target_pairs={{0,16},{1,17},{2,18},{3,19},{4,20},{5,21},{6,22},{7,23},{8,24},{9,... | collective-permute-start | bytes 1990664 | tf_op jit(solution)/shard_map/ppermute | solution.py:883
  397.2 21.2 %collective-permute-start.56 = (bf16[2,2,144,1152]{3,2,1,0:T(8,128)(2,1)}, bf16[2,2,144,1152]{3,2,1,0:T(8,128)(2,1)}, u32[]{:S(2)}, u32[]{:S(2)}) collective-permute-start(bf16[2,2,144,1152]{3,2,1,0:T(8,128)(2,1)} %get-tuple-element.476), channel_id=1, source_target_pairs={{0,8},{1,9},{2,10},{3,11},{4,12},{5,13},{6,14},{7,15},{8,0},{9,1},... | collective-permute-start | bytes 3981320 | tf_op jit(solution)/shard_map/ppermute | solution.py:883
  397.2 38.8 %collective-permute-start.59 = (f32[4,1152]{1,0:T(4,128)S(1)}, f32[4,1152]{1,0:T(4,128)S(1)}, u32[]{:S(2)}, u32[]{:S(2)}) collective-permute-start(f32[4,1152]{1,0:T(4,128)S(1)} %fusion.72), channel_id=1, source_target_pairs={{0,16},{1,17},{2,18},{3,19},{4,20},{5,21},{6,22},{7,23},{8,24},{9,... | collective-permute-start | bytes 55304 | tf_op jit(solution)/shard_map/ppermute | solution.py:883
  402.0 25.2 %collective-permute-start.53 = (bf16[2,144,1152]{2,1,0:T(8,128)(2,1)}, bf16[2,144,1152]{2,1,0:T(8,128)(2,1)}, u32[]{:S(2)}, u32[]{:S(2)}) collective-permute-start(bf16[2,144,1152]{2,1,0:T(8,128)(2,1)} %slice.246), channel_id=1, source_target_pairs={{0,2},{1,3},{2,0},{3,1},{4,6},{5,7},{6,4},{7,5},{8,10},{9,11},{10,... | collective-permute-start | bytes 1990664 | tf_op jit(solution)/shard_map/ppermute | solution.py:883
  411.6 17.1 %collective-permute-start.54 = (bf16[4,72,1152]{2,1,0:T(8,128)(2,1)}, bf16[4,72,1152]{2,1,0:T(8,128)(2,1)}, u32[]{:S(2)}, u32[]{:S(2)}) collective-permute-start(bf16[4,72,1152]{2,1,0:T(8,128)(2,1)} %pad_maximum_fusion.13), channel_id=1, source_target_pairs={{0,16},{1,17},{2,18},{3,19},{4,20},{5,21},{6,22},{7,23},{8,24},{9,... | collective-permute-start | bytes 1990664 | tf_op jit(solution)/shard_map/ppermute | solution.py:883
  413.1 16.8 %collective-permute-start.55 = (bf16[4,72,1152]{2,1,0:T(8,128)(2,1)}, bf16[4,72,1152]{2,1,0:T(8,128)(2,1)}, u32[]{:S(2)}, u32[]{:S(2)}) collective-permute-start(bf16[4,72,1152]{2,1,0:T(8,128)(2,1)} %pad_maximum_fusion.14), channel_id=1, source_target_pairs={{0,1},{1,0},{2,3},{3,2},{4,5},{5,4},{6,7},{7,6},{8,9},{9,8},{10,11... | collective-permute-start | bytes 1990664 | tf_op jit(solution)/shard_map/ppermute | solution.py:883
  431.3 16.6 %collective-permute-start.57 = (bf16[144,1152]{1,0:T(8,128)(2,1)S(1)}, bf16[144,1152]{1,0:T(8,128)(2,1)S(1)}, u32[]{:S(2)}, u32[]{:S(2)}) collective-permute-start(bf16[144,1152]{1,0:T(8,128)(2,1)S(1)} %slice_bitcast_fusion.4), channel_id=1, source_target_pairs={{0,4},{1,5},{2,6},{3,7},{4,0},{5,1},{6,2},{7,3},{8,12},{9,13},{10,... | collective-permute-start | bytes 995336 | tf_op jit(solution)/shard_map/ppermute | solution.py:883
  434.0 15.6 %collective-permute-start.58 = (bf16[2,72,1152]{2,1,0:T(8,128)(2,1)S(1)}, bf16[2,72,1152]{2,1,0:T(8,128)(2,1)S(1)}, u32[]{:S(2)}, u32[]{:S(2)}) collective-permute-start(bf16[2,72,1152]{2,1,0:T(8,128)(2,1)S(1)} %slice.252), channel_id=1, source_target_pairs={{0,2},{1,3},{2,0},{3,1},{4,6},{5,7},{6,4},{7,5},{8,10},{9,11},{10,... | collective-permute-start | bytes 995336 | tf_op jit(solution)/shard_map/ppermute | solution.py:883
  449.6 9.1 %collective-permute-start.60 = (bf16[144,1152]{1,0:T(8,128)(2,1)S(1)}, bf16[144,1152]{1,0:T(8,128)(2,1)S(1)}, u32[]{:S(2)}, u32[]{:S(2)}) collective-permute-start(bf16[144,1152]{1,0:T(8,128)(2,1)S(1)} %fusion.35), channel_id=1, source_target_pairs={{0,16},{1,17},{2,18},{3,19},{4,20},{5,21},{6,22},{7,23},{8,24},{9,... | collective-permute-start | bytes 995336 | tf_op jit(solution)/shard_map/ppermute | solution.py:883
  450.4 8.3 %collective-permute-start.61 = (bf16[72,1152]{1,0:T(8,128)(2,1)S(1)}, bf16[72,1152]{1,0:T(8,128)(2,1)S(1)}, u32[]{:S(2)}, u32[]{:S(2)}) collective-permute-start(bf16[72,1152]{1,0:T(8,128)(2,1)S(1)} %slice_bitcast_fusion.5), channel_id=1, source_target_pairs={{0,4},{1,5},{2,6},{3,7},{4,0},{5,1},{6,2},{7,3},{8,12},{9,13},{10,... | collective-permute-start | bytes 497672 | tf_op jit(solution)/shard_map/ppermute | solution.py:883
  460.3 7.6 %collective-permute-start.63 = (bf16[2,144,1152]{2,1,0:T(8,128)(2,1)}, bf16[2,144,1152]{2,1,0:T(8,128)(2,1)S(1)}, u32[]{:S(2)}, u32[]{:S(2)}) collective-permute-start(bf16[2,144,1152]{2,1,0:T(8,128)(2,1)} %get-tuple-element.485), channel_id=1, source_target_pairs={{0,8},{1,9},{2,10},{3,11},{4,12},{5,13},{6,14},{7,15},{8,0},{9,1},... | collective-permute-start | bytes 1990664 | tf_op jit(solution)/shard_map/ppermute | solution.py:883
  464.1 7.6 %collective-permute-start.62 = (bf16[72,1152]{1,0:T(8,128)(2,1)}, bf16[72,1152]{1,0:T(8,128)(2,1)S(1)}, u32[]{:S(2)}, u32[]{:S(2)}) collective-permute-start(bf16[72,1152]{1,0:T(8,128)(2,1)} %fusion.47), channel_id=1, source_target_pairs={{0,16},{1,17},{2,18},{3,19},{4,20},{5,21},{6,22},{7,23},{8,24},{9,... | collective-permute-start | bytes 497672 | tf_op jit(solution)/shard_map/ppermute | solution.py:883
  479.4 4.5 collective-permute-start.65
  483.9 4.4 collective-permute-start.66
  488.4 5.6 %collective-permute-start.67 = (f32[15,1152]{1,0:T(8,128)S(1)}, f32[15,1152]{1,0:T(8,128)S(1)}, u32[]{:S(2)}, u32[]{:S(2)}) collective-permute-start(f32[15,1152]{1,0:T(8,128)S(1)} %add.503), channel_id=1, source_target_pairs={{0,4},{1,5},{2,6},{3,7},{4,0},{5,1},{6,2},{7,3},{8,12},{9,13},{10,... | collective-permute-start | bytes 207368 | tf_op jit(solution)/shard_map/ppermute | solution.py:883
  (90 other events, 740.1 us)
Sparse Core Ops, SparseCore 0:
  93.5 95.4 all-gather.2

commit v7 on v6

--- a/solution.py
+++ b/solution.py
@@ -970,11 +970,10 @@
 
     def all_narrow(value):
         value = value + over_y(value)
-        bit = 1
-        while bit < ZS:
-            value = value + xor_z(value, bit)
-            bit *= 2
-        return value
+        parts = [value] + [xor_z(value, distance) for distance in range(1, ZS)]
+        while len(parts) > 1:
+            parts = [left + right for left, right in zip(parts[0::2], parts[1::2])]
+        return parts[0]
 
     def columns(array):
         size = D // wide_count

time: 525 us -> 522 us (level)
    ppermute x68 -> x69, starting transfers between devices: 73.1 us -> 76.1 us  [send(): return lax.ppermute(value, axes, perm(move))]
    ppermute x68 -> x69, waiting for transfers between devices: 207 us -> 205 us  [send(): return lax.ppermute(value, axes, perm(move))]
    unnamed x172 -> x170, local copies, waits for them, and re-layouts: 10.6 us -> 9.71 us
  transfers between devices with their start and end apart: 69 -> 70, of which waited for: 30 -> 31; matrix products, arithmetic and copies ran while one was open for 16% -> 15% of each run, Pallas kernels for 15% -> 15%
where the time goes in v7:
time: 522 us; the launch traced here: 516 us
  waiting for transfers between devices  205 us (39%)
  Pallas kernels  103 us (20%)
  starting transfers between devices  76.2 us (15%)
  other arithmetic  74.4 us (14%)
  local copies, waits for them, and re-layouts  32.7 us (6%)
  between operations  17.6 us (3%)
  matrix products  6.8 us (1%)
    ppermute x69, waiting for transfers between devices, send(): return lax.ppermute(value, axes, perm(move))  205 us
    ppermute x69, starting transfers between devices, send(): return lax.ppermute(value, axes, perm(move))  76.1 us
    pallas_call x1, Pallas kernels, attn_backward(): pl.pallas_call(attn_backward_kernel, out_shape=[jax.ShapeDtypeStruct((tok...  31.2 us
    pallas_call x1, Pallas kernels, ffn_second(): pl.pallas_call(ffn_second_kernel, out_shape=[part] * 4 + [side] * 2 + [tu...  22.6 us
    pallas_call x1, Pallas kernels, ffn_first(): pl.pallas_call(ffn_first_kernel, out_shape=[part] * 4 + [hidden] * 2, gri...  21.3 us
    pallas_call x1, Pallas kernels, attn_forward(): pl.pallas_call(attn_forward_kernel, out_shape=[jax.ShapeDtypeStruct((toke...  14.7 us
  transfers between devices with their start and end apart: 70, of which 31 were waited for; matrix products, arithmetic and copies ran while one was open for 15% of the time, Pallas kernels for 15%

profile of v7, /device:TPU:0, one launch (start us, length us, event | category | flops | bytes accessed | tf_op | source)
XLA Modules:
  0.0 515.6 jit_solution(9758472676673935271)
XLA Ops:
  11.6 2.2 pack_tokens.1
  13.9 4.1 collective-permute-start.4
  21.3 12.4 %collective-permute-done.4 = bf16[72,1152]{1,0:T(8,128)(2,1)S(1)} collective-permute-done((bf16[72,1152]{1,0:T(8,128)(2,1)S(1)}, bf16[72,1152]{1,0:T(8,128)(2,1)S(1)}, u32[]{:S(2)}, u32[]{:S(2)}) %collective-permute-start.4) | collective-permute-done | bytes 165920 | tf_op jit(solution)/shard_map/ppermute | solution.py:883
  33.8 6.2 %collective-permute-done.8 = bf16[144,1152]{1,0:T(8,128)(2,1)S(1)} collective-permute-done((bf16[144,1152]{1,0:T(8,128)(2,1)S(1)}, bf16[144,1152]{1,0:T(8,128)(2,1)S(1)}, u32[]{:S(2)}, u32[]{:S(2)}) %collective-permute-start.8) | collective-permute-done | bytes 331808 | tf_op jit(solution)/shard_map/ppermute | solution.py:883
  40.9 6.3 %collective-permute-done.5 = bf16[2,72,1152]{2,1,0:T(8,128)(2,1)S(1)} collective-permute-done((bf16[2,72,1152]{2,1,0:T(8,128)(2,1)S(1)}, bf16[2,72,1152]{2,1,0:T(8,128)(2,1)S(1)}, u32[]{:S(2)}, u32[]{:S(2)}) %collective-permute-start.5) | collective-permute-done | bytes 331808 | tf_op jit(solution)/shard_map/ppermute | solution.py:883
  47.3 1.6 collective-permute-start.6
  54.6 2.5 collective-permute-start.2
  59.1 5.2 %collective-permute-done.9 = bf16[2,144,1152]{2,1,0:T(8,128)(2,1)S(1)} collective-permute-done((bf16[2,144,1152]{2,1,0:T(8,128)(2,1)S(1)}, bf16[2,144,1152]{2,1,0:T(8,128)(2,1)S(1)}, u32[]{:S(2)}, u32[]{:S(2)}) %collective-permute-start.9) | collective-permute-done | bytes 663584 | tf_op jit(solution)/shard_map/ppermute | solution.py:883
  68.4 2.1 collective-permute-start.11
  71.2 2.4 collective-permute-start.10
  74.5 3.5 collective-permute-done.1.refs_1_
  78.6 13.2 %collective-permute-done.2.refs_2_ = bf16[258,864]{1,0:T(8,128)(2,1)S(1)} collective-permute-done((bf16[258,864]{1,0:T(8,128)(2,1)S(1)}, bf16[258,864]{1,0:T(8,128)(2,1)S(1)}, u32[]{:S(2)}, u32[]{:S(2)}) %collective-permute-start.2) | collective-permute-done | bytes 445856 | tf_op jit(solution)/shard_map/ppermute | solution.py:883
  94.7 2.6 take_tokens.1
  97.5 1.6 maximum_bitcast_fusion.3
  103.2 6.5 %collective-permute-done.17 = bf16[4,144,1152]{2,1,0:T(8,128)(2,1)} collective-permute-done((bf16[4,144,1152]{2,1,0:T(8,128)(2,1)}, bf16[4,144,1152]{2,1,0:T(8,128)(2,1)}, u32[]{:S(2)}, u32[]{:S(2)}) %collective-permute-start.17) | collective-permute-done | bytes 1327136 | tf_op jit(solution)/shard_map/ppermute | solution.py:883
  111.2 20.0 %collective-permute-done.15 = bf16[4,144,1152]{2,1,0:T(8,128)(2,1)} collective-permute-done((bf16[4,144,1152]{2,1,0:T(8,128)(2,1)}, bf16[4,144,1152]{2,1,0:T(8,128)(2,1)}, u32[]{:S(2)}, u32[]{:S(2)}) %collective-permute-start.15) | collective-permute-done | bytes 1327136 | tf_op jit(solution)/shard_map/ppermute | solution.py:883
  132.3 1.6 collective-permute-start.16
  136.1 1.9 maximum_bitcast_fusion
  138.0 12.8 %collective-permute-done.18 = bf16[2,144,1152]{2,1,0:T(8,128)(2,1)S(1)} collective-permute-done((bf16[2,144,1152]{2,1,0:T(8,128)(2,1)S(1)}, bf16[2,144,1152]{2,1,0:T(8,128)(2,1)S(1)}, u32[]{:S(2)}, u32[]{:S(2)}) %collective-permute-start.18) | collective-permute-done | bytes 663584 | tf_op jit(solution)/shard_map/ppermute | solution.py:883
  152.4 1.6 maximum_bitcast_fusion.1
  154.0 2.9 pad_maximum_fusion.qk_ref.vo_ref
  156.9 14.7 %attn_forward.1 = (f32[272,1152]{1,0:T(8,128)S(1)}, f32[272,1152]{1,0:T(8,128)S(1)}, bf16[2,544,864]{2,1,0:T(8,128)(2,1)}, bf16[2,544,288]{2,1,0:T(8,128)(2,1)S(1)}) custom-call(s32[1]{0:T(128)} %bitcast.meta_ref, bf16[272,1152]{1,0:T(8,128)(2,1)S(1)} %pad.16.normed_a.normed_first, bf16[272,1152]{1,0:T(8,128)(2,1)S(1)} %collective-permute-done.14.normed_b.normed_second, ...), custom_call_target="tpu_custom_call" | custom-call | bytes 1048576 | tf_op jit(solution)/shard_map/attn_forward/pallas_call | solution.py:531
  171.7 2.9 collective-permute-done.20
  177.6 15.2 %collective-permute-done.21.refs_1_ = bf16[272,1152]{1,0:T(8,128)(2,1)} collective-permute-done((bf16[272,1152]{1,0:T(8,128)(2,1)}, bf16[272,1152]{1,0:T(8,128)(2,1)}, u32[]{:S(2)}, u32[]{:S(2)}) %collective-permute-start.21) | collective-permute-done | bytes 626720 | tf_op jit(solution)/shard_map/ppermute | solution.py:883
  193.5 1.8 collective-permute-done.23.refs_3_
  195.3 21.3 %ffn_first.1 = (f32[272,1152]{1,0:T(8,128)}, f32[272,1152]{1,0:T(8,128)}, f32[272,1152]{1,0:T(8,128)}, f32[272,1152]{1,0:T(8,128)}, bf16[2,1088,576]{2,1,0:T(8,128)(2,1)}, /*index=5*/bf16[2,1088,576]{2,1,0:T(8,128)(2,1)}) custom-call(s32[8]{0:T(128)} %stack.265.order_ref, bf16[272,1152]{1,0:T(8,128)(2,1)} %pad.17.refs_0_, ...), custom_call_target="tpu_custom_call" | custom-call | flops 8663334912 | bytes 25165824 | tf_op jit(solution)/shard_map/ffn_first/pallas_call | solution.py:415
  217.1 2.7 collective-permute-done.27
  222.1 22.6 %ffn_second.1 = (f32[272,1152]{1,0:T(8,128)}, f32[272,1152]{1,0:T(8,128)}, f32[272,1152]{1,0:T(8,128)}, f32[272,1152]{1,0:T(8,128)}, bf16[4,144,1152]{2,1,0:T(8,...) custom-call(s32[8]{0:T(128)} %stack.265.order_ref, ...), custom_call_target="tpu_custom_call" | custom-call | flops 8663334912 | bytes 25165824 | tf_op jit(solution)/shard_map/ffn_second/pallas_call | solution.py:448
  244.6 2.6 collective-permute-start.30
  252.7 31.2 %attn_backward.1 = (f32[272,1152]{1,0:T(8,128)}, f32[272,1152]{1,0:T(8,128)}, bf16[8,144,1152]{2,1,0:T(8,128)(2,1)}, bf16[4,144,1152]{2,1,0:T(8,128)(2,1)}, bf16...) custom-call(s32[1]{0:T(128)} %bitcast.meta_ref, bf16[272,1152]{1,0:T(8,128)(2,1)} %copy-done.2, ...), custom_call_target="tpu_custom_call" | custom-call | flops 5775556608 | bytes 25165824 | tf_op jit(solution)/shard_map/attn_backward/pallas_call | solution.py:626
  287.0 1.7 add_convert_fusion.2
  288.8 1.7 collective-permute-start.35
  294.7 1.8 add_convert_fusion.1
  296.6 2.1 collective-permute-start.36
  298.7 8.6 %collective-permute-done.39 = bf16[2,144,1152]{2,1,0:T(8,128)(2,1)S(1)} collective-permute-done((bf16[2,144,1152]{2,1,0:T(8,128)(2,1)S(1)}, bf16[2,144,1152]{2,1,0:T(8,128)(2,1)S(1)}, u32[]{:S(2)}, u32[]{:S(2)}) %collective-permute-start.39) | collective-permute-done | bytes 663584 | tf_op jit(solution)/shard_map/ppermute | solution.py:883
  309.7 2.4 convolution_convert_fusion
  312.4 2.2 give_tokens.1
  314.6 3.5 collective-permute-done.35
  320.0 1.7 collective-permute-start.45
  323.8 4.3 collective-permute-start.47
  329.9 20.9 %collective-permute-done.45 = bf16[2,72,1152]{2,1,0:T(8,128)(2,1)S(1)} collective-permute-done((bf16[2,72,1152]{2,1,0:T(8,128)(2,1)S(1)}, bf16[2,72,1152]{2,1,0:T(8,128)(2,1)S(1)}, u32[]{:S(2)}, u32[]{:S(2)}) %collective-permute-start.45) | collective-permute-done | bytes 331808 | tf_op jit(solution)/shard_map/ppermute | solution.py:883
  350.9 5.0 collective-permute-done.47
  357.9 1.7 collective-permute-start.48
  360.2 4.3 collective-permute-start.49
  369.0 17.6 %collective-permute-done.49.refs_1_ = bf16[258,864]{1,0:T(8,128)(2,1)S(1)} collective-permute-done((bf16[258,864]{1,0:T(8,128)(2,1)S(1)}, bf16[258,864]{1,0:T(8,128)(2,1)S(1)}, u32[]{:S(2)}, u32[]{:S(2)}) %collective-permute-start.49) | collective-permute-done | bytes 445856 | tf_op jit(solution)/shard_map/ppermute | solution.py:883
  386.6 8.7 %collective-permute-done.50.refs_2_ = bf16[258,864]{1,0:T(8,128)(2,1)S(1)} collective-permute-done((bf16[258,864]{1,0:T(8,128)(2,1)S(1)}, bf16[258,864]{1,0:T(8,128)(2,1)S(1)}, u32[]{:S(2)}, u32[]{:S(2)}) %collective-permute-start.50) | collective-permute-done | bytes 445856 | tf_op jit(solution)/shard_map/ppermute | solution.py:883
  395.3 1.8 pad_maximum_fusion.6
  397.4 2.6 add_convert_fusion
  402.0 9.6 %collective-permute-start.53 = (bf16[2,144,1152]{2,1,0:T(8,128)(2,1)}, bf16[2,144,1152]{2,1,0:T(8,128)(2,1)}, u32[]{:S(2)}, u32[]{:S(2)}) collective-permute-start(bf16[2,144,1152]{2,1,0:T(8,128)(2,1)} %slice.246), channel_id=1, source_target_pairs={{0,2},{1,3},{2,0},{3,1},{4,6},{5,7},{6,4},{7,5},{8,10},{9,11},{10,... | collective-permute-start | bytes 1990664 | tf_op jit(solution)/shard_map/ppermute | solution.py:883
  413.7 4.7 back_tokens.1
  418.4 2.4 fusion.29
  434.0 1.8 collective-permute-start.58
  436.0 11.9 %collective-permute-done.57 = bf16[144,1152]{1,0:T(8,128)(2,1)S(1)} collective-permute-done((bf16[144,1152]{1,0:T(8,128)(2,1)S(1)}, bf16[144,1152]{1,0:T(8,128)(2,1)S(1)}, u32[]{:S(2)}, u32[]{:S(2)}) %collective-permute-start.57) | collective-permute-done | bytes 331808 | tf_op jit(solution)/shard_map/ppermute | solution.py:883
  451.0 7.7 %collective-permute-done.61 = bf16[72,1152]{1,0:T(8,128)(2,1)S(1)} collective-permute-done((bf16[72,1152]{1,0:T(8,128)(2,1)S(1)}, bf16[72,1152]{1,0:T(8,128)(2,1)S(1)}, u32[]{:S(2)}, u32[]{:S(2)}) %collective-permute-start.61) | collective-permute-done | bytes 165920 | tf_op jit(solution)/shard_map/ppermute | solution.py:883
  462.5 1.6 fusion.47
  469.2 1.7 fusion.75
  478.6 1.9 fusion.59
  483.0 2.0 collective-permute-done.65
  485.2 1.7 collective-permute-start.68
  486.9 1.8 collective-permute-start.66
  489.6 2.8 collective-permute-done.67
  498.8 3.9 bitcast_add_fusion
  502.8 2.0 multiply_add_fusion
  506.1 1.6 bitcast_add_fusion.1
  (449 shorter events, 118.0 us)
Async XLA Ops:
  7.2 188.0 %all-gather.3.cloned.1.call-start = ((), (), s32[]{:S(2)}) async-start(), calls=%async_computation | async-start | bytes 5971968 | tf_op jit(solution)/shard_map/all_gather | solution.py:1037
  13.9 19.8 %collective-permute-start.4 = (bf16[72,1152]{1,0:T(8,128)(2,1)S(1)}, bf16[72,1152]{1,0:T(8,128)(2,1)S(1)}, u32[]{:S(2)}, u32[]{:S(2)}) collective-permute-start(bf16[72,1152]{1,0:T(8,128)(2,1)S(1)} %dynamic-slice_bitcast_fusion.6), channel_id=1, source_target_pairs={{0,4},{1,5},{2,6},{3,7},{4,0},{5,1},{6,2},{7,3},{8,12},{9,13},{10,... | collective-permute-start | bytes 497672 | tf_op jit(solution)/shard_map/ppermute | solution.py:883
  19.5 30.9 %collective-permute-start = (bf16[4,258,432]{2,0,1:T(4,128)(2,1)}, bf16[4,258,432]{2,0,1:T(4,128)(2,1)}, u32[]{:S(2)}, u32[]{:S(2)}) collective-permute-start(bf16[4,258,432]{2,0,1:T(4,128)(2,1)} %copy.76), channel_id=1, source_target_pairs={{0,1},{1,0},{2,3},{3,2},{4,5},{5,4},{6,7},{7,6},{8,9},{9,8},{10,11... | collective-permute-start | bytes 2674952 | tf_op jit(solution)/shard_map/ppermute | solution.py:883
  21.0 19.1 %collective-permute-start.8 = (bf16[144,1152]{1,0:T(8,128)(2,1)S(1)}, bf16[144,1152]{1,0:T(8,128)(2,1)S(1)}, u32[]{:S(2)}, u32[]{:S(2)}) collective-permute-start(bf16[144,1152]{1,0:T(8,128)(2,1)S(1)} %dynamic-slice_bitcast_fusion.5), channel_id=1, source_target_pairs={{0,4},{1,5},{2,6},{3,7},{4,0},{5,1},{6,2},{7,3},{8,12},{9,13},{10,... | collective-permute-start | bytes 995336 | tf_op jit(solution)/shard_map/ppermute | solution.py:883
  33.8 13.4 %collective-permute-start.5 = (bf16[2,72,1152]{2,1,0:T(8,128)(2,1)S(1)}, bf16[2,72,1152]{2,1,0:T(8,128)(2,1)S(1)}, u32[]{:S(2)}, u32[]{:S(2)}) collective-permute-start(bf16[2,72,1152]{2,1,0:T(8,128)(2,1)S(1)} %pad_maximum_fusion.17), channel_id=1, source_target_pairs={{0,2},{1,3},{2,0},{3,1},{4,6},{5,7},{6,4},{7,5},{8,10},{9,11},{10,... | collective-permute-start | bytes 995336 | tf_op jit(solution)/shard_map/ppermute | solution.py:883
  40.2 24.0 %collective-permute-start.9 = (bf16[2,144,1152]{2,1,0:T(8,128)(2,1)S(1)}, bf16[2,144,1152]{2,1,0:T(8,128)(2,1)S(1)}, u32[]{:S(2)}, u32[]{:S(2)}) collective-permute-start(bf16[2,144,1152]{2,1,0:T(8,128)(2,1)S(1)} %pad_maximum_fusion.12), channel_id=1, source_target_pairs={{0,2},{1,3},{2,0},{3,1},{4,6},{5,7},{6,4},{7,5},{8,10},{9,11},{10,... | collective-permute-start | bytes 1990664 | tf_op jit(solution)/shard_map/ppermute | solution.py:883
  47.3 19.4 %collective-permute-start.6 = (bf16[4,72,1152]{2,1,0:T(8,128)(2,1)S(1)}, bf16[4,72,1152]{2,1,0:T(8,128)(2,1)S(1)}, u32[]{:S(2)}, u32[]{:S(2)}) collective-permute-start(bf16[4,72,1152]{2,1,0:T(8,128)(2,1)S(1)} %pad_maximum_fusion.11), channel_id=1, source_target_pairs={{0,1},{1,0},{2,3},{3,2},{4,5},{5,4},{6,7},{7,6},{8,9},{9,8},{10,11... | collective-permute-start | bytes 1990664 | tf_op jit(solution)/shard_map/ppermute | solution.py:883
  48.9 17.8 %collective-permute-start.7 = (bf16[4,72,1152]{2,1,0:T(8,128)(2,1)S(1)}, bf16[4,72,1152]{2,1,0:T(8,128)(2,1)S(1)}, u32[]{:S(2)}, u32[]{:S(2)}) collective-permute-start(bf16[4,72,1152]{2,1,0:T(8,128)(2,1)S(1)} %pad_maximum_fusion.11), channel_id=1, source_target_pairs={{0,16},{1,17},{2,18},{3,19},{4,20},{5,21},{6,22},{7,23},{8,24},{9,... | collective-permute-start | bytes 1990664 | tf_op jit(solution)/shard_map/ppermute | solution.py:883
  53.0 25.1 %collective-permute-start.1 = (bf16[258,864]{1,0:T(8,128)(2,1)}, bf16[258,864]{1,0:T(8,128)(2,1)S(1)}, u32[]{:S(2)}, u32[]{:S(2)}) collective-permute-start(bf16[258,864]{1,0:T(8,128)(2,1)} %get-tuple-element.158), channel_id=1, source_target_pairs={{0,4},{1,5},{2,6},{3,7},{4,0},{5,1},{6,2},{7,3},{8,12},{9,13},{10,... | collective-permute-start | bytes 1337480 | tf_op jit(solution)/shard_map/ppermute | solution.py:883
  54.6 37.2 %collective-permute-start.2 = (bf16[258,864]{1,0:T(8,128)(2,1)S(1)}, bf16[258,864]{1,0:T(8,128)(2,1)S(1)}, u32[]{:S(2)}, u32[]{:S(2)}) collective-permute-start(bf16[258,864]{1,0:T(8,128)(2,1)S(1)} %get-tuple-element.159), channel_id=1, source_target_pairs={{0,2},{1,3},{2,0},{3,1},{4,6},{5,7},{6,4},{7,5},{8,10},{9,11},{10,... | collective-permute-start | bytes 1337480 | tf_op jit(solution)/shard_map/ppermute | solution.py:883
  64.2 29.1 %collective-permute-start.3 = (bf16[258,864]{1,0:T(8,128)(2,1)S(1)}, bf16[258,864]{1,0:T(8,128)(2,1)S(1)}, u32[]{:S(2)}, u32[]{:S(2)}) collective-permute-start(bf16[258,864]{1,0:T(8,128)(2,1)S(1)} %get-tuple-element.160), channel_id=1, source_target_pairs={{0,6},{1,7},{2,4},{3,5},{4,2},{5,3},{6,0},{7,1},{8,14},{9,15},{10,... | collective-permute-start | bytes 1337480 | tf_op jit(solution)/shard_map/ppermute | solution.py:883
  68.4 29.1 %collective-permute-start.11 = (bf16[2,72,1152]{2,1,0:T(8,128)(2,1)}, bf16[2,72,1152]{2,1,0:T(8,128)(2,1)}, u32[]{:S(2)}, u32[]{:S(2)}) collective-permute-start(bf16[2,72,1152]{2,1,0:T(8,128)(2,1)} %slice.171), channel_id=1, source_target_pairs={{0,1},{1,0},{2,3},{3,2},{4,5},{5,4},{6,7},{7,6},{8,9},{9,8},{10,11... | collective-permute-start | bytes 995336 | tf_op jit(solution)/shard_map/ppermute | solution.py:883
  71.2 26.3 %collective-permute-start.10 = (bf16[2,72,1152]{2,1,0:T(8,128)(2,1)}, bf16[2,72,1152]{2,1,0:T(8,128)(2,1)}, u32[]{:S(2)}, u32[]{:S(2)}) collective-permute-start(bf16[2,72,1152]{2,1,0:T(8,128)(2,1)} %slice.170), channel_id=1, source_target_pairs={{0,16},{1,17},{2,18},{3,19},{4,20},{5,21},{6,22},{7,23},{8,24},{9,... | collective-permute-start | bytes 995336 | tf_op jit(solution)/shard_map/ppermute | solution.py:883
  78.0 31.6 %collective-permute-start.17 = (bf16[4,144,1152]{2,1,0:T(8,128)(2,1)}, bf16[4,144,1152]{2,1,0:T(8,128)(2,1)}, u32[]{:S(2)}, u32[]{:S(2)}) collective-permute-start(bf16[4,144,1152]{2,1,0:T(8,128)(2,1)} %pad_maximum_fusion.2), channel_id=1, source_target_pairs={{0,16},{1,17},{2,18},{3,19},{4,20},{5,21},{6,22},{7,23},{8,24},{9,... | collective-permute-start | bytes 3981320 | tf_op jit(solution)/shard_map/ppermute | solution.py:883
  91.7 39.4 %collective-permute-start.15 = (bf16[4,144,1152]{2,1,0:T(8,128)(2,1)}, bf16[4,144,1152]{2,1,0:T(8,128)(2,1)}, u32[]{:S(2)}, u32[]{:S(2)}) collective-permute-start(bf16[4,144,1152]{2,1,0:T(8,128)(2,1)} %pad_maximum_fusion.2), channel_id=1, source_target_pairs={{0,1},{1,0},{2,3},{3,2},{4,5},{5,4},{6,7},{7,6},{8,9},{9,8},{10,11... | collective-permute-start | bytes 3981320 | tf_op jit(solution)/shard_map/ppermute | solution.py:883
  101.7 32.2 %collective-permute-start.13 = (f32[272,1152]{1,0:T(8,128)S(1)}, f32[272,1152]{1,0:T(8,128)S(1)}, u32[]{:S(2)}, u32[]{:S(2)}) collective-permute-start(f32[272,1152]{1,0:T(8,128)S(1)} %fusion.93), channel_id=1, source_target_pairs={{0,8},{1,9},{2,10},{3,11},{4,12},{5,13},{6,14},{7,15},{8,0},{9,1},... | collective-permute-start | bytes 3760136 | tf_op jit(solution)/shard_map/ppermute | solution.py:883
  110.8 40.0 %collective-permute-start.18 = (bf16[2,144,1152]{2,1,0:T(8,128)(2,1)S(1)}, bf16[2,144,1152]{2,1,0:T(8,128)(2,1)S(1)}, u32[]{:S(2)}, u32[]{:S(2)}) collective-permute-start(bf16[2,144,1152]{2,1,0:T(8,128)(2,1)S(1)} %slice.229), channel_id=1, source_target_pairs={{0,1},{1,0},{2,3},{3,2},{4,5},{5,4},{6,7},{7,6},{8,9},{9,8},{10,11... | collective-permute-start | bytes 1990664 | tf_op jit(solution)/shard_map/ppermute | solution.py:883
  132.3 18.6 %collective-permute-start.16 = (bf16[2,144,1152]{2,1,0:T(8,128)(2,1)S(1)}, bf16[2,144,1152]{2,1,0:T(8,128)(2,1)S(1)}, u32[]{:S(2)}, u32[]{:S(2)}) collective-permute-start(bf16[2,144,1152]{2,1,0:T(8,128)(2,1)S(1)} %slice.228), channel_id=1, source_target_pairs={{0,16},{1,17},{2,18},{3,19},{4,20},{5,21},{6,22},{7,23},{8,24},{9,... | collective-permute-start | bytes 1990664 | tf_op jit(solution)/shard_map/ppermute | solution.py:883
  134.8 16.1 %collective-permute-start.14 = (bf16[272,1152]{1,0:T(8,128)(2,1)S(1)}, bf16[272,1152]{1,0:T(8,128)(2,1)S(1)}, u32[]{:S(2)}, u32[]{:S(2)}) collective-permute-start(bf16[272,1152]{1,0:T(8,128)(2,1)S(1)} %pad.16.normed_a.normed_first), channel_id=1, source_target_pairs={{0,8},{1,9},{2,10},{3,11},{4,12},{5,13},{6,14},{7,15},{8,0},{9,1},... | collective-permute-start | bytes 1880072 | tf_op jit(solution)/shard_map/ppermute | solution.py:883
  151.0 20.6 %collective-permute-start.19 = (bf16[272,1152]{1,0:T(8,128)(2,1)S(1)}, bf16[272,1152]{1,0:T(8,128)(2,1)}, u32[]{:S(2)}, u32[]{:S(2)}) collective-permute-start(bf16[272,1152]{1,0:T(8,128)(2,1)S(1)} %get-tuple-element.182.refs_4_), channel_id=1, source_target_pairs={{0,16},{1,17},{2,18},{3,19},{4,20},{5,21},{6,22},{7,23},{8,24},{9,... | collective-permute-start | bytes 1880072 | tf_op jit(solution)/shard_map/ppermute | solution.py:883
  176.4 16.5 %collective-permute-start.21 = (bf16[272,1152]{1,0:T(8,128)(2,1)}, bf16[272,1152]{1,0:T(8,128)(2,1)}, u32[]{:S(2)}, u32[]{:S(2)}) collective-permute-start(bf16[272,1152]{1,0:T(8,128)(2,1)} %pad.17.refs_0_), channel_id=1, source_target_pairs={{0,16},{1,17},{2,18},{3,19},{4,20},{5,21},{6,22},{7,23},{8,24},{9,... | collective-permute-start | bytes 1880072 | tf_op jit(solution)/shard_map/ppermute | solution.py:883
  177.1 16.4 %collective-permute-start.24 = (bf16[272,1152]{1,0:T(8,128)(2,1)S(1)}, bf16[272,1152]{1,0:T(8,128)(2,1)}, u32[]{:S(2)}, u32[]{:S(2)}) collective-permute-start(bf16[272,1152]{1,0:T(8,128)(2,1)S(1)} %get-tuple-element.182.refs_4_), channel_id=1, source_target_pairs={{0,8},{1,9},{2,10},{3,11},{4,12},{5,13},{6,14},{7,15},{8,0},{9,1},... | collective-permute-start | bytes 1880072 | tf_op jit(solution)/shard_map/ppermute | solution.py:883
  177.1 16.4 %collective-permute-start.25 = (bf16[272,1152]{1,0:T(8,128)(2,1)}, bf16[272,1152]{1,0:T(8,128)(2,1)}, u32[]{:S(2)}, u32[]{:S(2)}) collective-permute-start(bf16[272,1152]{1,0:T(8,128)(2,1)} %collective-permute-done.19.refs_5_), channel_id=1, source_target_pairs={{0,8},{1,9},{2,10},{3,11},{4,12},{5,13},{6,14},{7,15},{8,0},{9,1},... | collective-permute-start | bytes 1880072 | tf_op jit(solution)/shard_map/ppermute | solution.py:883
  177.6 15.9 %collective-permute-start.22 = (bf16[272,1152]{1,0:T(8,128)(2,1)}, bf16[272,1152]{1,0:T(8,128)(2,1)}, u32[]{:S(2)}, u32[]{:S(2)}) collective-permute-start(bf16[272,1152]{1,0:T(8,128)(2,1)} %pad.17.refs_0_), channel_id=1, source_target_pairs={{0,8},{1,9},{2,10},{3,11},{4,12},{5,13},{6,14},{7,15},{8,0},{9,1},... | collective-permute-start | bytes 1880072 | tf_op jit(solution)/shard_map/ppermute | solution.py:883
  216.6 3.2 collective-permute-start.27
  216.8 30.5 %collective-permute-start.26 = (f32[272,1152]{1,0:T(8,128)}, f32[272,1152]{1,0:T(8,128)S(1)}, u32[]{:S(2)}, u32[]{:S(2)}) collective-permute-start(f32[272,1152]{1,0:T(8,128)} %get-tuple-element.186), channel_id=1, source_target_pairs={{0,8},{1,9},{2,10},{3,11},{4,12},{5,13},{6,14},{7,15},{8,0},{9,1},... | collective-permute-start | bytes 3760136 | tf_op jit(solution)/shard_map/ppermute | solution.py:883
  221.3 25.9 %collective-permute-start.28 = (bf16[272,1152]{1,0:T(8,128)(2,1)S(1)}, bf16[272,1152]{1,0:T(8,128)(2,1)S(1)}, u32[]{:S(2)}, u32[]{:S(2)}) collective-permute-start(bf16[272,1152]{1,0:T(8,128)(2,1)S(1)} %add.458), channel_id=1, source_target_pairs={{0,16},{1,17},{2,18},{3,19},{4,20},{5,21},{6,22},{7,23},{8,24},{9,... | collective-permute-start | bytes 1880072 | tf_op jit(solution)/shard_map/ppermute | solution.py:883
  244.6 41.7 %collective-permute-start.30 = (bf16[4,144,1152]{2,1,0:T(8,128)(2,1)}, bf16[4,144,1152]{2,1,0:T(8,128)(2,1)}, u32[]{:S(2)}, u32[]{:S(2)}) collective-permute-start(bf16[4,144,1152]{2,1,0:T(8,128)(2,1)} %get-tuple-element.202), channel_id=1, source_target_pairs={{0,1},{1,0},{2,3},{3,2},{4,5},{5,4},{6,7},{7,6},{8,9},{9,8},{10,11... | collective-permute-start | bytes 3981320 | tf_op jit(solution)/shard_map/ppermute | solution.py:883
  247.2 39.1 %collective-permute-start.31 = (bf16[2,2,144,1152]{3,2,1,0:T(8,128)(2,1)}, bf16[2,2,144,1152]{3,2,1,0:T(8,128)(2,1)}, u32[]{:S(2)}, u32[]{:S(2)}) collective-permute-start(bf16[2,2,144,1152]{3,2,1,0:T(8,128)(2,1)} %get-tuple-element.203), channel_id=1, source_target_pairs={{0,2},{1,3},{2,0},{3,1},{4,6},{5,7},{6,4},{7,5},{8,10},{9,11},{10,... | collective-permute-start | bytes 3981320 | tf_op jit(solution)/shard_map/ppermute | solution.py:883
  247.2 3.2 collective-permute-start.32
  251.4 35.0 %collective-permute-start.33 = (bf16[272,1152]{1,0:T(8,128)(2,1)}, bf16[272,1152]{1,0:T(8,128)(2,1)}, u32[]{:S(2)}, u32[]{:S(2)}) collective-permute-start(bf16[272,1152]{1,0:T(8,128)(2,1)} %add_convert_fusion.8), channel_id=1, source_target_pairs={{0,16},{1,17},{2,18},{3,19},{4,20},{5,21},{6,22},{7,23},{8,24},{9,... | collective-permute-start | bytes 1880072 | tf_op jit(solution)/shard_map/ppermute | solution.py:883
  252.6 38.7 %collective-permute-start.41 = (f32[272,1152]{1,0:T(8,128)}, f32[272,1152]{1,0:T(8,128)S(1)}, u32[]{:S(2)}, u32[]{:S(2)}) collective-permute-start(f32[272,1152]{1,0:T(8,128)} %get-tuple-element.219), channel_id=1, source_target_pairs={{0,8},{1,9},{2,10},{3,11},{4,12},{5,13},{6,14},{7,15},{8,0},{9,1},... | collective-permute-start | bytes 3760136 | tf_op jit(solution)/shard_map/ppermute | solution.py:883
  286.3 28.3 %collective-permute-start.34 = (bf16[2,144,1152]{2,1,0:T(8,128)(2,1)}, bf16[2,144,1152]{2,1,0:T(8,128)(2,1)S(1)}, u32[]{:S(2)}, u32[]{:S(2)}) collective-permute-start(bf16[2,144,1152]{2,1,0:T(8,128)(2,1)} %get-tuple-element.208), channel_id=1, source_target_pairs={{0,1},{1,0},{2,3},{3,2},{4,5},{5,4},{6,7},{7,6},{8,9},{9,8},{10,11... | collective-permute-start | bytes 1990664 | tf_op jit(solution)/shard_map/ppermute | solution.py:883
  286.6 6.1 %collective-permute-start.37 = (f32[272,1152]{1,0:T(8,128)S(1)}, f32[272,1152]{1,0:T(8,128)S(1)}, u32[]{:S(2)}, u32[]{:S(2)}) collective-permute-start(f32[272,1152]{1,0:T(8,128)S(1)} %copy-done.80), channel_id=1, source_target_pairs={{0,8},{1,9},{2,10},{3,11},{4,12},{5,13},{6,14},{7,15},{8,0},{9,1},... | collective-permute-start | bytes 3760136 | tf_op jit(solution)/shard_map/ppermute | solution.py:883
  288.8 29.4 %collective-permute-start.35 = (bf16[2,144,1152]{2,1,0:T(8,128)(2,1)S(1)}, bf16[2,144,1152]{2,1,0:T(8,128)(2,1)S(1)}, u32[]{:S(2)}, u32[]{:S(2)}) collective-permute-start(bf16[2,144,1152]{2,1,0:T(8,128)(2,1)S(1)} %slice_bitcast_fusion.2), channel_id=1, source_target_pairs={{0,1},{1,0},{2,3},{3,2},{4,5},{5,4},{6,7},{7,6},{8,9},{9,8},{10,11... | collective-permute-start | bytes 1990664 | tf_op jit(solution)/shard_map/ppermute | solution.py:883
  290.5 16.8 %collective-permute-start.39 = (bf16[2,144,1152]{2,1,0:T(8,128)(2,1)S(1)}, bf16[2,144,1152]{2,1,0:T(8,128)(2,1)S(1)}, u32[]{:S(2)}, u32[]{:S(2)}) collective-permute-start(bf16[2,144,1152]{2,1,0:T(8,128)(2,1)S(1)} %copy-done.81), channel_id=1, source_target_pairs={{0,16},{1,17},{2,18},{3,19},{4,20},{5,21},{6,22},{7,23},{8,24},{9,... | collective-permute-start | bytes 1990664 | tf_op jit(solution)/shard_map/ppermute | solution.py:883
  293.9 13.4 %collective-permute-start.38 = (bf16[272,1152]{1,0:T(8,128)(2,1)S(1)}, bf16[272,1152]{1,0:T(8,128)(2,1)S(1)}, u32[]{:S(2)}, u32[]{:S(2)}) collective-permute-start(bf16[272,1152]{1,0:T(8,128)(2,1)S(1)} %pad.19), channel_id=1, source_target_pairs={{0,8},{1,9},{2,10},{3,11},{4,12},{5,13},{6,14},{7,15},{8,0},{9,1},... | collective-permute-start | bytes 1880072 | tf_op jit(solution)/shard_map/ppermute | solution.py:883
  296.6 21.6 %collective-permute-start.36 = (bf16[2,144,1152]{2,1,0:T(8,128)(2,1)S(1)}, bf16[2,144,1152]{2,1,0:T(8,128)(2,1)S(1)}, u32[]{:S(2)}, u32[]{:S(2)}) collective-permute-start(bf16[2,144,1152]{2,1,0:T(8,128)(2,1)S(1)} %slice.236), channel_id=1, source_target_pairs={{0,2},{1,3},{2,0},{3,1},{4,6},{5,7},{6,4},{7,5},{8,10},{9,11},{10,... | collective-permute-start | bytes 1990664 | tf_op jit(solution)/shard_map/ppermute | solution.py:883
  308.5 3.9 collective-permute-start.40
  318.7 37.1 %collective-permute-start.43 = (bf16[4,258,432]{2,0,1:T(4,128)(2,1)S(1)}, bf16[4,258,432]{2,0,1:T(4,128)(2,1)S(1)}, u32[]{:S(2)}, u32[]{:S(2)}) collective-permute-start(bf16[4,258,432]{2,0,1:T(4,128)(2,1)S(1)} %copy.78), channel_id=1, source_target_pairs={{0,1},{1,0},{2,3},{3,2},{4,5},{5,4},{6,7},{7,6},{8,9},{9,8},{10,11... | collective-permute-start | bytes 2674952 | tf_op jit(solution)/shard_map/ppermute | solution.py:883
  319.1 10.8 %collective-permute-start.44 = (bf16[2,72,1152]{2,1,0:T(8,128)(2,1)S(1)}, bf16[2,72,1152]{2,1,0:T(8,128)(2,1)S(1)}, u32[]{:S(2)}, u32[]{:S(2)}) collective-permute-start(bf16[2,72,1152]{2,1,0:T(8,128)(2,1)S(1)} %get-tuple-element.480), channel_id=1, source_target_pairs={{0,16},{1,17},{2,18},{3,19},{4,20},{5,21},{6,22},{7,23},{8,24},{9,... | collective-permute-start | bytes 995336 | tf_op jit(solution)/shard_map/ppermute | solution.py:883
  320.0 30.9 %collective-permute-start.45 = (bf16[2,72,1152]{2,1,0:T(8,128)(2,1)S(1)}, bf16[2,72,1152]{2,1,0:T(8,128)(2,1)S(1)}, u32[]{:S(2)}, u32[]{:S(2)}) collective-permute-start(bf16[2,72,1152]{2,1,0:T(8,128)(2,1)S(1)} %get-tuple-element.479), channel_id=1, source_target_pairs={{0,1},{1,0},{2,3},{3,2},{4,5},{5,4},{6,7},{7,6},{8,9},{9,8},{10,11... | collective-permute-start | bytes 995336 | tf_op jit(solution)/shard_map/ppermute | solution.py:883
  322.0 34.8 %collective-permute-start.46 = (bf16[4,144,1152]{2,1,0:T(8,128)(2,1)S(1)}, bf16[4,144,1152]{2,1,0:T(8,128)(2,1)S(1)}, u32[]{:S(2)}, u32[]{:S(2)}) collective-permute-start(bf16[4,144,1152]{2,1,0:T(8,128)(2,1)S(1)} %pad_maximum_fusion.4), channel_id=1, source_target_pairs={{0,16},{1,17},{2,18},{3,19},{4,20},{5,21},{6,22},{7,23},{8,24},{9,... | collective-permute-start | bytes 3981320 | tf_op jit(solution)/shard_map/ppermute | solution.py:883
  323.8 32.1 %collective-permute-start.47 = (bf16[2,144,1152]{2,1,0:T(8,128)(2,1)S(1)}, bf16[2,144,1152]{2,1,0:T(8,128)(2,1)S(1)}, u32[]{:S(2)}, u32[]{:S(2)}) collective-permute-start(bf16[2,144,1152]{2,1,0:T(8,128)(2,1)S(1)} %fusion.25), channel_id=1, source_target_pairs={{0,4},{1,5},{2,6},{3,7},{4,0},{5,1},{6,2},{7,3},{8,12},{9,13},{10,... | collective-permute-start | bytes 1990664 | tf_op jit(solution)/shard_map/ppermute | solution.py:883
  357.9 37.4 %collective-permute-start.48 = (bf16[4,144,1152]{2,1,0:T(8,128)(2,1)S(1)}, bf16[4,144,1152]{2,1,0:T(8,128)(2,1)S(1)}, u32[]{:S(2)}, u32[]{:S(2)}) collective-permute-start(bf16[4,144,1152]{2,1,0:T(8,128)(2,1)S(1)} %pad_maximum_fusion.5), channel_id=1, source_target_pairs={{0,1},{1,0},{2,3},{3,2},{4,5},{5,4},{6,7},{7,6},{8,9},{9,8},{10,11... | collective-permute-start | bytes 3981320 | tf_op jit(solution)/shard_map/ppermute | solution.py:883
  360.2 26.4 %collective-permute-start.49 = (bf16[258,864]{1,0:T(8,128)(2,1)S(1)}, bf16[258,864]{1,0:T(8,128)(2,1)S(1)}, u32[]{:S(2)}, u32[]{:S(2)}) collective-permute-start(bf16[258,864]{1,0:T(8,128)(2,1)S(1)} %get-tuple-element.233), channel_id=1, source_target_pairs={{0,4},{1,5},{2,6},{3,7},{4,0},{5,1},{6,2},{7,3},{8,12},{9,13},{10,... | collective-permute-start | bytes 1337480 | tf_op jit(solution)/shard_map/ppermute | solution.py:883
  364.4 30.9 %collective-permute-start.50 = (bf16[258,864]{1,0:T(8,128)(2,1)S(1)}, bf16[258,864]{1,0:T(8,128)(2,1)S(1)}, u32[]{:S(2)}, u32[]{:S(2)}) collective-permute-start(bf16[258,864]{1,0:T(8,128)(2,1)S(1)} %get-tuple-element.234), channel_id=1, source_target_pairs={{0,2},{1,3},{2,0},{3,1},{4,6},{5,7},{6,4},{7,5},{8,10},{9,11},{10,... | collective-permute-start | bytes 1337480 | tf_op jit(solution)/shard_map/ppermute | solution.py:883
  364.4 30.9 %collective-permute-start.51 = (bf16[258,864]{1,0:T(8,128)(2,1)S(1)}, bf16[258,864]{1,0:T(8,128)(2,1)S(1)}, u32[]{:S(2)}, u32[]{:S(2)}) collective-permute-start(bf16[258,864]{1,0:T(8,128)(2,1)S(1)} %get-tuple-element.235), channel_id=1, source_target_pairs={{0,6},{1,7},{2,4},{3,5},{4,2},{5,3},{6,0},{7,1},{8,14},{9,15},{10,... | collective-permute-start | bytes 1337480 | tf_op jit(solution)/shard_map/ppermute | solution.py:883
  366.4 28.9 %collective-permute-start.52 = (bf16[2,144,1152]{2,1,0:T(8,128)(2,1)S(1)}, bf16[2,144,1152]{2,1,0:T(8,128)(2,1)S(1)}, u32[]{:S(2)}, u32[]{:S(2)}) collective-permute-start(bf16[2,144,1152]{2,1,0:T(8,128)(2,1)S(1)} %fusion.7), channel_id=1, source_target_pairs={{0,16},{1,17},{2,18},{3,19},{4,20},{5,21},{6,22},{7,23},{8,24},{9,... | collective-permute-start | bytes 1990664 | tf_op jit(solution)/shard_map/ppermute | solution.py:883
  397.2 21.2 %collective-permute-start.56 = (bf16[2,2,144,1152]{3,2,1,0:T(8,128)(2,1)}, bf16[2,2,144,1152]{3,2,1,0:T(8,128)(2,1)}, u32[]{:S(2)}, u32[]{:S(2)}) collective-permute-start(bf16[2,2,144,1152]{3,2,1,0:T(8,128)(2,1)} %get-tuple-element.476), channel_id=1, source_target_pairs={{0,8},{1,9},{2,10},{3,11},{4,12},{5,13},{6,14},{7,15},{8,0},{9,1},... | collective-permute-start | bytes 3981320 | tf_op jit(solution)/shard_map/ppermute | solution.py:883
  397.2 38.8 %collective-permute-start.59 = (f32[4,1152]{1,0:T(4,128)S(1)}, f32[4,1152]{1,0:T(4,128)S(1)}, u32[]{:S(2)}, u32[]{:S(2)}) collective-permute-start(f32[4,1152]{1,0:T(4,128)S(1)} %fusion.72), channel_id=1, source_target_pairs={{0,16},{1,17},{2,18},{3,19},{4,20},{5,21},{6,22},{7,23},{8,24},{9,... | collective-permute-start | bytes 55304 | tf_op jit(solution)/shard_map/ppermute | solution.py:883
  402.0 25.2 %collective-permute-start.53 = (bf16[2,144,1152]{2,1,0:T(8,128)(2,1)}, bf16[2,144,1152]{2,1,0:T(8,128)(2,1)}, u32[]{:S(2)}, u32[]{:S(2)}) collective-permute-start(bf16[2,144,1152]{2,1,0:T(8,128)(2,1)} %slice.246), channel_id=1, source_target_pairs={{0,2},{1,3},{2,0},{3,1},{4,6},{5,7},{6,4},{7,5},{8,10},{9,11},{10,... | collective-permute-start | bytes 1990664 | tf_op jit(solution)/shard_map/ppermute | solution.py:883
  411.6 17.1 %collective-permute-start.54 = (bf16[4,72,1152]{2,1,0:T(8,128)(2,1)}, bf16[4,72,1152]{2,1,0:T(8,128)(2,1)}, u32[]{:S(2)}, u32[]{:S(2)}) collective-permute-start(bf16[4,72,1152]{2,1,0:T(8,128)(2,1)} %pad_maximum_fusion.13), channel_id=1, source_target_pairs={{0,16},{1,17},{2,18},{3,19},{4,20},{5,21},{6,22},{7,23},{8,24},{9,... | collective-permute-start | bytes 1990664 | tf_op jit(solution)/shard_map/ppermute | solution.py:883
  413.1 16.8 %collective-permute-start.55 = (bf16[4,72,1152]{2,1,0:T(8,128)(2,1)}, bf16[4,72,1152]{2,1,0:T(8,128)(2,1)}, u32[]{:S(2)}, u32[]{:S(2)}) collective-permute-start(bf16[4,72,1152]{2,1,0:T(8,128)(2,1)} %pad_maximum_fusion.14), channel_id=1, source_target_pairs={{0,1},{1,0},{2,3},{3,2},{4,5},{5,4},{6,7},{7,6},{8,9},{9,8},{10,11... | collective-permute-start | bytes 1990664 | tf_op jit(solution)/shard_map/ppermute | solution.py:883
  431.3 16.6 %collective-permute-start.57 = (bf16[144,1152]{1,0:T(8,128)(2,1)S(1)}, bf16[144,1152]{1,0:T(8,128)(2,1)S(1)}, u32[]{:S(2)}, u32[]{:S(2)}) collective-permute-start(bf16[144,1152]{1,0:T(8,128)(2,1)S(1)} %slice_bitcast_fusion.4), channel_id=1, source_target_pairs={{0,4},{1,5},{2,6},{3,7},{4,0},{5,1},{6,2},{7,3},{8,12},{9,13},{10,... | collective-permute-start | bytes 995336 | tf_op jit(solution)/shard_map/ppermute | solution.py:883
  434.0 15.6 %collective-permute-start.58 = (bf16[2,72,1152]{2,1,0:T(8,128)(2,1)S(1)}, bf16[2,72,1152]{2,1,0:T(8,128)(2,1)S(1)}, u32[]{:S(2)}, u32[]{:S(2)}) collective-permute-start(bf16[2,72,1152]{2,1,0:T(8,128)(2,1)S(1)} %slice.252), channel_id=1, source_target_pairs={{0,2},{1,3},{2,0},{3,1},{4,6},{5,7},{6,4},{7,5},{8,10},{9,11},{10,... | collective-permute-start | bytes 995336 | tf_op jit(solution)/shard_map/ppermute | solution.py:883
  449.6 9.1 %collective-permute-start.60 = (bf16[144,1152]{1,0:T(8,128)(2,1)S(1)}, bf16[144,1152]{1,0:T(8,128)(2,1)S(1)}, u32[]{:S(2)}, u32[]{:S(2)}) collective-permute-start(bf16[144,1152]{1,0:T(8,128)(2,1)S(1)} %fusion.35), channel_id=1, source_target_pairs={{0,16},{1,17},{2,18},{3,19},{4,20},{5,21},{6,22},{7,23},{8,24},{9,... | collective-permute-start | bytes 995336 | tf_op jit(solution)/shard_map/ppermute | solution.py:883
  450.4 8.3 %collective-permute-start.61 = (bf16[72,1152]{1,0:T(8,128)(2,1)S(1)}, bf16[72,1152]{1,0:T(8,128)(2,1)S(1)}, u32[]{:S(2)}, u32[]{:S(2)}) collective-permute-start(bf16[72,1152]{1,0:T(8,128)(2,1)S(1)} %slice_bitcast_fusion.5), channel_id=1, source_target_pairs={{0,4},{1,5},{2,6},{3,7},{4,0},{5,1},{6,2},{7,3},{8,12},{9,13},{10,... | collective-permute-start | bytes 497672 | tf_op jit(solution)/shard_map/ppermute | solution.py:883
  460.3 7.6 %collective-permute-start.63 = (bf16[2,144,1152]{2,1,0:T(8,128)(2,1)}, bf16[2,144,1152]{2,1,0:T(8,128)(2,1)S(1)}, u32[]{:S(2)}, u32[]{:S(2)}) collective-permute-start(bf16[2,144,1152]{2,1,0:T(8,128)(2,1)} %get-tuple-element.485), channel_id=1, source_target_pairs={{0,8},{1,9},{2,10},{3,11},{4,12},{5,13},{6,14},{7,15},{8,0},{9,1},... | collective-permute-start | bytes 1990664 | tf_op jit(solution)/shard_map/ppermute | solution.py:883
  464.1 9.1 %collective-permute-start.62 = (bf16[72,1152]{1,0:T(8,128)(2,1)}, bf16[72,1152]{1,0:T(8,128)(2,1)S(1)}, u32[]{:S(2)}, u32[]{:S(2)}) collective-permute-start(bf16[72,1152]{1,0:T(8,128)(2,1)} %fusion.47), channel_id=1, source_target_pairs={{0,16},{1,17},{2,18},{3,19},{4,20},{5,21},{6,22},{7,23},{8,24},{9,... | collective-permute-start | bytes 497672 | tf_op jit(solution)/shard_map/ppermute | solution.py:883
  480.6 4.5 collective-permute-start.65
  485.1 7.3 %collective-permute-start.67 = (f32[15,1152]{1,0:T(8,128)S(1)}, f32[15,1152]{1,0:T(8,128)S(1)}, u32[]{:S(2)}, u32[]{:S(2)}) collective-permute-start(f32[15,1152]{1,0:T(8,128)S(1)} %add.505), channel_id=1, source_target_pairs={{0,4},{1,5},{2,6},{3,7},{4,0},{5,1},{6,2},{7,3},{8,12},{9,13},{10,... | collective-permute-start | bytes 207368 | tf_op jit(solution)/shard_map/ppermute | solution.py:883
  485.2 7.3 %collective-permute-start.68 = (f32[15,1152]{1,0:T(8,128)S(1)}, f32[15,1152]{1,0:T(8,128)S(1)}, u32[]{:S(2)}, u32[]{:S(2)}) collective-permute-start(f32[15,1152]{1,0:T(8,128)S(1)} %add.505), channel_id=1, source_target_pairs={{0,6},{1,7},{2,4},{3,5},{4,2},{5,3},{6,0},{7,1},{8,14},{9,15},{10,... | collective-permute-start | bytes 207368 | tf_op jit(solution)/shard_map/ppermute | solution.py:883
  486.9 6.1 %collective-permute-start.66 = (f32[15,1152]{1,0:T(8,128)S(1)}, f32[15,1152]{1,0:T(8,128)S(1)}, u32[]{:S(2)}, u32[]{:S(2)}) collective-permute-start(f32[15,1152]{1,0:T(8,128)S(1)} %add.505), channel_id=1, source_target_pairs={{0,2},{1,3},{2,0},{3,1},{4,6},{5,7},{6,4},{7,5},{8,10},{9,11},{10,... | collective-permute-start | bytes 207368 | tf_op jit(solution)/shard_map/ppermute | solution.py:883
  (90 other events, 728.5 us)
Sparse Core Ops, SparseCore 0:
  93.5 95.4 all-gather.2
